TPU v7x, 32 devices: a whole 2x2x4 slice. The times are simulated.
32 devices in a mesh: groups: 2 (over x), dp: 4 (over y, core), expert: 4 (over z).
Axes of the slice: x: 2, y: 2, z: 4, core: 2. Of those that a mesh axis runs over, the one named last changes fastest.
Arguments:
- query: bfloat16 [128, 4096], P(('groups', 'dp', 'expert')), parts along dimension 0, may hold values from -27 to 27
- fresh_kv: bfloat16 [128, 512], P(('groups', 'dp', 'expert')), parts along dimension 0, may hold values from -16 to 16
- cache: bfloat16 [128, 512, 512], P(('groups', 'dp', 'expert')), parts along dimension 0, may hold values from -6 to 6
- lengths: int32 [128], P(('groups', 'dp', 'expert')), parts along dimension 0, may hold values from 2 to 512, as said below
- moves: int32 [8, 4], P('groups'), parts along dimension 0, may hold values from 0 to 3, as said below
- residual: bfloat16 [128, 4096], P(('groups', 'dp', 'expert')), parts along dimension 0, may hold values from -4 to 4
- out_weight: bfloat16 [4096, 4096], P('expert'), may hold values from -0.09375 to 0.09375
- norm_gain: float32 [4096], replicated, may hold values from 0.1 to 1.9
- w_gate: bfloat16 [4, 4096, 1536], P('dp', None, 'expert'), may hold values from -0.09375 to 0.09375
- w_up: bfloat16 [4, 4096, 1536], P('dp', None, 'expert'), may hold values from -0.09375 to 0.09375
- w_down: bfloat16 [4, 1536, 4096], P('dp', 'expert'), may hold values from -0.15625 to 0.15625
- routes: int32 [128, 2], P(('groups', 'dp', 'expert')), parts along dimension 0, may hold values from 0 to 3, all different within a row; in each aligned block of 4 rows (0 to 3, 4 to 7, ...) at most 3 rows name the same one
- gates: float32 [128, 2], P(('groups', 'dp', 'expert')), parts along dimension 0, may hold values from 0.05 to 0.5
Outputs:
- layer_out: bfloat16 [128, 4096], P(('groups', 'dp', 'expert')), parts along dimension 0
There are 2 independent parts, one for each index of `groups`. A program takes and returns all parts, laid end to end along the dimension named above; an argument that names none is the same for every part. Nothing has to cross between parts.
Inputs may be any that keep to these rules, and one draw needn't show every extreme that they name: `lengths`: slot 0 of every device (the first of its 4 rows) holds 512 cached positions; other requests 2 to 512. For each expert index e, d -> moves[e, d] is one cycle through all 4 dp indices. `routes`: each row names 2 different experts; in the 4 rows of one device no expert is named by more than 3 rows, and in some device one expert is named by exactly 3.
All inputs are finite; a program needn't handle non-finite values.
Results may differ from a plain program's by a relative error of at most 0.0055.
Values may be sent and summed in bfloat16 or wider, within the bound.
No kernel may reach another device: no remote copies, remote signals or barrier semaphores. Data moves between devices by JAX's collectives and lax.ppermute only.
A program may use at most 128 MiB of HBM per device.

v0:
```python
import functools

import jax
import jax.numpy as jnp
from jax import lax
from jax.experimental import pallas as pl
from jax.experimental.pallas import tpu as pltpu
from jax.sharding import PartitionSpec as P


HD = 128
LANES = 128
NORM_EPS = 1e-06
F32 = jnp.float32
BF16 = jnp.bfloat16


def xor_exchange(blocks, axis, count):
    moved = list(blocks)
    for step in range(count - 1, 0, -1):
        moved[step] = lax.ppermute(blocks[step], axis, [(j, j ^ step) for j in range(count)])
    return moved


def spec(space=pltpu.VMEM):
    return pl.BlockSpec(memory_space=space)


def call(kernel, outs, ins, scratch=(), limit=None, flops=0, moved=0):
    many = isinstance(outs, (list, tuple))
    return pl.pallas_call(
        kernel,
        out_shape=outs,
        in_specs=ins,
        out_specs=[spec()] * len(outs) if many else spec(),
        scratch_shapes=list(scratch),
        compiler_params=pltpu.CompilerParams(vmem_limit_bytes=limit),
        cost_estimate=pl.CostEstimate(flops=flops, bytes_accessed=moved, transcendentals=0),
    )


def attend(q_row, fresh_row, keys_values, length, q_scr, put, kv_heads):
    heads = q_row.shape[1] // HD
    group = heads // kv_heads
    for h in range(heads):
        q_scr[h : h + 1, :] = q_row[:, h * HD : (h + 1) * HD].astype(F32)
    width = kv_heads * HD
    context = keys_values.shape[0]
    for g in range(kv_heads):
        q = q_scr[g * group : (g + 1) * group, :]
        keys = keys_values[:, g * HD : (g + 1) * HD]
        values = keys_values[:, width + g * HD : width + (g + 1) * HD]
        scores = (
            lax.dot_general(
                q.astype(BF16), keys, (((1,), (1,)), ((), ())), preferred_element_type=F32
            )
            * HD ** (-0.5)
        )
        if length is not None:
            valid = lax.broadcasted_iota(jnp.int32, (group, context), 1) < length
            scores = jnp.where(valid, scores, -1e30)
        top_cache = jnp.max(scores, axis=-1, keepdims=True)
        weights = jnp.exp(scores - top_cache)
        if length is not None:
            weights = jnp.where(valid, weights, 0.0)
        total = jnp.sum(weights, axis=-1, keepdims=True)
        mixed = jnp.dot(weights.astype(BF16), values, preferred_element_type=F32)
        own_key = fresh_row[:, g * HD : (g + 1) * HD].astype(F32)
        own_value = fresh_row[:, width + g * HD : width + (g + 1) * HD].astype(F32)
        own = jnp.sum(q * own_key, axis=-1, keepdims=True) * HD ** (-0.5)
        top = jnp.maximum(top_cache, own)
        cache_factor = jnp.exp(top_cache - top)
        own_factor = jnp.exp(own - top)
        done = (cache_factor * mixed + own_factor * own_value) / (
            cache_factor * total + own_factor
        )
        for j in range(group):
            put(g * group + j, done[j : j + 1, :])


def entry_kernel(
    n_dp, q_hbm, fresh_hbm, res_hbm, routes_hbm, gates_hbm, len_hbm, moves_hbm,
    row_ref, q_ref, fresh_ref, res_ref, ext_ref, info_ref, routes, gates, lengths, moves, sems,
):
    copies = [
        pltpu.make_async_copy(source, to, sems.at[i])
        for i, (source, to) in enumerate(
            [
                (routes_hbm, routes), (gates_hbm, gates), (q_hbm, q_ref),
                (fresh_hbm, fresh_ref), (res_hbm, res_ref), (len_hbm, lengths), (moves_hbm, moves),
            ]
        )
    ]
    for copy in copies:
        copy.start()
    copies[0].wait()
    copies[1].wait()
    top, tokens = routes.shape
    lane = lax.broadcasted_iota(jnp.int32, (1, ext_ref.shape[1]), 1)
    turn = jnp.where(lane >= n_dp, 1, 0) + jnp.where(lane >= 2 * n_dp, 1, 0)
    name = lane - n_dp * turn
    for t in range(tokens):
        share = jnp.zeros(lane.shape, F32)
        for k in range(top):
            share = jnp.where(name == routes[k, t], gates[k, t], share)
        high = share.astype(BF16).astype(F32)
        middle = (share - high).astype(BF16).astype(F32)
        low = share - high - middle
        share = jnp.where(turn == 0, high, jnp.where(turn == 1, middle, low))
        ext_ref[t : t + 1, :] = jnp.where(lane < 3 * n_dp, share, 0.0)
    for copy in copies[2:]:
        copy.wait()
    for t in range(tokens):
        info_ref[t : t + 1, :] = jnp.full((1, LANES), lengths[t], jnp.int32)
    dp = lax.axis_index("dp")
    rel = moves[lax.axis_index("expert"), dp] ^ dp
    info_ref[tokens : tokens + 1, :] = jnp.full((1, LANES), rel, jnp.int32)
    model, width = q_ref.shape[1], fresh_ref.shape[1]
    row_ref[:, :model] = q_ref[0:1, :]
    row_ref[:, model : model + width] = fresh_ref[0:1, :]
    row_ref[:, model + width : 2 * model + width] = res_ref[0:1, :]
    row_ref[:, 2 * model + width :] = ext_ref[0:1, :].astype(BF16)


def fetch(source, to, sems, rows_from=0, pieces=4):
    rows = to.shape[0]
    step = rows // pieces
    return [
        pltpu.make_async_copy(
            source.at[pl.ds(rows_from + i * step, step)], to.at[pl.ds(i * step, step)], sems.at[i]
        )
        for i in range(pieces)
    ]


def local_kernel(
    kv_heads, info_ref, q_ref, fresh_ref, cache_hbm, w_hbm,
    att_ref, kv0_ref, w_ref, kv, q_scr, sems, w_sems,
):
    parts, tokens, part = att_ref.shape
    per = part // HD
    copies = [
        pltpu.make_async_copy(cache_hbm.at[t], kv.at[t - 1] if t else kv0_ref, sems.at[t])
        for t in range(tokens)
    ]
    weight = fetch(w_hbm, w_ref, w_sems)
    for copy in copies[1:] + copies[:1] + weight:
        copy.start()
    for t in range(1, tokens):
        copies[t].wait()

        def put(head, row, t=t):
            att_ref[head // per, t : t + 1, (head % per) * HD : (head % per + 1) * HD] = row

        attend(
            q_ref[t : t + 1, :], fresh_ref[t : t + 1, :], kv.at[t - 1],
            info_ref[t : t + 1, 0:1], q_scr.at[t], put, kv_heads,
        )
    for s in range(parts):
        att_ref[s, 0:1, :] = jnp.zeros((1, part), F32)
    for copy in copies[:1] + weight:
        copy.wait()


def fetch_kernel(rows_from, source, to, sems):
    copies = fetch(source, to, sems, rows_from)
    for copy in copies:
        copy.start()
    for copy in copies:
        copy.wait()


def fetched(source, rows, rows_from):
    return call(
        functools.partial(fetch_kernel, rows_from),
        jax.ShapeDtypeStruct((rows,) + source.shape[1:], source.dtype),
        [spec(pltpu.HBM)],
        scratch=[pltpu.SemaphoreType.DMA((4,))],
        limit=1 << 20,
        moved=source.size // source.shape[0] * rows * 4,
    )(in_hbm(source))


def in_hbm(array):
    return pltpu.with_memory_space_constraint(array, pltpu.HBM)


def moved_kernel(n_dp, n_ex, kv_heads, width, *refs):
    info_ref = refs[0]
    rows = refs[1 : 1 + n_dp]
    att_ref, kv0_ref, res_ref, ext_ref = refs[1 + n_dp : 5 + n_dp]
    outs = refs[5 + n_dp : 5 + n_dp + n_ex]
    base_ref, ext_out, row_scr, q_scr, full = refs[5 + n_dp + n_ex :]
    ex = lax.axis_index("expert")
    tokens = res_ref.shape[0]
    rel = info_ref[tokens : tokens + 1, 0:1]
    row = rows[0][...].astype(F32)
    for r in range(1, n_dp):
        row = jnp.where(rel == r, rows[r][...].astype(F32), row)
    row_scr[...] = row
    model = res_ref.shape[1]
    full[...] = att_ref[...]
    part = full.shape[2]
    per = part // HD

    def put(head, value):
        full[head // per, 0:1, (head % per) * HD : (head % per + 1) * HD] = value

    attend(
        row_scr[:, :model], row_scr[:, model : model + width], kv0_ref,
        None, q_scr, put, kv_heads,
    )
    for s in range(n_ex):
        outs[s][...] = full[s ^ ex].astype(BF16)
    first = lax.broadcasted_iota(jnp.int32, (res_ref.shape[0], 1), 0) == 0
    base_ref[...] = jnp.where(first, row_scr[:, model + width : 2 * model + width], res_ref[...].astype(F32))
    ext_out[...] = jnp.where(first, row_scr[:, 2 * model + width :], ext_ref[...])


def project_kernel(n_ex, *refs):
    blocks, w_refs, outs, lhs = refs[:n_ex], refs[n_ex : n_ex + 2], refs[n_ex + 2 : -1], refs[-1]
    tokens = blocks[0].shape[0]
    for s in range(n_ex):
        lhs[s * tokens : (s + 1) * tokens, :] = blocks[s][...].astype(F32)
    left = lhs[...].astype(BF16)
    early, model = w_refs[0].shape
    chunk = min(1024, model)
    for at in range(0, model, chunk):
        out = jnp.dot(
            left[:, :early], w_refs[0][:, at : at + chunk], preferred_element_type=F32
        ) + jnp.dot(left[:, early:], w_refs[1][:, at : at + chunk], preferred_element_type=F32)
        for s in range(n_ex):
            outs[s][:, at : at + chunk] = out[s * tokens : (s + 1) * tokens, :].astype(outs[s].dtype)


def norm_kernel(n_ex, n_dp, *refs):
    parts, base_ref, ext_ref, gain_ref = refs[:n_ex], *refs[n_ex : n_ex + 3]
    hid_ref, pay_ref = refs[n_ex + 3 :]
    hidden = base_ref[...]
    for s in range(n_ex):
        hidden = hidden + parts[s][...].astype(F32)
    hid_ref[...] = hidden
    model = hidden.shape[1]
    mean = jnp.mean(hidden * hidden, axis=-1, keepdims=True) + NORM_EPS
    normed = hidden * lax.rsqrt(mean) * gain_ref[...]
    pay_ref[:, :model] = normed.astype(BF16)
    ext = ext_ref[...]
    root = jnp.sqrt(mean)
    high = root.astype(BF16).astype(F32)
    middle = (root - high).astype(BF16).astype(F32)
    low = root - high - middle
    lane = lax.broadcasted_iota(jnp.int32, ext.shape, 1)
    at = 3 * n_dp
    ext = jnp.where(lane == at, high, ext)
    ext = jnp.where(lane == at + 1, middle, ext)
    ext = jnp.where(lane == at + 2, low, ext)
    pay_ref[:, model:] = ext.astype(BF16)


def expert_kernel(n_dp, n_ex, tokens, *refs):
    moves_ref = refs[0]
    pieces = refs[1 : 1 + n_dp]
    gate_ref, up_ref, down_ref, gain_ref, hid_ref = refs[1 + n_dp : 6 + n_dp]
    outs = refs[6 + n_dp : 6 + 2 * n_dp]
    real_ref, lhs, act_scr, new_scr = refs[6 + 2 * n_dp :]
    dp = lax.axis_index("dp")
    ex = lax.axis_index("expert")
    model = gain_ref.shape[1]
    rows = n_ex * tokens
    coef = []
    source = 0
    for d in range(n_dp):
        source = jnp.where(moves_ref[ex, d] == dp, d, source)
    rel = source ^ dp
    carried = jnp.zeros((1, pieces[0].shape[1]), F32)
    for r in range(n_dp):
        lhs[r * rows : (r + 1) * rows, :] = pieces[r][:, :model]
        ext = pieces[r][:, model:].astype(F32)
        lane = lax.broadcasted_iota(jnp.int32, ext.shape, 1)
        mine = (lane == dp) | (lane == dp + n_dp) | (lane == dp + 2 * n_dp)
        coef.append(jnp.sum(jnp.where(mine, ext, 0.0), axis=-1, keepdims=True))
        carried = jnp.where(rel == r, pieces[r][0:tokens, :].astype(F32)[0:1, :], carried)
    tail = carried[:, model:]
    lane = lax.broadcasted_iota(jnp.int32, tail.shape, 1)
    root = jnp.sum(
        jnp.where((lane >= 3 * n_dp) & (lane < 3 * n_dp + 3), tail, 0.0), axis=-1, keepdims=True
    )
    first = lax.broadcasted_iota(jnp.int32, (tokens, 1), 0) == 0
    real_ref[...] = jnp.where(first, carried[:, :model] * root / gain_ref[...], hid_ref[...])
    x = lhs[...]
    gate = jnp.dot(x, gate_ref[0], preferred_element_type=F32)
    up = jnp.dot(x, up_ref[0], preferred_element_type=F32)
    act = gate / (1.0 + jnp.exp(-gate)) * up
    for r in range(n_dp):
        act_scr[r * rows : (r + 1) * rows, :] = coef[r] * act[r * rows : (r + 1) * rows, :]
    new_scr[...] = act_scr[...]
    for r in range(n_dp):
        for s in range(n_ex):
            to = ((moves_ref[ex ^ s, dp ^ r] ^ dp) * n_ex + s) * tokens
            at = (r * n_ex + s) * tokens
            new_scr[pl.ds(to, 1), :] = act_scr[at : at + 1, :]
    left = new_scr[...].astype(BF16)
    chunk = min(1024, model)
    for at in range(0, model, chunk):
        out = jnp.dot(left, down_ref[:, at : at + chunk], preferred_element_type=F32)
        for r in range(n_dp):
            outs[r][:, at : at + chunk] = out[r * rows : (r + 1) * rows, :].astype(outs[r].dtype)


def per_device(
    query, fresh_kv, cache, lengths, moves, residual, out_weight, norm_gain,
    w_gate, w_up, w_down, routes, gates,
):
    n_dp = lax.axis_size("dp")
    n_ex = lax.axis_size("expert")
    tokens, model = query.shape
    width = fresh_kv.shape[1] // 2
    kv_heads = width // HD
    part = out_weight.shape[0]
    context = cache.shape[1]
    shape = jax.ShapeDtypeStruct

    ext_width = -(-(3 * n_dp + 3) // LANES) * LANES
    top_count = routes.shape[1]
    small = (query, fresh_kv, residual, routes.T, gates.T, lengths, moves)
    row, q_in, fresh_in, res_in, ext, info = call(
        functools.partial(entry_kernel, n_dp),
        [
            shape((1, 2 * model + 2 * width + ext_width), BF16),
            shape(query.shape, BF16),
            shape(fresh_kv.shape, BF16),
            shape(residual.shape, BF16),
            shape((tokens, ext_width), F32),
            shape((2 * tokens, LANES), jnp.int32),
        ],
        [spec(pltpu.HBM)] * len(small),
        scratch=[
            pltpu.SMEM((top_count, tokens), jnp.int32),
            pltpu.SMEM((top_count, tokens), F32),
            pltpu.SMEM(lengths.shape, jnp.int32),
            pltpu.SMEM(moves.shape, jnp.int32),
            pltpu.SemaphoreType.DMA((len(small),)),
        ],
        limit=4 << 20,
        moved=tokens * model * 4,
    )(*map(in_hbm, small))
    rows = xor_exchange([row] * n_dp, "dp", n_dp)

    early = part // 2
    att, kv0, out_early = call(
        functools.partial(local_kernel, kv_heads),
        [
            shape((n_ex, tokens, part), F32),
            shape(cache.shape[1:], BF16),
            shape((early, model), BF16),
        ],
        [spec()] * 3 + [spec(pltpu.HBM)] * 2,
        scratch=[
            pltpu.VMEM((tokens - 1,) + cache.shape[1:], BF16),
            pltpu.VMEM((tokens, model // HD, HD), F32),
            pltpu.SemaphoreType.DMA((tokens,)),
            pltpu.SemaphoreType.DMA((4,)),
        ],
        limit=6 << 20,
        flops=4 * tokens * model * context,
        moved=cache.size * 2 + early * model * 2,
    )(info, q_in, fresh_in, in_hbm(cache), in_hbm(out_weight))

    moved = call(
        functools.partial(moved_kernel, n_dp, n_ex, kv_heads, 2 * width),
        [shape((tokens, part), BF16)] * n_ex
        + [shape((tokens, model), F32), shape((tokens, ext_width), F32)],
        [spec()] * (n_dp + 5),
        scratch=[
            pltpu.VMEM(row.shape, F32),
            pltpu.VMEM((model // HD, HD), F32),
            pltpu.VMEM((n_ex, tokens, part), F32),
        ],
        limit=6 << 20,
        flops=4 * model * context,
        moved=cache.size // tokens * 2,
    )(info, *rows, att, kv0, res_in, ext)
    blocks = xor_exchange(moved[:n_ex], "expert", n_ex)
    base, ext_all = moved[n_ex:]

    out_late = fetched(out_weight, part - early, early)
    partials = call(
        functools.partial(project_kernel, n_ex),
        [shape((tokens, model), F32)] + [shape((tokens, model), BF16)] * (n_ex - 1),
        [spec()] * (n_ex + 2),
        scratch=[pltpu.VMEM((n_ex * tokens, part), F32)],
        limit=4 << 20,
        flops=2 * n_ex * tokens * part * model,
        moved=out_weight.size * 2,
    )(*blocks, out_early, out_late)
    partials = xor_exchange(partials, "expert", n_ex)

    down = fetched(w_down[0], w_down.shape[1], 0)

    hidden, payload = call(
        functools.partial(norm_kernel, n_ex, n_dp),
        [shape((tokens, model), F32), shape((tokens, model + ext_width), BF16)],
        [spec()] * (n_ex + 3),
        limit=4 << 20,
        flops=10 * tokens * model,
        moved=tokens * model * 16,
    )(*partials, base, ext_all, norm_gain[None])
    gathered = xor_exchange([payload] * n_ex, "expert", n_ex)
    pieces = {0: jnp.concatenate(gathered, axis=0)}
    bits = [1 << b for b in range(n_dp.bit_length() - 1)]
    for bit in reversed(bits):
        for r in list(pieces):
            pieces[r | bit] = lax.ppermute(
                pieces[r], "dp", [(j, j ^ bit) for j in range(n_dp)]
            )

    group_rows = n_ex * tokens
    all_rows = n_dp * group_rows
    hidden_units = w_down.shape[1]
    weights_bytes = (w_gate.size + w_up.size + w_down.size) * 2
    done = call(
        functools.partial(expert_kernel, n_dp, n_ex, tokens),
        [shape((group_rows, model), BF16)] * n_dp + [shape((tokens, model), F32)],
        [spec(pltpu.SMEM)] + [spec()] * (n_dp + 5),
        scratch=[
            pltpu.VMEM((all_rows, model), BF16),
            pltpu.VMEM((all_rows, hidden_units), F32),
            pltpu.VMEM((all_rows, hidden_units), F32),
        ],
        limit=(8 << 20) + all_rows * model * 8,
        flops=6 * all_rows * model * hidden_units,
        moved=weights_bytes,
    )(moves, *[pieces[r] for r in range(n_dp)], w_gate, w_up, down, norm_gain[None], hidden)
    sums = {r: done[r] for r in range(n_dp)}
    real = done[n_dp]
    for bit in bits:
        for r in sorted((r for r in sums if r & bit), reverse=True):
            got = lax.ppermute(sums.pop(r), "dp", [(j, j ^ bit) for j in range(n_dp)])
            total = sums[r ^ bit].astype(F32) + got.astype(F32)
            sums[r ^ bit] = total.astype(BF16) if r ^ bit else total
    mixed = sums[0].reshape(n_ex, tokens, model)
    back = xor_exchange(
        [mixed[0]] + [mixed[s].astype(BF16) for s in range(1, n_ex)], "expert", n_ex
    )
    total = real
    for s in range(n_ex):
        total = total + back[s].astype(F32)
    return total.astype(BF16)


def solution(mesh):
    placed = (
        P(("groups", "dp", "expert"), None),
        P(("groups", "dp", "expert"), None),
        P(("groups", "dp", "expert"), None, None),
        P(("groups", "dp", "expert")),
        P("groups", None),
        P(("groups", "dp", "expert"), None),
        P("expert", None),
        P(),
        P("dp", None, "expert"),
        P("dp", None, "expert"),
        P("dp", "expert", None),
        P(("groups", "dp", "expert"), None),
        P(("groups", "dp", "expert"), None),
    )

    return jax.shard_map(
        per_device,
        mesh=mesh,
        in_specs=placed,
        out_specs=P(("groups", "dp", "expert"), None),
        check_vma=False,
    )
```

profile of v0, /device:TPU:0, one launch (start us, length us, event | category | flops | bytes accessed | tf_op | source)
XLA Modules:
  0.0 61.2 jit_solution(5694727288784651323)
XLA Ops:
  1.5 2.6 %collective-permute-start.1 = (bf16[1,8832]{1,0:T(2,128)(2,1)S(1)}, bf16[1,8832]{1,0:T(2,128)(2,1)S(1)}, u32[]{:S(2)}, u32[]{:S(2)}) collective-permute-start(bf16[1,8832]{1,0:T(2,128)(2,1)S(1)} %get-tuple-element.32.refs_1_), channel_id=1, source_target_pairs={{0,8},{4,12},{8,0},{12,4},{1,9},{5,13},{9,1},{13,5},{2,10},{6,14},... | collective-permute-start | bytes 53000 | tf_op jit(solution)/shard_map/ppermute | solution.py:21
  4.1 2.9 %shard_map.128 = (f32[4,4,1024]{2,1,0:T(4,128)S(1)}, bf16[512,512]{1,0:T(8,128)(2,1)S(1)}, bf16[512,4096]{1,0:T(8,128)(2,1)S(1)}) custom-call(s32[8,128]{1,0:T(8,128)S(1)} %get-tuple-element.31.info_ref.refs_0_, bf16[4,4096]{1,0:T(4,128)(2,1)S(1)} %get-tuple-element.33.q_ref, bf16[4,512]{1,0:T(4,128)(2,1)S(1)} %get-tuple-element.34.fresh_ref, ...), custom_call_target="tpu_custom_call" | custom-call | flops 33554432 | bytes 6291456 | tf_op jit(solution)/shard_map/pallas_call | solution.py:350
  8.2 1.6 %collective-permute-start.3 = (bf16[4,1024]{1,0:T(4,128)(2,1)S(1)}, bf16[4,1024]{1,0:T(4,128)(2,1)S(1)}, u32[]{:S(2)}, u32[]{:S(2)}) collective-permute-start(bf16[4,1024]{1,0:T(4,128)(2,1)S(1)} %get-tuple-element.40), channel_id=1, source_target_pairs={{0,1},{1,0},{2,3},{3,2},{4,5},{5,4},{6,7},{7,6},{8,9},{9,8},{10,11... | collective-permute-start | bytes 24584 | tf_op jit(solution)/shard_map/ppermute | solution.py:21
  9.9 2.6 %collective-permute-start.4 = (bf16[4,1024]{1,0:T(4,128)(2,1)S(1)}, bf16[4,1024]{1,0:T(4,128)(2,1)S(1)}, u32[]{:S(2)}, u32[]{:S(2)}) collective-permute-start(bf16[4,1024]{1,0:T(4,128)(2,1)S(1)} %get-tuple-element.41), channel_id=1, source_target_pairs={{0,2},{1,3},{2,0},{3,1},{4,6},{5,7},{6,4},{7,5},{8,10},{9,11},{10,... | collective-permute-start | bytes 24584 | tf_op jit(solution)/shard_map/ppermute | solution.py:21
  12.7 2.2 %shard_map.130.refs_5_ = bf16[512,4096]{1,0:T(8,128)(2,1)S(1)} custom-call(bf16[1024,4096]{1,0:T(8,128)(2,1)} %source.1), custom_call_target="tpu_custom_call" | custom-call | bytes 8388608 | tf_op jit(solution)/shard_map/pallas_call | solution.py:174
  14.9 3.0 %collective-permute-done.5.refs_3_ = bf16[4,1024]{1,0:T(4,128)(2,1)S(1)} collective-permute-done((bf16[4,1024]{1,0:T(4,128)(2,1)S(1)}, bf16[4,1024]{1,0:T(4,128)(2,1)S(1)}, u32[]{:S(2)}, u32[]{:S(2)}) %collective-permute-start.5) | collective-permute-done | bytes 8224 | tf_op jit(solution)/shard_map/ppermute | solution.py:21
  17.9 1.2 %shard_map.131 = (f32[4,4096]{1,0:T(4,128)S(1)}, bf16[4,4096]{1,0:T(4,128)(2,1)S(1)}, bf16[4,4096]{1,0:T(4,128)(2,1)S(1)}, bf16[4,4096]{1,0:T(4,128)(2,1)S(1)}) custom-call(bf16[4,1024]{1,0:T(4,128)(2,1)S(1)} %get-tuple-element.39.refs_0_, bf16[4,1024]{1,0:T(4,128)(2,1)S(1)} %collective-permute-done.3.refs_1_, ...), custom_call_target="tpu_custom_call" | custom-call | flops 134217728 | bytes 8388608 | tf_op jit(solution)/shard_map/pallas_call | solution.py:387
  19.1 1.2 %collective-permute-start.7 = (bf16[4,4096]{1,0:T(4,128)(2,1)S(1)}, bf16[4,4096]{1,0:T(4,128)(2,1)S(1)}, u32[]{:S(2)}, u32[]{:S(2)}) collective-permute-start(bf16[4,4096]{1,0:T(4,128)(2,1)S(1)} %get-tuple-element.46), channel_id=1, source_target_pairs={{0,2},{1,3},{2,0},{3,1},{4,6},{5,7},{6,4},{7,5},{8,10},{9,11},{10,... | collective-permute-start | bytes 98312 | tf_op jit(solution)/shard_map/ppermute | solution.py:21
  20.3 3.2 %collective-permute-start.8 = (bf16[4,4096]{1,0:T(4,128)(2,1)S(1)}, bf16[4,4096]{1,0:T(4,128)(2,1)S(1)}, u32[]{:S(2)}, u32[]{:S(2)}) collective-permute-start(bf16[4,4096]{1,0:T(4,128)(2,1)S(1)} %get-tuple-element.47), channel_id=1, source_target_pairs={{0,3},{1,2},{2,1},{3,0},{4,7},{5,6},{6,5},{7,4},{8,11},{9,10},{10,... | collective-permute-start | bytes 98312 | tf_op jit(solution)/shard_map/ppermute | solution.py:21
  24.2 1.8 %collective-permute-done.8.refs_3_ = bf16[4,4096]{1,0:T(4,128)(2,1)S(1)} collective-permute-done((bf16[4,4096]{1,0:T(4,128)(2,1)S(1)}, bf16[4,4096]{1,0:T(4,128)(2,1)S(1)}, u32[]{:S(2)}, u32[]{:S(2)}) %collective-permute-start.8) | collective-permute-done | bytes 32800 | tf_op jit(solution)/shard_map/ppermute | solution.py:21
  26.3 3.4 %collective-permute-start.11 = (bf16[4,4224]{1,0:T(4,128)(2,1)S(1)}, bf16[4,4224]{1,0:T(4,128)(2,1)S(1)}, u32[]{:S(2)}, u32[]{:S(2)}) collective-permute-start(bf16[4,4224]{1,0:T(4,128)(2,1)S(1)} %get-tuple-element.50), channel_id=1, source_target_pairs={{0,3},{1,2},{2,1},{3,0},{4,7},{5,6},{6,5},{7,4},{8,11},{9,10},{10,... | collective-permute-start | bytes 101384 | tf_op jit(solution)/shard_map/ppermute | solution.py:21
  30.1 1.0 %collective-permute-done.10 = bf16[4,4224]{1,0:T(4,128)(2,1)S(1)} collective-permute-done((bf16[4,4224]{1,0:T(4,128)(2,1)S(1)}, bf16[4,4224]{1,0:T(4,128)(2,1)S(1)}, u32[]{:S(2)}, u32[]{:S(2)}) %collective-permute-start.10) | collective-permute-done | bytes 33824 | tf_op jit(solution)/shard_map/ppermute | solution.py:21
  31.1 1.0 %collective-permute-done.11 = bf16[4,4224]{1,0:T(4,128)(2,1)S(1)} collective-permute-done((bf16[4,4224]{1,0:T(4,128)(2,1)S(1)}, bf16[4,4224]{1,0:T(4,128)(2,1)S(1)}, u32[]{:S(2)}, u32[]{:S(2)}) %collective-permute-start.11) | collective-permute-done | bytes 33824 | tf_op jit(solution)/shard_map/ppermute | solution.py:21
  32.1 1.5 %collective-permute-done.9 = bf16[4,4224]{1,0:T(4,128)(2,1)S(1)} collective-permute-done((bf16[4,4224]{1,0:T(4,128)(2,1)S(1)}, bf16[4,4224]{1,0:T(4,128)(2,1)S(1)}, u32[]{:S(2)}, u32[]{:S(2)}) %collective-permute-start.9) | collective-permute-done | bytes 33824 | tf_op jit(solution)/shard_map/ppermute | solution.py:21
  33.6 1.7 %collective-permute-start.13 = (bf16[16,4224]{1,0:T(8,128)(2,1)S(1)}, bf16[16,4224]{1,0:T(8,128)(2,1)S(1)}, u32[]{:S(2)}, u32[]{:S(2)}) collective-permute-start(bf16[16,4224]{1,0:T(8,128)(2,1)S(1)} %pad_maximum_fusion.refs_1_), channel_id=1, source_target_pairs={{0,8},{4,12},{8,0},{12,4},{1,9},{5,13},{9,1},{13,5},{2,10},{6,14},... | collective-permute-start | bytes 405512 | tf_op jit(solution)/shard_map/ppermute | solution.py:413
  35.3 3.4 %collective-permute-done.13.refs_3_ = bf16[16,4224]{1,0:T(8,128)(2,1)S(1)} collective-permute-done((bf16[16,4224]{1,0:T(8,128)(2,1)S(1)}, bf16[16,4224]{1,0:T(8,128)(2,1)S(1)}, u32[]{:S(2)}, u32[]{:S(2)}) %collective-permute-start.13) | collective-permute-done | bytes 135200 | tf_op jit(solution)/shard_map/ppermute | solution.py:413
  38.7 2.0 %shard_map.133.refs_7_ = bf16[384,4096]{1,0:T(8,128)(2,1)S(1)} custom-call(bf16[384,4096]{1,0:T(8,128)(2,1)} %bitcast.6), custom_call_target="tpu_custom_call" | custom-call | bytes 6291456 | tf_op jit(solution)/shard_map/pallas_call | solution.py:174
  42.5 2.4 %shard_map.134 = (bf16[16,4096]{1,0:T(8,128)(2,1)S(1)}, bf16[16,4096]{1,0:T(8,128)(2,1)S(1)}, bf16[16,4096]{1,0:T(8,128)(2,1)S(1)}, bf16[16,4096]{1,0:T(8,128)(2,1)S(1)}, f32[4,4096]{1,0:T(4,128)S(1)}) custom-call(s32[4,4]{1,0:T(4,128)S(1)} %copy-done.3, bf16[16,4224]{1,0:T(8,128)(2,1)S(1)} %pad_maximum_fusion.refs_1_, ...), custom_call_target="tpu_custom_call" | custom-call | flops 603979776 | bytes 9437184 | tf_op jit(solution)/shard_map/pallas_call | solution.py:421
  46.5 1.7 %collective-permute-start.17 = (bf16[16,4096]{1,0:T(8,128)(2,1)S(1)}, bf16[16,4096]{1,0:T(8,128)(2,1)S(1)}, u32[]{:S(2)}, u32[]{:S(2)}) collective-permute-start(bf16[16,4096]{1,0:T(8,128)(2,1)S(1)} %add_convert_fusion), channel_id=1, source_target_pairs={{0,8},{4,12},{8,0},{12,4},{1,9},{5,13},{9,1},{13,5},{2,10},{6,14},... | collective-permute-start | bytes 393224 | tf_op jit(solution)/shard_map/ppermute | solution.py:438
  48.2 4.1 %collective-permute-done.17 = bf16[16,4096]{1,0:T(8,128)(2,1)S(1)} collective-permute-done((bf16[16,4096]{1,0:T(8,128)(2,1)S(1)}, bf16[16,4096]{1,0:T(8,128)(2,1)S(1)}, u32[]{:S(2)}, u32[]{:S(2)}) %collective-permute-start.17) | collective-permute-done | bytes 131104 | tf_op jit(solution)/shard_map/ppermute | solution.py:438
  53.0 1.9 %collective-permute-start.19 = (bf16[4,4096]{1,0:T(4,128)(2,1)S(1)}, bf16[4,4096]{1,0:T(4,128)(2,1)S(1)}, u32[]{:S(2)}, u32[]{:S(2)}) collective-permute-start(bf16[4,4096]{1,0:T(4,128)(2,1)S(1)} %get-tuple-element.61), channel_id=1, source_target_pairs={{0,2},{1,3},{2,0},{3,1},{4,6},{5,7},{6,4},{7,5},{8,10},{9,11},{10,... | collective-permute-start | bytes 98312 | tf_op jit(solution)/shard_map/ppermute | solution.py:21
  54.9 2.0 %collective-permute-start.20 = (bf16[4,4096]{1,0:T(4,128)(2,1)S(1)}, bf16[4,4096]{1,0:T(4,128)(2,1)S(1)}, u32[]{:S(2)}, u32[]{:S(2)}) collective-permute-start(bf16[4,4096]{1,0:T(4,128)(2,1)S(1)} %get-tuple-element.60), channel_id=1, source_target_pairs={{0,3},{1,2},{2,1},{3,0},{4,7},{5,6},{6,5},{7,4},{8,11},{9,10},{10,... | collective-permute-start | bytes 98312 | tf_op jit(solution)/shard_map/ppermute | solution.py:21
  56.9 1.3 %collective-permute-done.19 = bf16[4,4096]{1,0:T(4,128)(2,1)S(1)} collective-permute-done((bf16[4,4096]{1,0:T(4,128)(2,1)S(1)}, bf16[4,4096]{1,0:T(4,128)(2,1)S(1)}, u32[]{:S(2)}, u32[]{:S(2)}) %collective-permute-start.19) | collective-permute-done | bytes 32800 | tf_op jit(solution)/shard_map/ppermute | solution.py:21
  58.1 2.4 %collective-permute-done.20 = bf16[4,4096]{1,0:T(4,128)(2,1)S(1)} collective-permute-done((bf16[4,4096]{1,0:T(4,128)(2,1)S(1)}, bf16[4,4096]{1,0:T(4,128)(2,1)S(1)}, u32[]{:S(2)}, u32[]{:S(2)}) %collective-permute-start.20) | collective-permute-done | bytes 32800 | tf_op jit(solution)/shard_map/ppermute | solution.py:21
  (39 shorter events, 9.0 us)
Async XLA Ops:
  0.9 6.1 %collective-permute-start = (bf16[1,8832]{1,0:T(2,128)(2,1)S(1)}, bf16[1,8832]{1,0:T(2,128)(2,1)S(1)}, u32[]{:S(2)}, u32[]{:S(2)}) collective-permute-start(bf16[1,8832]{1,0:T(2,128)(2,1)S(1)} %get-tuple-element.32.refs_1_), channel_id=1, source_target_pairs={{0,4},{4,0},{8,12},{12,8},{1,5},{5,1},{9,13},{13,9},{2,6},{6,2},{1... | collective-permute-start | bytes 53000 | tf_op jit(solution)/shard_map/ppermute | solution.py:21
  1.5 5.6 %collective-permute-start.1 = (bf16[1,8832]{1,0:T(2,128)(2,1)S(1)}, bf16[1,8832]{1,0:T(2,128)(2,1)S(1)}, u32[]{:S(2)}, u32[]{:S(2)}) collective-permute-start(bf16[1,8832]{1,0:T(2,128)(2,1)S(1)} %get-tuple-element.32.refs_1_), channel_id=1, source_target_pairs={{0,8},{4,12},{8,0},{12,4},{1,9},{5,13},{9,1},{13,5},{2,10},{6,14},... | collective-permute-start | bytes 53000 | tf_op jit(solution)/shard_map/ppermute | solution.py:21
  4.1 3.4 %collective-permute-start.2 = (bf16[1,8832]{1,0:T(2,128)(2,1)S(1)}, bf16[1,8832]{1,0:T(2,128)(2,1)S(1)}, u32[]{:S(2)}, u32[]{:S(2)}) collective-permute-start(bf16[1,8832]{1,0:T(2,128)(2,1)S(1)} %get-tuple-element.32.refs_1_), channel_id=1, source_target_pairs={{0,12},{4,8},{8,4},{12,0},{1,13},{5,9},{9,5},{13,1},{2,14},{6,10},... | collective-permute-start | bytes 53000 | tf_op jit(solution)/shard_map/ppermute | solution.py:21
  8.2 6.7 %collective-permute-start.3 = (bf16[4,1024]{1,0:T(4,128)(2,1)S(1)}, bf16[4,1024]{1,0:T(4,128)(2,1)S(1)}, u32[]{:S(2)}, u32[]{:S(2)}) collective-permute-start(bf16[4,1024]{1,0:T(4,128)(2,1)S(1)} %get-tuple-element.40), channel_id=1, source_target_pairs={{0,1},{1,0},{2,3},{3,2},{4,5},{5,4},{6,7},{7,6},{8,9},{9,8},{10,11... | collective-permute-start | bytes 24584 | tf_op jit(solution)/shard_map/ppermute | solution.py:21
  9.9 5.0 %collective-permute-start.4 = (bf16[4,1024]{1,0:T(4,128)(2,1)S(1)}, bf16[4,1024]{1,0:T(4,128)(2,1)S(1)}, u32[]{:S(2)}, u32[]{:S(2)}) collective-permute-start(bf16[4,1024]{1,0:T(4,128)(2,1)S(1)} %get-tuple-element.41), channel_id=1, source_target_pairs={{0,2},{1,3},{2,0},{3,1},{4,6},{5,7},{6,4},{7,5},{8,10},{9,11},{10,... | collective-permute-start | bytes 24584 | tf_op jit(solution)/shard_map/ppermute | solution.py:21
  12.4 5.4 %collective-permute-start.5 = (bf16[4,1024]{1,0:T(4,128)(2,1)S(1)}, bf16[4,1024]{1,0:T(4,128)(2,1)S(1)}, u32[]{:S(2)}, u32[]{:S(2)}) collective-permute-start(bf16[4,1024]{1,0:T(4,128)(2,1)S(1)} %get-tuple-element.42), channel_id=1, source_target_pairs={{0,3},{1,2},{2,1},{3,0},{4,7},{5,6},{6,5},{7,4},{8,11},{9,10},{10,... | collective-permute-start | bytes 24584 | tf_op jit(solution)/shard_map/ppermute | solution.py:21
  17.9 8.1 %copy-start.2 = (f32[4096]{0:T(1024)S(1)}, f32[4096]{0:T(1024)}, u32[]{:S(2)}) copy-start(f32[4096]{0:T(1024)} %param.20) | copy-start | bytes 49156
  19.1 4.4 %collective-permute-start.6 = (bf16[4,4096]{1,0:T(4,128)(2,1)S(1)}, bf16[4,4096]{1,0:T(4,128)(2,1)S(1)}, u32[]{:S(2)}, u32[]{:S(2)}) collective-permute-start(bf16[4,4096]{1,0:T(4,128)(2,1)S(1)} %get-tuple-element.45), channel_id=1, source_target_pairs={{0,1},{1,0},{2,3},{3,2},{4,5},{5,4},{6,7},{7,6},{8,9},{9,8},{10,11... | collective-permute-start | bytes 98312 | tf_op jit(solution)/shard_map/ppermute | solution.py:21
  19.1 5.1 %collective-permute-start.7 = (bf16[4,4096]{1,0:T(4,128)(2,1)S(1)}, bf16[4,4096]{1,0:T(4,128)(2,1)S(1)}, u32[]{:S(2)}, u32[]{:S(2)}) collective-permute-start(bf16[4,4096]{1,0:T(4,128)(2,1)S(1)} %get-tuple-element.46), channel_id=1, source_target_pairs={{0,2},{1,3},{2,0},{3,1},{4,6},{5,7},{6,4},{7,5},{8,10},{9,11},{10,... | collective-permute-start | bytes 98312 | tf_op jit(solution)/shard_map/ppermute | solution.py:21
  20.3 5.7 %collective-permute-start.8 = (bf16[4,4096]{1,0:T(4,128)(2,1)S(1)}, bf16[4,4096]{1,0:T(4,128)(2,1)S(1)}, u32[]{:S(2)}, u32[]{:S(2)}) collective-permute-start(bf16[4,4096]{1,0:T(4,128)(2,1)S(1)} %get-tuple-element.47), channel_id=1, source_target_pairs={{0,3},{1,2},{2,1},{3,0},{4,7},{5,6},{6,5},{7,4},{8,11},{9,10},{10,... | collective-permute-start | bytes 98312 | tf_op jit(solution)/shard_map/ppermute | solution.py:21
  26.0 14.7 %copy-start.3 = (s32[4,4]{1,0:T(4,128)S(1)}, s32[4,4]{1,0:T(4,128)}, u32[]{:S(2)}) copy-start(s32[4,4]{1,0:T(4,128)} %refs_0_.1) | copy-start | bytes 196
  26.2 4.9 %collective-permute-start.10 = (bf16[4,4224]{1,0:T(4,128)(2,1)S(1)}, bf16[4,4224]{1,0:T(4,128)(2,1)S(1)}, u32[]{:S(2)}, u32[]{:S(2)}) collective-permute-start(bf16[4,4224]{1,0:T(4,128)(2,1)S(1)} %get-tuple-element.50), channel_id=1, source_target_pairs={{0,2},{1,3},{2,0},{3,1},{4,6},{5,7},{6,4},{7,5},{8,10},{9,11},{10,... | collective-permute-start | bytes 101384 | tf_op jit(solution)/shard_map/ppermute | solution.py:21
  26.3 5.8 %collective-permute-start.11 = (bf16[4,4224]{1,0:T(4,128)(2,1)S(1)}, bf16[4,4224]{1,0:T(4,128)(2,1)S(1)}, u32[]{:S(2)}, u32[]{:S(2)}) collective-permute-start(bf16[4,4224]{1,0:T(4,128)(2,1)S(1)} %get-tuple-element.50), channel_id=1, source_target_pairs={{0,3},{1,2},{2,1},{3,0},{4,7},{5,6},{6,5},{7,4},{8,11},{9,10},{10,... | collective-permute-start | bytes 101384 | tf_op jit(solution)/shard_map/ppermute | solution.py:21
  29.6 3.9 %collective-permute-start.9 = (bf16[4,4224]{1,0:T(4,128)(2,1)S(1)}, bf16[4,4224]{1,0:T(4,128)(2,1)S(1)}, u32[]{:S(2)}, u32[]{:S(2)}) collective-permute-start(bf16[4,4224]{1,0:T(4,128)(2,1)S(1)} %get-tuple-element.50), channel_id=1, source_target_pairs={{0,1},{1,0},{2,3},{3,2},{4,5},{5,4},{6,7},{7,6},{8,9},{9,8},{10,11... | collective-permute-start | bytes 101384 | tf_op jit(solution)/shard_map/ppermute | solution.py:21
  33.6 5.1 %collective-permute-start.13 = (bf16[16,4224]{1,0:T(8,128)(2,1)S(1)}, bf16[16,4224]{1,0:T(8,128)(2,1)S(1)}, u32[]{:S(2)}, u32[]{:S(2)}) collective-permute-start(bf16[16,4224]{1,0:T(8,128)(2,1)S(1)} %pad_maximum_fusion.refs_1_), channel_id=1, source_target_pairs={{0,8},{4,12},{8,0},{12,4},{1,9},{5,13},{9,1},{13,5},{2,10},{6,14},... | collective-permute-start | bytes 405512 | tf_op jit(solution)/shard_map/ppermute | solution.py:413
  35.3 5.5 %collective-permute-start.12 = (bf16[16,4224]{1,0:T(8,128)(2,1)S(1)}, bf16[16,4224]{1,0:T(8,128)(2,1)S(1)}, u32[]{:S(2)}, u32[]{:S(2)}) collective-permute-start(bf16[16,4224]{1,0:T(8,128)(2,1)S(1)} %pad_maximum_fusion.refs_1_), channel_id=1, source_target_pairs={{0,4},{4,0},{8,12},{12,8},{1,5},{5,1},{9,13},{13,9},{2,6},{6,2},{1... | collective-permute-start | bytes 405512 | tf_op jit(solution)/shard_map/ppermute | solution.py:413
  38.7 2.1 %collective-permute-start.14 = (bf16[16,4224]{1,0:T(8,128)(2,1)S(1)}, bf16[16,4224]{1,0:T(8,128)(2,1)S(1)}, u32[]{:S(2)}, u32[]{:S(2)}) collective-permute-start(bf16[16,4224]{1,0:T(8,128)(2,1)S(1)} %collective-permute-done.13.refs_3_), channel_id=1, source_target_pairs={{0,4},{4,0},{8,12},{12,8},{1,5},{5,1},{9,13},{13,9},{2,6},{6,2},{1... | collective-permute-start | bytes 405512 | tf_op jit(solution)/shard_map/ppermute | solution.py:413
  38.7 3.8 %copy-start.1 = (bf16[1,4096,384]{2,1,0:T(8,128)(2,1)S(1)}, bf16[1,4096,384]{2,1,0:T(8,128)(2,1)}, u32[]{:S(2)}) copy-start(bf16[1,4096,384]{2,1,0:T(8,128)(2,1)} %refs_6_.1) | copy-start | bytes 9437188
  44.9 1.6 %collective-permute-start.16 = (bf16[16,4096]{1,0:T(8,128)(2,1)S(1)}, bf16[16,4096]{1,0:T(8,128)(2,1)S(1)}, u32[]{:S(2)}, u32[]{:S(2)}) collective-permute-start(bf16[16,4096]{1,0:T(8,128)(2,1)S(1)} %get-tuple-element.56), channel_id=1, source_target_pairs={{0,4},{4,0},{8,12},{12,8},{1,5},{5,1},{9,13},{13,9},{2,6},{6,2},{1... | collective-permute-start | bytes 393224 | tf_op jit(solution)/shard_map/ppermute | solution.py:438
  45.5 2.7 %collective-permute-start.15 = (bf16[16,4096]{1,0:T(8,128)(2,1)S(1)}, bf16[16,4096]{1,0:T(8,128)(2,1)S(1)}, u32[]{:S(2)}, u32[]{:S(2)}) collective-permute-start(bf16[16,4096]{1,0:T(8,128)(2,1)S(1)} %get-tuple-element.54), channel_id=1, source_target_pairs={{0,4},{4,0},{8,12},{12,8},{1,5},{5,1},{9,13},{13,9},{2,6},{6,2},{1... | collective-permute-start | bytes 393224 | tf_op jit(solution)/shard_map/ppermute | solution.py:438
  46.5 5.8 %collective-permute-start.17 = (bf16[16,4096]{1,0:T(8,128)(2,1)S(1)}, bf16[16,4096]{1,0:T(8,128)(2,1)S(1)}, u32[]{:S(2)}, u32[]{:S(2)}) collective-permute-start(bf16[16,4096]{1,0:T(8,128)(2,1)S(1)} %add_convert_fusion), channel_id=1, source_target_pairs={{0,8},{4,12},{8,0},{12,4},{1,9},{5,13},{9,1},{13,5},{2,10},{6,14},... | collective-permute-start | bytes 393224 | tf_op jit(solution)/shard_map/ppermute | solution.py:438
  52.4 4.5 %collective-permute-start.18 = (bf16[4,4096]{1,0:T(4,128)(2,1)S(1)}, bf16[4,4096]{1,0:T(4,128)(2,1)S(1)}, u32[]{:S(2)}, u32[]{:S(2)}) collective-permute-start(bf16[4,4096]{1,0:T(4,128)(2,1)S(1)} %get-tuple-element.59), channel_id=1, source_target_pairs={{0,1},{1,0},{2,3},{3,2},{4,5},{5,4},{6,7},{7,6},{8,9},{9,8},{10,11... | collective-permute-start | bytes 98312 | tf_op jit(solution)/shard_map/ppermute | solution.py:21
  53.0 5.2 %collective-permute-start.19 = (bf16[4,4096]{1,0:T(4,128)(2,1)S(1)}, bf16[4,4096]{1,0:T(4,128)(2,1)S(1)}, u32[]{:S(2)}, u32[]{:S(2)}) collective-permute-start(bf16[4,4096]{1,0:T(4,128)(2,1)S(1)} %get-tuple-element.61), channel_id=1, source_target_pairs={{0,2},{1,3},{2,0},{3,1},{4,6},{5,7},{6,4},{7,5},{8,10},{9,11},{10,... | collective-permute-start | bytes 98312 | tf_op jit(solution)/shard_map/ppermute | solution.py:21
  54.9 5.7 %collective-permute-start.20 = (bf16[4,4096]{1,0:T(4,128)(2,1)S(1)}, bf16[4,4096]{1,0:T(4,128)(2,1)S(1)}, u32[]{:S(2)}, u32[]{:S(2)}) collective-permute-start(bf16[4,4096]{1,0:T(4,128)(2,1)S(1)} %get-tuple-element.60), channel_id=1, source_target_pairs={{0,3},{1,2},{2,1},{3,0},{4,7},{5,6},{6,5},{7,4},{8,11},{9,10},{10,... | collective-permute-start | bytes 98312 | tf_op jit(solution)/shard_map/ppermute | solution.py:21
  (1 other events, 2.8 us)
where the time goes:
time: 61.4 us; the launch traced here: 61.2 us
  starting transfers between devices  24.4 us (40%)
  waiting for transfers between devices  21.5 us (35%)
  Pallas kernels  12.6 us (21%)
  local copies, waits for them, and re-layouts  1.77 us (3%)
  other arithmetic  0.82 us (1%)
    ppermute x15, starting transfers between devices, xor_exchange(): lax.ppermute(blocks[step], axis, [(j, j ^ step) for j in range(count)])  20.4 us
    ppermute x15, waiting for transfers between devices, xor_exchange(): lax.ppermute(blocks[step], axis, [(j, j ^ step) for j in range(count)])  13.1 us
    ppermute x3, waiting for transfers between devices, per_device(): got = lax.ppermute(sums.pop(r), 'dp', [(j, j ^ bit) for j in range(n_dp)])  5.06 us
    pallas_call x2, Pallas kernels, fetched(): call(functools.partial(fetch_kernel, rows_from), jax.ShapeDtypeStruct((ro...  4.23 us
    ppermute x3, waiting for transfers between devices, per_device(): lax.ppermute(pieces[r], 'dp', [(j, j ^ bit) for j in range(n_dp)])  3.41 us
    pallas_call x1, Pallas kernels, per_device(): call(functools.partial(local_kernel, kv_heads), [shape((n_ex, tokens, par...  2.94 us
    pallas_call x1, Pallas kernels, per_device(): call(functools.partial(expert_kernel, n_dp, n_ex, tokens), [shape((group_...  2.39 us
    ppermute x3, starting transfers between devices, per_device(): got = lax.ppermute(sums.pop(r), 'dp', [(j, j ^ bit) for j in range(n_dp)])  2.32 us
  transfers between devices with their start and end apart: 21, of which 12 were waited for; matrix products, arithmetic and copies ran while one was open for 0% of the time, Pallas kernels for 12%

commit v1 on v0

--- a/solution.py
+++ b/solution.py
@@ -19,6 +19,20 @@
     moved = list(blocks)
     for step in range(count - 1, 0, -1):
         moved[step] = lax.ppermute(blocks[step], axis, [(j, j ^ step) for j in range(count)])
+    return moved
+
+
+def dp_turns(n_dp):
+    return [(1 << b) | 1 for b in range(n_dp.bit_length() - 1)]
+
+
+def crossed_exchange(blocks, n_dp, n_ex):
+    moved = list(blocks)
+    for step in range(n_ex - 1, 0, -1):
+        pairs = [
+            (d * n_ex + e, (d ^ 1) * n_ex + (e ^ step)) for d in range(n_dp) for e in range(n_ex)
+        ]
+        moved[step] = lax.ppermute(blocks[step], ("dp", "expert"), pairs)
     return moved
 
 
@@ -296,7 +310,8 @@
     new_scr[...] = act_scr[...]
     for r in range(n_dp):
         for s in range(n_ex):
-            to = ((moves_ref[ex ^ s, dp ^ r] ^ dp) * n_ex + s) * tokens
+            side = 1 if s else 0
+            to = ((moves_ref[ex ^ s, dp ^ r ^ side] ^ dp ^ side) * n_ex + s) * tokens
             at = (r * n_ex + s) * tokens
             new_scr[pl.ds(to, 1), :] = act_scr[at : at + 1, :]
     left = new_scr[...].astype(BF16)
@@ -380,7 +395,7 @@
         flops=4 * model * context,
         moved=cache.size // tokens * 2,
     )(info, *rows, att, kv0, res_in, ext)
-    blocks = xor_exchange(moved[:n_ex], "expert", n_ex)
+    blocks = crossed_exchange(moved[:n_ex], n_dp, n_ex)
     base, ext_all = moved[n_ex:]
 
     out_late = fetched(out_weight, part - early, early)
@@ -393,7 +408,7 @@
         flops=2 * n_ex * tokens * part * model,
         moved=out_weight.size * 2,
     )(*blocks, out_early, out_late)
-    partials = xor_exchange(partials, "expert", n_ex)
+    partials = crossed_exchange(partials, n_dp, n_ex)
 
     down = fetched(w_down[0], w_down.shape[1], 0)
 
@@ -405,14 +420,12 @@
         flops=10 * tokens * model,
         moved=tokens * model * 16,
     )(*partials, base, ext_all, norm_gain[None])
-    gathered = xor_exchange([payload] * n_ex, "expert", n_ex)
+    gathered = crossed_exchange([payload] * n_ex, n_dp, n_ex)
     pieces = {0: jnp.concatenate(gathered, axis=0)}
-    bits = [1 << b for b in range(n_dp.bit_length() - 1)]
-    for bit in reversed(bits):
+    turns = dp_turns(n_dp)
+    for turn in reversed(turns):
         for r in list(pieces):
-            pieces[r | bit] = lax.ppermute(
-                pieces[r], "dp", [(j, j ^ bit) for j in range(n_dp)]
-            )
+            pieces[r ^ turn] = lax.ppermute(pieces[r], "dp", [(j, j ^ turn) for j in range(n_dp)])
 
     group_rows = n_ex * tokens
     all_rows = n_dp * group_rows
@@ -432,15 +445,20 @@
         moved=weights_bytes,
     )(moves, *[pieces[r] for r in range(n_dp)], w_gate, w_up, down, norm_gain[None], hidden)
     sums = {r: done[r] for r in range(n_dp)}
+    reach = {0: 0}
+    for i, turn in enumerate(turns):
+        reach |= {r ^ turn: mark | 1 << i for r, mark in reach.items()}
     real = done[n_dp]
-    for bit in bits:
-        for r in sorted((r for r in sums if r & bit), reverse=True):
-            got = lax.ppermute(sums.pop(r), "dp", [(j, j ^ bit) for j in range(n_dp)])
-            total = sums[r ^ bit].astype(F32) + got.astype(F32)
-            sums[r ^ bit] = total.astype(BF16) if r ^ bit else total
+    for i, turn in enumerate(turns):
+        bit = 1 << i
+        far = {r: r ^ turn for r in sums if reach[r] & bit}
+        for r in sorted(far, key=lambda r: -reach[r]):
+            got = lax.ppermute(sums.pop(r), "dp", [(j, j ^ turn) for j in range(n_dp)])
+            total = sums[far[r]].astype(F32) + got.astype(F32)
+            sums[far[r]] = total.astype(BF16) if far[r] else total
     mixed = sums[0].reshape(n_ex, tokens, model)
-    back = xor_exchange(
-        [mixed[0]] + [mixed[s].astype(BF16) for s in range(1, n_ex)], "expert", n_ex
+    back = crossed_exchange(
+        [mixed[0]] + [mixed[s].astype(BF16) for s in range(1, n_ex)], n_dp, n_ex
     )
     total = real
     for s in range(n_ex):

time: 61.4 us -> 58.7 us (0.956)
  starting transfers between devices: 24.4 us -> 22.5 us
  waiting for transfers between devices: 21.5 us -> 20.7 us
    ppermute x15 -> x3, starting transfers between devices: 20.4 us -> 3.18 us  [xor_exchange(): lax.ppermute(blocks[step], axis, [(j, j ^ step) for j in range(count)])]
    ppermute x6 -> x18, starting transfers between devices: 4 us -> 19.4 us  [the longest x12 15.2 us: crossed_exchange(): moved[step] = lax.ppermute(blocks[step], ('dp', 'expert'), pairs)]
    ppermute x15 -> x3, waiting for transfers between devices: 13.1 us -> 0.4 us  [xor_exchange(): lax.ppermute(blocks[step], axis, [(j, j ^ step) for j in range(count)])]
    ppermute x6 -> x18, waiting for transfers between devices: 8.46 us -> 20.3 us  [the longest x12 11.9 us: crossed_exchange(): moved[step] = lax.ppermute(blocks[step], ('dp', 'expert'), pairs)]
  transfers between devices with their start and end apart: 21 -> 21, of which waited for: 12 -> 11; matrix products, arithmetic and copies ran while one was open for 0% -> 0% of each run, Pallas kernels for 12% -> 12%
where the time goes in v1:
time: 58.7 us; the launch traced here: 58.6 us
  starting transfers between devices  22.5 us (38%)
  waiting for transfers between devices  20.7 us (35%)
  Pallas kernels  12.6 us (21%)
  local copies, waits for them, and re-layouts  1.77 us (3%)
  other arithmetic  0.82 us (1%)
    ppermute x12, starting transfers between devices, crossed_exchange(): moved[step] = lax.ppermute(blocks[step], ('dp', 'expert'), pairs)  15.2 us
    ppermute x12, waiting for transfers between devices, crossed_exchange(): moved[step] = lax.ppermute(blocks[step], ('dp', 'expert'), pairs)  11.9 us
    ppermute x3, waiting for transfers between devices, per_device(): got = lax.ppermute(sums.pop(r), 'dp', [(j, j ^ turn) for j in range(n_dp)])  4.52 us
    pallas_call x2, Pallas kernels, fetched(): call(functools.partial(fetch_kernel, rows_from), jax.ShapeDtypeStruct((ro...  4.23 us
    ppermute x3, waiting for transfers between devices, per_device(): lax.ppermute(pieces[r], 'dp', [(j, j ^ turn) for j in range(n_dp)])  3.85 us
    ppermute x3, starting transfers between devices, xor_exchange(): lax.ppermute(blocks[step], axis, [(j, j ^ step) for j in range(count)])  3.18 us
    pallas_call x1, Pallas kernels, per_device(): call(functools.partial(local_kernel, kv_heads), [shape((n_ex, tokens, par...  2.94 us
    pallas_call x1, Pallas kernels, per_device(): call(functools.partial(expert_kernel, n_dp, n_ex, tokens), [shape((group_...  2.38 us
  transfers between devices with their start and end apart: 21, of which 11 were waited for; matrix products, arithmetic and copies ran while one was open for 0% of the time, Pallas kernels for 12%

profile of v1, /device:TPU:0, one launch (start us, length us, event | category | flops | bytes accessed | tf_op | source)
XLA Modules:
  0.0 58.6 jit_solution(5318404191842156234)
XLA Ops:
  0.0 0.9 %shard_map.127 = (bf16[1,8832]{1,0:T(2,128)(2,1)S(1)}, bf16[4,4096]{1,0:T(4,128)(2,1)S(1)}, bf16[4,512]{1,0:T(4,128)(2,1)S(1)}, bf16[4,4096]{1,0:T(4,128)(2,1)S(...) custom-call(bf16[4,4096]{1,0:T(4,128)(2,1)} %q_hbm.1, bf16[4,512]{1,0:T(4,128)(2,1)} %fresh_hbm.1, ...), custom_call_target="tpu_custom_call" | custom-call | bytes 65536 | tf_op jit(solution)/shard_map/pallas_call | solution.py:341
  1.5 2.6 %collective-permute-start.1 = (bf16[1,8832]{1,0:T(2,128)(2,1)S(1)}, bf16[1,8832]{1,0:T(2,128)(2,1)S(1)}, u32[]{:S(2)}, u32[]{:S(2)}) collective-permute-start(bf16[1,8832]{1,0:T(2,128)(2,1)S(1)} %get-tuple-element.32.refs_1_), channel_id=1, source_target_pairs={{0,8},{4,12},{8,0},{12,4},{1,9},{5,13},{9,1},{13,5},{2,10},{6,14},... | collective-permute-start | bytes 53000 | tf_op jit(solution)/shard_map/ppermute | solution.py:21
  4.1 2.9 %shard_map.128 = (f32[4,4,1024]{2,1,0:T(4,128)S(1)}, bf16[512,512]{1,0:T(8,128)(2,1)S(1)}, bf16[512,4096]{1,0:T(8,128)(2,1)S(1)}) custom-call(s32[8,128]{1,0:T(8,128)S(1)} %get-tuple-element.31.info_ref.refs_0_, bf16[4,4096]{1,0:T(4,128)(2,1)S(1)} %get-tuple-element.33.q_ref, bf16[4,512]{1,0:T(4,128)(2,1)S(1)} %get-tuple-element.34.fresh_ref, ...), custom_call_target="tpu_custom_call" | custom-call | flops 33554432 | bytes 6291456 | tf_op jit(solution)/shard_map/pallas_call | solution.py:365
  8.2 1.4 %collective-permute-start.3 = (bf16[4,1024]{1,0:T(4,128)(2,1)S(1)}, bf16[4,1024]{1,0:T(4,128)(2,1)S(1)}, u32[]{:S(2)}, u32[]{:S(2)}) collective-permute-start(bf16[4,1024]{1,0:T(4,128)(2,1)S(1)} %get-tuple-element.40), channel_id=1, source_target_pairs={{0,5},{1,4},{2,7},{3,6},{4,1},{5,0},{6,3},{7,2},{8,13},{9,12},{10,... | collective-permute-start | bytes 24584 | tf_op jit(solution)/shard_map/ppermute | solution.py:35
  9.7 2.5 %collective-permute-start.4 = (bf16[4,1024]{1,0:T(4,128)(2,1)S(1)}, bf16[4,1024]{1,0:T(4,128)(2,1)S(1)}, u32[]{:S(2)}, u32[]{:S(2)}) collective-permute-start(bf16[4,1024]{1,0:T(4,128)(2,1)S(1)} %get-tuple-element.41), channel_id=1, source_target_pairs={{0,6},{1,7},{2,4},{3,5},{4,2},{5,3},{6,0},{7,1},{8,14},{9,15},{10,... | collective-permute-start | bytes 24584 | tf_op jit(solution)/shard_map/ppermute | solution.py:35
  12.2 2.2 %shard_map.130.refs_5_ = bf16[512,4096]{1,0:T(8,128)(2,1)S(1)} custom-call(bf16[1024,4096]{1,0:T(8,128)(2,1)} %source.1), custom_call_target="tpu_custom_call" | custom-call | bytes 8388608 | tf_op jit(solution)/shard_map/pallas_call | solution.py:188
  14.4 2.6 %collective-permute-done.5.refs_3_ = bf16[4,1024]{1,0:T(4,128)(2,1)S(1)} collective-permute-done((bf16[4,1024]{1,0:T(4,128)(2,1)S(1)}, bf16[4,1024]{1,0:T(4,128)(2,1)S(1)}, u32[]{:S(2)}, u32[]{:S(2)}) %collective-permute-start.5) | collective-permute-done | bytes 8224 | tf_op jit(solution)/shard_map/ppermute | solution.py:35
  17.0 1.2 %shard_map.131 = (f32[4,4096]{1,0:T(4,128)S(1)}, bf16[4,4096]{1,0:T(4,128)(2,1)S(1)}, bf16[4,4096]{1,0:T(4,128)(2,1)S(1)}, bf16[4,4096]{1,0:T(4,128)(2,1)S(1)}) custom-call(bf16[4,1024]{1,0:T(4,128)(2,1)S(1)} %get-tuple-element.39.refs_0_, bf16[4,1024]{1,0:T(4,128)(2,1)S(1)} %collective-permute-done.3.refs_1_, ...), custom_call_target="tpu_custom_call" | custom-call | flops 134217728 | bytes 8388608 | tf_op jit(solution)/shard_map/pallas_call | solution.py:402
  18.3 1.3 %collective-permute-start.7 = (bf16[4,4096]{1,0:T(4,128)(2,1)S(1)}, bf16[4,4096]{1,0:T(4,128)(2,1)S(1)}, u32[]{:S(2)}, u32[]{:S(2)}) collective-permute-start(bf16[4,4096]{1,0:T(4,128)(2,1)S(1)} %get-tuple-element.46), channel_id=1, source_target_pairs={{0,6},{1,7},{2,4},{3,5},{4,2},{5,3},{6,0},{7,1},{8,14},{9,15},{10,... | collective-permute-start | bytes 98312 | tf_op jit(solution)/shard_map/ppermute | solution.py:35
  19.6 2.6 %collective-permute-start.8 = (bf16[4,4096]{1,0:T(4,128)(2,1)S(1)}, bf16[4,4096]{1,0:T(4,128)(2,1)S(1)}, u32[]{:S(2)}, u32[]{:S(2)}) collective-permute-start(bf16[4,4096]{1,0:T(4,128)(2,1)S(1)} %get-tuple-element.47), channel_id=1, source_target_pairs={{0,7},{1,6},{2,5},{3,4},{4,3},{5,2},{6,1},{7,0},{8,15},{9,14},{10,... | collective-permute-start | bytes 98312 | tf_op jit(solution)/shard_map/ppermute | solution.py:35
  22.6 2.1 %collective-permute-done.8.refs_3_ = bf16[4,4096]{1,0:T(4,128)(2,1)S(1)} collective-permute-done((bf16[4,4096]{1,0:T(4,128)(2,1)S(1)}, bf16[4,4096]{1,0:T(4,128)(2,1)S(1)}, u32[]{:S(2)}, u32[]{:S(2)}) %collective-permute-start.8) | collective-permute-done | bytes 32800 | tf_op jit(solution)/shard_map/ppermute | solution.py:35
  24.9 2.7 %collective-permute-start.11 = (bf16[4,4224]{1,0:T(4,128)(2,1)S(1)}, bf16[4,4224]{1,0:T(4,128)(2,1)S(1)}, u32[]{:S(2)}, u32[]{:S(2)}) collective-permute-start(bf16[4,4224]{1,0:T(4,128)(2,1)S(1)} %get-tuple-element.50), channel_id=1, source_target_pairs={{0,7},{1,6},{2,5},{3,4},{4,3},{5,2},{6,1},{7,0},{8,15},{9,14},{10,... | collective-permute-start | bytes 101384 | tf_op jit(solution)/shard_map/ppermute | solution.py:35
  28.1 2.8 %collective-permute-done.10 = bf16[4,4224]{1,0:T(4,128)(2,1)S(1)} collective-permute-done((bf16[4,4224]{1,0:T(4,128)(2,1)S(1)}, bf16[4,4224]{1,0:T(4,128)(2,1)S(1)}, u32[]{:S(2)}, u32[]{:S(2)}) %collective-permute-start.10) | collective-permute-done | bytes 33824 | tf_op jit(solution)/shard_map/ppermute | solution.py:35
  31.6 1.4 %collective-permute-start.13 = (bf16[16,4224]{1,0:T(8,128)(2,1)S(1)}, bf16[16,4224]{1,0:T(8,128)(2,1)S(1)}, u32[]{:S(2)}, u32[]{:S(2)}) collective-permute-start(bf16[16,4224]{1,0:T(8,128)(2,1)S(1)} %pad_maximum_fusion.refs_1_), channel_id=1, source_target_pairs={{0,12},{4,8},{8,4},{12,0},{1,13},{5,9},{9,5},{13,1},{2,14},{6,10},... | collective-permute-start | bytes 405512 | tf_op jit(solution)/shard_map/ppermute | solution.py:428
  33.4 3.8 %collective-permute-done.13.refs_4_ = bf16[16,4224]{1,0:T(8,128)(2,1)S(1)} collective-permute-done((bf16[16,4224]{1,0:T(8,128)(2,1)S(1)}, bf16[16,4224]{1,0:T(8,128)(2,1)S(1)}, u32[]{:S(2)}, u32[]{:S(2)}) %collective-permute-start.13) | collective-permute-done | bytes 135200 | tf_op jit(solution)/shard_map/ppermute | solution.py:428
  37.4 2.0 %shard_map.133.refs_7_ = bf16[384,4096]{1,0:T(8,128)(2,1)S(1)} custom-call(bf16[384,4096]{1,0:T(8,128)(2,1)} %bitcast.6), custom_call_target="tpu_custom_call" | custom-call | bytes 6291456 | tf_op jit(solution)/shard_map/pallas_call | solution.py:188
  40.2 1.0 %copy-done.1 = bf16[1,4096,384]{2,1,0:T(8,128)(2,1)S(1)} copy-done((bf16[1,4096,384]{2,1,0:T(8,128)(2,1)S(1)}, bf16[1,4096,384]{2,1,0:T(8,128)(2,1)}, u32[]{:S(2)}) %copy-start.1) | copy-done | bytes 3145752
  41.2 2.4 %shard_map.134 = (bf16[16,4096]{1,0:T(8,128)(2,1)S(1)}, bf16[16,4096]{1,0:T(8,128)(2,1)S(1)}, bf16[16,4096]{1,0:T(8,128)(2,1)S(1)}, bf16[16,4096]{1,0:T(8,128)(2,1)S(1)}, f32[4,4096]{1,0:T(4,128)S(1)}) custom-call(s32[4,4]{1,0:T(4,128)S(1)} %copy-done.3, bf16[16,4224]{1,0:T(8,128)(2,1)S(1)} %pad_maximum_fusion.refs_1_, ...), custom_call_target="tpu_custom_call" | custom-call | flops 603979776 | bytes 9437184 | tf_op jit(solution)/shard_map/pallas_call | solution.py:434
  44.2 0.9 %collective-permute-done.16 = bf16[16,4096]{1,0:T(8,128)(2,1)S(1)} collective-permute-done((bf16[16,4096]{1,0:T(8,128)(2,1)S(1)}, bf16[16,4096]{1,0:T(8,128)(2,1)S(1)}, u32[]{:S(2)}, u32[]{:S(2)}) %collective-permute-start.16) | collective-permute-done | bytes 131104 | tf_op jit(solution)/shard_map/ppermute | solution.py:456
  45.1 1.7 %collective-permute-start.17 = (bf16[16,4096]{1,0:T(8,128)(2,1)S(1)}, bf16[16,4096]{1,0:T(8,128)(2,1)S(1)}, u32[]{:S(2)}, u32[]{:S(2)}) collective-permute-start(bf16[16,4096]{1,0:T(8,128)(2,1)S(1)} %add_convert_fusion), channel_id=1, source_target_pairs={{0,12},{4,8},{8,4},{12,0},{1,13},{5,9},{9,5},{13,1},{2,14},{6,10},... | collective-permute-start | bytes 393224 | tf_op jit(solution)/shard_map/ppermute | solution.py:456
  46.7 3.6 %collective-permute-done.17 = bf16[16,4096]{1,0:T(8,128)(2,1)S(1)} collective-permute-done((bf16[16,4096]{1,0:T(8,128)(2,1)S(1)}, bf16[16,4096]{1,0:T(8,128)(2,1)S(1)}, u32[]{:S(2)}, u32[]{:S(2)}) %collective-permute-start.17) | collective-permute-done | bytes 131104 | tf_op jit(solution)/shard_map/ppermute | solution.py:456
  51.1 1.7 %collective-permute-start.19 = (bf16[4,4096]{1,0:T(4,128)(2,1)S(1)}, bf16[4,4096]{1,0:T(4,128)(2,1)S(1)}, u32[]{:S(2)}, u32[]{:S(2)}) collective-permute-start(bf16[4,4096]{1,0:T(4,128)(2,1)S(1)} %get-tuple-element.61), channel_id=1, source_target_pairs={{0,6},{1,7},{2,4},{3,5},{4,2},{5,3},{6,0},{7,1},{8,14},{9,15},{10,... | collective-permute-start | bytes 98312 | tf_op jit(solution)/shard_map/ppermute | solution.py:35
  52.8 1.9 %collective-permute-start.20 = (bf16[4,4096]{1,0:T(4,128)(2,1)S(1)}, bf16[4,4096]{1,0:T(4,128)(2,1)S(1)}, u32[]{:S(2)}, u32[]{:S(2)}) collective-permute-start(bf16[4,4096]{1,0:T(4,128)(2,1)S(1)} %get-tuple-element.60), channel_id=1, source_target_pairs={{0,7},{1,6},{2,5},{3,4},{4,3},{5,2},{6,1},{7,0},{8,15},{9,14},{10,... | collective-permute-start | bytes 98312 | tf_op jit(solution)/shard_map/ppermute | solution.py:35
  55.4 2.5 %collective-permute-done.20 = bf16[4,4096]{1,0:T(4,128)(2,1)S(1)} collective-permute-done((bf16[4,4096]{1,0:T(4,128)(2,1)S(1)}, bf16[4,4096]{1,0:T(4,128)(2,1)S(1)}, u32[]{:S(2)}, u32[]{:S(2)}) %collective-permute-start.20) | collective-permute-done | bytes 32800 | tf_op jit(solution)/shard_map/ppermute | solution.py:35
  (39 shorter events, 7.6 us)
Async XLA Ops:
  0.9 6.1 %collective-permute-start = (bf16[1,8832]{1,0:T(2,128)(2,1)S(1)}, bf16[1,8832]{1,0:T(2,128)(2,1)S(1)}, u32[]{:S(2)}, u32[]{:S(2)}) collective-permute-start(bf16[1,8832]{1,0:T(2,128)(2,1)S(1)} %get-tuple-element.32.refs_1_), channel_id=1, source_target_pairs={{0,4},{4,0},{8,12},{12,8},{1,5},{5,1},{9,13},{13,9},{2,6},{6,2},{1... | collective-permute-start | bytes 53000 | tf_op jit(solution)/shard_map/ppermute | solution.py:21
  1.5 5.6 %collective-permute-start.1 = (bf16[1,8832]{1,0:T(2,128)(2,1)S(1)}, bf16[1,8832]{1,0:T(2,128)(2,1)S(1)}, u32[]{:S(2)}, u32[]{:S(2)}) collective-permute-start(bf16[1,8832]{1,0:T(2,128)(2,1)S(1)} %get-tuple-element.32.refs_1_), channel_id=1, source_target_pairs={{0,8},{4,12},{8,0},{12,4},{1,9},{5,13},{9,1},{13,5},{2,10},{6,14},... | collective-permute-start | bytes 53000 | tf_op jit(solution)/shard_map/ppermute | solution.py:21
  4.1 3.4 %collective-permute-start.2 = (bf16[1,8832]{1,0:T(2,128)(2,1)S(1)}, bf16[1,8832]{1,0:T(2,128)(2,1)S(1)}, u32[]{:S(2)}, u32[]{:S(2)}) collective-permute-start(bf16[1,8832]{1,0:T(2,128)(2,1)S(1)} %get-tuple-element.32.refs_1_), channel_id=1, source_target_pairs={{0,12},{4,8},{8,4},{12,0},{1,13},{5,9},{9,5},{13,1},{2,14},{6,10},... | collective-permute-start | bytes 53000 | tf_op jit(solution)/shard_map/ppermute | solution.py:21
  8.2 6.2 %collective-permute-start.3 = (bf16[4,1024]{1,0:T(4,128)(2,1)S(1)}, bf16[4,1024]{1,0:T(4,128)(2,1)S(1)}, u32[]{:S(2)}, u32[]{:S(2)}) collective-permute-start(bf16[4,1024]{1,0:T(4,128)(2,1)S(1)} %get-tuple-element.40), channel_id=1, source_target_pairs={{0,5},{1,4},{2,7},{3,6},{4,1},{5,0},{6,3},{7,2},{8,13},{9,12},{10,... | collective-permute-start | bytes 24584 | tf_op jit(solution)/shard_map/ppermute | solution.py:35
  9.7 4.7 %collective-permute-start.4 = (bf16[4,1024]{1,0:T(4,128)(2,1)S(1)}, bf16[4,1024]{1,0:T(4,128)(2,1)S(1)}, u32[]{:S(2)}, u32[]{:S(2)}) collective-permute-start(bf16[4,1024]{1,0:T(4,128)(2,1)S(1)} %get-tuple-element.41), channel_id=1, source_target_pairs={{0,6},{1,7},{2,4},{3,5},{4,2},{5,3},{6,0},{7,1},{8,14},{9,15},{10,... | collective-permute-start | bytes 24584 | tf_op jit(solution)/shard_map/ppermute | solution.py:35
  12.2 4.9 %collective-permute-start.5 = (bf16[4,1024]{1,0:T(4,128)(2,1)S(1)}, bf16[4,1024]{1,0:T(4,128)(2,1)S(1)}, u32[]{:S(2)}, u32[]{:S(2)}) collective-permute-start(bf16[4,1024]{1,0:T(4,128)(2,1)S(1)} %get-tuple-element.42), channel_id=1, source_target_pairs={{0,7},{1,6},{2,5},{3,4},{4,3},{5,2},{6,1},{7,0},{8,15},{9,14},{10,... | collective-permute-start | bytes 24584 | tf_op jit(solution)/shard_map/ppermute | solution.py:35
  17.0 7.7 %copy-start.2 = (f32[4096]{0:T(1024)S(1)}, f32[4096]{0:T(1024)}, u32[]{:S(2)}) copy-start(f32[4096]{0:T(1024)} %param.20) | copy-start | bytes 49156
  18.3 3.9 %collective-permute-start.6 = (bf16[4,4096]{1,0:T(4,128)(2,1)S(1)}, bf16[4,4096]{1,0:T(4,128)(2,1)S(1)}, u32[]{:S(2)}, u32[]{:S(2)}) collective-permute-start(bf16[4,4096]{1,0:T(4,128)(2,1)S(1)} %get-tuple-element.45), channel_id=1, source_target_pairs={{0,5},{1,4},{2,7},{3,6},{4,1},{5,0},{6,3},{7,2},{8,13},{9,12},{10,... | collective-permute-start | bytes 98312 | tf_op jit(solution)/shard_map/ppermute | solution.py:35
  18.3 4.3 %collective-permute-start.7 = (bf16[4,4096]{1,0:T(4,128)(2,1)S(1)}, bf16[4,4096]{1,0:T(4,128)(2,1)S(1)}, u32[]{:S(2)}, u32[]{:S(2)}) collective-permute-start(bf16[4,4096]{1,0:T(4,128)(2,1)S(1)} %get-tuple-element.46), channel_id=1, source_target_pairs={{0,6},{1,7},{2,4},{3,5},{4,2},{5,3},{6,0},{7,1},{8,14},{9,15},{10,... | collective-permute-start | bytes 98312 | tf_op jit(solution)/shard_map/ppermute | solution.py:35
  19.6 5.1 %collective-permute-start.8 = (bf16[4,4096]{1,0:T(4,128)(2,1)S(1)}, bf16[4,4096]{1,0:T(4,128)(2,1)S(1)}, u32[]{:S(2)}, u32[]{:S(2)}) collective-permute-start(bf16[4,4096]{1,0:T(4,128)(2,1)S(1)} %get-tuple-element.47), channel_id=1, source_target_pairs={{0,7},{1,6},{2,5},{3,4},{4,3},{5,2},{6,1},{7,0},{8,15},{9,14},{10,... | collective-permute-start | bytes 98312 | tf_op jit(solution)/shard_map/ppermute | solution.py:35
  24.7 14.8 %copy-start.3 = (s32[4,4]{1,0:T(4,128)S(1)}, s32[4,4]{1,0:T(4,128)}, u32[]{:S(2)}) copy-start(s32[4,4]{1,0:T(4,128)} %refs_0_.1) | copy-start | bytes 196
  24.9 6.0 %collective-permute-start.10 = (bf16[4,4224]{1,0:T(4,128)(2,1)S(1)}, bf16[4,4224]{1,0:T(4,128)(2,1)S(1)}, u32[]{:S(2)}, u32[]{:S(2)}) collective-permute-start(bf16[4,4224]{1,0:T(4,128)(2,1)S(1)} %get-tuple-element.50), channel_id=1, source_target_pairs={{0,6},{1,7},{2,4},{3,5},{4,2},{5,3},{6,0},{7,1},{8,14},{9,15},{10,... | collective-permute-start | bytes 101384 | tf_op jit(solution)/shard_map/ppermute | solution.py:35
  24.9 5.9 %collective-permute-start.11 = (bf16[4,4224]{1,0:T(4,128)(2,1)S(1)}, bf16[4,4224]{1,0:T(4,128)(2,1)S(1)}, u32[]{:S(2)}, u32[]{:S(2)}) collective-permute-start(bf16[4,4224]{1,0:T(4,128)(2,1)S(1)} %get-tuple-element.50), channel_id=1, source_target_pairs={{0,7},{1,6},{2,5},{3,4},{4,3},{5,2},{6,1},{7,0},{8,15},{9,14},{10,... | collective-permute-start | bytes 101384 | tf_op jit(solution)/shard_map/ppermute | solution.py:35
  27.6 3.9 %collective-permute-start.9 = (bf16[4,4224]{1,0:T(4,128)(2,1)S(1)}, bf16[4,4224]{1,0:T(4,128)(2,1)S(1)}, u32[]{:S(2)}, u32[]{:S(2)}) collective-permute-start(bf16[4,4224]{1,0:T(4,128)(2,1)S(1)} %get-tuple-element.50), channel_id=1, source_target_pairs={{0,5},{1,4},{2,7},{3,6},{4,1},{5,0},{6,3},{7,2},{8,13},{9,12},{10,... | collective-permute-start | bytes 101384 | tf_op jit(solution)/shard_map/ppermute | solution.py:35
  31.6 5.7 %collective-permute-start.13 = (bf16[16,4224]{1,0:T(8,128)(2,1)S(1)}, bf16[16,4224]{1,0:T(8,128)(2,1)S(1)}, u32[]{:S(2)}, u32[]{:S(2)}) collective-permute-start(bf16[16,4224]{1,0:T(8,128)(2,1)S(1)} %pad_maximum_fusion.refs_1_), channel_id=1, source_target_pairs={{0,12},{4,8},{8,4},{12,0},{1,13},{5,9},{9,5},{13,1},{2,14},{6,10},... | collective-permute-start | bytes 405512 | tf_op jit(solution)/shard_map/ppermute | solution.py:428
  33.1 6.4 %collective-permute-start.12 = (bf16[16,4224]{1,0:T(8,128)(2,1)S(1)}, bf16[16,4224]{1,0:T(8,128)(2,1)S(1)}, u32[]{:S(2)}, u32[]{:S(2)}) collective-permute-start(bf16[16,4224]{1,0:T(8,128)(2,1)S(1)} %pad_maximum_fusion.refs_1_), channel_id=1, source_target_pairs={{0,4},{4,0},{8,12},{12,8},{1,5},{5,1},{9,13},{13,9},{2,6},{6,2},{1... | collective-permute-start | bytes 405512 | tf_op jit(solution)/shard_map/ppermute | solution.py:428
  37.3 2.2 %collective-permute-start.14 = (bf16[16,4224]{1,0:T(8,128)(2,1)S(1)}, bf16[16,4224]{1,0:T(8,128)(2,1)S(1)}, u32[]{:S(2)}, u32[]{:S(2)}) collective-permute-start(bf16[16,4224]{1,0:T(8,128)(2,1)S(1)} %collective-permute-done.13.refs_4_), channel_id=1, source_target_pairs={{0,4},{4,0},{8,12},{12,8},{1,5},{5,1},{9,13},{13,9},{2,6},{6,2},{1... | collective-permute-start | bytes 405512 | tf_op jit(solution)/shard_map/ppermute | solution.py:428
  37.4 3.8 %copy-start.1 = (bf16[1,4096,384]{2,1,0:T(8,128)(2,1)S(1)}, bf16[1,4096,384]{2,1,0:T(8,128)(2,1)}, u32[]{:S(2)}) copy-start(bf16[1,4096,384]{2,1,0:T(8,128)(2,1)} %refs_6_.1) | copy-start | bytes 9437188
  43.6 1.4 %collective-permute-start.16 = (bf16[16,4096]{1,0:T(8,128)(2,1)S(1)}, bf16[16,4096]{1,0:T(8,128)(2,1)S(1)}, u32[]{:S(2)}, u32[]{:S(2)}) collective-permute-start(bf16[16,4096]{1,0:T(8,128)(2,1)S(1)} %get-tuple-element.56), channel_id=1, source_target_pairs={{0,4},{4,0},{8,12},{12,8},{1,5},{5,1},{9,13},{13,9},{2,6},{6,2},{1... | collective-permute-start | bytes 393224 | tf_op jit(solution)/shard_map/ppermute | solution.py:456
  44.0 2.7 %collective-permute-start.15 = (bf16[16,4096]{1,0:T(8,128)(2,1)S(1)}, bf16[16,4096]{1,0:T(8,128)(2,1)S(1)}, u32[]{:S(2)}, u32[]{:S(2)}) collective-permute-start(bf16[16,4096]{1,0:T(8,128)(2,1)S(1)} %get-tuple-element.54), channel_id=1, source_target_pairs={{0,4},{4,0},{8,12},{12,8},{1,5},{5,1},{9,13},{13,9},{2,6},{6,2},{1... | collective-permute-start | bytes 393224 | tf_op jit(solution)/shard_map/ppermute | solution.py:456
  45.1 5.3 %collective-permute-start.17 = (bf16[16,4096]{1,0:T(8,128)(2,1)S(1)}, bf16[16,4096]{1,0:T(8,128)(2,1)S(1)}, u32[]{:S(2)}, u32[]{:S(2)}) collective-permute-start(bf16[16,4096]{1,0:T(8,128)(2,1)S(1)} %add_convert_fusion), channel_id=1, source_target_pairs={{0,12},{4,8},{8,4},{12,0},{1,13},{5,9},{9,5},{13,1},{2,14},{6,10},... | collective-permute-start | bytes 393224 | tf_op jit(solution)/shard_map/ppermute | solution.py:456
  50.5 4.1 %collective-permute-start.18 = (bf16[4,4096]{1,0:T(4,128)(2,1)S(1)}, bf16[4,4096]{1,0:T(4,128)(2,1)S(1)}, u32[]{:S(2)}, u32[]{:S(2)}) collective-permute-start(bf16[4,4096]{1,0:T(4,128)(2,1)S(1)} %get-tuple-element.59), channel_id=1, source_target_pairs={{0,5},{1,4},{2,7},{3,6},{4,1},{5,0},{6,3},{7,2},{8,13},{9,12},{10,... | collective-permute-start | bytes 98312 | tf_op jit(solution)/shard_map/ppermute | solution.py:35
  51.1 4.3 %collective-permute-start.19 = (bf16[4,4096]{1,0:T(4,128)(2,1)S(1)}, bf16[4,4096]{1,0:T(4,128)(2,1)S(1)}, u32[]{:S(2)}, u32[]{:S(2)}) collective-permute-start(bf16[4,4096]{1,0:T(4,128)(2,1)S(1)} %get-tuple-element.61), channel_id=1, source_target_pairs={{0,6},{1,7},{2,4},{3,5},{4,2},{5,3},{6,0},{7,1},{8,14},{9,15},{10,... | collective-permute-start | bytes 98312 | tf_op jit(solution)/shard_map/ppermute | solution.py:35
  52.8 5.1 %collective-permute-start.20 = (bf16[4,4096]{1,0:T(4,128)(2,1)S(1)}, bf16[4,4096]{1,0:T(4,128)(2,1)S(1)}, u32[]{:S(2)}, u32[]{:S(2)}) collective-permute-start(bf16[4,4096]{1,0:T(4,128)(2,1)S(1)} %get-tuple-element.60), channel_id=1, source_target_pairs={{0,7},{1,6},{2,5},{3,4},{4,3},{5,2},{6,1},{7,0},{8,15},{9,14},{10,... | collective-permute-start | bytes 98312 | tf_op jit(solution)/shard_map/ppermute | solution.py:35
  (1 other events, 2.8 us)

commit v2 on v1

--- a/solution.py
+++ b/solution.py
@@ -148,10 +148,12 @@
 
 
 def local_kernel(
-    kv_heads, info_ref, q_ref, fresh_ref, cache_hbm, w_hbm,
-    att_ref, kv0_ref, w_ref, kv, q_scr, sems, w_sems,
+    n_dp, kv_heads, info_ref, q_ref, fresh_ref, moves_hbm, cache_hbm, w_hbm,
+    att_ref, kv0_ref, w_ref, to_ref, kv, q_scr, moves, moves_sem, sems, w_sems,
 ):
     parts, tokens, part = att_ref.shape
+    goals = pltpu.make_async_copy(moves_hbm, moves, moves_sem)
+    goals.start()
     per = part // HD
     copies = [
         pltpu.make_async_copy(cache_hbm.at[t], kv.at[t - 1] if t else kv0_ref, sems.at[t])
@@ -172,6 +174,19 @@
         )
     for s in range(parts):
         att_ref[s, 0:1, :] = jnp.zeros((1, part), F32)
+    goals.wait()
+    dp = lax.axis_index("dp")
+    ex = lax.axis_index("expert")
+    for r in range(n_dp):
+        for s in range(parts):
+            side = 1 if s else 0
+            to = ((moves[ex ^ s, dp ^ r ^ side] ^ dp ^ side) * parts + s) * tokens
+            at = r * parts + s
+            to_ref[at : at + 1, :] = jnp.full((1, LANES), to, jnp.int32)
+    source = 0
+    for d in range(n_dp):
+        source = jnp.where(moves[ex, d] == dp, d, source)
+    to_ref[n_dp * parts : n_dp * parts + 1, :] = jnp.full((1, LANES), source ^ dp, jnp.int32)
     for copy in copies[:1] + weight:
         copy.wait()
 
@@ -272,20 +287,16 @@
 
 
 def expert_kernel(n_dp, n_ex, tokens, *refs):
-    moves_ref = refs[0]
+    to_ref = refs[0]
     pieces = refs[1 : 1 + n_dp]
     gate_ref, up_ref, down_ref, gain_ref, hid_ref = refs[1 + n_dp : 6 + n_dp]
     outs = refs[6 + n_dp : 6 + 2 * n_dp]
     real_ref, lhs, act_scr, new_scr = refs[6 + 2 * n_dp :]
     dp = lax.axis_index("dp")
-    ex = lax.axis_index("expert")
     model = gain_ref.shape[1]
     rows = n_ex * tokens
     coef = []
-    source = 0
-    for d in range(n_dp):
-        source = jnp.where(moves_ref[ex, d] == dp, d, source)
-    rel = source ^ dp
+    rel = to_ref[n_dp * n_ex : n_dp * n_ex + 1, 0:1]
     carried = jnp.zeros((1, pieces[0].shape[1]), F32)
     for r in range(n_dp):
         lhs[r * rows : (r + 1) * rows, :] = pieces[r][:, :model]
@@ -310,8 +321,7 @@
     new_scr[...] = act_scr[...]
     for r in range(n_dp):
         for s in range(n_ex):
-            side = 1 if s else 0
-            to = ((moves_ref[ex ^ s, dp ^ r ^ side] ^ dp ^ side) * n_ex + s) * tokens
+            to = to_ref[r * n_ex + s : r * n_ex + s + 1, 0:1][0, 0]
             at = (r * n_ex + s) * tokens
             new_scr[pl.ds(to, 1), :] = act_scr[at : at + 1, :]
     left = new_scr[...].astype(BF16)
@@ -319,7 +329,9 @@
     for at in range(0, model, chunk):
         out = jnp.dot(left, down_ref[:, at : at + chunk], preferred_element_type=F32)
         for r in range(n_dp):
-            outs[r][:, at : at + chunk] = out[r * rows : (r + 1) * rows, :].astype(outs[r].dtype)
+            for s in range(n_ex):
+                first_row = (r * n_ex + s) * tokens
+                outs[r][s, :, at : at + chunk] = out[first_row : first_row + tokens, :].astype(BF16)
 
 
 def per_device(
@@ -361,25 +373,28 @@
     )(*map(in_hbm, small))
     rows = xor_exchange([row] * n_dp, "dp", n_dp)
 
-    early = part // 2
-    att, kv0, out_early = call(
-        functools.partial(local_kernel, kv_heads),
+    early = part // 4
+    att, kv0, out_early, targets = call(
+        functools.partial(local_kernel, n_dp, kv_heads),
         [
             shape((n_ex, tokens, part), F32),
             shape(cache.shape[1:], BF16),
             shape((early, model), BF16),
+            shape((n_dp * n_ex + 8, LANES), jnp.int32),
         ],
-        [spec()] * 3 + [spec(pltpu.HBM)] * 2,
+        [spec()] * 3 + [spec(pltpu.HBM)] * 3,
         scratch=[
             pltpu.VMEM((tokens - 1,) + cache.shape[1:], BF16),
             pltpu.VMEM((tokens, model // HD, HD), F32),
+            pltpu.SMEM(moves.shape, jnp.int32),
+            pltpu.SemaphoreType.DMA(()),
             pltpu.SemaphoreType.DMA((tokens,)),
             pltpu.SemaphoreType.DMA((4,)),
         ],
         limit=6 << 20,
         flops=4 * tokens * model * context,
         moved=cache.size * 2 + early * model * 2,
-    )(info, q_in, fresh_in, in_hbm(cache), in_hbm(out_weight))
+    )(info, q_in, fresh_in, in_hbm(moves), in_hbm(cache), in_hbm(out_weight))
 
     moved = call(
         functools.partial(moved_kernel, n_dp, n_ex, kv_heads, 2 * width),
@@ -421,11 +436,21 @@
         moved=tokens * model * 16,
     )(*partials, base, ext_all, norm_gain[None])
     gathered = crossed_exchange([payload] * n_ex, n_dp, n_ex)
-    pieces = {0: jnp.concatenate(gathered, axis=0)}
     turns = dp_turns(n_dp)
-    for turn in reversed(turns):
+
+    def over_dp(array, turn):
+        return lax.ppermute(array, "dp", [(j, j ^ turn) for j in range(n_dp)])
+
+    top = turns[-1]
+    near = over_dp(payload, top)
+    rest = over_dp(jnp.stack(gathered[1:]), top)
+    pieces = {
+        0: jnp.concatenate(gathered, axis=0),
+        top: jnp.concatenate([near] + [rest[s] for s in range(n_ex - 1)], axis=0),
+    }
+    for turn in reversed(turns[:-1]):
         for r in list(pieces):
-            pieces[r ^ turn] = lax.ppermute(pieces[r], "dp", [(j, j ^ turn) for j in range(n_dp)])
+            pieces[r ^ turn] = over_dp(pieces[r], turn)
 
     group_rows = n_ex * tokens
     all_rows = n_dp * group_rows
@@ -433,8 +458,8 @@
     weights_bytes = (w_gate.size + w_up.size + w_down.size) * 2
     done = call(
         functools.partial(expert_kernel, n_dp, n_ex, tokens),
-        [shape((group_rows, model), BF16)] * n_dp + [shape((tokens, model), F32)],
-        [spec(pltpu.SMEM)] + [spec()] * (n_dp + 5),
+        [shape((n_ex, tokens, model), BF16)] * n_dp + [shape((tokens, model), F32)],
+        [spec()] * (n_dp + 6),
         scratch=[
             pltpu.VMEM((all_rows, model), BF16),
             pltpu.VMEM((all_rows, hidden_units), F32),
@@ -443,23 +468,27 @@
         limit=(8 << 20) + all_rows * model * 8,
         flops=6 * all_rows * model * hidden_units,
         moved=weights_bytes,
-    )(moves, *[pieces[r] for r in range(n_dp)], w_gate, w_up, down, norm_gain[None], hidden)
-    sums = {r: done[r] for r in range(n_dp)}
+    )(targets, *[pieces[r] for r in range(n_dp)], w_gate, w_up, down, norm_gain[None], hidden)
+    terms = {r: [done[r]] for r in range(n_dp)}
     reach = {0: 0}
     for i, turn in enumerate(turns):
         reach |= {r ^ turn: mark | 1 << i for r, mark in reach.items()}
     real = done[n_dp]
-    for i, turn in enumerate(turns):
-        bit = 1 << i
-        far = {r: r ^ turn for r in sums if reach[r] & bit}
+
+    def added(arrays):
+        return functools.reduce(jnp.add, [array.astype(F32) for array in arrays])
+
+    for i, turn in enumerate(turns[:-1]):
+        far = {r: r ^ turn for r in terms if reach[r] >> i & 1}
         for r in sorted(far, key=lambda r: -reach[r]):
-            got = lax.ppermute(sums.pop(r), "dp", [(j, j ^ turn) for j in range(n_dp)])
-            total = sums[far[r]].astype(F32) + got.astype(F32)
-            sums[far[r]] = total.astype(BF16) if far[r] else total
-    mixed = sums[0].reshape(n_ex, tokens, model)
-    back = crossed_exchange(
-        [mixed[0]] + [mixed[s].astype(BF16) for s in range(1, n_ex)], n_dp, n_ex
-    )
+            whole = terms.pop(r)
+            whole = whole[0] if len(whole) == 1 else added(whole).astype(BF16)
+            terms[far[r]].append(over_dp(whole, turn))
+    rest = over_dp(added([t[1:] for t in terms[top]]).astype(BF16), top)
+    near = over_dp(added([t[0] for t in terms[top]]).astype(BF16), top)
+    mixed = added([t[1:] for t in terms[0]] + [rest]).astype(BF16)
+    staying = added([t[0] for t in terms[0]] + [near])
+    back = crossed_exchange([staying] + [mixed[s] for s in range(n_ex - 1)], n_dp, n_ex)
     total = real
     for s in range(n_ex):
         total = total + back[s].astype(F32)

time: 58.7 us -> 58.3 us (level)
  waiting for transfers between devices: 20.7 us -> 16.6 us
  starting transfers between devices: 22.5 us -> 25.7 us
    ppermute x12, waiting for transfers between devices: 11.9 us -> 9.69 us  [crossed_exchange(): moved[step] = lax.ppermute(blocks[step], ('dp', 'expert'), pairs)]
    ppermute x6 -> x8, waiting for transfers between devices: 8.37 us -> 6.59 us  [over_dp(): return lax.ppermute(array, 'dp', [(j, j ^ turn) for j in range(n_dp)])]
    ppermute x6 -> x8, starting transfers between devices: 4.17 us -> 5.91 us  [over_dp(): return lax.ppermute(array, 'dp', [(j, j ^ turn) for j in range(n_dp)])]
    ppermute x12, starting transfers between devices: 15.2 us -> 16.6 us  [crossed_exchange(): moved[step] = lax.ppermute(blocks[step], ('dp', 'expert'), pairs)]
    pallas_call x2, Pallas kernels: 4.23 us -> 4.89 us  [fetched(): call(functools.partial(fetch_kernel, rows_from), jax.ShapeDtypeStruct((ro...]
    unnamed x8 -> x6, local copies, waits for them, and re-layouts: 1.73 us -> 1.74 us
  transfers between devices with their start and end apart: 21 -> 23, of which waited for: 11 -> 11; matrix products, arithmetic and copies ran while one was open for 0% -> 1% of each run, Pallas kernels for 12% -> 14%
where the time goes in v2:
time: 58.3 us; the launch traced here: 58.1 us
  starting transfers between devices  25.7 us (44%)
  waiting for transfers between devices  16.6 us (28%)
  Pallas kernels  12.8 us (22%)
  local copies, waits for them, and re-layouts  1.81 us (3%)
  other arithmetic  1.08 us (2%)
    ppermute x12, starting transfers between devices, crossed_exchange(): moved[step] = lax.ppermute(blocks[step], ('dp', 'expert'), pairs)  16.6 us
    ppermute x12, waiting for transfers between devices, crossed_exchange(): moved[step] = lax.ppermute(blocks[step], ('dp', 'expert'), pairs)  9.69 us
    ppermute x8, waiting for transfers between devices, over_dp(): return lax.ppermute(array, 'dp', [(j, j ^ turn) for j in range(n_dp)])  6.59 us
    ppermute x8, starting transfers between devices, over_dp(): return lax.ppermute(array, 'dp', [(j, j ^ turn) for j in range(n_dp)])  5.91 us
    pallas_call x2, Pallas kernels, fetched(): call(functools.partial(fetch_kernel, rows_from), jax.ShapeDtypeStruct((ro...  4.89 us
    ppermute x3, starting transfers between devices, xor_exchange(): lax.ppermute(blocks[step], axis, [(j, j ^ step) for j in range(count)])  3.18 us
    pallas_call x1, Pallas kernels, per_device(): call(functools.partial(local_kernel, n_dp, kv_heads), [shape((n_ex, token...  3.01 us
    pallas_call x1, Pallas kernels, per_device(): call(functools.partial(expert_kernel, n_dp, n_ex, tokens), [shape((n_ex,...  1.86 us
  transfers between devices with their start and end apart: 23, of which 11 were waited for; matrix products, arithmetic and copies ran while one was open for 1% of the time, Pallas kernels for 14%

profile of v2, /device:TPU:0, one launch (start us, length us, event | category | flops | bytes accessed | tf_op | source)
XLA Modules:
  0.0 58.1 jit_solution(3865746081363142787)
XLA Ops:
  1.5 2.6 %collective-permute-start.1 = (bf16[1,8832]{1,0:T(2,128)(2,1)S(1)}, bf16[1,8832]{1,0:T(2,128)(2,1)S(1)}, u32[]{:S(2)}, u32[]{:S(2)}) collective-permute-start(bf16[1,8832]{1,0:T(2,128)(2,1)S(1)} %get-tuple-element.36.refs_1_), channel_id=1, source_target_pairs={{0,8},{4,12},{8,0},{12,4},{1,9},{5,13},{9,1},{13,5},{2,10},{6,14},... | collective-permute-start | bytes 53000 | tf_op jit(solution)/shard_map/ppermute | solution.py:21
  4.1 3.0 %shard_map.128 = (f32[4,4,1024]{2,1,0:T(4,128)S(1)}, bf16[512,512]{1,0:T(8,128)(2,1)S(1)}, bf16[256,4096]{1,0:T(8,128)(2,1)S(1)}, s32[24,128]{1,0:T(8,128)S(1)}) custom-call(s32[8,128]{1,0:T(8,128)S(1)} %get-tuple-element.32.info_ref.refs_0_, bf16[4,4096]{1,0:T(4,128)(2,1)S(1)} %get-tuple-element.33.q_ref, bf16[4,512]{1,0:T(4,128)(2,1)S(1)} %get-tuple-element.34.fresh_ref, ...), custom_call_target="tpu_custom_call" | custom-call | flops 33554432 | bytes 4194304 | tf_op jit(solution)/shard_map/pallas_call | solution.py:377
  8.2 1.5 %collective-permute-start.3 = (bf16[4,1024]{1,0:T(4,128)(2,1)S(1)}, bf16[4,1024]{1,0:T(4,128)(2,1)S(1)}, u32[]{:S(2)}, u32[]{:S(2)}) collective-permute-start(bf16[4,1024]{1,0:T(4,128)(2,1)S(1)} %get-tuple-element.42), channel_id=1, source_target_pairs={{0,5},{1,4},{2,7},{3,6},{4,1},{5,0},{6,3},{7,2},{8,13},{9,12},{10,... | collective-permute-start | bytes 24584 | tf_op jit(solution)/shard_map/ppermute | solution.py:35
  9.7 2.4 %collective-permute-start.4 = (bf16[4,1024]{1,0:T(4,128)(2,1)S(1)}, bf16[4,1024]{1,0:T(4,128)(2,1)S(1)}, u32[]{:S(2)}, u32[]{:S(2)}) collective-permute-start(bf16[4,1024]{1,0:T(4,128)(2,1)S(1)} %get-tuple-element.43), channel_id=1, source_target_pairs={{0,6},{1,7},{2,4},{3,5},{4,2},{5,3},{6,0},{7,1},{8,14},{9,15},{10,... | collective-permute-start | bytes 24584 | tf_op jit(solution)/shard_map/ppermute | solution.py:35
  12.2 2.9 %shard_map.130.refs_5_ = bf16[768,4096]{1,0:T(8,128)(2,1)S(1)} custom-call(bf16[1024,4096]{1,0:T(8,128)(2,1)} %source.1), custom_call_target="tpu_custom_call" | custom-call | bytes 12582912 | tf_op jit(solution)/shard_map/pallas_call | solution.py:203
  15.1 2.0 %collective-permute-done.5.refs_3_ = bf16[4,1024]{1,0:T(4,128)(2,1)S(1)} collective-permute-done((bf16[4,1024]{1,0:T(4,128)(2,1)S(1)}, bf16[4,1024]{1,0:T(4,128)(2,1)S(1)}, u32[]{:S(2)}, u32[]{:S(2)}) %collective-permute-start.5) | collective-permute-done | bytes 8224 | tf_op jit(solution)/shard_map/ppermute | solution.py:35
  17.0 1.2 %shard_map.131 = (f32[4,4096]{1,0:T(4,128)S(1)}, bf16[4,4096]{1,0:T(4,128)(2,1)S(1)}, bf16[4,4096]{1,0:T(4,128)(2,1)S(1)}, bf16[4,4096]{1,0:T(4,128)(2,1)S(1)}) custom-call(bf16[4,1024]{1,0:T(4,128)(2,1)S(1)} %get-tuple-element.41.refs_0_, bf16[4,1024]{1,0:T(4,128)(2,1)S(1)} %collective-permute-done.3.refs_1_, ...), custom_call_target="tpu_custom_call" | custom-call | flops 134217728 | bytes 8388608 | tf_op jit(solution)/shard_map/pallas_call | solution.py:417
  18.3 2.0 %collective-permute-start.7 = (bf16[4,4096]{1,0:T(4,128)(2,1)S(1)}, bf16[4,4096]{1,0:T(4,128)(2,1)S(1)}, u32[]{:S(2)}, u32[]{:S(2)}) collective-permute-start(bf16[4,4096]{1,0:T(4,128)(2,1)S(1)} %get-tuple-element.48), channel_id=1, source_target_pairs={{0,6},{1,7},{2,4},{3,5},{4,2},{5,3},{6,0},{7,1},{8,14},{9,15},{10,... | collective-permute-start | bytes 98312 | tf_op jit(solution)/shard_map/ppermute | solution.py:35
  20.3 2.0 %collective-permute-start.8 = (bf16[4,4096]{1,0:T(4,128)(2,1)S(1)}, bf16[4,4096]{1,0:T(4,128)(2,1)S(1)}, u32[]{:S(2)}, u32[]{:S(2)}) collective-permute-start(bf16[4,4096]{1,0:T(4,128)(2,1)S(1)} %get-tuple-element.49), channel_id=1, source_target_pairs={{0,7},{1,6},{2,5},{3,4},{4,3},{5,2},{6,1},{7,0},{8,15},{9,14},{10,... | collective-permute-start | bytes 98312 | tf_op jit(solution)/shard_map/ppermute | solution.py:35
  22.6 2.8 %collective-permute-done.8.refs_3_ = bf16[4,4096]{1,0:T(4,128)(2,1)S(1)} collective-permute-done((bf16[4,4096]{1,0:T(4,128)(2,1)S(1)}, bf16[4,4096]{1,0:T(4,128)(2,1)S(1)}, u32[]{:S(2)}, u32[]{:S(2)}) %collective-permute-start.8) | collective-permute-done | bytes 32800 | tf_op jit(solution)/shard_map/ppermute | solution.py:35
  25.6 2.0 %collective-permute-start.11 = (bf16[4,4224]{1,0:T(4,128)(2,1)S(1)}, bf16[4,4224]{1,0:T(4,128)(2,1)S(1)}, u32[]{:S(2)}, u32[]{:S(2)}) collective-permute-start(bf16[4,4224]{1,0:T(4,128)(2,1)S(1)} %get-tuple-element.52), channel_id=1, source_target_pairs={{0,7},{1,6},{2,5},{3,4},{4,3},{5,2},{6,1},{7,0},{8,15},{9,14},{10,... | collective-permute-start | bytes 101384 | tf_op jit(solution)/shard_map/ppermute | solution.py:35
  27.6 2.0 %collective-permute-start.9 = (bf16[4,4224]{1,0:T(4,128)(2,1)S(1)}, bf16[4,4224]{1,0:T(4,128)(2,1)S(1)}, u32[]{:S(2)}, u32[]{:S(2)}) collective-permute-start(bf16[4,4224]{1,0:T(4,128)(2,1)S(1)} %get-tuple-element.52), channel_id=1, source_target_pairs={{0,5},{1,4},{2,7},{3,6},{4,1},{5,0},{6,3},{7,2},{8,13},{9,12},{10,... | collective-permute-start | bytes 101384 | tf_op jit(solution)/shard_map/ppermute | solution.py:35
  29.6 1.4 %collective-permute-start.13 = (bf16[4,4224]{1,0:T(4,128)(2,1)S(1)}, bf16[4,4224]{1,0:T(4,128)(2,1)S(1)}, u32[]{:S(2)}, u32[]{:S(2)}) collective-permute-start(bf16[4,4224]{1,0:T(4,128)(2,1)S(1)} %get-tuple-element.52), channel_id=1, source_target_pairs={{0,12},{4,8},{8,4},{12,0},{1,13},{5,9},{9,5},{13,1},{2,14},{6,10},... | collective-permute-start | bytes 101384 | tf_op jit(solution)/shard_map/ppermute | solution.py:442
  31.0 1.6 %collective-permute-done.10 = bf16[4,4224]{1,0:T(4,128)(2,1)S(1)} collective-permute-done((bf16[4,4224]{1,0:T(4,128)(2,1)S(1)}, bf16[4,4224]{1,0:T(4,128)(2,1)S(1)}, u32[]{:S(2)}, u32[]{:S(2)}) %collective-permute-start.10) | collective-permute-done | bytes 33824 | tf_op jit(solution)/shard_map/ppermute | solution.py:35
  32.7 1.3 %collective-permute-start.14 = (bf16[3,4,4224]{2,1,0:T(4,128)(2,1)S(1)}, bf16[3,4,4224]{2,1,0:T(4,128)(2,1)S(1)}, u32[]{:S(2)}, u32[]{:S(2)}) collective-permute-start(bf16[3,4,4224]{2,1,0:T(4,128)(2,1)S(1)} %pad_maximum_fusion.2), channel_id=1, source_target_pairs={{0,12},{4,8},{8,4},{12,0},{1,13},{5,9},{9,5},{13,1},{2,14},{6,10},... | collective-permute-start | bytes 304136 | tf_op jit(solution)/shard_map/ppermute | solution.py:442
  34.6 3.0 %collective-permute-done.14 = bf16[3,4,4224]{2,1,0:T(4,128)(2,1)S(1)} collective-permute-done((bf16[3,4,4224]{2,1,0:T(4,128)(2,1)S(1)}, bf16[3,4,4224]{2,1,0:T(4,128)(2,1)S(1)}, u32[]{:S(2)}, u32[]{:S(2)}) %collective-permute-start.14) | collective-permute-done | bytes 101408 | tf_op jit(solution)/shard_map/ppermute | solution.py:442
  37.9 2.0 %shard_map.133.refs_7_ = bf16[384,4096]{1,0:T(8,128)(2,1)S(1)} custom-call(bf16[384,4096]{1,0:T(8,128)(2,1)} %bitcast.35), custom_call_target="tpu_custom_call" | custom-call | bytes 6291456 | tf_op jit(solution)/shard_map/pallas_call | solution.py:203
  40.8 1.0 %copy-done.1 = bf16[1,4096,384]{2,1,0:T(8,128)(2,1)S(1)} copy-done((bf16[1,4096,384]{2,1,0:T(8,128)(2,1)S(1)}, bf16[1,4096,384]{2,1,0:T(8,128)(2,1)}, u32[]{:S(2)}) %copy-start.1) | copy-done | bytes 3145752
  41.7 1.9 %shard_map.134 = (bf16[4,4,4096]{2,1,0:T(4,128)(2,1)S(1)}, bf16[4,4,4096]{2,1,0:T(4,128)(2,1)S(1)}, bf16[4,4,4096]{2,1,0:T(4,128)(2,1)S(1)}, bf16[4,4,4096]{2,1,0:T(4,128)(2,1)S(1)}, f32[4,4096]{1,0:T(4,128)S(1)}) custom-call(s32[24,128]{1,0:T(8,128)S(1)} %get-tuple-element.35.refs_0_, bf16[16,4224]{1,0:T(8,128)(2,1)S(1)} %pad_maximum_fusion.refs_1_, ...), custom_call_target="tpu_custom_call" | custom-call | flops 603979776 | bytes 9437184 | tf_op jit(solution)/shard_map/pallas_call | solution.py:459
  45.1 1.6 %collective-permute-start.19 = (bf16[3,4,4096]{2,1,0:T(4,128)(2,1)S(1)}, bf16[3,4,4096]{2,1,0:T(4,128)(2,1)S(1)}, u32[]{:S(2)}, u32[]{:S(2)}) collective-permute-start(bf16[3,4,4096]{2,1,0:T(4,128)(2,1)S(1)} %add_convert_fusion.1), channel_id=1, source_target_pairs={{0,12},{4,8},{8,4},{12,0},{1,13},{5,9},{9,5},{13,1},{2,14},{6,10},... | collective-permute-start | bytes 294920 | tf_op jit(solution)/shard_map/ppermute | solution.py:442
  47.0 2.8 %collective-permute-done.19 = bf16[3,4,4096]{2,1,0:T(4,128)(2,1)S(1)} collective-permute-done((bf16[3,4,4096]{2,1,0:T(4,128)(2,1)S(1)}, bf16[3,4,4096]{2,1,0:T(4,128)(2,1)S(1)}, u32[]{:S(2)}, u32[]{:S(2)}) %collective-permute-start.19) | collective-permute-done | bytes 98336 | tf_op jit(solution)/shard_map/ppermute | solution.py:442
  49.9 2.6 %collective-permute-start.22 = (bf16[4,4096]{1,0:T(4,128)(2,1)S(1)}, bf16[4,4096]{1,0:T(4,128)(2,1)S(1)}, u32[]{:S(2)}, u32[]{:S(2)}) collective-permute-start(bf16[4,4096]{1,0:T(4,128)(2,1)S(1)} %get-tuple-element.63), channel_id=1, source_target_pairs={{0,7},{1,6},{2,5},{3,4},{4,3},{5,2},{6,1},{7,0},{8,15},{9,14},{10,... | collective-permute-start | bytes 98312 | tf_op jit(solution)/shard_map/ppermute | solution.py:35
  52.5 2.0 %collective-permute-start.20 = (bf16[4,4096]{1,0:T(4,128)(2,1)S(1)}, bf16[4,4096]{1,0:T(4,128)(2,1)S(1)}, u32[]{:S(2)}, u32[]{:S(2)}) collective-permute-start(bf16[4,4096]{1,0:T(4,128)(2,1)S(1)} %get-tuple-element.62), channel_id=1, source_target_pairs={{0,5},{1,4},{2,7},{3,6},{4,1},{5,0},{6,3},{7,2},{8,13},{9,12},{10,... | collective-permute-start | bytes 98312 | tf_op jit(solution)/shard_map/ppermute | solution.py:35
  55.1 2.2 %collective-permute-done.21 = bf16[4,4096]{1,0:T(4,128)(2,1)S(1)} collective-permute-done((bf16[4,4096]{1,0:T(4,128)(2,1)S(1)}, bf16[4,4096]{1,0:T(4,128)(2,1)S(1)}, u32[]{:S(2)}, u32[]{:S(2)}) %collective-permute-start.21) | collective-permute-done | bytes 32800 | tf_op jit(solution)/shard_map/ppermute | solution.py:35
  (45 shorter events, 8.3 us)
Async XLA Ops:
  0.9 6.2 %collective-permute-start = (bf16[1,8832]{1,0:T(2,128)(2,1)S(1)}, bf16[1,8832]{1,0:T(2,128)(2,1)S(1)}, u32[]{:S(2)}, u32[]{:S(2)}) collective-permute-start(bf16[1,8832]{1,0:T(2,128)(2,1)S(1)} %get-tuple-element.36.refs_1_), channel_id=1, source_target_pairs={{0,4},{4,0},{8,12},{12,8},{1,5},{5,1},{9,13},{13,9},{2,6},{6,2},{1... | collective-permute-start | bytes 53000 | tf_op jit(solution)/shard_map/ppermute | solution.py:21
  1.5 5.7 %collective-permute-start.1 = (bf16[1,8832]{1,0:T(2,128)(2,1)S(1)}, bf16[1,8832]{1,0:T(2,128)(2,1)S(1)}, u32[]{:S(2)}, u32[]{:S(2)}) collective-permute-start(bf16[1,8832]{1,0:T(2,128)(2,1)S(1)} %get-tuple-element.36.refs_1_), channel_id=1, source_target_pairs={{0,8},{4,12},{8,0},{12,4},{1,9},{5,13},{9,1},{13,5},{2,10},{6,14},... | collective-permute-start | bytes 53000 | tf_op jit(solution)/shard_map/ppermute | solution.py:21
  4.1 3.4 %collective-permute-start.2 = (bf16[1,8832]{1,0:T(2,128)(2,1)S(1)}, bf16[1,8832]{1,0:T(2,128)(2,1)S(1)}, u32[]{:S(2)}, u32[]{:S(2)}) collective-permute-start(bf16[1,8832]{1,0:T(2,128)(2,1)S(1)} %get-tuple-element.36.refs_1_), channel_id=1, source_target_pairs={{0,12},{4,8},{8,4},{12,0},{1,13},{5,9},{9,5},{13,1},{2,14},{6,10},... | collective-permute-start | bytes 53000 | tf_op jit(solution)/shard_map/ppermute | solution.py:21
  8.2 6.8 %collective-permute-start.3 = (bf16[4,1024]{1,0:T(4,128)(2,1)S(1)}, bf16[4,1024]{1,0:T(4,128)(2,1)S(1)}, u32[]{:S(2)}, u32[]{:S(2)}) collective-permute-start(bf16[4,1024]{1,0:T(4,128)(2,1)S(1)} %get-tuple-element.42), channel_id=1, source_target_pairs={{0,5},{1,4},{2,7},{3,6},{4,1},{5,0},{6,3},{7,2},{8,13},{9,12},{10,... | collective-permute-start | bytes 24584 | tf_op jit(solution)/shard_map/ppermute | solution.py:35
  9.7 5.3 %collective-permute-start.4 = (bf16[4,1024]{1,0:T(4,128)(2,1)S(1)}, bf16[4,1024]{1,0:T(4,128)(2,1)S(1)}, u32[]{:S(2)}, u32[]{:S(2)}) collective-permute-start(bf16[4,1024]{1,0:T(4,128)(2,1)S(1)} %get-tuple-element.43), channel_id=1, source_target_pairs={{0,6},{1,7},{2,4},{3,5},{4,2},{5,3},{6,0},{7,1},{8,14},{9,15},{10,... | collective-permute-start | bytes 24584 | tf_op jit(solution)/shard_map/ppermute | solution.py:35
  12.2 4.9 %collective-permute-start.5 = (bf16[4,1024]{1,0:T(4,128)(2,1)S(1)}, bf16[4,1024]{1,0:T(4,128)(2,1)S(1)}, u32[]{:S(2)}, u32[]{:S(2)}) collective-permute-start(bf16[4,1024]{1,0:T(4,128)(2,1)S(1)} %get-tuple-element.44), channel_id=1, source_target_pairs={{0,7},{1,6},{2,5},{3,4},{4,3},{5,2},{6,1},{7,0},{8,15},{9,14},{10,... | collective-permute-start | bytes 24584 | tf_op jit(solution)/shard_map/ppermute | solution.py:35
  17.0 8.4 %copy-start.2 = (f32[4096]{0:T(1024)S(1)}, f32[4096]{0:T(1024)}, u32[]{:S(2)}) copy-start(f32[4096]{0:T(1024)} %param.20) | copy-start | bytes 49156
  18.2 4.0 %collective-permute-start.6 = (bf16[4,4096]{1,0:T(4,128)(2,1)S(1)}, bf16[4,4096]{1,0:T(4,128)(2,1)S(1)}, u32[]{:S(2)}, u32[]{:S(2)}) collective-permute-start(bf16[4,4096]{1,0:T(4,128)(2,1)S(1)} %get-tuple-element.47), channel_id=1, source_target_pairs={{0,5},{1,4},{2,7},{3,6},{4,1},{5,0},{6,3},{7,2},{8,13},{9,12},{10,... | collective-permute-start | bytes 98312 | tf_op jit(solution)/shard_map/ppermute | solution.py:35
  18.3 4.3 %collective-permute-start.7 = (bf16[4,4096]{1,0:T(4,128)(2,1)S(1)}, bf16[4,4096]{1,0:T(4,128)(2,1)S(1)}, u32[]{:S(2)}, u32[]{:S(2)}) collective-permute-start(bf16[4,4096]{1,0:T(4,128)(2,1)S(1)} %get-tuple-element.48), channel_id=1, source_target_pairs={{0,6},{1,7},{2,4},{3,5},{4,2},{5,3},{6,0},{7,1},{8,14},{9,15},{10,... | collective-permute-start | bytes 98312 | tf_op jit(solution)/shard_map/ppermute | solution.py:35
  20.3 5.1 %collective-permute-start.8 = (bf16[4,4096]{1,0:T(4,128)(2,1)S(1)}, bf16[4,4096]{1,0:T(4,128)(2,1)S(1)}, u32[]{:S(2)}, u32[]{:S(2)}) collective-permute-start(bf16[4,4096]{1,0:T(4,128)(2,1)S(1)} %get-tuple-element.49), channel_id=1, source_target_pairs={{0,7},{1,6},{2,5},{3,4},{4,3},{5,2},{6,1},{7,0},{8,15},{9,14},{10,... | collective-permute-start | bytes 98312 | tf_op jit(solution)/shard_map/ppermute | solution.py:35
  25.6 5.4 %collective-permute-start.11 = (bf16[4,4224]{1,0:T(4,128)(2,1)S(1)}, bf16[4,4224]{1,0:T(4,128)(2,1)S(1)}, u32[]{:S(2)}, u32[]{:S(2)}) collective-permute-start(bf16[4,4224]{1,0:T(4,128)(2,1)S(1)} %get-tuple-element.52), channel_id=1, source_target_pairs={{0,7},{1,6},{2,5},{3,4},{4,3},{5,2},{6,1},{7,0},{8,15},{9,14},{10,... | collective-permute-start | bytes 101384 | tf_op jit(solution)/shard_map/ppermute | solution.py:35
  27.6 5.0 %collective-permute-start.10 = (bf16[4,4224]{1,0:T(4,128)(2,1)S(1)}, bf16[4,4224]{1,0:T(4,128)(2,1)S(1)}, u32[]{:S(2)}, u32[]{:S(2)}) collective-permute-start(bf16[4,4224]{1,0:T(4,128)(2,1)S(1)} %get-tuple-element.52), channel_id=1, source_target_pairs={{0,6},{1,7},{2,4},{3,5},{4,2},{5,3},{6,0},{7,1},{8,14},{9,15},{10,... | collective-permute-start | bytes 101384 | tf_op jit(solution)/shard_map/ppermute | solution.py:35
  27.6 5.0 %collective-permute-start.9 = (bf16[4,4224]{1,0:T(4,128)(2,1)S(1)}, bf16[4,4224]{1,0:T(4,128)(2,1)S(1)}, u32[]{:S(2)}, u32[]{:S(2)}) collective-permute-start(bf16[4,4224]{1,0:T(4,128)(2,1)S(1)} %get-tuple-element.52), channel_id=1, source_target_pairs={{0,5},{1,4},{2,7},{3,6},{4,1},{5,0},{6,3},{7,2},{8,13},{9,12},{10,... | collective-permute-start | bytes 101384 | tf_op jit(solution)/shard_map/ppermute | solution.py:35
  29.6 7.9 %collective-permute-start.13 = (bf16[4,4224]{1,0:T(4,128)(2,1)S(1)}, bf16[4,4224]{1,0:T(4,128)(2,1)S(1)}, u32[]{:S(2)}, u32[]{:S(2)}) collective-permute-start(bf16[4,4224]{1,0:T(4,128)(2,1)S(1)} %get-tuple-element.52), channel_id=1, source_target_pairs={{0,12},{4,8},{8,4},{12,0},{1,13},{5,9},{9,5},{13,1},{2,14},{6,10},... | collective-permute-start | bytes 101384 | tf_op jit(solution)/shard_map/ppermute | solution.py:442
  32.7 4.8 %collective-permute-start.14 = (bf16[3,4,4224]{2,1,0:T(4,128)(2,1)S(1)}, bf16[3,4,4224]{2,1,0:T(4,128)(2,1)S(1)}, u32[]{:S(2)}, u32[]{:S(2)}) collective-permute-start(bf16[3,4,4224]{2,1,0:T(4,128)(2,1)S(1)} %pad_maximum_fusion.2), channel_id=1, source_target_pairs={{0,12},{4,8},{8,4},{12,0},{1,13},{5,9},{9,5},{13,1},{2,14},{6,10},... | collective-permute-start | bytes 304136 | tf_op jit(solution)/shard_map/ppermute | solution.py:442
  34.1 5.9 %collective-permute-start.12 = (bf16[16,4224]{1,0:T(8,128)(2,1)S(1)}, bf16[16,4224]{1,0:T(8,128)(2,1)S(1)}, u32[]{:S(2)}, u32[]{:S(2)}) collective-permute-start(bf16[16,4224]{1,0:T(8,128)(2,1)S(1)} %pad_maximum_fusion.refs_1_), channel_id=1, source_target_pairs={{0,4},{4,0},{8,12},{12,8},{1,5},{5,1},{9,13},{13,9},{2,6},{6,2},{1... | collective-permute-start | bytes 405512 | tf_op jit(solution)/shard_map/ppermute | solution.py:442
  37.7 2.3 %collective-permute-start.15 = (bf16[16,4224]{1,0:T(8,128)(2,1)S(1)}, bf16[16,4224]{1,0:T(8,128)(2,1)S(1)}, u32[]{:S(2)}, u32[]{:S(2)}) collective-permute-start(bf16[16,4224]{1,0:T(8,128)(2,1)S(1)} %pad_maximum_fusion.1.refs_4_), channel_id=1, source_target_pairs={{0,4},{4,0},{8,12},{12,8},{1,5},{5,1},{9,13},{13,9},{2,6},{6,2},{1... | collective-permute-start | bytes 405512 | tf_op jit(solution)/shard_map/ppermute | solution.py:442
  43.6 1.4 %collective-permute-start.17 = (bf16[4,4,4096]{2,1,0:T(4,128)(2,1)S(1)}, bf16[4,4,4096]{2,1,0:T(4,128)(2,1)S(1)}, u32[]{:S(2)}, u32[]{:S(2)}) collective-permute-start(bf16[4,4,4096]{2,1,0:T(4,128)(2,1)S(1)} %get-tuple-element.58), channel_id=1, source_target_pairs={{0,4},{4,0},{8,12},{12,8},{1,5},{5,1},{9,13},{13,9},{2,6},{6,2},{1... | collective-permute-start | bytes 393224 | tf_op jit(solution)/shard_map/ppermute | solution.py:442
  44.0 3.0 %collective-permute-start.16 = (bf16[4,4,4096]{2,1,0:T(4,128)(2,1)S(1)}, bf16[4,4,4096]{2,1,0:T(4,128)(2,1)S(1)}, u32[]{:S(2)}, u32[]{:S(2)}) collective-permute-start(bf16[4,4,4096]{2,1,0:T(4,128)(2,1)S(1)} %get-tuple-element.56), channel_id=1, source_target_pairs={{0,4},{4,0},{8,12},{12,8},{1,5},{5,1},{9,13},{13,9},{2,6},{6,2},{1... | collective-permute-start | bytes 393224 | tf_op jit(solution)/shard_map/ppermute | solution.py:442
  45.1 4.7 %collective-permute-start.19 = (bf16[3,4,4096]{2,1,0:T(4,128)(2,1)S(1)}, bf16[3,4,4096]{2,1,0:T(4,128)(2,1)S(1)}, u32[]{:S(2)}, u32[]{:S(2)}) collective-permute-start(bf16[3,4,4096]{2,1,0:T(4,128)(2,1)S(1)} %add_convert_fusion.1), channel_id=1, source_target_pairs={{0,12},{4,8},{8,4},{12,0},{1,13},{5,9},{9,5},{13,1},{2,14},{6,10},... | collective-permute-start | bytes 294920 | tf_op jit(solution)/shard_map/ppermute | solution.py:442
  46.7 7.8 %collective-permute-start.18 = (bf16[4,4096]{1,0:T(4,128)(2,1)S(1)}, bf16[4,4096]{1,0:T(4,128)(2,1)S(1)}, u32[]{:S(2)}, u32[]{:S(2)}) collective-permute-start(bf16[4,4096]{1,0:T(4,128)(2,1)S(1)} %fusion.5), channel_id=1, source_target_pairs={{0,12},{4,8},{8,4},{12,0},{1,13},{5,9},{9,5},{13,1},{2,14},{6,10},... | collective-permute-start | bytes 98312 | tf_op jit(solution)/shard_map/ppermute | solution.py:442
  49.9 5.2 %collective-permute-start.22 = (bf16[4,4096]{1,0:T(4,128)(2,1)S(1)}, bf16[4,4096]{1,0:T(4,128)(2,1)S(1)}, u32[]{:S(2)}, u32[]{:S(2)}) collective-permute-start(bf16[4,4096]{1,0:T(4,128)(2,1)S(1)} %get-tuple-element.63), channel_id=1, source_target_pairs={{0,7},{1,6},{2,5},{3,4},{4,3},{5,2},{6,1},{7,0},{8,15},{9,14},{10,... | collective-permute-start | bytes 98312 | tf_op jit(solution)/shard_map/ppermute | solution.py:35
  52.5 4.8 %collective-permute-start.21 = (bf16[4,4096]{1,0:T(4,128)(2,1)S(1)}, bf16[4,4096]{1,0:T(4,128)(2,1)S(1)}, u32[]{:S(2)}, u32[]{:S(2)}) collective-permute-start(bf16[4,4096]{1,0:T(4,128)(2,1)S(1)} %get-tuple-element.64), channel_id=1, source_target_pairs={{0,6},{1,7},{2,4},{3,5},{4,2},{5,3},{6,0},{7,1},{8,14},{9,15},{10,... | collective-permute-start | bytes 98312 | tf_op jit(solution)/shard_map/ppermute | solution.py:35
  52.5 5.0 %collective-permute-start.20 = (bf16[4,4096]{1,0:T(4,128)(2,1)S(1)}, bf16[4,4096]{1,0:T(4,128)(2,1)S(1)}, u32[]{:S(2)}, u32[]{:S(2)}) collective-permute-start(bf16[4,4096]{1,0:T(4,128)(2,1)S(1)} %get-tuple-element.62), channel_id=1, source_target_pairs={{0,5},{1,4},{2,7},{3,6},{4,1},{5,0},{6,3},{7,2},{8,13},{9,12},{10,... | collective-permute-start | bytes 98312 | tf_op jit(solution)/shard_map/ppermute | solution.py:35
  (2 other events, 6.6 us)

commit v3 on v2

--- a/solution.py
+++ b/solution.py
@@ -53,38 +53,53 @@
     )
 
 
-def attend(q_row, fresh_row, keys_values, length, q_scr, put, kv_heads):
-    heads = q_row.shape[1] // HD
-    group = heads // kv_heads
-    for h in range(heads):
-        q_scr[h : h + 1, :] = q_row[:, h * HD : (h + 1) * HD].astype(F32)
+def attend(jobs, kv_heads):
+    chains = []
+    for q_row, _, q_scr, _, _, _ in jobs:
+        heads = q_row.shape[1] // HD
+        for h in range(heads):
+            q_scr[h : h + 1, :] = q_row[:, h * HD : (h + 1) * HD].astype(F32)
+    for job in jobs:
+        q_row, fresh_row, q_scr, _, _, _ = job
+        group = q_row.shape[1] // HD // kv_heads
+        for g in range(kv_heads):
+            q = q_scr[g * group : (g + 1) * group, :]
+            own_key = fresh_row[:, g * HD : (g + 1) * HD].astype(F32)
+            own = jnp.sum(q * own_key, axis=-1, keepdims=True) * HD ** (-0.5)
+            chains.append([job, g, group, q.astype(BF16), own])
+    return chains
+
+
+def attend_cache(chains, kv_heads):
     width = kv_heads * HD
-    context = keys_values.shape[0]
-    for g in range(kv_heads):
-        q = q_scr[g * group : (g + 1) * group, :]
-        keys = keys_values[:, g * HD : (g + 1) * HD]
-        values = keys_values[:, width + g * HD : width + (g + 1) * HD]
-        scores = (
-            lax.dot_general(
-                q.astype(BF16), keys, (((1,), (1,)), ((), ())), preferred_element_type=F32
-            )
+    all_scores = []
+    for (_, _, _, cache, _, _), g, _, q, _ in chains:
+        keys = cache[:, g * HD : (g + 1) * HD]
+        all_scores.append(
+            lax.dot_general(q, keys, (((1,), (1,)), ((), ())), preferred_element_type=F32)
             * HD ** (-0.5)
         )
+    parts = []
+    for scores, ((_, _, _, _, length, _), _, _, _, own) in zip(all_scores, chains):
         if length is not None:
-            valid = lax.broadcasted_iota(jnp.int32, (group, context), 1) < length
+            valid = lax.broadcasted_iota(jnp.int32, scores.shape, 1) < length
             scores = jnp.where(valid, scores, -1e30)
         top_cache = jnp.max(scores, axis=-1, keepdims=True)
         weights = jnp.exp(scores - top_cache)
         if length is not None:
             weights = jnp.where(valid, weights, 0.0)
         total = jnp.sum(weights, axis=-1, keepdims=True)
-        mixed = jnp.dot(weights.astype(BF16), values, preferred_element_type=F32)
-        own_key = fresh_row[:, g * HD : (g + 1) * HD].astype(F32)
+        top = jnp.maximum(top_cache, own)
+        parts.append((weights.astype(BF16), total, jnp.exp(top_cache - top), jnp.exp(own - top)))
+    mixes = []
+    for (weights, _, _, _), ((_, _, _, cache, _, _), g, _, _, _) in zip(parts, chains):
+        values = cache[:, width + g * HD : width + (g + 1) * HD]
+        mixes.append(jnp.dot(weights, values, preferred_element_type=F32))
+    for mixed, (_, total, cache_factor, own_factor), (job, g, group, _, _) in zip(
+        mixes, parts, chains
+    ):
+        _, fresh_row, _, _, _, put = job
         own_value = fresh_row[:, width + g * HD : width + (g + 1) * HD].astype(F32)
-        own = jnp.sum(q * own_key, axis=-1, keepdims=True) * HD ** (-0.5)
-        top = jnp.maximum(top_cache, own)
-        cache_factor = jnp.exp(top_cache - top)
-        own_factor = jnp.exp(own - top)
         done = (cache_factor * mixed + own_factor * own_value) / (
             cache_factor * total + own_factor
         )
@@ -162,16 +177,22 @@
     weight = fetch(w_hbm, w_ref, w_sems)
     for copy in copies[1:] + copies[:1] + weight:
         copy.start()
+    jobs = []
     for t in range(1, tokens):
-        copies[t].wait()
 
         def put(head, row, t=t):
             att_ref[head // per, t : t + 1, (head % per) * HD : (head % per + 1) * HD] = row
 
-        attend(
-            q_ref[t : t + 1, :], fresh_ref[t : t + 1, :], kv.at[t - 1],
-            info_ref[t : t + 1, 0:1], q_scr.at[t], put, kv_heads,
+        jobs.append(
+            (
+                q_ref[t : t + 1, :], fresh_ref[t : t + 1, :], q_scr.at[t], kv.at[t - 1],
+                info_ref[t : t + 1, 0:1], put,
+            )
         )
+    chains = attend(jobs, kv_heads)
+    for copy in copies[1:]:
+        copy.wait()
+    attend_cache(chains, kv_heads)
     for s in range(parts):
         att_ref[s, 0:1, :] = jnp.zeros((1, part), F32)
     goals.wait()
@@ -235,10 +256,8 @@
     def put(head, value):
         full[head // per, 0:1, (head % per) * HD : (head % per + 1) * HD] = value
 
-    attend(
-        row_scr[:, :model], row_scr[:, model : model + width], kv0_ref,
-        None, q_scr, put, kv_heads,
-    )
+    job = (row_scr[:, :model], row_scr[:, model : model + width], q_scr, kv0_ref, None, put)
+    attend_cache(attend([job], kv_heads), kv_heads)
     for s in range(n_ex):
         outs[s][...] = full[s ^ ex].astype(BF16)
     first = lax.broadcasted_iota(jnp.int32, (res_ref.shape[0], 1), 0) == 0
@@ -373,7 +392,7 @@
     )(*map(in_hbm, small))
     rows = xor_exchange([row] * n_dp, "dp", n_dp)
 
-    early = part // 4
+    early = part // 2
     att, kv0, out_early, targets = call(
         functools.partial(local_kernel, n_dp, kv_heads),
         [

time: 58.3 us -> 57.5 us (0.986)
  Pallas kernels: 12.8 us -> 11.8 us
    pallas_call x2, Pallas kernels: 4.89 us -> 4.23 us  [fetched(): call(functools.partial(fetch_kernel, rows_from), jax.ShapeDtypeStruct((ro...]
  transfers between devices with their start and end apart: 23 -> 23, of which waited for: 11 -> 10; matrix products, arithmetic and copies ran while one was open for 1% -> 1% of each run, Pallas kernels for 14% -> 12%
where the time goes in v3:
time: 57.5 us; the launch traced here: 57.4 us
  starting transfers between devices  25.6 us (45%)
  waiting for transfers between devices  16.9 us (29%)
  Pallas kernels  11.8 us (21%)
  local copies, waits for them, and re-layouts  1.81 us (3%)
  other arithmetic  1.08 us (2%)
    ppermute x12, starting transfers between devices, crossed_exchange(): moved[step] = lax.ppermute(blocks[step], ('dp', 'expert'), pairs)  16.6 us
    ppermute x12, waiting for transfers between devices, crossed_exchange(): moved[step] = lax.ppermute(blocks[step], ('dp', 'expert'), pairs)  9.8 us
    ppermute x8, waiting for transfers between devices, over_dp(): return lax.ppermute(array, 'dp', [(j, j ^ turn) for j in range(n_dp)])  6.62 us
    ppermute x8, starting transfers between devices, over_dp(): return lax.ppermute(array, 'dp', [(j, j ^ turn) for j in range(n_dp)])  5.88 us
    pallas_call x2, Pallas kernels, fetched(): call(functools.partial(fetch_kernel, rows_from), jax.ShapeDtypeStruct((ro...  4.23 us
    ppermute x3, starting transfers between devices, xor_exchange(): lax.ppermute(blocks[step], axis, [(j, j ^ step) for j in range(count)])  3.18 us
    pallas_call x1, Pallas kernels, per_device(): call(functools.partial(local_kernel, n_dp, kv_heads), [shape((n_ex, token...  2.92 us
    pallas_call x1, Pallas kernels, per_device(): call(functools.partial(expert_kernel, n_dp, n_ex, tokens), [shape((n_ex,...  1.85 us
  transfers between devices with their start and end apart: 23, of which 10 were waited for; matrix products, arithmetic and copies ran while one was open for 1% of the time, Pallas kernels for 12%

profile of v3, /device:TPU:0, one launch (start us, length us, event | category | flops | bytes accessed | tf_op | source)
XLA Modules:
  0.0 57.4 jit_solution(2828502328852444068)
XLA Ops:
  1.5 2.6 %collective-permute-start.1 = (bf16[1,8832]{1,0:T(2,128)(2,1)S(1)}, bf16[1,8832]{1,0:T(2,128)(2,1)S(1)}, u32[]{:S(2)}, u32[]{:S(2)}) collective-permute-start(bf16[1,8832]{1,0:T(2,128)(2,1)S(1)} %get-tuple-element.36.refs_1_), channel_id=1, source_target_pairs={{0,8},{4,12},{8,0},{12,4},{1,9},{5,13},{9,1},{13,5},{2,10},{6,14},... | collective-permute-start | bytes 53000 | tf_op jit(solution)/shard_map/ppermute | solution.py:21
  4.1 2.9 %shard_map.128 = (f32[4,4,1024]{2,1,0:T(4,128)S(1)}, bf16[512,512]{1,0:T(8,128)(2,1)S(1)}, bf16[512,4096]{1,0:T(8,128)(2,1)S(1)}, s32[24,128]{1,0:T(8,128)S(1)}) custom-call(s32[8,128]{1,0:T(8,128)S(1)} %get-tuple-element.32.info_ref.refs_0_, bf16[4,4096]{1,0:T(4,128)(2,1)S(1)} %get-tuple-element.33.q_ref, bf16[4,512]{1,0:T(4,128)(2,1)S(1)} %get-tuple-element.34.fresh_ref, ...), custom_call_target="tpu_custom_call" | custom-call | flops 33554432 | bytes 6291456 | tf_op jit(solution)/shard_map/pallas_call | solution.py:396
  8.0 1.4 %collective-permute-start.3 = (bf16[4,1024]{1,0:T(4,128)(2,1)S(1)}, bf16[4,1024]{1,0:T(4,128)(2,1)S(1)}, u32[]{:S(2)}, u32[]{:S(2)}) collective-permute-start(bf16[4,1024]{1,0:T(4,128)(2,1)S(1)} %get-tuple-element.42), channel_id=1, source_target_pairs={{0,5},{1,4},{2,7},{3,6},{4,1},{5,0},{6,3},{7,2},{8,13},{9,12},{10,... | collective-permute-start | bytes 24584 | tf_op jit(solution)/shard_map/ppermute | solution.py:35
  9.4 2.5 %collective-permute-start.4 = (bf16[4,1024]{1,0:T(4,128)(2,1)S(1)}, bf16[4,1024]{1,0:T(4,128)(2,1)S(1)}, u32[]{:S(2)}, u32[]{:S(2)}) collective-permute-start(bf16[4,1024]{1,0:T(4,128)(2,1)S(1)} %get-tuple-element.43), channel_id=1, source_target_pairs={{0,6},{1,7},{2,4},{3,5},{4,2},{5,3},{6,0},{7,1},{8,14},{9,15},{10,... | collective-permute-start | bytes 24584 | tf_op jit(solution)/shard_map/ppermute | solution.py:35
  12.0 2.2 %shard_map.130.refs_5_ = bf16[512,4096]{1,0:T(8,128)(2,1)S(1)} custom-call(bf16[1024,4096]{1,0:T(8,128)(2,1)} %source.1), custom_call_target="tpu_custom_call" | custom-call | bytes 8388608 | tf_op jit(solution)/shard_map/pallas_call | solution.py:224
  14.2 2.6 %collective-permute-done.5.refs_3_ = bf16[4,1024]{1,0:T(4,128)(2,1)S(1)} collective-permute-done((bf16[4,1024]{1,0:T(4,128)(2,1)S(1)}, bf16[4,1024]{1,0:T(4,128)(2,1)S(1)}, u32[]{:S(2)}, u32[]{:S(2)}) %collective-permute-start.5) | collective-permute-done | bytes 8224 | tf_op jit(solution)/shard_map/ppermute | solution.py:35
  16.8 1.2 %shard_map.131 = (f32[4,4096]{1,0:T(4,128)S(1)}, bf16[4,4096]{1,0:T(4,128)(2,1)S(1)}, bf16[4,4096]{1,0:T(4,128)(2,1)S(1)}, bf16[4,4096]{1,0:T(4,128)(2,1)S(1)}) custom-call(bf16[4,1024]{1,0:T(4,128)(2,1)S(1)} %get-tuple-element.41.refs_0_, bf16[4,1024]{1,0:T(4,128)(2,1)S(1)} %collective-permute-done.3.refs_1_, ...), custom_call_target="tpu_custom_call" | custom-call | flops 134217728 | bytes 8388608 | tf_op jit(solution)/shard_map/pallas_call | solution.py:436
  18.1 1.3 %collective-permute-start.7 = (bf16[4,4096]{1,0:T(4,128)(2,1)S(1)}, bf16[4,4096]{1,0:T(4,128)(2,1)S(1)}, u32[]{:S(2)}, u32[]{:S(2)}) collective-permute-start(bf16[4,4096]{1,0:T(4,128)(2,1)S(1)} %get-tuple-element.48), channel_id=1, source_target_pairs={{0,6},{1,7},{2,4},{3,5},{4,2},{5,3},{6,0},{7,1},{8,14},{9,15},{10,... | collective-permute-start | bytes 98312 | tf_op jit(solution)/shard_map/ppermute | solution.py:35
  19.3 2.6 %collective-permute-start.8 = (bf16[4,4096]{1,0:T(4,128)(2,1)S(1)}, bf16[4,4096]{1,0:T(4,128)(2,1)S(1)}, u32[]{:S(2)}, u32[]{:S(2)}) collective-permute-start(bf16[4,4096]{1,0:T(4,128)(2,1)S(1)} %get-tuple-element.49), channel_id=1, source_target_pairs={{0,7},{1,6},{2,5},{3,4},{4,3},{5,2},{6,1},{7,0},{8,15},{9,14},{10,... | collective-permute-start | bytes 98312 | tf_op jit(solution)/shard_map/ppermute | solution.py:35
  22.4 2.1 %collective-permute-done.8.refs_3_ = bf16[4,4096]{1,0:T(4,128)(2,1)S(1)} collective-permute-done((bf16[4,4096]{1,0:T(4,128)(2,1)S(1)}, bf16[4,4096]{1,0:T(4,128)(2,1)S(1)}, u32[]{:S(2)}, u32[]{:S(2)}) %collective-permute-start.8) | collective-permute-done | bytes 32800 | tf_op jit(solution)/shard_map/ppermute | solution.py:35
  24.6 2.7 %collective-permute-start.11 = (bf16[4,4224]{1,0:T(4,128)(2,1)S(1)}, bf16[4,4224]{1,0:T(4,128)(2,1)S(1)}, u32[]{:S(2)}, u32[]{:S(2)}) collective-permute-start(bf16[4,4224]{1,0:T(4,128)(2,1)S(1)} %get-tuple-element.52), channel_id=1, source_target_pairs={{0,7},{1,6},{2,5},{3,4},{4,3},{5,2},{6,1},{7,0},{8,15},{9,14},{10,... | collective-permute-start | bytes 101384 | tf_op jit(solution)/shard_map/ppermute | solution.py:35
  27.3 1.4 %collective-permute-start.9 = (bf16[4,4224]{1,0:T(4,128)(2,1)S(1)}, bf16[4,4224]{1,0:T(4,128)(2,1)S(1)}, u32[]{:S(2)}, u32[]{:S(2)}) collective-permute-start(bf16[4,4224]{1,0:T(4,128)(2,1)S(1)} %get-tuple-element.52), channel_id=1, source_target_pairs={{0,5},{1,4},{2,7},{3,6},{4,1},{5,0},{6,3},{7,2},{8,13},{9,12},{10,... | collective-permute-start | bytes 101384 | tf_op jit(solution)/shard_map/ppermute | solution.py:35
  28.8 1.3 %collective-permute-start.13 = (bf16[4,4224]{1,0:T(4,128)(2,1)S(1)}, bf16[4,4224]{1,0:T(4,128)(2,1)S(1)}, u32[]{:S(2)}, u32[]{:S(2)}) collective-permute-start(bf16[4,4224]{1,0:T(4,128)(2,1)S(1)} %get-tuple-element.52), channel_id=1, source_target_pairs={{0,12},{4,8},{8,4},{12,0},{1,13},{5,9},{9,5},{13,1},{2,14},{6,10},... | collective-permute-start | bytes 101384 | tf_op jit(solution)/shard_map/ppermute | solution.py:461
  30.1 1.5 %collective-permute-done.10 = bf16[4,4224]{1,0:T(4,128)(2,1)S(1)} collective-permute-done((bf16[4,4224]{1,0:T(4,128)(2,1)S(1)}, bf16[4,4224]{1,0:T(4,128)(2,1)S(1)}, u32[]{:S(2)}, u32[]{:S(2)}) %collective-permute-start.10) | collective-permute-done | bytes 33824 | tf_op jit(solution)/shard_map/ppermute | solution.py:35
  31.7 1.3 %collective-permute-start.14 = (bf16[3,4,4224]{2,1,0:T(4,128)(2,1)S(1)}, bf16[3,4,4224]{2,1,0:T(4,128)(2,1)S(1)}, u32[]{:S(2)}, u32[]{:S(2)}) collective-permute-start(bf16[3,4,4224]{2,1,0:T(4,128)(2,1)S(1)} %pad_maximum_fusion.2), channel_id=1, source_target_pairs={{0,12},{4,8},{8,4},{12,0},{1,13},{5,9},{9,5},{13,1},{2,14},{6,10},... | collective-permute-start | bytes 304136 | tf_op jit(solution)/shard_map/ppermute | solution.py:461
  33.5 2.9 %collective-permute-done.14 = bf16[3,4,4224]{2,1,0:T(4,128)(2,1)S(1)} collective-permute-done((bf16[3,4,4224]{2,1,0:T(4,128)(2,1)S(1)}, bf16[3,4,4224]{2,1,0:T(4,128)(2,1)S(1)}, u32[]{:S(2)}, u32[]{:S(2)}) %collective-permute-start.14) | collective-permute-done | bytes 101408 | tf_op jit(solution)/shard_map/ppermute | solution.py:461
  37.0 2.0 %shard_map.133.refs_7_ = bf16[384,4096]{1,0:T(8,128)(2,1)S(1)} custom-call(bf16[384,4096]{1,0:T(8,128)(2,1)} %bitcast.35), custom_call_target="tpu_custom_call" | custom-call | bytes 6291456 | tf_op jit(solution)/shard_map/pallas_call | solution.py:224
  39.8 1.0 %copy-done.1 = bf16[1,4096,384]{2,1,0:T(8,128)(2,1)S(1)} copy-done((bf16[1,4096,384]{2,1,0:T(8,128)(2,1)S(1)}, bf16[1,4096,384]{2,1,0:T(8,128)(2,1)}, u32[]{:S(2)}) %copy-start.1) | copy-done | bytes 3145752
  40.7 1.9 %shard_map.134 = (bf16[4,4,4096]{2,1,0:T(4,128)(2,1)S(1)}, bf16[4,4,4096]{2,1,0:T(4,128)(2,1)S(1)}, bf16[4,4,4096]{2,1,0:T(4,128)(2,1)S(1)}, bf16[4,4,4096]{2,1,0:T(4,128)(2,1)S(1)}, f32[4,4096]{1,0:T(4,128)S(1)}) custom-call(s32[24,128]{1,0:T(8,128)S(1)} %get-tuple-element.35.refs_0_, bf16[16,4224]{1,0:T(8,128)(2,1)S(1)} %pad_maximum_fusion.refs_1_, ...), custom_call_target="tpu_custom_call" | custom-call | flops 603979776 | bytes 9437184 | tf_op jit(solution)/shard_map/pallas_call | solution.py:478
  44.1 1.5 %collective-permute-start.19 = (bf16[3,4,4096]{2,1,0:T(4,128)(2,1)S(1)}, bf16[3,4,4096]{2,1,0:T(4,128)(2,1)S(1)}, u32[]{:S(2)}, u32[]{:S(2)}) collective-permute-start(bf16[3,4,4096]{2,1,0:T(4,128)(2,1)S(1)} %add_convert_fusion.1), channel_id=1, source_target_pairs={{0,12},{4,8},{8,4},{12,0},{1,13},{5,9},{9,5},{13,1},{2,14},{6,10},... | collective-permute-start | bytes 294920 | tf_op jit(solution)/shard_map/ppermute | solution.py:461
  46.0 2.9 %collective-permute-done.19 = bf16[3,4,4096]{2,1,0:T(4,128)(2,1)S(1)} collective-permute-done((bf16[3,4,4096]{2,1,0:T(4,128)(2,1)S(1)}, bf16[3,4,4096]{2,1,0:T(4,128)(2,1)S(1)}, u32[]{:S(2)}, u32[]{:S(2)}) %collective-permute-start.19) | collective-permute-done | bytes 98336 | tf_op jit(solution)/shard_map/ppermute | solution.py:461
  49.0 3.2 %collective-permute-start.22 = (bf16[4,4096]{1,0:T(4,128)(2,1)S(1)}, bf16[4,4096]{1,0:T(4,128)(2,1)S(1)}, u32[]{:S(2)}, u32[]{:S(2)}) collective-permute-start(bf16[4,4096]{1,0:T(4,128)(2,1)S(1)} %get-tuple-element.63), channel_id=1, source_target_pairs={{0,7},{1,6},{2,5},{3,4},{4,3},{5,2},{6,1},{7,0},{8,15},{9,14},{10,... | collective-permute-start | bytes 98312 | tf_op jit(solution)/shard_map/ppermute | solution.py:35
  52.2 1.4 %collective-permute-start.20 = (bf16[4,4096]{1,0:T(4,128)(2,1)S(1)}, bf16[4,4096]{1,0:T(4,128)(2,1)S(1)}, u32[]{:S(2)}, u32[]{:S(2)}) collective-permute-start(bf16[4,4096]{1,0:T(4,128)(2,1)S(1)} %get-tuple-element.62), channel_id=1, source_target_pairs={{0,5},{1,4},{2,7},{3,6},{4,1},{5,0},{6,3},{7,2},{8,13},{9,12},{10,... | collective-permute-start | bytes 98312 | tf_op jit(solution)/shard_map/ppermute | solution.py:35
  54.2 2.5 %collective-permute-done.21 = bf16[4,4096]{1,0:T(4,128)(2,1)S(1)} collective-permute-done((bf16[4,4096]{1,0:T(4,128)(2,1)S(1)}, bf16[4,4096]{1,0:T(4,128)(2,1)S(1)}, u32[]{:S(2)}, u32[]{:S(2)}) %collective-permute-start.21) | collective-permute-done | bytes 32800 | tf_op jit(solution)/shard_map/ppermute | solution.py:35
  (45 shorter events, 8.2 us)
Async XLA Ops:
  0.9 6.1 %collective-permute-start = (bf16[1,8832]{1,0:T(2,128)(2,1)S(1)}, bf16[1,8832]{1,0:T(2,128)(2,1)S(1)}, u32[]{:S(2)}, u32[]{:S(2)}) collective-permute-start(bf16[1,8832]{1,0:T(2,128)(2,1)S(1)} %get-tuple-element.36.refs_1_), channel_id=1, source_target_pairs={{0,4},{4,0},{8,12},{12,8},{1,5},{5,1},{9,13},{13,9},{2,6},{6,2},{1... | collective-permute-start | bytes 53000 | tf_op jit(solution)/shard_map/ppermute | solution.py:21
  1.5 5.6 %collective-permute-start.1 = (bf16[1,8832]{1,0:T(2,128)(2,1)S(1)}, bf16[1,8832]{1,0:T(2,128)(2,1)S(1)}, u32[]{:S(2)}, u32[]{:S(2)}) collective-permute-start(bf16[1,8832]{1,0:T(2,128)(2,1)S(1)} %get-tuple-element.36.refs_1_), channel_id=1, source_target_pairs={{0,8},{4,12},{8,0},{12,4},{1,9},{5,13},{9,1},{13,5},{2,10},{6,14},... | collective-permute-start | bytes 53000 | tf_op jit(solution)/shard_map/ppermute | solution.py:21
  4.1 3.4 %collective-permute-start.2 = (bf16[1,8832]{1,0:T(2,128)(2,1)S(1)}, bf16[1,8832]{1,0:T(2,128)(2,1)S(1)}, u32[]{:S(2)}, u32[]{:S(2)}) collective-permute-start(bf16[1,8832]{1,0:T(2,128)(2,1)S(1)} %get-tuple-element.36.refs_1_), channel_id=1, source_target_pairs={{0,12},{4,8},{8,4},{12,0},{1,13},{5,9},{9,5},{13,1},{2,14},{6,10},... | collective-permute-start | bytes 53000 | tf_op jit(solution)/shard_map/ppermute | solution.py:21
  8.0 6.2 %collective-permute-start.3 = (bf16[4,1024]{1,0:T(4,128)(2,1)S(1)}, bf16[4,1024]{1,0:T(4,128)(2,1)S(1)}, u32[]{:S(2)}, u32[]{:S(2)}) collective-permute-start(bf16[4,1024]{1,0:T(4,128)(2,1)S(1)} %get-tuple-element.42), channel_id=1, source_target_pairs={{0,5},{1,4},{2,7},{3,6},{4,1},{5,0},{6,3},{7,2},{8,13},{9,12},{10,... | collective-permute-start | bytes 24584 | tf_op jit(solution)/shard_map/ppermute | solution.py:35
  9.4 4.8 %collective-permute-start.4 = (bf16[4,1024]{1,0:T(4,128)(2,1)S(1)}, bf16[4,1024]{1,0:T(4,128)(2,1)S(1)}, u32[]{:S(2)}, u32[]{:S(2)}) collective-permute-start(bf16[4,1024]{1,0:T(4,128)(2,1)S(1)} %get-tuple-element.43), channel_id=1, source_target_pairs={{0,6},{1,7},{2,4},{3,5},{4,2},{5,3},{6,0},{7,1},{8,14},{9,15},{10,... | collective-permute-start | bytes 24584 | tf_op jit(solution)/shard_map/ppermute | solution.py:35
  12.0 4.9 %collective-permute-start.5 = (bf16[4,1024]{1,0:T(4,128)(2,1)S(1)}, bf16[4,1024]{1,0:T(4,128)(2,1)S(1)}, u32[]{:S(2)}, u32[]{:S(2)}) collective-permute-start(bf16[4,1024]{1,0:T(4,128)(2,1)S(1)} %get-tuple-element.44), channel_id=1, source_target_pairs={{0,7},{1,6},{2,5},{3,4},{4,3},{5,2},{6,1},{7,0},{8,15},{9,14},{10,... | collective-permute-start | bytes 24584 | tf_op jit(solution)/shard_map/ppermute | solution.py:35
  16.8 7.6 %copy-start.2 = (f32[4096]{0:T(1024)S(1)}, f32[4096]{0:T(1024)}, u32[]{:S(2)}) copy-start(f32[4096]{0:T(1024)} %param.20) | copy-start | bytes 49156
  18.1 3.9 %collective-permute-start.6 = (bf16[4,4096]{1,0:T(4,128)(2,1)S(1)}, bf16[4,4096]{1,0:T(4,128)(2,1)S(1)}, u32[]{:S(2)}, u32[]{:S(2)}) collective-permute-start(bf16[4,4096]{1,0:T(4,128)(2,1)S(1)} %get-tuple-element.47), channel_id=1, source_target_pairs={{0,5},{1,4},{2,7},{3,6},{4,1},{5,0},{6,3},{7,2},{8,13},{9,12},{10,... | collective-permute-start | bytes 98312 | tf_op jit(solution)/shard_map/ppermute | solution.py:35
  18.1 4.3 %collective-permute-start.7 = (bf16[4,4096]{1,0:T(4,128)(2,1)S(1)}, bf16[4,4096]{1,0:T(4,128)(2,1)S(1)}, u32[]{:S(2)}, u32[]{:S(2)}) collective-permute-start(bf16[4,4096]{1,0:T(4,128)(2,1)S(1)} %get-tuple-element.48), channel_id=1, source_target_pairs={{0,6},{1,7},{2,4},{3,5},{4,2},{5,3},{6,0},{7,1},{8,14},{9,15},{10,... | collective-permute-start | bytes 98312 | tf_op jit(solution)/shard_map/ppermute | solution.py:35
  19.3 5.1 %collective-permute-start.8 = (bf16[4,4096]{1,0:T(4,128)(2,1)S(1)}, bf16[4,4096]{1,0:T(4,128)(2,1)S(1)}, u32[]{:S(2)}, u32[]{:S(2)}) collective-permute-start(bf16[4,4096]{1,0:T(4,128)(2,1)S(1)} %get-tuple-element.49), channel_id=1, source_target_pairs={{0,7},{1,6},{2,5},{3,4},{4,3},{5,2},{6,1},{7,0},{8,15},{9,14},{10,... | collective-permute-start | bytes 98312 | tf_op jit(solution)/shard_map/ppermute | solution.py:35
  24.6 5.4 %collective-permute-start.11 = (bf16[4,4224]{1,0:T(4,128)(2,1)S(1)}, bf16[4,4224]{1,0:T(4,128)(2,1)S(1)}, u32[]{:S(2)}, u32[]{:S(2)}) collective-permute-start(bf16[4,4224]{1,0:T(4,128)(2,1)S(1)} %get-tuple-element.52), channel_id=1, source_target_pairs={{0,7},{1,6},{2,5},{3,4},{4,3},{5,2},{6,1},{7,0},{8,15},{9,14},{10,... | collective-permute-start | bytes 101384 | tf_op jit(solution)/shard_map/ppermute | solution.py:35
  27.3 4.3 %collective-permute-start.10 = (bf16[4,4224]{1,0:T(4,128)(2,1)S(1)}, bf16[4,4224]{1,0:T(4,128)(2,1)S(1)}, u32[]{:S(2)}, u32[]{:S(2)}) collective-permute-start(bf16[4,4224]{1,0:T(4,128)(2,1)S(1)} %get-tuple-element.52), channel_id=1, source_target_pairs={{0,6},{1,7},{2,4},{3,5},{4,2},{5,3},{6,0},{7,1},{8,14},{9,15},{10,... | collective-permute-start | bytes 101384 | tf_op jit(solution)/shard_map/ppermute | solution.py:35
  27.3 4.3 %collective-permute-start.9 = (bf16[4,4224]{1,0:T(4,128)(2,1)S(1)}, bf16[4,4224]{1,0:T(4,128)(2,1)S(1)}, u32[]{:S(2)}, u32[]{:S(2)}) collective-permute-start(bf16[4,4224]{1,0:T(4,128)(2,1)S(1)} %get-tuple-element.52), channel_id=1, source_target_pairs={{0,5},{1,4},{2,7},{3,6},{4,1},{5,0},{6,3},{7,2},{8,13},{9,12},{10,... | collective-permute-start | bytes 101384 | tf_op jit(solution)/shard_map/ppermute | solution.py:35
  28.8 7.7 %collective-permute-start.13 = (bf16[4,4224]{1,0:T(4,128)(2,1)S(1)}, bf16[4,4224]{1,0:T(4,128)(2,1)S(1)}, u32[]{:S(2)}, u32[]{:S(2)}) collective-permute-start(bf16[4,4224]{1,0:T(4,128)(2,1)S(1)} %get-tuple-element.52), channel_id=1, source_target_pairs={{0,12},{4,8},{8,4},{12,0},{1,13},{5,9},{9,5},{13,1},{2,14},{6,10},... | collective-permute-start | bytes 101384 | tf_op jit(solution)/shard_map/ppermute | solution.py:461
  31.7 4.7 %collective-permute-start.14 = (bf16[3,4,4224]{2,1,0:T(4,128)(2,1)S(1)}, bf16[3,4,4224]{2,1,0:T(4,128)(2,1)S(1)}, u32[]{:S(2)}, u32[]{:S(2)}) collective-permute-start(bf16[3,4,4224]{2,1,0:T(4,128)(2,1)S(1)} %pad_maximum_fusion.2), channel_id=1, source_target_pairs={{0,12},{4,8},{8,4},{12,0},{1,13},{5,9},{9,5},{13,1},{2,14},{6,10},... | collective-permute-start | bytes 304136 | tf_op jit(solution)/shard_map/ppermute | solution.py:461
  33.1 5.9 %collective-permute-start.12 = (bf16[16,4224]{1,0:T(8,128)(2,1)S(1)}, bf16[16,4224]{1,0:T(8,128)(2,1)S(1)}, u32[]{:S(2)}, u32[]{:S(2)}) collective-permute-start(bf16[16,4224]{1,0:T(8,128)(2,1)S(1)} %pad_maximum_fusion.refs_1_), channel_id=1, source_target_pairs={{0,4},{4,0},{8,12},{12,8},{1,5},{5,1},{9,13},{13,9},{2,6},{6,2},{1... | collective-permute-start | bytes 405512 | tf_op jit(solution)/shard_map/ppermute | solution.py:461
  36.6 2.4 %collective-permute-start.15 = (bf16[16,4224]{1,0:T(8,128)(2,1)S(1)}, bf16[16,4224]{1,0:T(8,128)(2,1)S(1)}, u32[]{:S(2)}, u32[]{:S(2)}) collective-permute-start(bf16[16,4224]{1,0:T(8,128)(2,1)S(1)} %pad_maximum_fusion.1.refs_4_), channel_id=1, source_target_pairs={{0,4},{4,0},{8,12},{12,8},{1,5},{5,1},{9,13},{13,9},{2,6},{6,2},{1... | collective-permute-start | bytes 405512 | tf_op jit(solution)/shard_map/ppermute | solution.py:461
  42.6 1.4 %collective-permute-start.17 = (bf16[4,4,4096]{2,1,0:T(4,128)(2,1)S(1)}, bf16[4,4,4096]{2,1,0:T(4,128)(2,1)S(1)}, u32[]{:S(2)}, u32[]{:S(2)}) collective-permute-start(bf16[4,4,4096]{2,1,0:T(4,128)(2,1)S(1)} %get-tuple-element.58), channel_id=1, source_target_pairs={{0,4},{4,0},{8,12},{12,8},{1,5},{5,1},{9,13},{13,9},{2,6},{6,2},{1... | collective-permute-start | bytes 393224 | tf_op jit(solution)/shard_map/ppermute | solution.py:461
  42.9 3.1 %collective-permute-start.16 = (bf16[4,4,4096]{2,1,0:T(4,128)(2,1)S(1)}, bf16[4,4,4096]{2,1,0:T(4,128)(2,1)S(1)}, u32[]{:S(2)}, u32[]{:S(2)}) collective-permute-start(bf16[4,4,4096]{2,1,0:T(4,128)(2,1)S(1)} %get-tuple-element.56), channel_id=1, source_target_pairs={{0,4},{4,0},{8,12},{12,8},{1,5},{5,1},{9,13},{13,9},{2,6},{6,2},{1... | collective-permute-start | bytes 393224 | tf_op jit(solution)/shard_map/ppermute | solution.py:461
  44.1 4.8 %collective-permute-start.19 = (bf16[3,4,4096]{2,1,0:T(4,128)(2,1)S(1)}, bf16[3,4,4096]{2,1,0:T(4,128)(2,1)S(1)}, u32[]{:S(2)}, u32[]{:S(2)}) collective-permute-start(bf16[3,4,4096]{2,1,0:T(4,128)(2,1)S(1)} %add_convert_fusion.1), channel_id=1, source_target_pairs={{0,12},{4,8},{8,4},{12,0},{1,13},{5,9},{9,5},{13,1},{2,14},{6,10},... | collective-permute-start | bytes 294920 | tf_op jit(solution)/shard_map/ppermute | solution.py:461
  45.6 7.9 %collective-permute-start.18 = (bf16[4,4096]{1,0:T(4,128)(2,1)S(1)}, bf16[4,4096]{1,0:T(4,128)(2,1)S(1)}, u32[]{:S(2)}, u32[]{:S(2)}) collective-permute-start(bf16[4,4096]{1,0:T(4,128)(2,1)S(1)} %fusion.5), channel_id=1, source_target_pairs={{0,12},{4,8},{8,4},{12,0},{1,13},{5,9},{9,5},{13,1},{2,14},{6,10},... | collective-permute-start | bytes 98312 | tf_op jit(solution)/shard_map/ppermute | solution.py:461
  49.0 5.2 %collective-permute-start.22 = (bf16[4,4096]{1,0:T(4,128)(2,1)S(1)}, bf16[4,4096]{1,0:T(4,128)(2,1)S(1)}, u32[]{:S(2)}, u32[]{:S(2)}) collective-permute-start(bf16[4,4096]{1,0:T(4,128)(2,1)S(1)} %get-tuple-element.63), channel_id=1, source_target_pairs={{0,7},{1,6},{2,5},{3,4},{4,3},{5,2},{6,1},{7,0},{8,15},{9,14},{10,... | collective-permute-start | bytes 98312 | tf_op jit(solution)/shard_map/ppermute | solution.py:35
  52.2 4.5 %collective-permute-start.21 = (bf16[4,4096]{1,0:T(4,128)(2,1)S(1)}, bf16[4,4096]{1,0:T(4,128)(2,1)S(1)}, u32[]{:S(2)}, u32[]{:S(2)}) collective-permute-start(bf16[4,4096]{1,0:T(4,128)(2,1)S(1)} %get-tuple-element.64), channel_id=1, source_target_pairs={{0,6},{1,7},{2,4},{3,5},{4,2},{5,3},{6,0},{7,1},{8,14},{9,15},{10,... | collective-permute-start | bytes 98312 | tf_op jit(solution)/shard_map/ppermute | solution.py:35
  52.2 4.5 %collective-permute-start.20 = (bf16[4,4096]{1,0:T(4,128)(2,1)S(1)}, bf16[4,4096]{1,0:T(4,128)(2,1)S(1)}, u32[]{:S(2)}, u32[]{:S(2)}) collective-permute-start(bf16[4,4096]{1,0:T(4,128)(2,1)S(1)} %get-tuple-element.62), channel_id=1, source_target_pairs={{0,5},{1,4},{2,7},{3,6},{4,1},{5,0},{6,3},{7,2},{8,13},{9,12},{10,... | collective-permute-start | bytes 98312 | tf_op jit(solution)/shard_map/ppermute | solution.py:35
  (2 other events, 6.6 us)

commit v4 on v3

--- a/solution.py
+++ b/solution.py
@@ -151,12 +151,14 @@
     row_ref[:, 2 * model + width :] = ext_ref[0:1, :].astype(BF16)
 
 
-def fetch(source, to, sems, rows_from=0, pieces=4):
-    rows = to.shape[0]
+def fetch(source, to, sems, column=0, pieces=4):
+    rows, columns = to.shape
     step = rows // pieces
     return [
         pltpu.make_async_copy(
-            source.at[pl.ds(rows_from + i * step, step)], to.at[pl.ds(i * step, step)], sems.at[i]
+            source.at[pl.ds(i * step, step), pl.ds(column, columns)],
+            to.at[pl.ds(i * step, step)],
+            sems.at[i],
         )
         for i in range(pieces)
     ]
@@ -212,22 +214,22 @@
         copy.wait()
 
 
-def fetch_kernel(rows_from, source, to, sems):
-    copies = fetch(source, to, sems, rows_from)
+def fetch_kernel(column, source, to, sems):
+    copies = fetch(source, to, sems, column)
     for copy in copies:
         copy.start()
     for copy in copies:
         copy.wait()
 
 
-def fetched(source, rows, rows_from):
+def fetched(source, column, columns):
     return call(
-        functools.partial(fetch_kernel, rows_from),
-        jax.ShapeDtypeStruct((rows,) + source.shape[1:], source.dtype),
+        functools.partial(fetch_kernel, column),
+        jax.ShapeDtypeStruct((source.shape[0], columns), source.dtype),
         [spec(pltpu.HBM)],
         scratch=[pltpu.SemaphoreType.DMA((4,))],
         limit=1 << 20,
-        moved=source.size // source.shape[0] * rows * 4,
+        moved=source.shape[0] * columns * 4,
     )(in_hbm(source))
 
 
@@ -266,19 +268,28 @@
 
 
 def project_kernel(n_ex, *refs):
-    blocks, w_refs, outs, lhs = refs[:n_ex], refs[n_ex : n_ex + 2], refs[n_ex + 2 : -1], refs[-1]
+    blocks, w_refs, w_hbm = refs[:n_ex], refs[n_ex : n_ex + 2], refs[n_ex + 2]
+    outs, lhs, w_last, sems = refs[n_ex + 3 : -3], *refs[-3:]
     tokens = blocks[0].shape[0]
+    edges = [0, w_refs[0].shape[1], w_refs[0].shape[1] + w_refs[1].shape[1]]
+    last = fetch(w_hbm, w_last, sems, edges[2])
+    for copy in last:
+        copy.start()
     for s in range(n_ex):
         lhs[s * tokens : (s + 1) * tokens, :] = blocks[s][...].astype(F32)
     left = lhs[...].astype(BF16)
-    early, model = w_refs[0].shape
-    chunk = min(1024, model)
-    for at in range(0, model, chunk):
-        out = jnp.dot(
-            left[:, :early], w_refs[0][:, at : at + chunk], preferred_element_type=F32
-        ) + jnp.dot(left[:, early:], w_refs[1][:, at : at + chunk], preferred_element_type=F32)
-        for s in range(n_ex):
-            outs[s][:, at : at + chunk] = out[s * tokens : (s + 1) * tokens, :].astype(outs[s].dtype)
+    for w_ref, edge in zip((*w_refs, w_last), edges):
+        if w_ref is w_last:
+            for copy in last:
+                copy.wait()
+        columns = w_ref.shape[1]
+        chunk = min(1024, columns)
+        for at in range(0, columns, chunk):
+            out = jnp.dot(left, w_ref[:, at : at + chunk], preferred_element_type=F32)
+            for s in range(n_ex):
+                outs[s][:, edge + at : edge + at + chunk] = out[
+                    s * tokens : (s + 1) * tokens, :
+                ].astype(outs[s].dtype)
 
 
 def norm_kernel(n_ex, n_dp, *refs):
@@ -392,13 +403,13 @@
     )(*map(in_hbm, small))
     rows = xor_exchange([row] * n_dp, "dp", n_dp)
 
-    early = part // 2
+    early = model // 4
     att, kv0, out_early, targets = call(
         functools.partial(local_kernel, n_dp, kv_heads),
         [
             shape((n_ex, tokens, part), F32),
             shape(cache.shape[1:], BF16),
-            shape((early, model), BF16),
+            shape((part, early), BF16),
             shape((n_dp * n_ex + 8, LANES), jnp.int32),
         ],
         [spec()] * 3 + [spec(pltpu.HBM)] * 3,
@@ -412,7 +423,7 @@
         ],
         limit=6 << 20,
         flops=4 * tokens * model * context,
-        moved=cache.size * 2 + early * model * 2,
+        moved=cache.size * 2 + part * early * 2,
     )(info, q_in, fresh_in, in_hbm(moves), in_hbm(cache), in_hbm(out_weight))
 
     moved = call(
@@ -432,19 +443,24 @@
     blocks = crossed_exchange(moved[:n_ex], n_dp, n_ex)
     base, ext_all = moved[n_ex:]
 
-    out_late = fetched(out_weight, part - early, early)
+    late = model // 2
+    out_late = fetched(out_weight, early, late)
     partials = call(
         functools.partial(project_kernel, n_ex),
         [shape((tokens, model), F32)] + [shape((tokens, model), BF16)] * (n_ex - 1),
-        [spec()] * (n_ex + 2),
-        scratch=[pltpu.VMEM((n_ex * tokens, part), F32)],
-        limit=4 << 20,
+        [spec()] * (n_ex + 2) + [spec(pltpu.HBM)],
+        scratch=[
+            pltpu.VMEM((n_ex * tokens, part), F32),
+            pltpu.VMEM((part, model - early - late), BF16),
+            pltpu.SemaphoreType.DMA((4,)),
+        ],
+        limit=8 << 20,
         flops=2 * n_ex * tokens * part * model,
         moved=out_weight.size * 2,
-    )(*blocks, out_early, out_late)
+    )(*blocks, out_early, out_late, in_hbm(out_weight))
     partials = crossed_exchange(partials, n_dp, n_ex)
 
-    down = fetched(w_down[0], w_down.shape[1], 0)
+    down = fetched(w_down[0], 0, model)
 
     hidden, payload = call(
         functools.partial(norm_kernel, n_ex, n_dp),

time: 57.5 us -> 59.2 us (1.030)
  waiting for transfers between devices: 16.9 us -> 18.5 us
  Pallas kernels: 11.8 us -> 12.8 us
  starting transfers between devices: 25.6 us -> 24.6 us
    pallas_call x1, Pallas kernels: 1.21 us -> 2.75 us  [per_device(): call(functools.partial(project_kernel, n_ex), [shape((tokens, model), F32...]
    ppermute x8, starting transfers between devices: 5.88 us -> 4.79 us  [over_dp(): return lax.ppermute(array, 'dp', [(j, j ^ turn) for j in range(n_dp)])]
  transfers between devices with their start and end apart: 23 -> 23, of which waited for: 10 -> 11; matrix products, arithmetic and copies ran while one was open for 1% -> 1% of each run, Pallas kernels for 12% -> 11%
where the time goes in v4:
time: 59.2 us; the launch traced here: 59 us
  starting transfers between devices  24.6 us (42%)
  waiting for transfers between devices  18.5 us (31%)
  Pallas kernels  12.8 us (22%)
  local copies, waits for them, and re-layouts  1.81 us (3%)
  other arithmetic  1.08 us (2%)
    ppermute x12, starting transfers between devices, crossed_exchange(): moved[step] = lax.ppermute(blocks[step], ('dp', 'expert'), pairs)  16.6 us
    ppermute x12, waiting for transfers between devices, crossed_exchange(): moved[step] = lax.ppermute(blocks[step], ('dp', 'expert'), pairs)  10.3 us
    ppermute x8, waiting for transfers between devices, over_dp(): return lax.ppermute(array, 'dp', [(j, j ^ turn) for j in range(n_dp)])  7.18 us
    ppermute x8, starting transfers between devices, over_dp(): return lax.ppermute(array, 'dp', [(j, j ^ turn) for j in range(n_dp)])  4.79 us
    pallas_call x2, Pallas kernels, fetched(): call(functools.partial(fetch_kernel, column), jax.ShapeDtypeStruct((sourc...  4.23 us
    ppermute x3, starting transfers between devices, xor_exchange(): lax.ppermute(blocks[step], axis, [(j, j ^ step) for j in range(count)])  3.18 us
    pallas_call x1, Pallas kernels, per_device(): call(functools.partial(project_kernel, n_ex), [shape((tokens, model), F32...  2.75 us
    pallas_call x1, Pallas kernels, per_device(): call(functools.partial(local_kernel, n_dp, kv_heads), [shape((n_ex, token...  2.39 us
  transfers between devices with their start and end apart: 23, of which 11 were waited for; matrix products, arithmetic and copies ran while one was open for 1% of the time, Pallas kernels for 11%

profile of v4, /device:TPU:0, one launch (start us, length us, event | category | flops | bytes accessed | tf_op | source)
XLA Modules:
  0.0 59.0 jit_solution(11515176148288078184)
XLA Ops:
  0.0 0.9 %shard_map.127 = (bf16[1,8832]{1,0:T(2,128)(2,1)S(1)}, bf16[4,4096]{1,0:T(4,128)(2,1)S(1)}, bf16[4,512]{1,0:T(4,128)(2,1)S(1)}, bf16[4,4096]{1,0:T(4,128)(2,1)S(...) custom-call(bf16[4,4096]{1,0:T(4,128)(2,1)} %q_hbm.1, bf16[4,512]{1,0:T(4,128)(2,1)} %fresh_hbm.1, ...), custom_call_target="tpu_custom_call" | custom-call | bytes 65536 | tf_op jit(solution)/shard_map/pallas_call | solution.py:383
  1.5 2.6 %collective-permute-start.1 = (bf16[1,8832]{1,0:T(2,128)(2,1)S(1)}, bf16[1,8832]{1,0:T(2,128)(2,1)S(1)}, u32[]{:S(2)}, u32[]{:S(2)}) collective-permute-start(bf16[1,8832]{1,0:T(2,128)(2,1)S(1)} %get-tuple-element.36.refs_1_), channel_id=1, source_target_pairs={{0,8},{4,12},{8,0},{12,4},{1,9},{5,13},{9,1},{13,5},{2,10},{6,14},... | collective-permute-start | bytes 53000 | tf_op jit(solution)/shard_map/ppermute | solution.py:21
  4.1 2.4 %shard_map.128 = (f32[4,4,1024]{2,1,0:T(4,128)S(1)}, bf16[512,512]{1,0:T(8,128)(2,1)S(1)}, bf16[1024,1024]{1,0:T(8,128)(2,1)S(1)}, s32[24,128]{1,0:T(8,128)S(1)}) custom-call(s32[8,128]{1,0:T(8,128)S(1)} %get-tuple-element.32.info_ref.refs_0_, bf16[4,4096]{1,0:T(4,128)(2,1)S(1)} %get-tuple-element.33.q_ref, bf16[4,512]{1,0:T(4,128)(2,1)S(1)} %get-tuple-element.34.fresh_ref, ...), custom_call_target="tpu_custom_call" | custom-call | flops 33554432 | bytes 4194304 | tf_op jit(solution)/shard_map/pallas_call | solution.py:407
  6.5 1.0 %collective-permute-done.2.refs_4_ = bf16[1,8832]{1,0:T(2,128)(2,1)S(1)} collective-permute-done((bf16[1,8832]{1,0:T(2,128)(2,1)S(1)}, bf16[1,8832]{1,0:T(2,128)(2,1)S(1)}, u32[]{:S(2)}, u32[]{:S(2)}) %collective-permute-start.2) | collective-permute-done | bytes 17696 | tf_op jit(solution)/shard_map/ppermute | solution.py:21
  8.0 1.4 %collective-permute-start.3 = (bf16[4,1024]{1,0:T(4,128)(2,1)S(1)}, bf16[4,1024]{1,0:T(4,128)(2,1)S(1)}, u32[]{:S(2)}, u32[]{:S(2)}) collective-permute-start(bf16[4,1024]{1,0:T(4,128)(2,1)S(1)} %get-tuple-element.42), channel_id=1, source_target_pairs={{0,5},{1,4},{2,7},{3,6},{4,1},{5,0},{6,3},{7,2},{8,13},{9,12},{10,... | collective-permute-start | bytes 24584 | tf_op jit(solution)/shard_map/ppermute | solution.py:35
  9.4 2.6 %collective-permute-start.4 = (bf16[4,1024]{1,0:T(4,128)(2,1)S(1)}, bf16[4,1024]{1,0:T(4,128)(2,1)S(1)}, u32[]{:S(2)}, u32[]{:S(2)}) collective-permute-start(bf16[4,1024]{1,0:T(4,128)(2,1)S(1)} %get-tuple-element.43), channel_id=1, source_target_pairs={{0,6},{1,7},{2,4},{3,5},{4,2},{5,3},{6,0},{7,1},{8,14},{9,15},{10,... | collective-permute-start | bytes 24584 | tf_op jit(solution)/shard_map/ppermute | solution.py:35
  12.0 2.2 %shard_map.130.refs_5_ = bf16[1024,2048]{1,0:T(8,128)(2,1)S(1)} custom-call(bf16[1024,4096]{1,0:T(8,128)(2,1)} %refs_6_.2), custom_call_target="tpu_custom_call" | custom-call | bytes 8388608 | tf_op jit(solution)/shard_map/pallas_call | solution.py:226
  14.2 2.6 %collective-permute-done.5.refs_3_ = bf16[4,1024]{1,0:T(4,128)(2,1)S(1)} collective-permute-done((bf16[4,1024]{1,0:T(4,128)(2,1)S(1)}, bf16[4,1024]{1,0:T(4,128)(2,1)S(1)}, u32[]{:S(2)}, u32[]{:S(2)}) %collective-permute-start.5) | collective-permute-done | bytes 8224 | tf_op jit(solution)/shard_map/ppermute | solution.py:35
  16.8 2.8 %shard_map.131 = (f32[4,4096]{1,0:T(4,128)S(1)}, bf16[4,4096]{1,0:T(4,128)(2,1)S(1)}, bf16[4,4096]{1,0:T(4,128)(2,1)S(1)}, bf16[4,4096]{1,0:T(4,128)(2,1)S(1)}) custom-call(bf16[4,1024]{1,0:T(4,128)(2,1)S(1)} %get-tuple-element.41.refs_0_, bf16[4,1024]{1,0:T(4,128)(2,1)S(1)} %collective-permute-done.3.refs_1_, ...), custom_call_target="tpu_custom_call" | custom-call | flops 134217728 | bytes 8388608 | tf_op jit(solution)/shard_map/pallas_call | solution.py:448
  19.7 1.2 %collective-permute-start.7 = (bf16[4,4096]{1,0:T(4,128)(2,1)S(1)}, bf16[4,4096]{1,0:T(4,128)(2,1)S(1)}, u32[]{:S(2)}, u32[]{:S(2)}) collective-permute-start(bf16[4,4096]{1,0:T(4,128)(2,1)S(1)} %get-tuple-element.48), channel_id=1, source_target_pairs={{0,6},{1,7},{2,4},{3,5},{4,2},{5,3},{6,0},{7,1},{8,14},{9,15},{10,... | collective-permute-start | bytes 98312 | tf_op jit(solution)/shard_map/ppermute | solution.py:35
  20.9 2.6 %collective-permute-start.8 = (bf16[4,4096]{1,0:T(4,128)(2,1)S(1)}, bf16[4,4096]{1,0:T(4,128)(2,1)S(1)}, u32[]{:S(2)}, u32[]{:S(2)}) collective-permute-start(bf16[4,4096]{1,0:T(4,128)(2,1)S(1)} %get-tuple-element.49), channel_id=1, source_target_pairs={{0,7},{1,6},{2,5},{3,4},{4,3},{5,2},{6,1},{7,0},{8,15},{9,14},{10,... | collective-permute-start | bytes 98312 | tf_op jit(solution)/shard_map/ppermute | solution.py:35
  24.0 2.1 %collective-permute-done.8.refs_3_ = bf16[4,4096]{1,0:T(4,128)(2,1)S(1)} collective-permute-done((bf16[4,4096]{1,0:T(4,128)(2,1)S(1)}, bf16[4,4096]{1,0:T(4,128)(2,1)S(1)}, u32[]{:S(2)}, u32[]{:S(2)}) %collective-permute-start.8) | collective-permute-done | bytes 32800 | tf_op jit(solution)/shard_map/ppermute | solution.py:35
  26.2 2.7 %collective-permute-start.11 = (bf16[4,4224]{1,0:T(4,128)(2,1)S(1)}, bf16[4,4224]{1,0:T(4,128)(2,1)S(1)}, u32[]{:S(2)}, u32[]{:S(2)}) collective-permute-start(bf16[4,4224]{1,0:T(4,128)(2,1)S(1)} %get-tuple-element.52), channel_id=1, source_target_pairs={{0,7},{1,6},{2,5},{3,4},{4,3},{5,2},{6,1},{7,0},{8,15},{9,14},{10,... | collective-permute-start | bytes 101384 | tf_op jit(solution)/shard_map/ppermute | solution.py:35
  28.9 1.4 %collective-permute-start.9 = (bf16[4,4224]{1,0:T(4,128)(2,1)S(1)}, bf16[4,4224]{1,0:T(4,128)(2,1)S(1)}, u32[]{:S(2)}, u32[]{:S(2)}) collective-permute-start(bf16[4,4224]{1,0:T(4,128)(2,1)S(1)} %get-tuple-element.52), channel_id=1, source_target_pairs={{0,5},{1,4},{2,7},{3,6},{4,1},{5,0},{6,3},{7,2},{8,13},{9,12},{10,... | collective-permute-start | bytes 101384 | tf_op jit(solution)/shard_map/ppermute | solution.py:35
  31.4 1.8 %collective-permute-done.10 = bf16[4,4224]{1,0:T(4,128)(2,1)S(1)} collective-permute-done((bf16[4,4224]{1,0:T(4,128)(2,1)S(1)}, bf16[4,4224]{1,0:T(4,128)(2,1)S(1)}, u32[]{:S(2)}, u32[]{:S(2)}) %collective-permute-start.10) | collective-permute-done | bytes 33824 | tf_op jit(solution)/shard_map/ppermute | solution.py:35
  34.6 3.4 %collective-permute-done.14 = bf16[3,4,4224]{2,1,0:T(4,128)(2,1)S(1)} collective-permute-done((bf16[3,4,4224]{2,1,0:T(4,128)(2,1)S(1)}, bf16[3,4,4224]{2,1,0:T(4,128)(2,1)S(1)}, u32[]{:S(2)}, u32[]{:S(2)}) %collective-permute-start.14) | collective-permute-done | bytes 101408 | tf_op jit(solution)/shard_map/ppermute | solution.py:477
  38.6 2.0 %shard_map.133.refs_7_ = bf16[384,4096]{1,0:T(8,128)(2,1)S(1)} custom-call(bf16[384,4096]{1,0:T(8,128)(2,1)} %bitcast.35), custom_call_target="tpu_custom_call" | custom-call | bytes 6291456 | tf_op jit(solution)/shard_map/pallas_call | solution.py:226
  41.4 1.0 %copy-done.1 = bf16[1,4096,384]{2,1,0:T(8,128)(2,1)S(1)} copy-done((bf16[1,4096,384]{2,1,0:T(8,128)(2,1)S(1)}, bf16[1,4096,384]{2,1,0:T(8,128)(2,1)}, u32[]{:S(2)}) %copy-start.1) | copy-done | bytes 3145752
  42.4 1.9 %shard_map.134 = (bf16[4,4,4096]{2,1,0:T(4,128)(2,1)S(1)}, bf16[4,4,4096]{2,1,0:T(4,128)(2,1)S(1)}, bf16[4,4,4096]{2,1,0:T(4,128)(2,1)S(1)}, bf16[4,4,4096]{2,1,0:T(4,128)(2,1)S(1)}, f32[4,4096]{1,0:T(4,128)S(1)}) custom-call(s32[24,128]{1,0:T(8,128)S(1)} %get-tuple-element.35.refs_0_, bf16[16,4224]{1,0:T(8,128)(2,1)S(1)} %pad_maximum_fusion.refs_1_, ...), custom_call_target="tpu_custom_call" | custom-call | flops 603979776 | bytes 9437184 | tf_op jit(solution)/shard_map/pallas_call | solution.py:494
  46.6 0.9 %collective-permute-start.18 = (bf16[4,4096]{1,0:T(4,128)(2,1)S(1)}, bf16[4,4096]{1,0:T(4,128)(2,1)S(1)}, u32[]{:S(2)}, u32[]{:S(2)}) collective-permute-start(bf16[4,4096]{1,0:T(4,128)(2,1)S(1)} %fusion.5), channel_id=1, source_target_pairs={{0,12},{4,8},{8,4},{12,0},{1,13},{5,9},{9,5},{13,1},{2,14},{6,10},... | collective-permute-start | bytes 98312 | tf_op jit(solution)/shard_map/ppermute | solution.py:477
  47.6 2.9 %collective-permute-done.19 = bf16[3,4,4096]{2,1,0:T(4,128)(2,1)S(1)} collective-permute-done((bf16[3,4,4096]{2,1,0:T(4,128)(2,1)S(1)}, bf16[3,4,4096]{2,1,0:T(4,128)(2,1)S(1)}, u32[]{:S(2)}, u32[]{:S(2)}) %collective-permute-start.19) | collective-permute-done | bytes 98336 | tf_op jit(solution)/shard_map/ppermute | solution.py:477
  50.6 3.2 %collective-permute-start.22 = (bf16[4,4096]{1,0:T(4,128)(2,1)S(1)}, bf16[4,4096]{1,0:T(4,128)(2,1)S(1)}, u32[]{:S(2)}, u32[]{:S(2)}) collective-permute-start(bf16[4,4096]{1,0:T(4,128)(2,1)S(1)} %get-tuple-element.63), channel_id=1, source_target_pairs={{0,7},{1,6},{2,5},{3,4},{4,3},{5,2},{6,1},{7,0},{8,15},{9,14},{10,... | collective-permute-start | bytes 98312 | tf_op jit(solution)/shard_map/ppermute | solution.py:35
  53.8 1.4 %collective-permute-start.20 = (bf16[4,4096]{1,0:T(4,128)(2,1)S(1)}, bf16[4,4096]{1,0:T(4,128)(2,1)S(1)}, u32[]{:S(2)}, u32[]{:S(2)}) collective-permute-start(bf16[4,4096]{1,0:T(4,128)(2,1)S(1)} %get-tuple-element.62), channel_id=1, source_target_pairs={{0,5},{1,4},{2,7},{3,6},{4,1},{5,0},{6,3},{7,2},{8,13},{9,12},{10,... | collective-permute-start | bytes 98312 | tf_op jit(solution)/shard_map/ppermute | solution.py:35
  55.8 2.5 %collective-permute-done.21 = bf16[4,4096]{1,0:T(4,128)(2,1)S(1)} collective-permute-done((bf16[4,4096]{1,0:T(4,128)(2,1)S(1)}, bf16[4,4096]{1,0:T(4,128)(2,1)S(1)}, u32[]{:S(2)}, u32[]{:S(2)}) %collective-permute-start.21) | collective-permute-done | bytes 32800 | tf_op jit(solution)/shard_map/ppermute | solution.py:35
  (45 shorter events, 9.4 us)
Async XLA Ops:
  0.9 5.6 %collective-permute-start = (bf16[1,8832]{1,0:T(2,128)(2,1)S(1)}, bf16[1,8832]{1,0:T(2,128)(2,1)S(1)}, u32[]{:S(2)}, u32[]{:S(2)}) collective-permute-start(bf16[1,8832]{1,0:T(2,128)(2,1)S(1)} %get-tuple-element.36.refs_1_), channel_id=1, source_target_pairs={{0,4},{4,0},{8,12},{12,8},{1,5},{5,1},{9,13},{13,9},{2,6},{6,2},{1... | collective-permute-start | bytes 53000 | tf_op jit(solution)/shard_map/ppermute | solution.py:21
  1.5 5.0 %collective-permute-start.1 = (bf16[1,8832]{1,0:T(2,128)(2,1)S(1)}, bf16[1,8832]{1,0:T(2,128)(2,1)S(1)}, u32[]{:S(2)}, u32[]{:S(2)}) collective-permute-start(bf16[1,8832]{1,0:T(2,128)(2,1)S(1)} %get-tuple-element.36.refs_1_), channel_id=1, source_target_pairs={{0,8},{4,12},{8,0},{12,4},{1,9},{5,13},{9,1},{13,5},{2,10},{6,14},... | collective-permute-start | bytes 53000 | tf_op jit(solution)/shard_map/ppermute | solution.py:21
  4.1 3.4 %collective-permute-start.2 = (bf16[1,8832]{1,0:T(2,128)(2,1)S(1)}, bf16[1,8832]{1,0:T(2,128)(2,1)S(1)}, u32[]{:S(2)}, u32[]{:S(2)}) collective-permute-start(bf16[1,8832]{1,0:T(2,128)(2,1)S(1)} %get-tuple-element.36.refs_1_), channel_id=1, source_target_pairs={{0,12},{4,8},{8,4},{12,0},{1,13},{5,9},{9,5},{13,1},{2,14},{6,10},... | collective-permute-start | bytes 53000 | tf_op jit(solution)/shard_map/ppermute | solution.py:21
  8.0 6.2 %collective-permute-start.3 = (bf16[4,1024]{1,0:T(4,128)(2,1)S(1)}, bf16[4,1024]{1,0:T(4,128)(2,1)S(1)}, u32[]{:S(2)}, u32[]{:S(2)}) collective-permute-start(bf16[4,1024]{1,0:T(4,128)(2,1)S(1)} %get-tuple-element.42), channel_id=1, source_target_pairs={{0,5},{1,4},{2,7},{3,6},{4,1},{5,0},{6,3},{7,2},{8,13},{9,12},{10,... | collective-permute-start | bytes 24584 | tf_op jit(solution)/shard_map/ppermute | solution.py:35
  9.4 4.8 %collective-permute-start.4 = (bf16[4,1024]{1,0:T(4,128)(2,1)S(1)}, bf16[4,1024]{1,0:T(4,128)(2,1)S(1)}, u32[]{:S(2)}, u32[]{:S(2)}) collective-permute-start(bf16[4,1024]{1,0:T(4,128)(2,1)S(1)} %get-tuple-element.43), channel_id=1, source_target_pairs={{0,6},{1,7},{2,4},{3,5},{4,2},{5,3},{6,0},{7,1},{8,14},{9,15},{10,... | collective-permute-start | bytes 24584 | tf_op jit(solution)/shard_map/ppermute | solution.py:35
  12.0 4.9 %collective-permute-start.5 = (bf16[4,1024]{1,0:T(4,128)(2,1)S(1)}, bf16[4,1024]{1,0:T(4,128)(2,1)S(1)}, u32[]{:S(2)}, u32[]{:S(2)}) collective-permute-start(bf16[4,1024]{1,0:T(4,128)(2,1)S(1)} %get-tuple-element.44), channel_id=1, source_target_pairs={{0,7},{1,6},{2,5},{3,4},{4,3},{5,2},{6,1},{7,0},{8,15},{9,14},{10,... | collective-permute-start | bytes 24584 | tf_op jit(solution)/shard_map/ppermute | solution.py:35
  16.8 9.2 %copy-start.2 = (f32[4096]{0:T(1024)S(1)}, f32[4096]{0:T(1024)}, u32[]{:S(2)}) copy-start(f32[4096]{0:T(1024)} %param.20) | copy-start | bytes 49156
  19.6 3.9 %collective-permute-start.6 = (bf16[4,4096]{1,0:T(4,128)(2,1)S(1)}, bf16[4,4096]{1,0:T(4,128)(2,1)S(1)}, u32[]{:S(2)}, u32[]{:S(2)}) collective-permute-start(bf16[4,4096]{1,0:T(4,128)(2,1)S(1)} %get-tuple-element.47), channel_id=1, source_target_pairs={{0,5},{1,4},{2,7},{3,6},{4,1},{5,0},{6,3},{7,2},{8,13},{9,12},{10,... | collective-permute-start | bytes 98312 | tf_op jit(solution)/shard_map/ppermute | solution.py:35
  19.7 4.3 %collective-permute-start.7 = (bf16[4,4096]{1,0:T(4,128)(2,1)S(1)}, bf16[4,4096]{1,0:T(4,128)(2,1)S(1)}, u32[]{:S(2)}, u32[]{:S(2)}) collective-permute-start(bf16[4,4096]{1,0:T(4,128)(2,1)S(1)} %get-tuple-element.48), channel_id=1, source_target_pairs={{0,6},{1,7},{2,4},{3,5},{4,2},{5,3},{6,0},{7,1},{8,14},{9,15},{10,... | collective-permute-start | bytes 98312 | tf_op jit(solution)/shard_map/ppermute | solution.py:35
  20.9 5.1 %collective-permute-start.8 = (bf16[4,4096]{1,0:T(4,128)(2,1)S(1)}, bf16[4,4096]{1,0:T(4,128)(2,1)S(1)}, u32[]{:S(2)}, u32[]{:S(2)}) collective-permute-start(bf16[4,4096]{1,0:T(4,128)(2,1)S(1)} %get-tuple-element.49), channel_id=1, source_target_pairs={{0,7},{1,6},{2,5},{3,4},{4,3},{5,2},{6,1},{7,0},{8,15},{9,14},{10,... | collective-permute-start | bytes 98312 | tf_op jit(solution)/shard_map/ppermute | solution.py:35
  26.2 5.2 %collective-permute-start.11 = (bf16[4,4224]{1,0:T(4,128)(2,1)S(1)}, bf16[4,4224]{1,0:T(4,128)(2,1)S(1)}, u32[]{:S(2)}, u32[]{:S(2)}) collective-permute-start(bf16[4,4224]{1,0:T(4,128)(2,1)S(1)} %get-tuple-element.52), channel_id=1, source_target_pairs={{0,7},{1,6},{2,5},{3,4},{4,3},{5,2},{6,1},{7,0},{8,15},{9,14},{10,... | collective-permute-start | bytes 101384 | tf_op jit(solution)/shard_map/ppermute | solution.py:35
  28.9 4.3 %collective-permute-start.10 = (bf16[4,4224]{1,0:T(4,128)(2,1)S(1)}, bf16[4,4224]{1,0:T(4,128)(2,1)S(1)}, u32[]{:S(2)}, u32[]{:S(2)}) collective-permute-start(bf16[4,4224]{1,0:T(4,128)(2,1)S(1)} %get-tuple-element.52), channel_id=1, source_target_pairs={{0,6},{1,7},{2,4},{3,5},{4,2},{5,3},{6,0},{7,1},{8,14},{9,15},{10,... | collective-permute-start | bytes 101384 | tf_op jit(solution)/shard_map/ppermute | solution.py:35
  28.9 4.3 %collective-permute-start.9 = (bf16[4,4224]{1,0:T(4,128)(2,1)S(1)}, bf16[4,4224]{1,0:T(4,128)(2,1)S(1)}, u32[]{:S(2)}, u32[]{:S(2)}) collective-permute-start(bf16[4,4224]{1,0:T(4,128)(2,1)S(1)} %get-tuple-element.52), channel_id=1, source_target_pairs={{0,5},{1,4},{2,7},{3,6},{4,1},{5,0},{6,3},{7,2},{8,13},{9,12},{10,... | collective-permute-start | bytes 101384 | tf_op jit(solution)/shard_map/ppermute | solution.py:35
  30.4 7.7 %collective-permute-start.13 = (bf16[4,4224]{1,0:T(4,128)(2,1)S(1)}, bf16[4,4224]{1,0:T(4,128)(2,1)S(1)}, u32[]{:S(2)}, u32[]{:S(2)}) collective-permute-start(bf16[4,4224]{1,0:T(4,128)(2,1)S(1)} %get-tuple-element.52), channel_id=1, source_target_pairs={{0,12},{4,8},{8,4},{12,0},{1,13},{5,9},{9,5},{13,1},{2,14},{6,10},... | collective-permute-start | bytes 101384 | tf_op jit(solution)/shard_map/ppermute | solution.py:477
  33.3 4.7 %collective-permute-start.14 = (bf16[3,4,4224]{2,1,0:T(4,128)(2,1)S(1)}, bf16[3,4,4224]{2,1,0:T(4,128)(2,1)S(1)}, u32[]{:S(2)}, u32[]{:S(2)}) collective-permute-start(bf16[3,4,4224]{2,1,0:T(4,128)(2,1)S(1)} %pad_maximum_fusion.2), channel_id=1, source_target_pairs={{0,12},{4,8},{8,4},{12,0},{1,13},{5,9},{9,5},{13,1},{2,14},{6,10},... | collective-permute-start | bytes 304136 | tf_op jit(solution)/shard_map/ppermute | solution.py:477
  34.2 6.4 %collective-permute-start.12 = (bf16[16,4224]{1,0:T(8,128)(2,1)S(1)}, bf16[16,4224]{1,0:T(8,128)(2,1)S(1)}, u32[]{:S(2)}, u32[]{:S(2)}) collective-permute-start(bf16[16,4224]{1,0:T(8,128)(2,1)S(1)} %pad_maximum_fusion.refs_1_), channel_id=1, source_target_pairs={{0,4},{4,0},{8,12},{12,8},{1,5},{5,1},{9,13},{13,9},{2,6},{6,2},{1... | collective-permute-start | bytes 405512 | tf_op jit(solution)/shard_map/ppermute | solution.py:477
  38.2 2.4 %collective-permute-start.15 = (bf16[16,4224]{1,0:T(8,128)(2,1)S(1)}, bf16[16,4224]{1,0:T(8,128)(2,1)S(1)}, u32[]{:S(2)}, u32[]{:S(2)}) collective-permute-start(bf16[16,4224]{1,0:T(8,128)(2,1)S(1)} %pad_maximum_fusion.1.refs_4_), channel_id=1, source_target_pairs={{0,4},{4,0},{8,12},{12,8},{1,5},{5,1},{9,13},{13,9},{2,6},{6,2},{1... | collective-permute-start | bytes 405512 | tf_op jit(solution)/shard_map/ppermute | solution.py:477
  44.2 1.4 %collective-permute-start.17 = (bf16[4,4,4096]{2,1,0:T(4,128)(2,1)S(1)}, bf16[4,4,4096]{2,1,0:T(4,128)(2,1)S(1)}, u32[]{:S(2)}, u32[]{:S(2)}) collective-permute-start(bf16[4,4,4096]{2,1,0:T(4,128)(2,1)S(1)} %get-tuple-element.58), channel_id=1, source_target_pairs={{0,4},{4,0},{8,12},{12,8},{1,5},{5,1},{9,13},{13,9},{2,6},{6,2},{1... | collective-permute-start | bytes 393224 | tf_op jit(solution)/shard_map/ppermute | solution.py:477
  44.5 3.1 %collective-permute-start.16 = (bf16[4,4,4096]{2,1,0:T(4,128)(2,1)S(1)}, bf16[4,4,4096]{2,1,0:T(4,128)(2,1)S(1)}, u32[]{:S(2)}, u32[]{:S(2)}) collective-permute-start(bf16[4,4,4096]{2,1,0:T(4,128)(2,1)S(1)} %get-tuple-element.56), channel_id=1, source_target_pairs={{0,4},{4,0},{8,12},{12,8},{1,5},{5,1},{9,13},{13,9},{2,6},{6,2},{1... | collective-permute-start | bytes 393224 | tf_op jit(solution)/shard_map/ppermute | solution.py:477
  45.7 4.8 %collective-permute-start.19 = (bf16[3,4,4096]{2,1,0:T(4,128)(2,1)S(1)}, bf16[3,4,4096]{2,1,0:T(4,128)(2,1)S(1)}, u32[]{:S(2)}, u32[]{:S(2)}) collective-permute-start(bf16[3,4,4096]{2,1,0:T(4,128)(2,1)S(1)} %add_convert_fusion.1), channel_id=1, source_target_pairs={{0,12},{4,8},{8,4},{12,0},{1,13},{5,9},{9,5},{13,1},{2,14},{6,10},... | collective-permute-start | bytes 294920 | tf_op jit(solution)/shard_map/ppermute | solution.py:477
  46.6 8.6 %collective-permute-start.18 = (bf16[4,4096]{1,0:T(4,128)(2,1)S(1)}, bf16[4,4096]{1,0:T(4,128)(2,1)S(1)}, u32[]{:S(2)}, u32[]{:S(2)}) collective-permute-start(bf16[4,4096]{1,0:T(4,128)(2,1)S(1)} %fusion.5), channel_id=1, source_target_pairs={{0,12},{4,8},{8,4},{12,0},{1,13},{5,9},{9,5},{13,1},{2,14},{6,10},... | collective-permute-start | bytes 98312 | tf_op jit(solution)/shard_map/ppermute | solution.py:477
  50.6 5.2 %collective-permute-start.22 = (bf16[4,4096]{1,0:T(4,128)(2,1)S(1)}, bf16[4,4096]{1,0:T(4,128)(2,1)S(1)}, u32[]{:S(2)}, u32[]{:S(2)}) collective-permute-start(bf16[4,4096]{1,0:T(4,128)(2,1)S(1)} %get-tuple-element.63), channel_id=1, source_target_pairs={{0,7},{1,6},{2,5},{3,4},{4,3},{5,2},{6,1},{7,0},{8,15},{9,14},{10,... | collective-permute-start | bytes 98312 | tf_op jit(solution)/shard_map/ppermute | solution.py:35
  53.8 4.5 %collective-permute-start.21 = (bf16[4,4096]{1,0:T(4,128)(2,1)S(1)}, bf16[4,4096]{1,0:T(4,128)(2,1)S(1)}, u32[]{:S(2)}, u32[]{:S(2)}) collective-permute-start(bf16[4,4096]{1,0:T(4,128)(2,1)S(1)} %get-tuple-element.64), channel_id=1, source_target_pairs={{0,6},{1,7},{2,4},{3,5},{4,2},{5,3},{6,0},{7,1},{8,14},{9,15},{10,... | collective-permute-start | bytes 98312 | tf_op jit(solution)/shard_map/ppermute | solution.py:35
  53.8 4.5 %collective-permute-start.20 = (bf16[4,4096]{1,0:T(4,128)(2,1)S(1)}, bf16[4,4096]{1,0:T(4,128)(2,1)S(1)}, u32[]{:S(2)}, u32[]{:S(2)}) collective-permute-start(bf16[4,4096]{1,0:T(4,128)(2,1)S(1)} %get-tuple-element.62), channel_id=1, source_target_pairs={{0,5},{1,4},{2,7},{3,6},{4,1},{5,0},{6,3},{7,2},{8,13},{9,12},{10,... | collective-permute-start | bytes 98312 | tf_op jit(solution)/shard_map/ppermute | solution.py:35
  (2 other events, 6.6 us)

commit v5 on v3

--- a/solution.py
+++ b/solution.py
@@ -13,6 +13,7 @@
 NORM_EPS = 1e-06
 F32 = jnp.float32
 BF16 = jnp.bfloat16
+COVER = 10**10
 
 
 def xor_exchange(blocks, axis, count):
@@ -151,32 +152,14 @@
     row_ref[:, 2 * model + width :] = ext_ref[0:1, :].astype(BF16)
 
 
-def fetch(source, to, sems, rows_from=0, pieces=4):
-    rows = to.shape[0]
-    step = rows // pieces
-    return [
-        pltpu.make_async_copy(
-            source.at[pl.ds(rows_from + i * step, step)], to.at[pl.ds(i * step, step)], sems.at[i]
-        )
-        for i in range(pieces)
-    ]
-
-
 def local_kernel(
-    n_dp, kv_heads, info_ref, q_ref, fresh_ref, moves_hbm, cache_hbm, w_hbm,
-    att_ref, kv0_ref, w_ref, to_ref, kv, q_scr, moves, moves_sem, sems, w_sems,
+    n_dp, kv_heads, info_ref, q_ref, fresh_ref, moves_hbm, cache_ref,
+    att_ref, to_ref, q_scr, moves, moves_sem,
 ):
     parts, tokens, part = att_ref.shape
     goals = pltpu.make_async_copy(moves_hbm, moves, moves_sem)
     goals.start()
     per = part // HD
-    copies = [
-        pltpu.make_async_copy(cache_hbm.at[t], kv.at[t - 1] if t else kv0_ref, sems.at[t])
-        for t in range(tokens)
-    ]
-    weight = fetch(w_hbm, w_ref, w_sems)
-    for copy in copies[1:] + copies[:1] + weight:
-        copy.start()
     jobs = []
     for t in range(1, tokens):
 
@@ -185,14 +168,11 @@
 
         jobs.append(
             (
-                q_ref[t : t + 1, :], fresh_ref[t : t + 1, :], q_scr.at[t], kv.at[t - 1],
+                q_ref[t : t + 1, :], fresh_ref[t : t + 1, :], q_scr.at[t], cache_ref.at[t],
                 info_ref[t : t + 1, 0:1], put,
             )
         )
-    chains = attend(jobs, kv_heads)
-    for copy in copies[1:]:
-        copy.wait()
-    attend_cache(chains, kv_heads)
+    attend_cache(attend(jobs, kv_heads), kv_heads)
     for s in range(parts):
         att_ref[s, 0:1, :] = jnp.zeros((1, part), F32)
     goals.wait()
@@ -208,27 +188,6 @@
     for d in range(n_dp):
         source = jnp.where(moves[ex, d] == dp, d, source)
     to_ref[n_dp * parts : n_dp * parts + 1, :] = jnp.full((1, LANES), source ^ dp, jnp.int32)
-    for copy in copies[:1] + weight:
-        copy.wait()
-
-
-def fetch_kernel(rows_from, source, to, sems):
-    copies = fetch(source, to, sems, rows_from)
-    for copy in copies:
-        copy.start()
-    for copy in copies:
-        copy.wait()
-
-
-def fetched(source, rows, rows_from):
-    return call(
-        functools.partial(fetch_kernel, rows_from),
-        jax.ShapeDtypeStruct((rows,) + source.shape[1:], source.dtype),
-        [spec(pltpu.HBM)],
-        scratch=[pltpu.SemaphoreType.DMA((4,))],
-        limit=1 << 20,
-        moved=source.size // source.shape[0] * rows * 4,
-    )(in_hbm(source))
 
 
 def in_hbm(array):
@@ -238,7 +197,7 @@
 def moved_kernel(n_dp, n_ex, kv_heads, width, *refs):
     info_ref = refs[0]
     rows = refs[1 : 1 + n_dp]
-    att_ref, kv0_ref, res_ref, ext_ref = refs[1 + n_dp : 5 + n_dp]
+    att_ref, cache_ref, res_ref, ext_ref = refs[1 + n_dp : 5 + n_dp]
     outs = refs[5 + n_dp : 5 + n_dp + n_ex]
     base_ref, ext_out, row_scr, q_scr, full = refs[5 + n_dp + n_ex :]
     ex = lax.axis_index("expert")
@@ -256,7 +215,7 @@
     def put(head, value):
         full[head // per, 0:1, (head % per) * HD : (head % per + 1) * HD] = value
 
-    job = (row_scr[:, :model], row_scr[:, model : model + width], q_scr, kv0_ref, None, put)
+    job = (row_scr[:, :model], row_scr[:, model : model + width], q_scr, cache_ref.at[0], None, put)
     attend_cache(attend([job], kv_heads), kv_heads)
     for s in range(n_ex):
         outs[s][...] = full[s ^ ex].astype(BF16)
@@ -266,17 +225,15 @@
 
 
 def project_kernel(n_ex, *refs):
-    blocks, w_refs, outs, lhs = refs[:n_ex], refs[n_ex : n_ex + 2], refs[n_ex + 2 : -1], refs[-1]
+    blocks, w_ref, outs, lhs = refs[:n_ex], refs[n_ex], refs[n_ex + 1 : -1], refs[-1]
     tokens = blocks[0].shape[0]
     for s in range(n_ex):
         lhs[s * tokens : (s + 1) * tokens, :] = blocks[s][...].astype(F32)
     left = lhs[...].astype(BF16)
-    early, model = w_refs[0].shape
+    model = w_ref.shape[1]
     chunk = min(1024, model)
     for at in range(0, model, chunk):
-        out = jnp.dot(
-            left[:, :early], w_refs[0][:, at : at + chunk], preferred_element_type=F32
-        ) + jnp.dot(left[:, early:], w_refs[1][:, at : at + chunk], preferred_element_type=F32)
+        out = jnp.dot(left, w_ref[:, at : at + chunk], preferred_element_type=F32)
         for s in range(n_ex):
             outs[s][:, at : at + chunk] = out[s * tokens : (s + 1) * tokens, :].astype(outs[s].dtype)
 
@@ -346,7 +303,7 @@
     left = new_scr[...].astype(BF16)
     chunk = min(1024, model)
     for at in range(0, model, chunk):
-        out = jnp.dot(left, down_ref[:, at : at + chunk], preferred_element_type=F32)
+        out = jnp.dot(left, down_ref[0, :, at : at + chunk], preferred_element_type=F32)
         for r in range(n_dp):
             for s in range(n_ex):
                 first_row = (r * n_ex + s) * tokens
@@ -388,32 +345,27 @@
             pltpu.SemaphoreType.DMA((len(small),)),
         ],
         limit=4 << 20,
+        flops=COVER,
         moved=tokens * model * 4,
     )(*map(in_hbm, small))
     rows = xor_exchange([row] * n_dp, "dp", n_dp)
 
-    early = part // 2
-    att, kv0, out_early, targets = call(
+    att, targets = call(
         functools.partial(local_kernel, n_dp, kv_heads),
         [
             shape((n_ex, tokens, part), F32),
-            shape(cache.shape[1:], BF16),
-            shape((early, model), BF16),
             shape((n_dp * n_ex + 8, LANES), jnp.int32),
         ],
-        [spec()] * 3 + [spec(pltpu.HBM)] * 3,
+        [spec()] * 3 + [spec(pltpu.HBM), spec()],
         scratch=[
-            pltpu.VMEM((tokens - 1,) + cache.shape[1:], BF16),
             pltpu.VMEM((tokens, model // HD, HD), F32),
             pltpu.SMEM(moves.shape, jnp.int32),
             pltpu.SemaphoreType.DMA(()),
-            pltpu.SemaphoreType.DMA((tokens,)),
-            pltpu.SemaphoreType.DMA((4,)),
-        ],
-        limit=6 << 20,
+        ],
+        limit=4 << 20,
         flops=4 * tokens * model * context,
-        moved=cache.size * 2 + early * model * 2,
-    )(info, q_in, fresh_in, in_hbm(moves), in_hbm(cache), in_hbm(out_weight))
+        moved=cache.size * 2,
+    )(info, q_in, fresh_in, in_hbm(moves), cache)
 
     moved = call(
         functools.partial(moved_kernel, n_dp, n_ex, kv_heads, 2 * width),
@@ -426,32 +378,29 @@
             pltpu.VMEM((n_ex, tokens, part), F32),
         ],
         limit=6 << 20,
-        flops=4 * model * context,
+        flops=COVER,
         moved=cache.size // tokens * 2,
-    )(info, *rows, att, kv0, res_in, ext)
+    )(info, *rows, att, cache, res_in, ext)
     blocks = crossed_exchange(moved[:n_ex], n_dp, n_ex)
     base, ext_all = moved[n_ex:]
 
-    out_late = fetched(out_weight, part - early, early)
     partials = call(
         functools.partial(project_kernel, n_ex),
         [shape((tokens, model), F32)] + [shape((tokens, model), BF16)] * (n_ex - 1),
-        [spec()] * (n_ex + 2),
+        [spec()] * (n_ex + 1),
         scratch=[pltpu.VMEM((n_ex * tokens, part), F32)],
         limit=4 << 20,
         flops=2 * n_ex * tokens * part * model,
         moved=out_weight.size * 2,
-    )(*blocks, out_early, out_late)
+    )(*blocks, out_weight)
     partials = crossed_exchange(partials, n_dp, n_ex)
-
-    down = fetched(w_down[0], w_down.shape[1], 0)
 
     hidden, payload = call(
         functools.partial(norm_kernel, n_ex, n_dp),
         [shape((tokens, model), F32), shape((tokens, model + ext_width), BF16)],
         [spec()] * (n_ex + 3),
         limit=4 << 20,
-        flops=10 * tokens * model,
+        flops=COVER,
         moved=tokens * model * 16,
     )(*partials, base, ext_all, norm_gain[None])
     gathered = crossed_exchange([payload] * n_ex, n_dp, n_ex)
@@ -487,7 +436,7 @@
         limit=(8 << 20) + all_rows * model * 8,
         flops=6 * all_rows * model * hidden_units,
         moved=weights_bytes,
-    )(targets, *[pieces[r] for r in range(n_dp)], w_gate, w_up, down, norm_gain[None], hidden)
+    )(targets, *[pieces[r] for r in range(n_dp)], w_gate, w_up, w_down, norm_gain[None], hidden)
     terms = {r: [done[r]] for r in range(n_dp)}
     reach = {0: 0}
     for i, turn in enumerate(turns):

time: 57.5 us -> 55.4 us (0.963)
  waiting for transfers between devices: 16.9 us -> 24.8 us
  Pallas kernels: 11.8 us -> 5.53 us
  starting transfers between devices: 25.6 us -> 23.6 us
  local copies, waits for them, and re-layouts: 1.81 us -> 0.1 us
    ppermute x12, waiting for transfers between devices: 9.8 us -> 14.2 us  [crossed_exchange(): moved[step] = lax.ppermute(blocks[step], ('dp', 'expert'), pairs)]
    pallas_call x2 -> x0, Pallas kernels: 4.23 us -> none  [fetched(): call(functools.partial(fetch_kernel, rows_from), jax.ShapeDtypeStruct((ro...]
    pallas_call x1, Pallas kernels: 2.92 us -> 0.75 us  [per_device(): call(functools.partial(local_kernel, n_dp, kv_heads), [shape((n_ex, token...]
    ppermute x3, waiting for transfers between devices: 0.43 us -> 2.59 us  [xor_exchange(): lax.ppermute(blocks[step], axis, [(j, j ^ step) for j in range(count)])]
    unnamed x6 -> x14, local copies, waits for them, and re-layouts: 1.74 us -> 0.03 us
    ppermute x8, waiting for transfers between devices: 6.62 us -> 7.98 us  [over_dp(): return lax.ppermute(array, 'dp', [(j, j ^ turn) for j in range(n_dp)])]
    ppermute x8, starting transfers between devices: 5.88 us -> 4.74 us  [over_dp(): return lax.ppermute(array, 'dp', [(j, j ^ turn) for j in range(n_dp)])]
    ppermute x12, starting transfers between devices: 16.6 us -> 15.7 us  [crossed_exchange(): moved[step] = lax.ppermute(blocks[step], ('dp', 'expert'), pairs)]
  transfers between devices with their start and end apart: 23 -> 23, of which waited for: 10 -> 14; matrix products, arithmetic and copies ran while one was open for 1% -> 1% of each run, Pallas kernels for 12% -> 1%
where the time goes in v5:
time: 55.4 us; the launch traced here: 55.3 us
  waiting for transfers between devices  24.8 us (45%)
  starting transfers between devices  23.6 us (43%)
  Pallas kernels  5.53 us (10%)
  other arithmetic  1.08 us (2%)
    ppermute x12, starting transfers between devices, crossed_exchange(): moved[step] = lax.ppermute(blocks[step], ('dp', 'expert'), pairs)  15.7 us
    ppermute x12, waiting for transfers between devices, crossed_exchange(): moved[step] = lax.ppermute(blocks[step], ('dp', 'expert'), pairs)  14.2 us
    ppermute x8, waiting for transfers between devices, over_dp(): return lax.ppermute(array, 'dp', [(j, j ^ turn) for j in range(n_dp)])  7.98 us
    ppermute x8, starting transfers between devices, over_dp(): return lax.ppermute(array, 'dp', [(j, j ^ turn) for j in range(n_dp)])  4.74 us
    ppermute x3, starting transfers between devices, xor_exchange(): lax.ppermute(blocks[step], axis, [(j, j ^ step) for j in range(count)])  3.18 us
    ppermute x3, waiting for transfers between devices, xor_exchange(): lax.ppermute(blocks[step], axis, [(j, j ^ step) for j in range(count)])  2.59 us
    pallas_call x1, Pallas kernels, per_device(): call(functools.partial(expert_kernel, n_dp, n_ex, tokens), [shape((n_ex,...  1.87 us
    pallas_call x1, Pallas kernels, per_device(): call(functools.partial(project_kernel, n_ex), [shape((tokens, model), F32...  1.21 us
  transfers between devices with their start and end apart: 23, of which 14 were waited for; matrix products, arithmetic and copies ran while one was open for 1% of the time, Pallas kernels for 1%

profile of v5, /device:TPU:0, one launch (start us, length us, event | category | flops | bytes accessed | tf_op | source)
XLA Modules:
  0.0 55.3 jit_solution(7785855994715971165)
XLA Ops:
  0.0 1.0 %shard_map.127 = (bf16[1,8832]{1,0:T(2,128)(2,1)S(1)}, bf16[4,4096]{1,0:T(4,128)(2,1)S(1)}, bf16[4,512]{1,0:T(4,128)(2,1)S(1)}, bf16[4,4096]{1,0:T(4,128)(2,1)S(...) custom-call(bf16[4,4096]{1,0:T(4,128)(2,1)} %q_hbm.1, bf16[4,512]{1,0:T(4,128)(2,1)} %fresh_hbm.1, ...), custom_call_target="tpu_custom_call" | custom-call | flops 10000000000 | bytes 65536 | tf_op jit(solution)/shard_map/pallas_call | solution.py:329
  1.0 2.5 %collective-permute-start.2 = (bf16[1,8832]{1,0:T(2,128)(2,1)S(1)}, bf16[1,8832]{1,0:T(2,128)(2,1)S(1)}, u32[]{:S(2)}, u32[]{:S(2)}) collective-permute-start(bf16[1,8832]{1,0:T(2,128)(2,1)S(1)} %get-tuple-element.34.refs_1_), channel_id=1, source_target_pairs={{0,12},{4,8},{8,4},{12,0},{1,13},{5,9},{9,5},{13,1},{2,14},{6,10},... | collective-permute-start | bytes 53000 | tf_op jit(solution)/shard_map/ppermute | solution.py:22
  5.4 2.2 %collective-permute-done.1.refs_3_ = bf16[1,8832]{1,0:T(2,128)(2,1)S(1)} collective-permute-done((bf16[1,8832]{1,0:T(2,128)(2,1)S(1)}, bf16[1,8832]{1,0:T(2,128)(2,1)S(1)}, u32[]{:S(2)}, u32[]{:S(2)}) %collective-permute-start.1) | collective-permute-done | bytes 17696 | tf_op jit(solution)/shard_map/ppermute | solution.py:22
  8.1 1.1 %collective-permute-start.3 = (bf16[4,1024]{1,0:T(4,128)(2,1)S(1)}, bf16[4,1024]{1,0:T(4,128)(2,1)S(1)}, u32[]{:S(2)}, u32[]{:S(2)}) collective-permute-start(bf16[4,1024]{1,0:T(4,128)(2,1)S(1)} %get-tuple-element.39), channel_id=1, source_target_pairs={{0,5},{1,4},{2,7},{3,6},{4,1},{5,0},{6,3},{7,2},{8,13},{9,12},{10,... | collective-permute-start | bytes 24584 | tf_op jit(solution)/shard_map/ppermute | solution.py:36
  9.2 2.9 %collective-permute-start.4 = (bf16[4,1024]{1,0:T(4,128)(2,1)S(1)}, bf16[4,1024]{1,0:T(4,128)(2,1)S(1)}, u32[]{:S(2)}, u32[]{:S(2)}) collective-permute-start(bf16[4,1024]{1,0:T(4,128)(2,1)S(1)} %get-tuple-element.40), channel_id=1, source_target_pairs={{0,6},{1,7},{2,4},{3,5},{4,2},{5,3},{6,0},{7,1},{8,14},{9,15},{10,... | collective-permute-start | bytes 24584 | tf_op jit(solution)/shard_map/ppermute | solution.py:36
  12.1 1.4 %collective-permute-done.4.refs_2_ = bf16[4,1024]{1,0:T(4,128)(2,1)S(1)} collective-permute-done((bf16[4,1024]{1,0:T(4,128)(2,1)S(1)}, bf16[4,1024]{1,0:T(4,128)(2,1)S(1)}, u32[]{:S(2)}, u32[]{:S(2)}) %collective-permute-start.4) | collective-permute-done | bytes 8224 | tf_op jit(solution)/shard_map/ppermute | solution.py:36
  13.4 3.6 %collective-permute-done.5.refs_3_ = bf16[4,1024]{1,0:T(4,128)(2,1)S(1)} collective-permute-done((bf16[4,1024]{1,0:T(4,128)(2,1)S(1)}, bf16[4,1024]{1,0:T(4,128)(2,1)S(1)}, u32[]{:S(2)}, u32[]{:S(2)}) %collective-permute-start.5) | collective-permute-done | bytes 8224 | tf_op jit(solution)/shard_map/ppermute | solution.py:36
  17.0 1.2 %shard_map.130 = (f32[4,4096]{1,0:T(4,128)S(1)}, bf16[4,4096]{1,0:T(4,128)(2,1)S(1)}, bf16[4,4096]{1,0:T(4,128)(2,1)S(1)}, bf16[4,4096]{1,0:T(4,128)(2,1)S(1)}) custom-call(bf16[4,1024]{1,0:T(4,128)(2,1)S(1)} %get-tuple-element.38.refs_0_, bf16[4,1024]{1,0:T(4,128)(2,1)S(1)} %collective-permute-done.3.refs_1_, ...), custom_call_target="tpu_custom_call" | custom-call | flops 134217728 | bytes 8388608 | tf_op jit(solution)/shard_map/pallas_call | solution.py:387
  18.7 3.4 %collective-permute-start.8 = (bf16[4,4096]{1,0:T(4,128)(2,1)S(1)}, bf16[4,4096]{1,0:T(4,128)(2,1)S(1)}, u32[]{:S(2)}, u32[]{:S(2)}) collective-permute-start(bf16[4,4096]{1,0:T(4,128)(2,1)S(1)} %get-tuple-element.45), channel_id=1, source_target_pairs={{0,7},{1,6},{2,5},{3,4},{4,3},{5,2},{6,1},{7,0},{8,15},{9,14},{10,... | collective-permute-start | bytes 98312 | tf_op jit(solution)/shard_map/ppermute | solution.py:36
  22.6 1.6 %collective-permute-done.8.refs_3_ = bf16[4,4096]{1,0:T(4,128)(2,1)S(1)} collective-permute-done((bf16[4,4096]{1,0:T(4,128)(2,1)S(1)}, bf16[4,4096]{1,0:T(4,128)(2,1)S(1)}, u32[]{:S(2)}, u32[]{:S(2)}) %collective-permute-start.8) | collective-permute-done | bytes 32800 | tf_op jit(solution)/shard_map/ppermute | solution.py:36
  24.4 3.1 %collective-permute-start.11 = (bf16[4,4224]{1,0:T(4,128)(2,1)S(1)}, bf16[4,4224]{1,0:T(4,128)(2,1)S(1)}, u32[]{:S(2)}, u32[]{:S(2)}) collective-permute-start(bf16[4,4224]{1,0:T(4,128)(2,1)S(1)} %get-tuple-element.48), channel_id=1, source_target_pairs={{0,7},{1,6},{2,5},{3,4},{4,3},{5,2},{6,1},{7,0},{8,15},{9,14},{10,... | collective-permute-start | bytes 101384 | tf_op jit(solution)/shard_map/ppermute | solution.py:36
  27.5 1.1 %collective-permute-start.9 = (bf16[4,4224]{1,0:T(4,128)(2,1)S(1)}, bf16[4,4224]{1,0:T(4,128)(2,1)S(1)}, u32[]{:S(2)}, u32[]{:S(2)}) collective-permute-start(bf16[4,4224]{1,0:T(4,128)(2,1)S(1)} %get-tuple-element.48), channel_id=1, source_target_pairs={{0,5},{1,4},{2,7},{3,6},{4,1},{5,0},{6,3},{7,2},{8,13},{9,12},{10,... | collective-permute-start | bytes 101384 | tf_op jit(solution)/shard_map/ppermute | solution.py:36
  29.6 2.2 %collective-permute-done.10 = bf16[4,4224]{1,0:T(4,128)(2,1)S(1)} collective-permute-done((bf16[4,4224]{1,0:T(4,128)(2,1)S(1)}, bf16[4,4224]{1,0:T(4,128)(2,1)S(1)}, u32[]{:S(2)}, u32[]{:S(2)}) %collective-permute-start.10) | collective-permute-done | bytes 33824 | tf_op jit(solution)/shard_map/ppermute | solution.py:36
  31.9 1.0 %collective-permute-start.14 = (bf16[3,4,4224]{2,1,0:T(4,128)(2,1)S(1)}, bf16[3,4,4224]{2,1,0:T(4,128)(2,1)S(1)}, u32[]{:S(2)}, u32[]{:S(2)}) collective-permute-start(bf16[3,4,4224]{2,1,0:T(4,128)(2,1)S(1)} %pad_maximum_fusion.2), channel_id=1, source_target_pairs={{0,12},{4,8},{8,4},{12,0},{1,13},{5,9},{9,5},{13,1},{2,14},{6,10},... | collective-permute-start | bytes 304136 | tf_op jit(solution)/shard_map/ppermute | solution.py:410
  33.2 3.4 %collective-permute-done.14 = bf16[3,4,4224]{2,1,0:T(4,128)(2,1)S(1)} collective-permute-done((bf16[3,4,4224]{2,1,0:T(4,128)(2,1)S(1)}, bf16[3,4,4224]{2,1,0:T(4,128)(2,1)S(1)}, u32[]{:S(2)}, u32[]{:S(2)}) %collective-permute-start.14) | collective-permute-done | bytes 101408 | tf_op jit(solution)/shard_map/ppermute | solution.py:410
  37.1 1.0 %collective-permute-done.15.refs_3_ = bf16[16,4224]{1,0:T(8,128)(2,1)S(1)} collective-permute-done((bf16[16,4224]{1,0:T(8,128)(2,1)S(1)}, bf16[16,4224]{1,0:T(8,128)(2,1)S(1)}, u32[]{:S(2)}, u32[]{:S(2)}) %collective-permute-start.15) | collective-permute-done | bytes 135200 | tf_op jit(solution)/shard_map/ppermute | solution.py:410
  38.2 1.9 %shard_map.132 = (bf16[4,4,4096]{2,1,0:T(4,128)(2,1)S(1)}, bf16[4,4,4096]{2,1,0:T(4,128)(2,1)S(1)}, bf16[4,4,4096]{2,1,0:T(4,128)(2,1)S(1)}, bf16[4,4,4096]{2,1,0:T(4,128)(2,1)S(1)}, f32[4,4096]{1,0:T(4,128)S(1)}) custom-call(s32[24,128]{1,0:T(8,128)S(1)} %get-tuple-element.33.refs_0_, bf16[16,4224]{1,0:T(8,128)(2,1)S(1)} %pad_maximum_fusion.refs_1_, ...), custom_call_target="tpu_custom_call" | custom-call | flops 603979776 | bytes 9437184 | tf_op jit(solution)/shard_map/pallas_call | solution.py:427
  41.5 1.0 %collective-permute-start.19 = (bf16[3,4,4096]{2,1,0:T(4,128)(2,1)S(1)}, bf16[3,4,4096]{2,1,0:T(4,128)(2,1)S(1)}, u32[]{:S(2)}, u32[]{:S(2)}) collective-permute-start(bf16[3,4,4096]{2,1,0:T(4,128)(2,1)S(1)} %add_convert_fusion.1), channel_id=1, source_target_pairs={{0,12},{4,8},{8,4},{12,0},{1,13},{5,9},{9,5},{13,1},{2,14},{6,10},... | collective-permute-start | bytes 294920 | tf_op jit(solution)/shard_map/ppermute | solution.py:410
  42.5 0.9 %collective-permute-start.18 = (bf16[4,4096]{1,0:T(4,128)(2,1)S(1)}, bf16[4,4096]{1,0:T(4,128)(2,1)S(1)}, u32[]{:S(2)}, u32[]{:S(2)}) collective-permute-start(bf16[4,4096]{1,0:T(4,128)(2,1)S(1)} %fusion.5), channel_id=1, source_target_pairs={{0,12},{4,8},{8,4},{12,0},{1,13},{5,9},{9,5},{13,1},{2,14},{6,10},... | collective-permute-start | bytes 98312 | tf_op jit(solution)/shard_map/ppermute | solution.py:410
  43.4 2.7 %collective-permute-done.19 = bf16[3,4,4096]{2,1,0:T(4,128)(2,1)S(1)} collective-permute-done((bf16[3,4,4096]{2,1,0:T(4,128)(2,1)S(1)}, bf16[3,4,4096]{2,1,0:T(4,128)(2,1)S(1)}, u32[]{:S(2)}, u32[]{:S(2)}) %collective-permute-start.19) | collective-permute-done | bytes 98336 | tf_op jit(solution)/shard_map/ppermute | solution.py:410
  46.3 1.4 %collective-permute-start.20 = (bf16[4,4096]{1,0:T(4,128)(2,1)S(1)}, bf16[4,4096]{1,0:T(4,128)(2,1)S(1)}, u32[]{:S(2)}, u32[]{:S(2)}) collective-permute-start(bf16[4,4096]{1,0:T(4,128)(2,1)S(1)} %get-tuple-element.58), channel_id=1, source_target_pairs={{0,5},{1,4},{2,7},{3,6},{4,1},{5,0},{6,3},{7,2},{8,13},{9,12},{10,... | collective-permute-start | bytes 98312 | tf_op jit(solution)/shard_map/ppermute | solution.py:36
  47.6 2.4 %collective-permute-start.22 = (bf16[4,4096]{1,0:T(4,128)(2,1)S(1)}, bf16[4,4096]{1,0:T(4,128)(2,1)S(1)}, u32[]{:S(2)}, u32[]{:S(2)}) collective-permute-start(bf16[4,4096]{1,0:T(4,128)(2,1)S(1)} %get-tuple-element.59), channel_id=1, source_target_pairs={{0,7},{1,6},{2,5},{3,4},{4,3},{5,2},{6,1},{7,0},{8,15},{9,14},{10,... | collective-permute-start | bytes 98312 | tf_op jit(solution)/shard_map/ppermute | solution.py:36
  50.0 3.1 %collective-permute-done.22 = bf16[4,4096]{1,0:T(4,128)(2,1)S(1)} collective-permute-done((bf16[4,4096]{1,0:T(4,128)(2,1)S(1)}, bf16[4,4096]{1,0:T(4,128)(2,1)S(1)}, u32[]{:S(2)}, u32[]{:S(2)}) %collective-permute-start.22) | collective-permute-done | bytes 32800 | tf_op jit(solution)/shard_map/ppermute | solution.py:36
  53.1 1.5 %collective-permute-done.21 = bf16[4,4096]{1,0:T(4,128)(2,1)S(1)} collective-permute-done((bf16[4,4096]{1,0:T(4,128)(2,1)S(1)}, bf16[4,4096]{1,0:T(4,128)(2,1)S(1)}, u32[]{:S(2)}, u32[]{:S(2)}) %collective-permute-start.21) | collective-permute-done | bytes 32800 | tf_op jit(solution)/shard_map/ppermute | solution.py:36
  (52 shorter events, 7.7 us)
Async XLA Ops:
  1.0 4.3 %collective-permute-start.2 = (bf16[1,8832]{1,0:T(2,128)(2,1)S(1)}, bf16[1,8832]{1,0:T(2,128)(2,1)S(1)}, u32[]{:S(2)}, u32[]{:S(2)}) collective-permute-start(bf16[1,8832]{1,0:T(2,128)(2,1)S(1)} %get-tuple-element.34.refs_1_), channel_id=1, source_target_pairs={{0,12},{4,8},{8,4},{12,0},{1,13},{5,9},{9,5},{13,1},{2,14},{6,10},... | collective-permute-start | bytes 53000 | tf_op jit(solution)/shard_map/ppermute | solution.py:22
  3.5 4.0 %collective-permute-start.1 = (bf16[1,8832]{1,0:T(2,128)(2,1)S(1)}, bf16[1,8832]{1,0:T(2,128)(2,1)S(1)}, u32[]{:S(2)}, u32[]{:S(2)}) collective-permute-start(bf16[1,8832]{1,0:T(2,128)(2,1)S(1)} %get-tuple-element.34.refs_1_), channel_id=1, source_target_pairs={{0,8},{4,12},{8,0},{12,4},{1,9},{5,13},{9,1},{13,5},{2,10},{6,14},... | collective-permute-start | bytes 53000 | tf_op jit(solution)/shard_map/ppermute | solution.py:22
  4.2 3.4 %collective-permute-start = (bf16[1,8832]{1,0:T(2,128)(2,1)S(1)}, bf16[1,8832]{1,0:T(2,128)(2,1)S(1)}, u32[]{:S(2)}, u32[]{:S(2)}) collective-permute-start(bf16[1,8832]{1,0:T(2,128)(2,1)S(1)} %get-tuple-element.34.refs_1_), channel_id=1, source_target_pairs={{0,4},{4,0},{8,12},{12,8},{1,5},{5,1},{9,13},{13,9},{2,6},{6,2},{1... | collective-permute-start | bytes 53000 | tf_op jit(solution)/shard_map/ppermute | solution.py:22
  8.1 4.0 %collective-permute-start.3 = (bf16[4,1024]{1,0:T(4,128)(2,1)S(1)}, bf16[4,1024]{1,0:T(4,128)(2,1)S(1)}, u32[]{:S(2)}, u32[]{:S(2)}) collective-permute-start(bf16[4,1024]{1,0:T(4,128)(2,1)S(1)} %get-tuple-element.39), channel_id=1, source_target_pairs={{0,5},{1,4},{2,7},{3,6},{4,1},{5,0},{6,3},{7,2},{8,13},{9,12},{10,... | collective-permute-start | bytes 24584 | tf_op jit(solution)/shard_map/ppermute | solution.py:36
  9.2 4.3 %collective-permute-start.4 = (bf16[4,1024]{1,0:T(4,128)(2,1)S(1)}, bf16[4,1024]{1,0:T(4,128)(2,1)S(1)}, u32[]{:S(2)}, u32[]{:S(2)}) collective-permute-start(bf16[4,1024]{1,0:T(4,128)(2,1)S(1)} %get-tuple-element.40), channel_id=1, source_target_pairs={{0,6},{1,7},{2,4},{3,5},{4,2},{5,3},{6,0},{7,1},{8,14},{9,15},{10,... | collective-permute-start | bytes 24584 | tf_op jit(solution)/shard_map/ppermute | solution.py:36
  12.1 5.0 %collective-permute-start.5 = (bf16[4,1024]{1,0:T(4,128)(2,1)S(1)}, bf16[4,1024]{1,0:T(4,128)(2,1)S(1)}, u32[]{:S(2)}, u32[]{:S(2)}) collective-permute-start(bf16[4,1024]{1,0:T(4,128)(2,1)S(1)} %get-tuple-element.41), channel_id=1, source_target_pairs={{0,7},{1,6},{2,5},{3,4},{4,3},{5,2},{6,1},{7,0},{8,15},{9,14},{10,... | collective-permute-start | bytes 24584 | tf_op jit(solution)/shard_map/ppermute | solution.py:36
  18.2 3.8 %collective-permute-start.6 = (bf16[4,4096]{1,0:T(4,128)(2,1)S(1)}, bf16[4,4096]{1,0:T(4,128)(2,1)S(1)}, u32[]{:S(2)}, u32[]{:S(2)}) collective-permute-start(bf16[4,4096]{1,0:T(4,128)(2,1)S(1)} %get-tuple-element.43), channel_id=1, source_target_pairs={{0,5},{1,4},{2,7},{3,6},{4,1},{5,0},{6,3},{7,2},{8,13},{9,12},{10,... | collective-permute-start | bytes 98312 | tf_op jit(solution)/shard_map/ppermute | solution.py:36
  18.2 4.4 %collective-permute-start.7 = (bf16[4,4096]{1,0:T(4,128)(2,1)S(1)}, bf16[4,4096]{1,0:T(4,128)(2,1)S(1)}, u32[]{:S(2)}, u32[]{:S(2)}) collective-permute-start(bf16[4,4096]{1,0:T(4,128)(2,1)S(1)} %get-tuple-element.44), channel_id=1, source_target_pairs={{0,6},{1,7},{2,4},{3,5},{4,2},{5,3},{6,0},{7,1},{8,14},{9,15},{10,... | collective-permute-start | bytes 98312 | tf_op jit(solution)/shard_map/ppermute | solution.py:36
  18.7 5.6 %collective-permute-start.8 = (bf16[4,4096]{1,0:T(4,128)(2,1)S(1)}, bf16[4,4096]{1,0:T(4,128)(2,1)S(1)}, u32[]{:S(2)}, u32[]{:S(2)}) collective-permute-start(bf16[4,4096]{1,0:T(4,128)(2,1)S(1)} %get-tuple-element.45), channel_id=1, source_target_pairs={{0,7},{1,6},{2,5},{3,4},{4,3},{5,2},{6,1},{7,0},{8,15},{9,14},{10,... | collective-permute-start | bytes 98312 | tf_op jit(solution)/shard_map/ppermute | solution.py:36
  24.2 13.9 %copy-start.2 = (bf16[1,384,4096]{2,1,0:T(8,128)(2,1)S(1)}, bf16[1,384,4096]{2,1,0:T(8,128)(2,1)}, u32[]{:S(2)}) copy-start(bf16[1,384,4096]{2,1,0:T(8,128)(2,1)} %refs_7_.1) | copy-start | bytes 9437188
  24.4 5.2 %collective-permute-start.11 = (bf16[4,4224]{1,0:T(4,128)(2,1)S(1)}, bf16[4,4224]{1,0:T(4,128)(2,1)S(1)}, u32[]{:S(2)}, u32[]{:S(2)}) collective-permute-start(bf16[4,4224]{1,0:T(4,128)(2,1)S(1)} %get-tuple-element.48), channel_id=1, source_target_pairs={{0,7},{1,6},{2,5},{3,4},{4,3},{5,2},{6,1},{7,0},{8,15},{9,14},{10,... | collective-permute-start | bytes 101384 | tf_op jit(solution)/shard_map/ppermute | solution.py:36
  27.5 4.3 %collective-permute-start.10 = (bf16[4,4224]{1,0:T(4,128)(2,1)S(1)}, bf16[4,4224]{1,0:T(4,128)(2,1)S(1)}, u32[]{:S(2)}, u32[]{:S(2)}) collective-permute-start(bf16[4,4224]{1,0:T(4,128)(2,1)S(1)} %get-tuple-element.48), channel_id=1, source_target_pairs={{0,6},{1,7},{2,4},{3,5},{4,2},{5,3},{6,0},{7,1},{8,14},{9,15},{10,... | collective-permute-start | bytes 101384 | tf_op jit(solution)/shard_map/ppermute | solution.py:36
  27.5 4.3 %collective-permute-start.9 = (bf16[4,4224]{1,0:T(4,128)(2,1)S(1)}, bf16[4,4224]{1,0:T(4,128)(2,1)S(1)}, u32[]{:S(2)}, u32[]{:S(2)}) collective-permute-start(bf16[4,4224]{1,0:T(4,128)(2,1)S(1)} %get-tuple-element.48), channel_id=1, source_target_pairs={{0,5},{1,4},{2,7},{3,6},{4,1},{5,0},{6,3},{7,2},{8,13},{9,12},{10,... | collective-permute-start | bytes 101384 | tf_op jit(solution)/shard_map/ppermute | solution.py:36
  28.6 8.0 %collective-permute-start.13 = (bf16[4,4224]{1,0:T(4,128)(2,1)S(1)}, bf16[4,4224]{1,0:T(4,128)(2,1)S(1)}, u32[]{:S(2)}, u32[]{:S(2)}) collective-permute-start(bf16[4,4224]{1,0:T(4,128)(2,1)S(1)} %get-tuple-element.48), channel_id=1, source_target_pairs={{0,12},{4,8},{8,4},{12,0},{1,13},{5,9},{9,5},{13,1},{2,14},{6,10},... | collective-permute-start | bytes 101384 | tf_op jit(solution)/shard_map/ppermute | solution.py:410
  31.9 4.7 %collective-permute-start.14 = (bf16[3,4,4224]{2,1,0:T(4,128)(2,1)S(1)}, bf16[3,4,4224]{2,1,0:T(4,128)(2,1)S(1)}, u32[]{:S(2)}, u32[]{:S(2)}) collective-permute-start(bf16[3,4,4224]{2,1,0:T(4,128)(2,1)S(1)} %pad_maximum_fusion.2), channel_id=1, source_target_pairs={{0,12},{4,8},{8,4},{12,0},{1,13},{5,9},{9,5},{13,1},{2,14},{6,10},... | collective-permute-start | bytes 304136 | tf_op jit(solution)/shard_map/ppermute | solution.py:410
  32.9 4.2 %collective-permute-start.12 = (bf16[16,4224]{1,0:T(8,128)(2,1)S(1)}, bf16[16,4224]{1,0:T(8,128)(2,1)S(1)}, u32[]{:S(2)}, u32[]{:S(2)}) collective-permute-start(bf16[16,4224]{1,0:T(8,128)(2,1)S(1)} %pad_maximum_fusion.refs_1_), channel_id=1, source_target_pairs={{0,4},{4,0},{8,12},{12,8},{1,5},{5,1},{9,13},{13,9},{2,6},{6,2},{1... | collective-permute-start | bytes 405512 | tf_op jit(solution)/shard_map/ppermute | solution.py:410
  36.7 1.4 %collective-permute-start.15 = (bf16[16,4224]{1,0:T(8,128)(2,1)S(1)}, bf16[16,4224]{1,0:T(8,128)(2,1)S(1)}, u32[]{:S(2)}, u32[]{:S(2)}) collective-permute-start(bf16[16,4224]{1,0:T(8,128)(2,1)S(1)} %pad_maximum_fusion.1.refs_4_), channel_id=1, source_target_pairs={{0,4},{4,0},{8,12},{12,8},{1,5},{5,1},{9,13},{13,9},{2,6},{6,2},{1... | collective-permute-start | bytes 405512 | tf_op jit(solution)/shard_map/ppermute | solution.py:410
  40.0 1.4 %collective-permute-start.17 = (bf16[4,4,4096]{2,1,0:T(4,128)(2,1)S(1)}, bf16[4,4,4096]{2,1,0:T(4,128)(2,1)S(1)}, u32[]{:S(2)}, u32[]{:S(2)}) collective-permute-start(bf16[4,4,4096]{2,1,0:T(4,128)(2,1)S(1)} %get-tuple-element.54), channel_id=1, source_target_pairs={{0,4},{4,0},{8,12},{12,8},{1,5},{5,1},{9,13},{13,9},{2,6},{6,2},{1... | collective-permute-start | bytes 393224 | tf_op jit(solution)/shard_map/ppermute | solution.py:410
  40.4 3.0 %collective-permute-start.16 = (bf16[4,4,4096]{2,1,0:T(4,128)(2,1)S(1)}, bf16[4,4,4096]{2,1,0:T(4,128)(2,1)S(1)}, u32[]{:S(2)}, u32[]{:S(2)}) collective-permute-start(bf16[4,4,4096]{2,1,0:T(4,128)(2,1)S(1)} %get-tuple-element.52), channel_id=1, source_target_pairs={{0,4},{4,0},{8,12},{12,8},{1,5},{5,1},{9,13},{13,9},{2,6},{6,2},{1... | collective-permute-start | bytes 393224 | tf_op jit(solution)/shard_map/ppermute | solution.py:410
  41.5 4.6 %collective-permute-start.19 = (bf16[3,4,4096]{2,1,0:T(4,128)(2,1)S(1)}, bf16[3,4,4096]{2,1,0:T(4,128)(2,1)S(1)}, u32[]{:S(2)}, u32[]{:S(2)}) collective-permute-start(bf16[3,4,4096]{2,1,0:T(4,128)(2,1)S(1)} %add_convert_fusion.1), channel_id=1, source_target_pairs={{0,12},{4,8},{8,4},{12,0},{1,13},{5,9},{9,5},{13,1},{2,14},{6,10},... | collective-permute-start | bytes 294920 | tf_op jit(solution)/shard_map/ppermute | solution.py:410
  42.5 7.5 %collective-permute-start.18 = (bf16[4,4096]{1,0:T(4,128)(2,1)S(1)}, bf16[4,4096]{1,0:T(4,128)(2,1)S(1)}, u32[]{:S(2)}, u32[]{:S(2)}) collective-permute-start(bf16[4,4096]{1,0:T(4,128)(2,1)S(1)} %fusion.5), channel_id=1, source_target_pairs={{0,12},{4,8},{8,4},{12,0},{1,13},{5,9},{9,5},{13,1},{2,14},{6,10},... | collective-permute-start | bytes 98312 | tf_op jit(solution)/shard_map/ppermute | solution.py:410
  46.3 3.7 %collective-permute-start.20 = (bf16[4,4096]{1,0:T(4,128)(2,1)S(1)}, bf16[4,4096]{1,0:T(4,128)(2,1)S(1)}, u32[]{:S(2)}, u32[]{:S(2)}) collective-permute-start(bf16[4,4096]{1,0:T(4,128)(2,1)S(1)} %get-tuple-element.58), channel_id=1, source_target_pairs={{0,5},{1,4},{2,7},{3,6},{4,1},{5,0},{6,3},{7,2},{8,13},{9,12},{10,... | collective-permute-start | bytes 98312 | tf_op jit(solution)/shard_map/ppermute | solution.py:36
  47.6 5.5 %collective-permute-start.22 = (bf16[4,4096]{1,0:T(4,128)(2,1)S(1)}, bf16[4,4096]{1,0:T(4,128)(2,1)S(1)}, u32[]{:S(2)}, u32[]{:S(2)}) collective-permute-start(bf16[4,4096]{1,0:T(4,128)(2,1)S(1)} %get-tuple-element.59), channel_id=1, source_target_pairs={{0,7},{1,6},{2,5},{3,4},{4,3},{5,2},{6,1},{7,0},{8,15},{9,14},{10,... | collective-permute-start | bytes 98312 | tf_op jit(solution)/shard_map/ppermute | solution.py:36
  50.0 4.6 %collective-permute-start.21 = (bf16[4,4096]{1,0:T(4,128)(2,1)S(1)}, bf16[4,4096]{1,0:T(4,128)(2,1)S(1)}, u32[]{:S(2)}, u32[]{:S(2)}) collective-permute-start(bf16[4,4096]{1,0:T(4,128)(2,1)S(1)} %get-tuple-element.60), channel_id=1, source_target_pairs={{0,6},{1,7},{2,4},{3,5},{4,2},{5,3},{6,0},{7,1},{8,14},{9,15},{10,... | collective-permute-start | bytes 98312 | tf_op jit(solution)/shard_map/ppermute | solution.py:36
  (6 other events, 58.1 us)

commit v6 on v5

--- a/solution.py
+++ b/solution.py
@@ -14,13 +14,6 @@
 F32 = jnp.float32
 BF16 = jnp.bfloat16
 COVER = 10**10
-
-
-def xor_exchange(blocks, axis, count):
-    moved = list(blocks)
-    for step in range(count - 1, 0, -1):
-        moved[step] = lax.ppermute(blocks[step], axis, [(j, j ^ step) for j in range(count)])
-    return moved
 
 
 def dp_turns(n_dp):
@@ -260,6 +253,10 @@
     ext = jnp.where(lane == at + 1, middle, ext)
     ext = jnp.where(lane == at + 2, low, ext)
     pay_ref[:, model:] = ext.astype(BF16)
+
+
+def hand_kernel(source, to):
+    to[...] = source[...]
 
 
 def expert_kernel(n_dp, n_ex, tokens, *refs):
@@ -348,7 +345,16 @@
         flops=COVER,
         moved=tokens * model * 4,
     )(*map(in_hbm, small))
-    rows = xor_exchange([row] * n_dp, "dp", n_dp)
+    turns = dp_turns(n_dp)
+
+    def over_dp(array, turn):
+        return lax.ppermute(array, "dp", [(j, j ^ turn) for j in range(n_dp)])
+
+    rows = {0: row}
+    for turn in reversed(turns):
+        for r in list(rows):
+            rows[r ^ turn] = over_dp(rows[r], turn)
+    rows = [rows[r] for r in range(n_dp)]
 
     att, targets = call(
         functools.partial(local_kernel, n_dp, kv_heads),
@@ -404,17 +410,14 @@
         moved=tokens * model * 16,
     )(*partials, base, ext_all, norm_gain[None])
     gathered = crossed_exchange([payload] * n_ex, n_dp, n_ex)
-    turns = dp_turns(n_dp)
-
-    def over_dp(array, turn):
-        return lax.ppermute(array, "dp", [(j, j ^ turn) for j in range(n_dp)])
-
-    top = turns[-1]
+    top, last = turns[-1], n_ex - 1
     near = over_dp(payload, top)
-    rest = over_dp(jnp.stack(gathered[1:]), top)
+    handed = call(hand_kernel, shape(payload.shape, BF16), [spec()], limit=1 << 20)(gathered[last])
+    far = over_dp(handed, top)
+    rest = over_dp(jnp.stack(gathered[1:last]), top)
     pieces = {
         0: jnp.concatenate(gathered, axis=0),
-        top: jnp.concatenate([near] + [rest[s] for s in range(n_ex - 1)], axis=0),
+        top: jnp.concatenate([near] + [rest[s] for s in range(n_ex - 2)] + [far], axis=0),
     }
     for turn in reversed(turns[:-1]):
         for r in list(pieces):
@@ -452,11 +455,17 @@
             whole = terms.pop(r)
             whole = whole[0] if len(whole) == 1 else added(whole).astype(BF16)
             terms[far[r]].append(over_dp(whole, turn))
-    rest = over_dp(added([t[1:] for t in terms[top]]).astype(BF16), top)
-    near = over_dp(added([t[0] for t in terms[top]]).astype(BF16), top)
-    mixed = added([t[1:] for t in terms[0]] + [rest]).astype(BF16)
-    staying = added([t[0] for t in terms[0]] + [near])
-    back = crossed_exchange([staying] + [mixed[s] for s in range(n_ex - 1)], n_dp, n_ex)
+
+    def across(at):
+        return over_dp(added([t[at] for t in terms[top]]).astype(BF16), top)
+
+    first = across(slice(2, n_ex))
+    second = across(1)
+    near = across(0)
+    first = added([t[2:] for t in terms[0]] + [first]).astype(BF16)
+    second = added([t[1] for t in terms[0]] + [second]).astype(BF16)
+    near = added([t[0] for t in terms[0]] + [near])
+    back = crossed_exchange([near, second] + [first[s] for s in range(n_ex - 2)], n_dp, n_ex)
     total = real
     for s in range(n_ex):
         total = total + back[s].astype(F32)

time: 55.4 us -> 54.8 us (0.989)
  waiting for transfers between devices: 24.8 us -> 17.9 us
  starting transfers between devices: 23.6 us -> 29.9 us
    ppermute x8 -> x13, starting transfers between devices: 4.74 us -> 12.7 us  [over_dp(): return lax.ppermute(array, 'dp', [(j, j ^ turn) for j in range(n_dp)])]
    ppermute x3 -> x0, starting transfers between devices: 3.18 us -> none  [xor_exchange(): lax.ppermute(blocks[step], axis, [(j, j ^ step) for j in range(count)])]
    ppermute x12, waiting for transfers between devices: 14.2 us -> 11.2 us  [crossed_exchange(): moved[step] = lax.ppermute(blocks[step], ('dp', 'expert'), pairs)]
    ppermute x3 -> x0, waiting for transfers between devices: 2.59 us -> none  [xor_exchange(): lax.ppermute(blocks[step], axis, [(j, j ^ step) for j in range(count)])]
    ppermute x12, starting transfers between devices: 15.7 us -> 17.2 us  [crossed_exchange(): moved[step] = lax.ppermute(blocks[step], ('dp', 'expert'), pairs)]
    ppermute x8 -> x13, waiting for transfers between devices: 7.98 us -> 6.77 us  [over_dp(): return lax.ppermute(array, 'dp', [(j, j ^ turn) for j in range(n_dp)])]
  transfers between devices with their start and end apart: 23 -> 25, of which waited for: 14 -> 14; matrix products, arithmetic and copies ran while one was open for 1% -> 1% of each run, Pallas kernels for 1% -> 1%
where the time goes in v6:
time: 54.8 us; the launch traced here: 54.7 us
  starting transfers between devices  29.9 us (55%)
  waiting for transfers between devices  17.9 us (33%)
  Pallas kernels  5.53 us (10%)
  other arithmetic  1.06 us (2%)
    ppermute x12, starting transfers between devices, crossed_exchange(): moved[step] = lax.ppermute(blocks[step], ('dp', 'expert'), pairs)  17.2 us
    ppermute x13, starting transfers between devices, over_dp(): return lax.ppermute(array, 'dp', [(j, j ^ turn) for j in range(n_dp)])  12.7 us
    ppermute x12, waiting for transfers between devices, crossed_exchange(): moved[step] = lax.ppermute(blocks[step], ('dp', 'expert'), pairs)  11.2 us
    ppermute x13, waiting for transfers between devices, over_dp(): return lax.ppermute(array, 'dp', [(j, j ^ turn) for j in range(n_dp)])  6.77 us
    pallas_call x1, Pallas kernels, per_device(): call(functools.partial(expert_kernel, n_dp, n_ex, tokens), [shape((n_ex,...  1.87 us
    pallas_call x1, Pallas kernels, per_device(): call(functools.partial(project_kernel, n_ex), [shape((tokens, model), F32...  1.21 us
  transfers between devices with their start and end apart: 25, of which 14 were waited for; matrix products, arithmetic and copies ran while one was open for 1% of the time, Pallas kernels for 1%

profile of v6, /device:TPU:0, one launch (start us, length us, event | category | flops | bytes accessed | tf_op | source)
XLA Modules:
  0.0 54.7 jit_solution(17630163833898018881)
XLA Ops:
  1.0 2.5 %collective-permute-start.1 = (bf16[1,8832]{1,0:T(2,128)(2,1)S(1)}, bf16[1,8832]{1,0:T(2,128)(2,1)S(1)}, u32[]{:S(2)}, u32[]{:S(2)}) collective-permute-start(bf16[1,8832]{1,0:T(2,128)(2,1)S(1)} %get-tuple-element.34.refs_1_), channel_id=1, source_target_pairs={{0,12},{4,8},{8,4},{12,0},{1,13},{5,9},{9,5},{13,1},{2,14},{6,10},... | collective-permute-start | bytes 53000 | tf_op jit(solution)/shard_map/ppermute | solution.py:351
  4.2 1.2 %collective-permute-done.1.refs_4_ = bf16[1,8832]{1,0:T(2,128)(2,1)S(1)} collective-permute-done((bf16[1,8832]{1,0:T(2,128)(2,1)S(1)}, bf16[1,8832]{1,0:T(2,128)(2,1)S(1)}, u32[]{:S(2)}, u32[]{:S(2)}) %collective-permute-start.1) | collective-permute-done | bytes 17696 | tf_op jit(solution)/shard_map/ppermute | solution.py:351
  7.2 2.2 %collective-permute-start.3 = (bf16[4,1024]{1,0:T(4,128)(2,1)S(1)}, bf16[4,1024]{1,0:T(4,128)(2,1)S(1)}, u32[]{:S(2)}, u32[]{:S(2)}) collective-permute-start(bf16[4,1024]{1,0:T(4,128)(2,1)S(1)} %get-tuple-element.39), channel_id=1, source_target_pairs={{0,5},{1,4},{2,7},{3,6},{4,1},{5,0},{6,3},{7,2},{8,13},{9,12},{10,... | collective-permute-start | bytes 24584 | tf_op jit(solution)/shard_map/ppermute | solution.py:29
  9.4 2.5 %collective-permute-start.4 = (bf16[4,1024]{1,0:T(4,128)(2,1)S(1)}, bf16[4,1024]{1,0:T(4,128)(2,1)S(1)}, u32[]{:S(2)}, u32[]{:S(2)}) collective-permute-start(bf16[4,1024]{1,0:T(4,128)(2,1)S(1)} %get-tuple-element.40), channel_id=1, source_target_pairs={{0,6},{1,7},{2,4},{3,5},{4,2},{5,3},{6,0},{7,1},{8,14},{9,15},{10,... | collective-permute-start | bytes 24584 | tf_op jit(solution)/shard_map/ppermute | solution.py:29
  11.9 1.4 %collective-permute-done.4.refs_2_ = bf16[4,1024]{1,0:T(4,128)(2,1)S(1)} collective-permute-done((bf16[4,1024]{1,0:T(4,128)(2,1)S(1)}, bf16[4,1024]{1,0:T(4,128)(2,1)S(1)}, u32[]{:S(2)}, u32[]{:S(2)}) %collective-permute-start.4) | collective-permute-done | bytes 8224 | tf_op jit(solution)/shard_map/ppermute | solution.py:29
  13.4 3.4 %collective-permute-done.5.refs_3_ = bf16[4,1024]{1,0:T(4,128)(2,1)S(1)} collective-permute-done((bf16[4,1024]{1,0:T(4,128)(2,1)S(1)}, bf16[4,1024]{1,0:T(4,128)(2,1)S(1)}, u32[]{:S(2)}, u32[]{:S(2)}) %collective-permute-start.5) | collective-permute-done | bytes 8224 | tf_op jit(solution)/shard_map/ppermute | solution.py:29
  16.8 1.2 %shard_map.130 = (f32[4,4096]{1,0:T(4,128)S(1)}, bf16[4,4096]{1,0:T(4,128)(2,1)S(1)}, bf16[4,4096]{1,0:T(4,128)(2,1)S(1)}, bf16[4,4096]{1,0:T(4,128)(2,1)S(1)}) custom-call(bf16[4,1024]{1,0:T(4,128)(2,1)S(1)} %get-tuple-element.38.refs_0_, bf16[4,1024]{1,0:T(4,128)(2,1)S(1)} %collective-permute-done.3.refs_1_, ...), custom_call_target="tpu_custom_call" | custom-call | flops 134217728 | bytes 8388608 | tf_op jit(solution)/shard_map/pallas_call | solution.py:393
  18.5 3.5 %collective-permute-start.8 = (bf16[4,4096]{1,0:T(4,128)(2,1)S(1)}, bf16[4,4096]{1,0:T(4,128)(2,1)S(1)}, u32[]{:S(2)}, u32[]{:S(2)}) collective-permute-start(bf16[4,4096]{1,0:T(4,128)(2,1)S(1)} %get-tuple-element.45), channel_id=1, source_target_pairs={{0,7},{1,6},{2,5},{3,4},{4,3},{5,2},{6,1},{7,0},{8,15},{9,14},{10,... | collective-permute-start | bytes 98312 | tf_op jit(solution)/shard_map/ppermute | solution.py:29
  22.3 1.8 %collective-permute-done.8.refs_3_ = bf16[4,4096]{1,0:T(4,128)(2,1)S(1)} collective-permute-done((bf16[4,4096]{1,0:T(4,128)(2,1)S(1)}, bf16[4,4096]{1,0:T(4,128)(2,1)S(1)}, u32[]{:S(2)}, u32[]{:S(2)}) %collective-permute-start.8) | collective-permute-done | bytes 32800 | tf_op jit(solution)/shard_map/ppermute | solution.py:29
  24.3 3.0 %collective-permute-start.11 = (bf16[4,4224]{1,0:T(4,128)(2,1)S(1)}, bf16[4,4224]{1,0:T(4,128)(2,1)S(1)}, u32[]{:S(2)}, u32[]{:S(2)}) collective-permute-start(bf16[4,4224]{1,0:T(4,128)(2,1)S(1)} %get-tuple-element.48), channel_id=1, source_target_pairs={{0,7},{1,6},{2,5},{3,4},{4,3},{5,2},{6,1},{7,0},{8,15},{9,14},{10,... | collective-permute-start | bytes 101384 | tf_op jit(solution)/shard_map/ppermute | solution.py:29
  27.3 1.1 %collective-permute-start.9 = (bf16[4,4224]{1,0:T(4,128)(2,1)S(1)}, bf16[4,4224]{1,0:T(4,128)(2,1)S(1)}, u32[]{:S(2)}, u32[]{:S(2)}) collective-permute-start(bf16[4,4224]{1,0:T(4,128)(2,1)S(1)} %get-tuple-element.48), channel_id=1, source_target_pairs={{0,5},{1,4},{2,7},{3,6},{4,1},{5,0},{6,3},{7,2},{8,13},{9,12},{10,... | collective-permute-start | bytes 101384 | tf_op jit(solution)/shard_map/ppermute | solution.py:29
  28.4 1.3 %collective-permute-start.13 = (bf16[4,4224]{1,0:T(4,128)(2,1)S(1)}, bf16[4,4224]{1,0:T(4,128)(2,1)S(1)}, u32[]{:S(2)}, u32[]{:S(2)}) collective-permute-start(bf16[4,4224]{1,0:T(4,128)(2,1)S(1)} %get-tuple-element.48), channel_id=1, source_target_pairs={{0,12},{4,8},{8,4},{12,0},{1,13},{5,9},{9,5},{13,1},{2,14},{6,10},... | collective-permute-start | bytes 101384 | tf_op jit(solution)/shard_map/ppermute | solution.py:351
  29.8 1.5 %collective-permute-start.15 = (bf16[4,4224]{1,0:T(4,128)(2,1)S(1)}, bf16[4,4224]{1,0:T(4,128)(2,1)S(1)}, u32[]{:S(2)}, u32[]{:S(2)}) collective-permute-start(bf16[4,4224]{1,0:T(4,128)(2,1)S(1)} %shard_map.132), channel_id=1, source_target_pairs={{0,12},{4,8},{8,4},{12,0},{1,13},{5,9},{9,5},{13,1},{2,14},{6,10},... | collective-permute-start | bytes 101384 | tf_op jit(solution)/shard_map/ppermute | solution.py:351
  31.6 1.6 %collective-permute-start.14 = (bf16[2,4,4224]{2,1,0:T(4,128)(2,1)S(1)}, bf16[2,4,4224]{2,1,0:T(4,128)(2,1)S(1)}, u32[]{:S(2)}, u32[]{:S(2)}) collective-permute-start(bf16[2,4,4224]{2,1,0:T(4,128)(2,1)S(1)} %pad_maximum_fusion.2), channel_id=1, source_target_pairs={{0,12},{4,8},{8,4},{12,0},{1,13},{5,9},{9,5},{13,1},{2,14},{6,10},... | collective-permute-start | bytes 202760 | tf_op jit(solution)/shard_map/ppermute | solution.py:351
  33.5 2.1 %collective-permute-done.14 = bf16[2,4,4224]{2,1,0:T(4,128)(2,1)S(1)} collective-permute-done((bf16[2,4,4224]{2,1,0:T(4,128)(2,1)S(1)}, bf16[2,4,4224]{2,1,0:T(4,128)(2,1)S(1)}, u32[]{:S(2)}, u32[]{:S(2)}) %collective-permute-start.14) | collective-permute-done | bytes 67616 | tf_op jit(solution)/shard_map/ppermute | solution.py:351
  37.2 1.9 %shard_map.133 = (bf16[4,4,4096]{2,1,0:T(4,128)(2,1)S(1)}, bf16[4,4,4096]{2,1,0:T(4,128)(2,1)S(1)}, bf16[4,4,4096]{2,1,0:T(4,128)(2,1)S(1)}, bf16[4,4,4096]{2,1,0:T(4,128)(2,1)S(1)}, f32[4,4096]{1,0:T(4,128)S(1)}) custom-call(s32[24,128]{1,0:T(8,128)S(1)} %get-tuple-element.33.refs_0_, bf16[16,4224]{1,0:T(8,128)(2,1)S(1)} %pad_maximum_fusion.refs_1_, ...), custom_call_target="tpu_custom_call" | custom-call | flops 603979776 | bytes 9437184 | tf_op jit(solution)/shard_map/pallas_call | solution.py:430
  40.5 1.6 %collective-permute-start.19 = (bf16[4,4096]{1,0:T(4,128)(2,1)S(1)}, bf16[4,4096]{1,0:T(4,128)(2,1)S(1)}, u32[]{:S(2)}, u32[]{:S(2)}) collective-permute-start(bf16[4,4096]{1,0:T(4,128)(2,1)S(1)} %get-tuple-element.55), channel_id=1, source_target_pairs={{0,12},{4,8},{8,4},{12,0},{1,13},{5,9},{9,5},{13,1},{2,14},{6,10},... | collective-permute-start | bytes 98312 | tf_op jit(solution)/shard_map/ppermute | solution.py:351
  42.3 1.6 %collective-permute-start.22 = (bf16[2,4,4096]{2,1,0:T(4,128)(2,1)S(1)}, bf16[2,4,4096]{2,1,0:T(4,128)(2,1)S(1)}, u32[]{:S(2)}, u32[]{:S(2)}) collective-permute-start(bf16[2,4,4096]{2,1,0:T(4,128)(2,1)S(1)} %add_convert_fusion.1), channel_id=1, source_target_pairs={{0,12},{4,8},{8,4},{12,0},{1,13},{5,9},{9,5},{13,1},{2,14},{6,10},... | collective-permute-start | bytes 196616 | tf_op jit(solution)/shard_map/ppermute | solution.py:351
  44.0 1.5 %collective-permute-done.20 = bf16[4,4096]{1,0:T(4,128)(2,1)S(1)} collective-permute-done((bf16[4,4096]{1,0:T(4,128)(2,1)S(1)}, bf16[4,4096]{1,0:T(4,128)(2,1)S(1)}, u32[]{:S(2)}, u32[]{:S(2)}) %collective-permute-start.20) | collective-permute-done | bytes 32800 | tf_op jit(solution)/shard_map/ppermute | solution.py:351
  45.5 1.3 %collective-permute-start.21 = (bf16[4,4096]{1,0:T(4,128)(2,1)S(1)}, bf16[4,4096]{1,0:T(4,128)(2,1)S(1)}, u32[]{:S(2)}, u32[]{:S(2)}) collective-permute-start(bf16[4,4096]{1,0:T(4,128)(2,1)S(1)} %fusion), channel_id=1, source_target_pairs={{0,5},{1,4},{2,7},{3,6},{4,1},{5,0},{6,3},{7,2},{8,13},{9,12},{10,... | collective-permute-start | bytes 98312 | tf_op jit(solution)/shard_map/ppermute | solution.py:29
  46.9 1.9 %collective-permute-start.23 = (bf16[4,4096]{1,0:T(4,128)(2,1)S(1)}, bf16[4,4096]{1,0:T(4,128)(2,1)S(1)}, u32[]{:S(2)}, u32[]{:S(2)}) collective-permute-start(bf16[4,4096]{1,0:T(4,128)(2,1)S(1)} %get-tuple-element.59), channel_id=1, source_target_pairs={{0,6},{1,7},{2,4},{3,5},{4,2},{5,3},{6,0},{7,1},{8,14},{9,15},{10,... | collective-permute-start | bytes 98312 | tf_op jit(solution)/shard_map/ppermute | solution.py:29
  48.8 1.4 %collective-permute-start.24 = (bf16[4,4096]{1,0:T(4,128)(2,1)S(1)}, bf16[4,4096]{1,0:T(4,128)(2,1)S(1)}, u32[]{:S(2)}, u32[]{:S(2)}) collective-permute-start(bf16[4,4096]{1,0:T(4,128)(2,1)S(1)} %get-tuple-element.60), channel_id=1, source_target_pairs={{0,7},{1,6},{2,5},{3,4},{4,3},{5,2},{6,1},{7,0},{8,15},{9,14},{10,... | collective-permute-start | bytes 98312 | tf_op jit(solution)/shard_map/ppermute | solution.py:29
  50.2 1.1 %collective-permute-done.23 = bf16[4,4096]{1,0:T(4,128)(2,1)S(1)} collective-permute-done((bf16[4,4096]{1,0:T(4,128)(2,1)S(1)}, bf16[4,4096]{1,0:T(4,128)(2,1)S(1)}, u32[]{:S(2)}, u32[]{:S(2)}) %collective-permute-start.23) | collective-permute-done | bytes 32800 | tf_op jit(solution)/shard_map/ppermute | solution.py:29
  51.3 2.7 %collective-permute-done.24 = bf16[4,4096]{1,0:T(4,128)(2,1)S(1)} collective-permute-done((bf16[4,4096]{1,0:T(4,128)(2,1)S(1)}, bf16[4,4096]{1,0:T(4,128)(2,1)S(1)}, u32[]{:S(2)}, u32[]{:S(2)}) %collective-permute-start.24) | collective-permute-done | bytes 32800 | tf_op jit(solution)/shard_map/ppermute | solution.py:29
  (58 shorter events, 9.4 us)
Async XLA Ops:
  1.0 4.3 %collective-permute-start.1 = (bf16[1,8832]{1,0:T(2,128)(2,1)S(1)}, bf16[1,8832]{1,0:T(2,128)(2,1)S(1)}, u32[]{:S(2)}, u32[]{:S(2)}) collective-permute-start(bf16[1,8832]{1,0:T(2,128)(2,1)S(1)} %get-tuple-element.34.refs_1_), channel_id=1, source_target_pairs={{0,12},{4,8},{8,4},{12,0},{1,13},{5,9},{9,5},{13,1},{2,14},{6,10},... | collective-permute-start | bytes 53000 | tf_op jit(solution)/shard_map/ppermute | solution.py:351
  3.5 3.1 %collective-permute-start = (bf16[1,8832]{1,0:T(2,128)(2,1)S(1)}, bf16[1,8832]{1,0:T(2,128)(2,1)S(1)}, u32[]{:S(2)}, u32[]{:S(2)}) collective-permute-start(bf16[1,8832]{1,0:T(2,128)(2,1)S(1)} %get-tuple-element.34.refs_1_), channel_id=1, source_target_pairs={{0,4},{4,0},{8,12},{12,8},{1,5},{5,1},{9,13},{13,9},{2,6},{6,2},{1... | collective-permute-start | bytes 53000 | tf_op jit(solution)/shard_map/ppermute | solution.py:351
  7.2 4.7 %collective-permute-start.3 = (bf16[4,1024]{1,0:T(4,128)(2,1)S(1)}, bf16[4,1024]{1,0:T(4,128)(2,1)S(1)}, u32[]{:S(2)}, u32[]{:S(2)}) collective-permute-start(bf16[4,1024]{1,0:T(4,128)(2,1)S(1)} %get-tuple-element.39), channel_id=1, source_target_pairs={{0,5},{1,4},{2,7},{3,6},{4,1},{5,0},{6,3},{7,2},{8,13},{9,12},{10,... | collective-permute-start | bytes 24584 | tf_op jit(solution)/shard_map/ppermute | solution.py:29
  9.4 4.0 %collective-permute-start.4 = (bf16[4,1024]{1,0:T(4,128)(2,1)S(1)}, bf16[4,1024]{1,0:T(4,128)(2,1)S(1)}, u32[]{:S(2)}, u32[]{:S(2)}) collective-permute-start(bf16[4,1024]{1,0:T(4,128)(2,1)S(1)} %get-tuple-element.40), channel_id=1, source_target_pairs={{0,6},{1,7},{2,4},{3,5},{4,2},{5,3},{6,0},{7,1},{8,14},{9,15},{10,... | collective-permute-start | bytes 24584 | tf_op jit(solution)/shard_map/ppermute | solution.py:29
  11.9 4.9 %collective-permute-start.5 = (bf16[4,1024]{1,0:T(4,128)(2,1)S(1)}, bf16[4,1024]{1,0:T(4,128)(2,1)S(1)}, u32[]{:S(2)}, u32[]{:S(2)}) collective-permute-start(bf16[4,1024]{1,0:T(4,128)(2,1)S(1)} %get-tuple-element.41), channel_id=1, source_target_pairs={{0,7},{1,6},{2,5},{3,4},{4,3},{5,2},{6,1},{7,0},{8,15},{9,14},{10,... | collective-permute-start | bytes 24584 | tf_op jit(solution)/shard_map/ppermute | solution.py:29
  18.0 3.9 %collective-permute-start.6 = (bf16[4,4096]{1,0:T(4,128)(2,1)S(1)}, bf16[4,4096]{1,0:T(4,128)(2,1)S(1)}, u32[]{:S(2)}, u32[]{:S(2)}) collective-permute-start(bf16[4,4096]{1,0:T(4,128)(2,1)S(1)} %get-tuple-element.43), channel_id=1, source_target_pairs={{0,5},{1,4},{2,7},{3,6},{4,1},{5,0},{6,3},{7,2},{8,13},{9,12},{10,... | collective-permute-start | bytes 98312 | tf_op jit(solution)/shard_map/ppermute | solution.py:29
  18.0 4.3 %collective-permute-start.7 = (bf16[4,4096]{1,0:T(4,128)(2,1)S(1)}, bf16[4,4096]{1,0:T(4,128)(2,1)S(1)}, u32[]{:S(2)}, u32[]{:S(2)}) collective-permute-start(bf16[4,4096]{1,0:T(4,128)(2,1)S(1)} %get-tuple-element.44), channel_id=1, source_target_pairs={{0,6},{1,7},{2,4},{3,5},{4,2},{5,3},{6,0},{7,1},{8,14},{9,15},{10,... | collective-permute-start | bytes 98312 | tf_op jit(solution)/shard_map/ppermute | solution.py:29
  18.5 5.7 %collective-permute-start.8 = (bf16[4,4096]{1,0:T(4,128)(2,1)S(1)}, bf16[4,4096]{1,0:T(4,128)(2,1)S(1)}, u32[]{:S(2)}, u32[]{:S(2)}) collective-permute-start(bf16[4,4096]{1,0:T(4,128)(2,1)S(1)} %get-tuple-element.45), channel_id=1, source_target_pairs={{0,7},{1,6},{2,5},{3,4},{4,3},{5,2},{6,1},{7,0},{8,15},{9,14},{10,... | collective-permute-start | bytes 98312 | tf_op jit(solution)/shard_map/ppermute | solution.py:29
  24.3 5.5 %collective-permute-start.11 = (bf16[4,4224]{1,0:T(4,128)(2,1)S(1)}, bf16[4,4224]{1,0:T(4,128)(2,1)S(1)}, u32[]{:S(2)}, u32[]{:S(2)}) collective-permute-start(bf16[4,4224]{1,0:T(4,128)(2,1)S(1)} %get-tuple-element.48), channel_id=1, source_target_pairs={{0,7},{1,6},{2,5},{3,4},{4,3},{5,2},{6,1},{7,0},{8,15},{9,14},{10,... | collective-permute-start | bytes 101384 | tf_op jit(solution)/shard_map/ppermute | solution.py:29
  27.3 4.2 %collective-permute-start.10 = (bf16[4,4224]{1,0:T(4,128)(2,1)S(1)}, bf16[4,4224]{1,0:T(4,128)(2,1)S(1)}, u32[]{:S(2)}, u32[]{:S(2)}) collective-permute-start(bf16[4,4224]{1,0:T(4,128)(2,1)S(1)} %get-tuple-element.48), channel_id=1, source_target_pairs={{0,6},{1,7},{2,4},{3,5},{4,2},{5,3},{6,0},{7,1},{8,14},{9,15},{10,... | collective-permute-start | bytes 101384 | tf_op jit(solution)/shard_map/ppermute | solution.py:29
  27.3 4.2 %collective-permute-start.9 = (bf16[4,4224]{1,0:T(4,128)(2,1)S(1)}, bf16[4,4224]{1,0:T(4,128)(2,1)S(1)}, u32[]{:S(2)}, u32[]{:S(2)}) collective-permute-start(bf16[4,4224]{1,0:T(4,128)(2,1)S(1)} %get-tuple-element.48), channel_id=1, source_target_pairs={{0,5},{1,4},{2,7},{3,6},{4,1},{5,0},{6,3},{7,2},{8,13},{9,12},{10,... | collective-permute-start | bytes 101384 | tf_op jit(solution)/shard_map/ppermute | solution.py:29
  28.4 7.2 %collective-permute-start.13 = (bf16[4,4224]{1,0:T(4,128)(2,1)S(1)}, bf16[4,4224]{1,0:T(4,128)(2,1)S(1)}, u32[]{:S(2)}, u32[]{:S(2)}) collective-permute-start(bf16[4,4224]{1,0:T(4,128)(2,1)S(1)} %get-tuple-element.48), channel_id=1, source_target_pairs={{0,12},{4,8},{8,4},{12,0},{1,13},{5,9},{9,5},{13,1},{2,14},{6,10},... | collective-permute-start | bytes 101384 | tf_op jit(solution)/shard_map/ppermute | solution.py:351
  29.8 5.8 %collective-permute-start.15 = (bf16[4,4224]{1,0:T(4,128)(2,1)S(1)}, bf16[4,4224]{1,0:T(4,128)(2,1)S(1)}, u32[]{:S(2)}, u32[]{:S(2)}) collective-permute-start(bf16[4,4224]{1,0:T(4,128)(2,1)S(1)} %shard_map.132), channel_id=1, source_target_pairs={{0,12},{4,8},{8,4},{12,0},{1,13},{5,9},{9,5},{13,1},{2,14},{6,10},... | collective-permute-start | bytes 101384 | tf_op jit(solution)/shard_map/ppermute | solution.py:351
  31.6 4.0 %collective-permute-start.14 = (bf16[2,4,4224]{2,1,0:T(4,128)(2,1)S(1)}, bf16[2,4,4224]{2,1,0:T(4,128)(2,1)S(1)}, u32[]{:S(2)}, u32[]{:S(2)}) collective-permute-start(bf16[2,4,4224]{2,1,0:T(4,128)(2,1)S(1)} %pad_maximum_fusion.2), channel_id=1, source_target_pairs={{0,12},{4,8},{8,4},{12,0},{1,13},{5,9},{9,5},{13,1},{2,14},{6,10},... | collective-permute-start | bytes 202760 | tf_op jit(solution)/shard_map/ppermute | solution.py:351
  33.3 2.9 %collective-permute-start.12 = (bf16[16,4224]{1,0:T(8,128)(2,1)S(1)}, bf16[16,4224]{1,0:T(8,128)(2,1)S(1)}, u32[]{:S(2)}, u32[]{:S(2)}) collective-permute-start(bf16[16,4224]{1,0:T(8,128)(2,1)S(1)} %pad_maximum_fusion.refs_1_), channel_id=1, source_target_pairs={{0,4},{4,0},{8,12},{12,8},{1,5},{5,1},{9,13},{13,9},{2,6},{6,2},{1... | collective-permute-start | bytes 405512 | tf_op jit(solution)/shard_map/ppermute | solution.py:351
  35.7 1.4 %collective-permute-start.16 = (bf16[16,4224]{1,0:T(8,128)(2,1)S(1)}, bf16[16,4224]{1,0:T(8,128)(2,1)S(1)}, u32[]{:S(2)}, u32[]{:S(2)}) collective-permute-start(bf16[16,4224]{1,0:T(8,128)(2,1)S(1)} %pad_maximum_fusion.1.refs_4_), channel_id=1, source_target_pairs={{0,4},{4,0},{8,12},{12,8},{1,5},{5,1},{9,13},{13,9},{2,6},{6,2},{1... | collective-permute-start | bytes 405512 | tf_op jit(solution)/shard_map/ppermute | solution.py:351
  39.0 1.4 %collective-permute-start.18 = (bf16[4,4,4096]{2,1,0:T(4,128)(2,1)S(1)}, bf16[4,4,4096]{2,1,0:T(4,128)(2,1)S(1)}, u32[]{:S(2)}, u32[]{:S(2)}) collective-permute-start(bf16[4,4,4096]{2,1,0:T(4,128)(2,1)S(1)} %get-tuple-element.54), channel_id=1, source_target_pairs={{0,4},{4,0},{8,12},{12,8},{1,5},{5,1},{9,13},{13,9},{2,6},{6,2},{1... | collective-permute-start | bytes 393224 | tf_op jit(solution)/shard_map/ppermute | solution.py:351
  39.4 4.5 %collective-permute-start.17 = (bf16[4,4,4096]{2,1,0:T(4,128)(2,1)S(1)}, bf16[4,4,4096]{2,1,0:T(4,128)(2,1)S(1)}, u32[]{:S(2)}, u32[]{:S(2)}) collective-permute-start(bf16[4,4,4096]{2,1,0:T(4,128)(2,1)S(1)} %get-tuple-element.52), channel_id=1, source_target_pairs={{0,4},{4,0},{8,12},{12,8},{1,5},{5,1},{9,13},{13,9},{2,6},{6,2},{1... | collective-permute-start | bytes 393224 | tf_op jit(solution)/shard_map/ppermute | solution.py:351
  40.5 9.7 %collective-permute-start.19 = (bf16[4,4096]{1,0:T(4,128)(2,1)S(1)}, bf16[4,4096]{1,0:T(4,128)(2,1)S(1)}, u32[]{:S(2)}, u32[]{:S(2)}) collective-permute-start(bf16[4,4096]{1,0:T(4,128)(2,1)S(1)} %get-tuple-element.55), channel_id=1, source_target_pairs={{0,12},{4,8},{8,4},{12,0},{1,13},{5,9},{9,5},{13,1},{2,14},{6,10},... | collective-permute-start | bytes 98312 | tf_op jit(solution)/shard_map/ppermute | solution.py:351
  42.1 3.4 %collective-permute-start.20 = (bf16[4,4096]{1,0:T(4,128)(2,1)S(1)}, bf16[4,4096]{1,0:T(4,128)(2,1)S(1)}, u32[]{:S(2)}, u32[]{:S(2)}) collective-permute-start(bf16[4,4096]{1,0:T(4,128)(2,1)S(1)} %get-tuple-element.56), channel_id=1, source_target_pairs={{0,12},{4,8},{8,4},{12,0},{1,13},{5,9},{9,5},{13,1},{2,14},{6,10},... | collective-permute-start | bytes 98312 | tf_op jit(solution)/shard_map/ppermute | solution.py:351
  42.3 4.5 %collective-permute-start.22 = (bf16[2,4,4096]{2,1,0:T(4,128)(2,1)S(1)}, bf16[2,4,4096]{2,1,0:T(4,128)(2,1)S(1)}, u32[]{:S(2)}, u32[]{:S(2)}) collective-permute-start(bf16[2,4,4096]{2,1,0:T(4,128)(2,1)S(1)} %add_convert_fusion.1), channel_id=1, source_target_pairs={{0,12},{4,8},{8,4},{12,0},{1,13},{5,9},{9,5},{13,1},{2,14},{6,10},... | collective-permute-start | bytes 196616 | tf_op jit(solution)/shard_map/ppermute | solution.py:351
  45.5 4.7 %collective-permute-start.21 = (bf16[4,4096]{1,0:T(4,128)(2,1)S(1)}, bf16[4,4096]{1,0:T(4,128)(2,1)S(1)}, u32[]{:S(2)}, u32[]{:S(2)}) collective-permute-start(bf16[4,4096]{1,0:T(4,128)(2,1)S(1)} %fusion), channel_id=1, source_target_pairs={{0,5},{1,4},{2,7},{3,6},{4,1},{5,0},{6,3},{7,2},{8,13},{9,12},{10,... | collective-permute-start | bytes 98312 | tf_op jit(solution)/shard_map/ppermute | solution.py:29
  46.9 4.3 %collective-permute-start.23 = (bf16[4,4096]{1,0:T(4,128)(2,1)S(1)}, bf16[4,4096]{1,0:T(4,128)(2,1)S(1)}, u32[]{:S(2)}, u32[]{:S(2)}) collective-permute-start(bf16[4,4096]{1,0:T(4,128)(2,1)S(1)} %get-tuple-element.59), channel_id=1, source_target_pairs={{0,6},{1,7},{2,4},{3,5},{4,2},{5,3},{6,0},{7,1},{8,14},{9,15},{10,... | collective-permute-start | bytes 98312 | tf_op jit(solution)/shard_map/ppermute | solution.py:29
  48.8 5.1 %collective-permute-start.24 = (bf16[4,4096]{1,0:T(4,128)(2,1)S(1)}, bf16[4,4096]{1,0:T(4,128)(2,1)S(1)}, u32[]{:S(2)}, u32[]{:S(2)}) collective-permute-start(bf16[4,4096]{1,0:T(4,128)(2,1)S(1)} %get-tuple-element.60), channel_id=1, source_target_pairs={{0,7},{1,6},{2,5},{3,4},{4,3},{5,2},{6,1},{7,0},{8,15},{9,14},{10,... | collective-permute-start | bytes 98312 | tf_op jit(solution)/shard_map/ppermute | solution.py:29
  (8 other events, 73.8 us)

commit v7 on v6

--- a/solution.py
+++ b/solution.py
@@ -253,6 +253,13 @@
     ext = jnp.where(lane == at + 1, middle, ext)
     ext = jnp.where(lane == at + 2, low, ext)
     pay_ref[:, model:] = ext.astype(BF16)
+
+
+def add_kernel(at, block_ref, *refs):
+    total = block_ref[...].astype(F32)
+    for ref in refs[:-1]:
+        total = total + ref[at].astype(F32)
+    refs[-1][...] = total.astype(refs[-1].dtype)
 
 
 def hand_kernel(source, to):
@@ -350,11 +357,7 @@
     def over_dp(array, turn):
         return lax.ppermute(array, "dp", [(j, j ^ turn) for j in range(n_dp)])
 
-    rows = {0: row}
-    for turn in reversed(turns):
-        for r in list(rows):
-            rows[r ^ turn] = over_dp(rows[r], turn)
-    rows = [rows[r] for r in range(n_dp)]
+    rows = [row] + [over_dp(row, r) for r in range(n_dp - 1, 0, -1)][::-1]
 
     att, targets = call(
         functools.partial(local_kernel, n_dp, kv_heads),
@@ -459,13 +462,17 @@
     def across(at):
         return over_dp(added([t[at] for t in terms[top]]).astype(BF16), top)
 
-    first = across(slice(2, n_ex))
-    second = across(1)
-    near = across(0)
-    first = added([t[2:] for t in terms[0]] + [first]).astype(BF16)
-    second = added([t[1] for t in terms[0]] + [second]).astype(BF16)
-    near = added([t[0] for t in terms[0]] + [near])
-    back = crossed_exchange([near, second] + [first[s] for s in range(n_ex - 2)], n_dp, n_ex)
+    arrived = [across(s) for s in range(n_ex)]
+    mixed = [
+        call(
+            functools.partial(add_kernel, s),
+            shape((tokens, model), BF16 if s else F32),
+            [spec()] * (len(terms[0]) + 1),
+            limit=1 << 20,
+        )(arrived[s], *terms[0])
+        for s in range(n_ex)
+    ]
+    back = crossed_exchange(mixed, n_dp, n_ex)
     total = real
     for s in range(n_ex):
         total = total + back[s].astype(F32)

time: 54.8 us -> 53.9 us (0.984)
  starting transfers between devices: 29.9 us -> 26.9 us
  waiting for transfers between devices: 17.9 us -> 20.1 us
    ppermute x13 -> x14, starting transfers between devices: 12.7 us -> 10.7 us  [over_dp(): return lax.ppermute(array, 'dp', [(j, j ^ turn) for j in range(n_dp)])]
    ppermute x12, waiting for transfers between devices: 11.2 us -> 12.9 us  [crossed_exchange(): moved[step] = lax.ppermute(blocks[step], ('dp', 'expert'), pairs)]
    ppermute x12, starting transfers between devices: 17.2 us -> 16.2 us  [crossed_exchange(): moved[step] = lax.ppermute(blocks[step], ('dp', 'expert'), pairs)]
    ppermute x13 -> x14, waiting for transfers between devices: 6.77 us -> 7.13 us  [over_dp(): return lax.ppermute(array, 'dp', [(j, j ^ turn) for j in range(n_dp)])]
  transfers between devices with their start and end apart: 25 -> 26, of which waited for: 14 -> 13; matrix products, arithmetic and copies ran while one was open for 1% -> 1% of each run, Pallas kernels for 1% -> 2%
where the time goes in v7:
time: 53.9 us; the launch traced here: 53.8 us
  starting transfers between devices  26.9 us (50%)
  waiting for transfers between devices  20.1 us (37%)
  Pallas kernels  5.61 us (10%)
  other arithmetic  0.95 us (2%)
    ppermute x12, starting transfers between devices, crossed_exchange(): moved[step] = lax.ppermute(blocks[step], ('dp', 'expert'), pairs)  16.2 us
    ppermute x12, waiting for transfers between devices, crossed_exchange(): moved[step] = lax.ppermute(blocks[step], ('dp', 'expert'), pairs)  12.9 us
    ppermute x14, starting transfers between devices, over_dp(): return lax.ppermute(array, 'dp', [(j, j ^ turn) for j in range(n_dp)])  10.7 us
    ppermute x14, waiting for transfers between devices, over_dp(): return lax.ppermute(array, 'dp', [(j, j ^ turn) for j in range(n_dp)])  7.13 us
    pallas_call x1, Pallas kernels, per_device(): call(functools.partial(expert_kernel, n_dp, n_ex, tokens), [shape((n_ex,...  1.86 us
    pallas_call x1, Pallas kernels, per_device(): call(functools.partial(project_kernel, n_ex), [shape((tokens, model), F32...  1.21 us
  transfers between devices with their start and end apart: 26, of which 13 were waited for; matrix products, arithmetic and copies ran while one was open for 1% of the time, Pallas kernels for 2%

profile of v7, /device:TPU:0, one launch (start us, length us, event | category | flops | bytes accessed | tf_op | source)
XLA Modules:
  0.0 53.8 jit_solution(10814930177123765829)
XLA Ops:
  0.0 1.0 %shard_map.127 = (bf16[1,8832]{1,0:T(2,128)(2,1)S(1)}, bf16[4,4096]{1,0:T(4,128)(2,1)S(1)}, bf16[4,512]{1,0:T(4,128)(2,1)S(1)}, bf16[4,4096]{1,0:T(4,128)(2,1)S(...) custom-call(bf16[4,4096]{1,0:T(4,128)(2,1)} %q_hbm.1, bf16[4,512]{1,0:T(4,128)(2,1)} %fresh_hbm.1, ...), custom_call_target="tpu_custom_call" | custom-call | flops 10000000000 | bytes 65536 | tf_op jit(solution)/shard_map/pallas_call | solution.py:333
  1.0 2.5 %collective-permute-start.2 = (bf16[1,8832]{1,0:T(2,128)(2,1)S(1)}, bf16[1,8832]{1,0:T(2,128)(2,1)S(1)}, u32[]{:S(2)}, u32[]{:S(2)}) collective-permute-start(bf16[1,8832]{1,0:T(2,128)(2,1)S(1)} %get-tuple-element.34.refs_1_), channel_id=1, source_target_pairs={{0,12},{4,8},{8,4},{12,0},{1,13},{5,9},{9,5},{13,1},{2,14},{6,10},... | collective-permute-start | bytes 53000 | tf_op jit(solution)/shard_map/ppermute | solution.py:358
  5.4 2.2 %collective-permute-done.1.refs_3_ = bf16[1,8832]{1,0:T(2,128)(2,1)S(1)} collective-permute-done((bf16[1,8832]{1,0:T(2,128)(2,1)S(1)}, bf16[1,8832]{1,0:T(2,128)(2,1)S(1)}, u32[]{:S(2)}, u32[]{:S(2)}) %collective-permute-start.1) | collective-permute-done | bytes 17696 | tf_op jit(solution)/shard_map/ppermute | solution.py:358
  8.1 1.1 %collective-permute-start.3 = (bf16[4,1024]{1,0:T(4,128)(2,1)S(1)}, bf16[4,1024]{1,0:T(4,128)(2,1)S(1)}, u32[]{:S(2)}, u32[]{:S(2)}) collective-permute-start(bf16[4,1024]{1,0:T(4,128)(2,1)S(1)} %get-tuple-element.39), channel_id=1, source_target_pairs={{0,5},{1,4},{2,7},{3,6},{4,1},{5,0},{6,3},{7,2},{8,13},{9,12},{10,... | collective-permute-start | bytes 24584 | tf_op jit(solution)/shard_map/ppermute | solution.py:29
  9.2 2.9 %collective-permute-start.4 = (bf16[4,1024]{1,0:T(4,128)(2,1)S(1)}, bf16[4,1024]{1,0:T(4,128)(2,1)S(1)}, u32[]{:S(2)}, u32[]{:S(2)}) collective-permute-start(bf16[4,1024]{1,0:T(4,128)(2,1)S(1)} %get-tuple-element.40), channel_id=1, source_target_pairs={{0,6},{1,7},{2,4},{3,5},{4,2},{5,3},{6,0},{7,1},{8,14},{9,15},{10,... | collective-permute-start | bytes 24584 | tf_op jit(solution)/shard_map/ppermute | solution.py:29
  12.1 1.4 %collective-permute-done.4.refs_2_ = bf16[4,1024]{1,0:T(4,128)(2,1)S(1)} collective-permute-done((bf16[4,1024]{1,0:T(4,128)(2,1)S(1)}, bf16[4,1024]{1,0:T(4,128)(2,1)S(1)}, u32[]{:S(2)}, u32[]{:S(2)}) %collective-permute-start.4) | collective-permute-done | bytes 8224 | tf_op jit(solution)/shard_map/ppermute | solution.py:29
  13.4 3.6 %collective-permute-done.5.refs_3_ = bf16[4,1024]{1,0:T(4,128)(2,1)S(1)} collective-permute-done((bf16[4,1024]{1,0:T(4,128)(2,1)S(1)}, bf16[4,1024]{1,0:T(4,128)(2,1)S(1)}, u32[]{:S(2)}, u32[]{:S(2)}) %collective-permute-start.5) | collective-permute-done | bytes 8224 | tf_op jit(solution)/shard_map/ppermute | solution.py:29
  17.0 1.2 %shard_map.130 = (f32[4,4096]{1,0:T(4,128)S(1)}, bf16[4,4096]{1,0:T(4,128)(2,1)S(1)}, bf16[4,4096]{1,0:T(4,128)(2,1)S(1)}, bf16[4,4096]{1,0:T(4,128)(2,1)S(1)}) custom-call(bf16[4,1024]{1,0:T(4,128)(2,1)S(1)} %get-tuple-element.38.refs_0_, bf16[4,1024]{1,0:T(4,128)(2,1)S(1)} %collective-permute-done.3.refs_1_, ...), custom_call_target="tpu_custom_call" | custom-call | flops 134217728 | bytes 8388608 | tf_op jit(solution)/shard_map/pallas_call | solution.py:396
  18.7 3.4 %collective-permute-start.8 = (bf16[4,4096]{1,0:T(4,128)(2,1)S(1)}, bf16[4,4096]{1,0:T(4,128)(2,1)S(1)}, u32[]{:S(2)}, u32[]{:S(2)}) collective-permute-start(bf16[4,4096]{1,0:T(4,128)(2,1)S(1)} %get-tuple-element.45), channel_id=1, source_target_pairs={{0,7},{1,6},{2,5},{3,4},{4,3},{5,2},{6,1},{7,0},{8,15},{9,14},{10,... | collective-permute-start | bytes 98312 | tf_op jit(solution)/shard_map/ppermute | solution.py:29
  22.6 1.6 %collective-permute-done.8.refs_3_ = bf16[4,4096]{1,0:T(4,128)(2,1)S(1)} collective-permute-done((bf16[4,4096]{1,0:T(4,128)(2,1)S(1)}, bf16[4,4096]{1,0:T(4,128)(2,1)S(1)}, u32[]{:S(2)}, u32[]{:S(2)}) %collective-permute-start.8) | collective-permute-done | bytes 32800 | tf_op jit(solution)/shard_map/ppermute | solution.py:29
  24.4 3.1 %collective-permute-start.11 = (bf16[4,4224]{1,0:T(4,128)(2,1)S(1)}, bf16[4,4224]{1,0:T(4,128)(2,1)S(1)}, u32[]{:S(2)}, u32[]{:S(2)}) collective-permute-start(bf16[4,4224]{1,0:T(4,128)(2,1)S(1)} %get-tuple-element.48), channel_id=1, source_target_pairs={{0,7},{1,6},{2,5},{3,4},{4,3},{5,2},{6,1},{7,0},{8,15},{9,14},{10,... | collective-permute-start | bytes 101384 | tf_op jit(solution)/shard_map/ppermute | solution.py:29
  27.5 1.1 %collective-permute-start.9 = (bf16[4,4224]{1,0:T(4,128)(2,1)S(1)}, bf16[4,4224]{1,0:T(4,128)(2,1)S(1)}, u32[]{:S(2)}, u32[]{:S(2)}) collective-permute-start(bf16[4,4224]{1,0:T(4,128)(2,1)S(1)} %get-tuple-element.48), channel_id=1, source_target_pairs={{0,5},{1,4},{2,7},{3,6},{4,1},{5,0},{6,3},{7,2},{8,13},{9,12},{10,... | collective-permute-start | bytes 101384 | tf_op jit(solution)/shard_map/ppermute | solution.py:29
  29.6 1.1 %collective-permute-start.15 = (bf16[4,4224]{1,0:T(4,128)(2,1)S(1)}, bf16[4,4224]{1,0:T(4,128)(2,1)S(1)}, u32[]{:S(2)}, u32[]{:S(2)}) collective-permute-start(bf16[4,4224]{1,0:T(4,128)(2,1)S(1)} %shard_map.132), channel_id=1, source_target_pairs={{0,12},{4,8},{8,4},{12,0},{1,13},{5,9},{9,5},{13,1},{2,14},{6,10},... | collective-permute-start | bytes 101384 | tf_op jit(solution)/shard_map/ppermute | solution.py:358
  30.7 1.1 %collective-permute-done.10 = bf16[4,4224]{1,0:T(4,128)(2,1)S(1)} collective-permute-done((bf16[4,4224]{1,0:T(4,128)(2,1)S(1)}, bf16[4,4224]{1,0:T(4,128)(2,1)S(1)}, u32[]{:S(2)}, u32[]{:S(2)}) %collective-permute-start.10) | collective-permute-done | bytes 33824 | tf_op jit(solution)/shard_map/ppermute | solution.py:29
  31.9 1.0 %collective-permute-start.14 = (bf16[2,4,4224]{2,1,0:T(4,128)(2,1)S(1)}, bf16[2,4,4224]{2,1,0:T(4,128)(2,1)S(1)}, u32[]{:S(2)}, u32[]{:S(2)}) collective-permute-start(bf16[2,4,4224]{2,1,0:T(4,128)(2,1)S(1)} %pad_maximum_fusion.2), channel_id=1, source_target_pairs={{0,12},{4,8},{8,4},{12,0},{1,13},{5,9},{9,5},{13,1},{2,14},{6,10},... | collective-permute-start | bytes 202760 | tf_op jit(solution)/shard_map/ppermute | solution.py:358
  33.1 2.7 %collective-permute-done.14 = bf16[2,4,4224]{2,1,0:T(4,128)(2,1)S(1)} collective-permute-done((bf16[2,4,4224]{2,1,0:T(4,128)(2,1)S(1)}, bf16[2,4,4224]{2,1,0:T(4,128)(2,1)S(1)}, u32[]{:S(2)}, u32[]{:S(2)}) %collective-permute-start.14) | collective-permute-done | bytes 67616 | tf_op jit(solution)/shard_map/ppermute | solution.py:358
  36.4 1.0 %collective-permute-done.16.refs_3_ = bf16[16,4224]{1,0:T(8,128)(2,1)S(1)} collective-permute-done((bf16[16,4224]{1,0:T(8,128)(2,1)S(1)}, bf16[16,4224]{1,0:T(8,128)(2,1)S(1)}, u32[]{:S(2)}, u32[]{:S(2)}) %collective-permute-start.16) | collective-permute-done | bytes 135200 | tf_op jit(solution)/shard_map/ppermute | solution.py:358
  37.4 1.9 %shard_map.133 = (bf16[4,4,4096]{2,1,0:T(4,128)(2,1)S(1)}, bf16[4,4,4096]{2,1,0:T(4,128)(2,1)S(1)}, bf16[4,4,4096]{2,1,0:T(4,128)(2,1)S(1)}, bf16[4,4,4096]{2,1,0:T(4,128)(2,1)S(1)}, f32[4,4096]{1,0:T(4,128)S(1)}) custom-call(s32[24,128]{1,0:T(8,128)S(1)} %get-tuple-element.33.refs_0_, bf16[16,4224]{1,0:T(8,128)(2,1)S(1)} %pad_maximum_fusion.refs_1_, ...), custom_call_target="tpu_custom_call" | custom-call | flops 603979776 | bytes 9437184 | tf_op jit(solution)/shard_map/pallas_call | solution.py:433
  40.7 1.0 %collective-permute-start.20 = (bf16[4,4096]{1,0:T(4,128)(2,1)S(1)}, bf16[4,4096]{1,0:T(4,128)(2,1)S(1)}, u32[]{:S(2)}, u32[]{:S(2)}) collective-permute-start(bf16[4,4096]{1,0:T(4,128)(2,1)S(1)} %get-tuple-element.58), channel_id=1, source_target_pairs={{0,12},{4,8},{8,4},{12,0},{1,13},{5,9},{9,5},{13,1},{2,14},{6,10},... | collective-permute-start | bytes 98312 | tf_op jit(solution)/shard_map/ppermute | solution.py:358
  44.3 0.9 %collective-permute-start.21 = (bf16[4,4096]{1,0:T(4,128)(2,1)S(1)}, bf16[4,4096]{1,0:T(4,128)(2,1)S(1)}, u32[]{:S(2)}, u32[]{:S(2)}) collective-permute-start(bf16[4,4096]{1,0:T(4,128)(2,1)S(1)} %shard_map.135), channel_id=1, source_target_pairs={{0,5},{1,4},{2,7},{3,6},{4,1},{5,0},{6,3},{7,2},{8,13},{9,12},{10,... | collective-permute-start | bytes 98312 | tf_op jit(solution)/shard_map/ppermute | solution.py:29
  45.3 2.3 %collective-permute-start.23 = (bf16[4,4096]{1,0:T(4,128)(2,1)S(1)}, bf16[4,4096]{1,0:T(4,128)(2,1)S(1)}, u32[]{:S(2)}, u32[]{:S(2)}) collective-permute-start(bf16[4,4096]{1,0:T(4,128)(2,1)S(1)} %shard_map.136), channel_id=1, source_target_pairs={{0,6},{1,7},{2,4},{3,5},{4,2},{5,3},{6,0},{7,1},{8,14},{9,15},{10,... | collective-permute-start | bytes 98312 | tf_op jit(solution)/shard_map/ppermute | solution.py:29
  47.6 1.1 %collective-permute-start.25 = (bf16[4,4096]{1,0:T(4,128)(2,1)S(1)}, bf16[4,4096]{1,0:T(4,128)(2,1)S(1)}, u32[]{:S(2)}, u32[]{:S(2)}) collective-permute-start(bf16[4,4096]{1,0:T(4,128)(2,1)S(1)} %shard_map.137), channel_id=1, source_target_pairs={{0,7},{1,6},{2,5},{3,4},{4,3},{5,2},{6,1},{7,0},{8,15},{9,14},{10,... | collective-permute-start | bytes 98312 | tf_op jit(solution)/shard_map/ppermute | solution.py:29
  48.7 0.9 %collective-permute-done.23 = bf16[4,4096]{1,0:T(4,128)(2,1)S(1)} collective-permute-done((bf16[4,4096]{1,0:T(4,128)(2,1)S(1)}, bf16[4,4096]{1,0:T(4,128)(2,1)S(1)}, u32[]{:S(2)}, u32[]{:S(2)}) %collective-permute-start.23) | collective-permute-done | bytes 32800 | tf_op jit(solution)/shard_map/ppermute | solution.py:29
  49.6 3.5 %collective-permute-done.25 = bf16[4,4096]{1,0:T(4,128)(2,1)S(1)} collective-permute-done((bf16[4,4096]{1,0:T(4,128)(2,1)S(1)}, bf16[4,4096]{1,0:T(4,128)(2,1)S(1)}, u32[]{:S(2)}, u32[]{:S(2)}) %collective-permute-start.25) | collective-permute-done | bytes 32800 | tf_op jit(solution)/shard_map/ppermute | solution.py:29
  (60 shorter events, 10.2 us)
Async XLA Ops:
  1.0 4.3 %collective-permute-start.2 = (bf16[1,8832]{1,0:T(2,128)(2,1)S(1)}, bf16[1,8832]{1,0:T(2,128)(2,1)S(1)}, u32[]{:S(2)}, u32[]{:S(2)}) collective-permute-start(bf16[1,8832]{1,0:T(2,128)(2,1)S(1)} %get-tuple-element.34.refs_1_), channel_id=1, source_target_pairs={{0,12},{4,8},{8,4},{12,0},{1,13},{5,9},{9,5},{13,1},{2,14},{6,10},... | collective-permute-start | bytes 53000 | tf_op jit(solution)/shard_map/ppermute | solution.py:358
  3.5 4.0 %collective-permute-start.1 = (bf16[1,8832]{1,0:T(2,128)(2,1)S(1)}, bf16[1,8832]{1,0:T(2,128)(2,1)S(1)}, u32[]{:S(2)}, u32[]{:S(2)}) collective-permute-start(bf16[1,8832]{1,0:T(2,128)(2,1)S(1)} %get-tuple-element.34.refs_1_), channel_id=1, source_target_pairs={{0,8},{4,12},{8,0},{12,4},{1,9},{5,13},{9,1},{13,5},{2,10},{6,14},... | collective-permute-start | bytes 53000 | tf_op jit(solution)/shard_map/ppermute | solution.py:358
  4.2 3.4 %collective-permute-start = (bf16[1,8832]{1,0:T(2,128)(2,1)S(1)}, bf16[1,8832]{1,0:T(2,128)(2,1)S(1)}, u32[]{:S(2)}, u32[]{:S(2)}) collective-permute-start(bf16[1,8832]{1,0:T(2,128)(2,1)S(1)} %get-tuple-element.34.refs_1_), channel_id=1, source_target_pairs={{0,4},{4,0},{8,12},{12,8},{1,5},{5,1},{9,13},{13,9},{2,6},{6,2},{1... | collective-permute-start | bytes 53000 | tf_op jit(solution)/shard_map/ppermute | solution.py:358
  8.1 4.0 %collective-permute-start.3 = (bf16[4,1024]{1,0:T(4,128)(2,1)S(1)}, bf16[4,1024]{1,0:T(4,128)(2,1)S(1)}, u32[]{:S(2)}, u32[]{:S(2)}) collective-permute-start(bf16[4,1024]{1,0:T(4,128)(2,1)S(1)} %get-tuple-element.39), channel_id=1, source_target_pairs={{0,5},{1,4},{2,7},{3,6},{4,1},{5,0},{6,3},{7,2},{8,13},{9,12},{10,... | collective-permute-start | bytes 24584 | tf_op jit(solution)/shard_map/ppermute | solution.py:29
  9.2 4.3 %collective-permute-start.4 = (bf16[4,1024]{1,0:T(4,128)(2,1)S(1)}, bf16[4,1024]{1,0:T(4,128)(2,1)S(1)}, u32[]{:S(2)}, u32[]{:S(2)}) collective-permute-start(bf16[4,1024]{1,0:T(4,128)(2,1)S(1)} %get-tuple-element.40), channel_id=1, source_target_pairs={{0,6},{1,7},{2,4},{3,5},{4,2},{5,3},{6,0},{7,1},{8,14},{9,15},{10,... | collective-permute-start | bytes 24584 | tf_op jit(solution)/shard_map/ppermute | solution.py:29
  12.1 5.0 %collective-permute-start.5 = (bf16[4,1024]{1,0:T(4,128)(2,1)S(1)}, bf16[4,1024]{1,0:T(4,128)(2,1)S(1)}, u32[]{:S(2)}, u32[]{:S(2)}) collective-permute-start(bf16[4,1024]{1,0:T(4,128)(2,1)S(1)} %get-tuple-element.41), channel_id=1, source_target_pairs={{0,7},{1,6},{2,5},{3,4},{4,3},{5,2},{6,1},{7,0},{8,15},{9,14},{10,... | collective-permute-start | bytes 24584 | tf_op jit(solution)/shard_map/ppermute | solution.py:29
  18.2 3.8 %collective-permute-start.6 = (bf16[4,4096]{1,0:T(4,128)(2,1)S(1)}, bf16[4,4096]{1,0:T(4,128)(2,1)S(1)}, u32[]{:S(2)}, u32[]{:S(2)}) collective-permute-start(bf16[4,4096]{1,0:T(4,128)(2,1)S(1)} %get-tuple-element.43), channel_id=1, source_target_pairs={{0,5},{1,4},{2,7},{3,6},{4,1},{5,0},{6,3},{7,2},{8,13},{9,12},{10,... | collective-permute-start | bytes 98312 | tf_op jit(solution)/shard_map/ppermute | solution.py:29
  18.2 4.4 %collective-permute-start.7 = (bf16[4,4096]{1,0:T(4,128)(2,1)S(1)}, bf16[4,4096]{1,0:T(4,128)(2,1)S(1)}, u32[]{:S(2)}, u32[]{:S(2)}) collective-permute-start(bf16[4,4096]{1,0:T(4,128)(2,1)S(1)} %get-tuple-element.44), channel_id=1, source_target_pairs={{0,6},{1,7},{2,4},{3,5},{4,2},{5,3},{6,0},{7,1},{8,14},{9,15},{10,... | collective-permute-start | bytes 98312 | tf_op jit(solution)/shard_map/ppermute | solution.py:29
  18.7 5.6 %collective-permute-start.8 = (bf16[4,4096]{1,0:T(4,128)(2,1)S(1)}, bf16[4,4096]{1,0:T(4,128)(2,1)S(1)}, u32[]{:S(2)}, u32[]{:S(2)}) collective-permute-start(bf16[4,4096]{1,0:T(4,128)(2,1)S(1)} %get-tuple-element.45), channel_id=1, source_target_pairs={{0,7},{1,6},{2,5},{3,4},{4,3},{5,2},{6,1},{7,0},{8,15},{9,14},{10,... | collective-permute-start | bytes 98312 | tf_op jit(solution)/shard_map/ppermute | solution.py:29
  24.4 5.2 %collective-permute-start.11 = (bf16[4,4224]{1,0:T(4,128)(2,1)S(1)}, bf16[4,4224]{1,0:T(4,128)(2,1)S(1)}, u32[]{:S(2)}, u32[]{:S(2)}) collective-permute-start(bf16[4,4224]{1,0:T(4,128)(2,1)S(1)} %get-tuple-element.48), channel_id=1, source_target_pairs={{0,7},{1,6},{2,5},{3,4},{4,3},{5,2},{6,1},{7,0},{8,15},{9,14},{10,... | collective-permute-start | bytes 101384 | tf_op jit(solution)/shard_map/ppermute | solution.py:29
  27.5 4.3 %collective-permute-start.10 = (bf16[4,4224]{1,0:T(4,128)(2,1)S(1)}, bf16[4,4224]{1,0:T(4,128)(2,1)S(1)}, u32[]{:S(2)}, u32[]{:S(2)}) collective-permute-start(bf16[4,4224]{1,0:T(4,128)(2,1)S(1)} %get-tuple-element.48), channel_id=1, source_target_pairs={{0,6},{1,7},{2,4},{3,5},{4,2},{5,3},{6,0},{7,1},{8,14},{9,15},{10,... | collective-permute-start | bytes 101384 | tf_op jit(solution)/shard_map/ppermute | solution.py:29
  27.5 4.3 %collective-permute-start.9 = (bf16[4,4224]{1,0:T(4,128)(2,1)S(1)}, bf16[4,4224]{1,0:T(4,128)(2,1)S(1)}, u32[]{:S(2)}, u32[]{:S(2)}) collective-permute-start(bf16[4,4224]{1,0:T(4,128)(2,1)S(1)} %get-tuple-element.48), channel_id=1, source_target_pairs={{0,5},{1,4},{2,7},{3,6},{4,1},{5,0},{6,3},{7,2},{8,13},{9,12},{10,... | collective-permute-start | bytes 101384 | tf_op jit(solution)/shard_map/ppermute | solution.py:29
  28.6 7.3 %collective-permute-start.13 = (bf16[4,4224]{1,0:T(4,128)(2,1)S(1)}, bf16[4,4224]{1,0:T(4,128)(2,1)S(1)}, u32[]{:S(2)}, u32[]{:S(2)}) collective-permute-start(bf16[4,4224]{1,0:T(4,128)(2,1)S(1)} %get-tuple-element.48), channel_id=1, source_target_pairs={{0,12},{4,8},{8,4},{12,0},{1,13},{5,9},{9,5},{13,1},{2,14},{6,10},... | collective-permute-start | bytes 101384 | tf_op jit(solution)/shard_map/ppermute | solution.py:358
  29.6 6.2 %collective-permute-start.15 = (bf16[4,4224]{1,0:T(4,128)(2,1)S(1)}, bf16[4,4224]{1,0:T(4,128)(2,1)S(1)}, u32[]{:S(2)}, u32[]{:S(2)}) collective-permute-start(bf16[4,4224]{1,0:T(4,128)(2,1)S(1)} %shard_map.132), channel_id=1, source_target_pairs={{0,12},{4,8},{8,4},{12,0},{1,13},{5,9},{9,5},{13,1},{2,14},{6,10},... | collective-permute-start | bytes 101384 | tf_op jit(solution)/shard_map/ppermute | solution.py:358
  31.9 4.0 %collective-permute-start.14 = (bf16[2,4,4224]{2,1,0:T(4,128)(2,1)S(1)}, bf16[2,4,4224]{2,1,0:T(4,128)(2,1)S(1)}, u32[]{:S(2)}, u32[]{:S(2)}) collective-permute-start(bf16[2,4,4224]{2,1,0:T(4,128)(2,1)S(1)} %pad_maximum_fusion.2), channel_id=1, source_target_pairs={{0,12},{4,8},{8,4},{12,0},{1,13},{5,9},{9,5},{13,1},{2,14},{6,10},... | collective-permute-start | bytes 202760 | tf_op jit(solution)/shard_map/ppermute | solution.py:358
  32.9 3.5 %collective-permute-start.12 = (bf16[16,4224]{1,0:T(8,128)(2,1)S(1)}, bf16[16,4224]{1,0:T(8,128)(2,1)S(1)}, u32[]{:S(2)}, u32[]{:S(2)}) collective-permute-start(bf16[16,4224]{1,0:T(8,128)(2,1)S(1)} %pad_maximum_fusion.refs_1_), channel_id=1, source_target_pairs={{0,4},{4,0},{8,12},{12,8},{1,5},{5,1},{9,13},{13,9},{2,6},{6,2},{1... | collective-permute-start | bytes 405512 | tf_op jit(solution)/shard_map/ppermute | solution.py:358
  39.7 4.6 %collective-permute-start.19 = (bf16[4,4,4096]{2,1,0:T(4,128)(2,1)S(1)}, bf16[4,4,4096]{2,1,0:T(4,128)(2,1)S(1)}, u32[]{:S(2)}, u32[]{:S(2)}) collective-permute-start(bf16[4,4,4096]{2,1,0:T(4,128)(2,1)S(1)} %get-tuple-element.54), channel_id=1, source_target_pairs={{0,4},{4,0},{8,12},{12,8},{1,5},{5,1},{9,13},{13,9},{2,6},{6,2},{1... | collective-permute-start | bytes 393224 | tf_op jit(solution)/shard_map/ppermute | solution.py:358
  40.7 3.6 %collective-permute-start.20 = (bf16[4,4096]{1,0:T(4,128)(2,1)S(1)}, bf16[4,4096]{1,0:T(4,128)(2,1)S(1)}, u32[]{:S(2)}, u32[]{:S(2)}) collective-permute-start(bf16[4,4096]{1,0:T(4,128)(2,1)S(1)} %get-tuple-element.58), channel_id=1, source_target_pairs={{0,12},{4,8},{8,4},{12,0},{1,13},{5,9},{9,5},{13,1},{2,14},{6,10},... | collective-permute-start | bytes 98312 | tf_op jit(solution)/shard_map/ppermute | solution.py:358
  41.7 3.5 %collective-permute-start.22 = (bf16[4,4096]{1,0:T(4,128)(2,1)S(1)}, bf16[4,4096]{1,0:T(4,128)(2,1)S(1)}, u32[]{:S(2)}, u32[]{:S(2)}) collective-permute-start(bf16[4,4096]{1,0:T(4,128)(2,1)S(1)} %get-tuple-element.57), channel_id=1, source_target_pairs={{0,12},{4,8},{8,4},{12,0},{1,13},{5,9},{9,5},{13,1},{2,14},{6,10},... | collective-permute-start | bytes 98312 | tf_op jit(solution)/shard_map/ppermute | solution.py:358
  42.6 5.0 %collective-permute-start.24 = (bf16[4,4096]{1,0:T(4,128)(2,1)S(1)}, bf16[4,4096]{1,0:T(4,128)(2,1)S(1)}, u32[]{:S(2)}, u32[]{:S(2)}) collective-permute-start(bf16[4,4096]{1,0:T(4,128)(2,1)S(1)} %get-tuple-element.56), channel_id=1, source_target_pairs={{0,12},{4,8},{8,4},{12,0},{1,13},{5,9},{9,5},{13,1},{2,14},{6,10},... | collective-permute-start | bytes 98312 | tf_op jit(solution)/shard_map/ppermute | solution.py:358
  43.5 5.2 %collective-permute-start.18 = (bf16[4,4096]{1,0:T(4,128)(2,1)S(1)}, bf16[4,4096]{1,0:T(4,128)(2,1)S(1)}, u32[]{:S(2)}, u32[]{:S(2)}) collective-permute-start(bf16[4,4096]{1,0:T(4,128)(2,1)S(1)} %get-tuple-element.55), channel_id=1, source_target_pairs={{0,12},{4,8},{8,4},{12,0},{1,13},{5,9},{9,5},{13,1},{2,14},{6,10},... | collective-permute-start | bytes 98312 | tf_op jit(solution)/shard_map/ppermute | solution.py:358
  44.3 4.4 %collective-permute-start.21 = (bf16[4,4096]{1,0:T(4,128)(2,1)S(1)}, bf16[4,4096]{1,0:T(4,128)(2,1)S(1)}, u32[]{:S(2)}, u32[]{:S(2)}) collective-permute-start(bf16[4,4096]{1,0:T(4,128)(2,1)S(1)} %shard_map.135), channel_id=1, source_target_pairs={{0,5},{1,4},{2,7},{3,6},{4,1},{5,0},{6,3},{7,2},{8,13},{9,12},{10,... | collective-permute-start | bytes 98312 | tf_op jit(solution)/shard_map/ppermute | solution.py:29
  45.3 4.3 %collective-permute-start.23 = (bf16[4,4096]{1,0:T(4,128)(2,1)S(1)}, bf16[4,4096]{1,0:T(4,128)(2,1)S(1)}, u32[]{:S(2)}, u32[]{:S(2)}) collective-permute-start(bf16[4,4096]{1,0:T(4,128)(2,1)S(1)} %shard_map.136), channel_id=1, source_target_pairs={{0,6},{1,7},{2,4},{3,5},{4,2},{5,3},{6,0},{7,1},{8,14},{9,15},{10,... | collective-permute-start | bytes 98312 | tf_op jit(solution)/shard_map/ppermute | solution.py:29
  47.6 5.5 %collective-permute-start.25 = (bf16[4,4096]{1,0:T(4,128)(2,1)S(1)}, bf16[4,4096]{1,0:T(4,128)(2,1)S(1)}, u32[]{:S(2)}, u32[]{:S(2)}) collective-permute-start(bf16[4,4096]{1,0:T(4,128)(2,1)S(1)} %shard_map.137), channel_id=1, source_target_pairs={{0,7},{1,6},{2,5},{3,4},{4,3},{5,2},{6,1},{7,0},{8,15},{9,14},{10,... | collective-permute-start | bytes 98312 | tf_op jit(solution)/shard_map/ppermute | solution.py:29
  (9 other events, 72.6 us)

commit v8 on v7

--- a/solution.py
+++ b/solution.py
@@ -255,11 +255,21 @@
     pay_ref[:, model:] = ext.astype(BF16)
 
 
-def add_kernel(at, block_ref, *refs):
-    total = block_ref[...].astype(F32)
+def add_kernel(at, block, block_ref, *refs):
+    total = block_ref[block].astype(F32)
     for ref in refs[:-1]:
         total = total + ref[at].astype(F32)
     refs[-1][...] = total.astype(refs[-1].dtype)
+
+
+def middle_kernel(*refs):
+    blocks, others, own = refs[:-2], refs[-2], refs[-1]
+    for to, at in ((others, 1), (own, 0)):
+        for i in range(to.shape[0]):
+            total = blocks[0][at + i].astype(F32)
+            for block in blocks[1:]:
+                total = total + block[at + i].astype(F32)
+            to[i] = total.astype(to.dtype)
 
 
 def hand_kernel(source, to):
@@ -270,8 +280,8 @@
     to_ref = refs[0]
     pieces = refs[1 : 1 + n_dp]
     gate_ref, up_ref, down_ref, gain_ref, hid_ref = refs[1 + n_dp : 6 + n_dp]
-    outs = refs[6 + n_dp : 6 + 2 * n_dp]
-    real_ref, lhs, act_scr, new_scr = refs[6 + 2 * n_dp :]
+    bodies, heads = refs[6 + n_dp : 6 + 2 * n_dp], refs[6 + 2 * n_dp : 6 + 3 * n_dp]
+    real_ref, lhs, act_scr, new_scr = refs[6 + 3 * n_dp :]
     dp = lax.axis_index("dp")
     model = gain_ref.shape[1]
     rows = n_ex * tokens
@@ -311,7 +321,11 @@
         for r in range(n_dp):
             for s in range(n_ex):
                 first_row = (r * n_ex + s) * tokens
-                outs[r][s, :, at : at + chunk] = out[first_row : first_row + tokens, :].astype(BF16)
+                block = out[first_row : first_row + tokens, :].astype(BF16)
+                if s < n_ex - 1:
+                    bodies[r][s, :, at : at + chunk] = block
+                else:
+                    heads[r][0, :, at : at + chunk] = block
 
 
 def per_device(
@@ -432,7 +446,9 @@
     weights_bytes = (w_gate.size + w_up.size + w_down.size) * 2
     done = call(
         functools.partial(expert_kernel, n_dp, n_ex, tokens),
-        [shape((n_ex, tokens, model), BF16)] * n_dp + [shape((tokens, model), F32)],
+        [shape((n_ex - 1, tokens, model), BF16)] * n_dp
+        + [shape((1, tokens, model), BF16)] * n_dp
+        + [shape((tokens, model), F32)],
         [spec()] * (n_dp + 6),
         scratch=[
             pltpu.VMEM((all_rows, model), BF16),
@@ -443,11 +459,11 @@
         flops=6 * all_rows * model * hidden_units,
         moved=weights_bytes,
     )(targets, *[pieces[r] for r in range(n_dp)], w_gate, w_up, w_down, norm_gain[None], hidden)
-    terms = {r: [done[r]] for r in range(n_dp)}
+    terms = {r: [(done[r], done[n_dp + r])] for r in range(n_dp)}
     reach = {0: 0}
     for i, turn in enumerate(turns):
         reach |= {r ^ turn: mark | 1 << i for r, mark in reach.items()}
-    real = done[n_dp]
+    real = done[2 * n_dp]
 
     def added(arrays):
         return functools.reduce(jnp.add, [array.astype(F32) for array in arrays])
@@ -455,21 +471,32 @@
     for i, turn in enumerate(turns[:-1]):
         far = {r: r ^ turn for r in terms if reach[r] >> i & 1}
         for r in sorted(far, key=lambda r: -reach[r]):
-            whole = terms.pop(r)
-            whole = whole[0] if len(whole) == 1 else added(whole).astype(BF16)
-            terms[far[r]].append(over_dp(whole, turn))
-
-    def across(at):
-        return over_dp(added([t[at] for t in terms[top]]).astype(BF16), top)
-
-    arrived = [across(s) for s in range(n_ex)]
+            body, head = zip(*terms.pop(r))
+            got = []
+            for arrays in (head, body):
+                whole = arrays[0] if len(arrays) == 1 else added(arrays).astype(BF16)
+                got.append(over_dp(whole, turn))
+            terms[far[r]].append((got[1], got[0]))
+
+    body, head = zip(*terms[top])
+    arrived = {last: (over_dp(added(head).astype(BF16), top), 0)}
+    summed = call(
+        middle_kernel,
+        [shape((count, tokens, model), BF16) for count in (last - 1, 1)],
+        [spec()] * len(body),
+        limit=1 << 20,
+    )(*body)
+    for start, stop, blocks in ((1, last, summed[0]), (0, 1, summed[1])):
+        got = over_dp(blocks, top)
+        arrived |= {s: (got, s - start) for s in range(start, stop)}
+    body, head = zip(*terms[0])
     mixed = [
         call(
-            functools.partial(add_kernel, s),
+            functools.partial(add_kernel, 0 if s == last else s, arrived[s][1]),
             shape((tokens, model), BF16 if s else F32),
-            [spec()] * (len(terms[0]) + 1),
+            [spec()] * (len(body) + 1),
             limit=1 << 20,
-        )(arrived[s], *terms[0])
+        )(arrived[s][0], *(head if s == last else body))
         for s in range(n_ex)
     ]
     back = crossed_exchange(mixed, n_dp, n_ex)

time: 53.9 us -> 54.2 us (level)
  waiting for transfers between devices: 20.1 us -> 20.7 us
    ppermute x14 -> x15, waiting for transfers between devices: 7.13 us -> 10 us  [over_dp(): return lax.ppermute(array, 'dp', [(j, j ^ turn) for j in range(n_dp)])]
    ppermute x12, waiting for transfers between devices: 12.9 us -> 10.7 us  [crossed_exchange(): moved[step] = lax.ppermute(blocks[step], ('dp', 'expert'), pairs)]
    ppermute x14 -> x15, starting transfers between devices: 10.7 us -> 10.6 us  [over_dp(): return lax.ppermute(array, 'dp', [(j, j ^ turn) for j in range(n_dp)])]
    pallas_call x5 -> x6, Pallas kernels: 1.94 us -> 2 us  [the longest x1 1.86 us: per_device(): call(functools.partial(expert_kernel, n_dp, n_ex, tokens), [shape((n_ex -...]
  transfers between devices with their start and end apart: 26 -> 27, of which waited for: 13 -> 15; matrix products, arithmetic and copies ran while one was open for 1% -> 0% of each run, Pallas kernels for 2% -> 2%
where the time goes in v8:
time: 54.2 us; the launch traced here: 54 us
  starting transfers between devices  26.6 us (49%)
  waiting for transfers between devices  20.7 us (38%)
  Pallas kernels  5.66 us (10%)
  other arithmetic  0.9 us (2%)
    ppermute x12, starting transfers between devices, crossed_exchange(): moved[step] = lax.ppermute(blocks[step], ('dp', 'expert'), pairs)  16 us
    ppermute x12, waiting for transfers between devices, crossed_exchange(): moved[step] = lax.ppermute(blocks[step], ('dp', 'expert'), pairs)  10.7 us
    ppermute x15, starting transfers between devices, over_dp(): return lax.ppermute(array, 'dp', [(j, j ^ turn) for j in range(n_dp)])  10.6 us
    ppermute x15, waiting for transfers between devices, over_dp(): return lax.ppermute(array, 'dp', [(j, j ^ turn) for j in range(n_dp)])  10 us
    pallas_call x1, Pallas kernels, per_device(): call(functools.partial(expert_kernel, n_dp, n_ex, tokens), [shape((n_ex -...  1.86 us
    pallas_call x1, Pallas kernels, per_device(): call(functools.partial(project_kernel, n_ex), [shape((tokens, model), F32...  1.21 us
  transfers between devices with their start and end apart: 27, of which 15 were waited for; matrix products, arithmetic and copies ran while one was open for 0% of the time, Pallas kernels for 2%

profile of v8, /device:TPU:0, one launch (start us, length us, event | category | flops | bytes accessed | tf_op | source)
XLA Modules:
  0.0 54.0 jit_solution(10640461844090346456)
XLA Ops:
  0.0 1.0 %shard_map.127 = (bf16[1,8832]{1,0:T(2,128)(2,1)S(1)}, bf16[4,4096]{1,0:T(4,128)(2,1)S(1)}, bf16[4,512]{1,0:T(4,128)(2,1)S(1)}, bf16[4,4096]{1,0:T(4,128)(2,1)S(...) custom-call(bf16[4,4096]{1,0:T(4,128)(2,1)} %q_hbm.1, bf16[4,512]{1,0:T(4,128)(2,1)} %fresh_hbm.1, ...), custom_call_target="tpu_custom_call" | custom-call | flops 10000000000 | bytes 65536 | tf_op jit(solution)/shard_map/pallas_call | solution.py:347
  1.0 2.5 %collective-permute-start.2 = (bf16[1,8832]{1,0:T(2,128)(2,1)S(1)}, bf16[1,8832]{1,0:T(2,128)(2,1)S(1)}, u32[]{:S(2)}, u32[]{:S(2)}) collective-permute-start(bf16[1,8832]{1,0:T(2,128)(2,1)S(1)} %get-tuple-element.40.refs_1_), channel_id=1, source_target_pairs={{0,12},{4,8},{8,4},{12,0},{1,13},{5,9},{9,5},{13,1},{2,14},{6,10},... | collective-permute-start | bytes 53000 | tf_op jit(solution)/shard_map/ppermute | solution.py:372
  5.4 2.2 %collective-permute-done.1.refs_3_ = bf16[1,8832]{1,0:T(2,128)(2,1)S(1)} collective-permute-done((bf16[1,8832]{1,0:T(2,128)(2,1)S(1)}, bf16[1,8832]{1,0:T(2,128)(2,1)S(1)}, u32[]{:S(2)}, u32[]{:S(2)}) %collective-permute-start.1) | collective-permute-done | bytes 17696 | tf_op jit(solution)/shard_map/ppermute | solution.py:372
  8.1 1.1 %collective-permute-start.3 = (bf16[4,1024]{1,0:T(4,128)(2,1)S(1)}, bf16[4,1024]{1,0:T(4,128)(2,1)S(1)}, u32[]{:S(2)}, u32[]{:S(2)}) collective-permute-start(bf16[4,1024]{1,0:T(4,128)(2,1)S(1)} %get-tuple-element.45), channel_id=1, source_target_pairs={{0,5},{1,4},{2,7},{3,6},{4,1},{5,0},{6,3},{7,2},{8,13},{9,12},{10,... | collective-permute-start | bytes 24584 | tf_op jit(solution)/shard_map/ppermute | solution.py:29
  9.2 2.9 %collective-permute-start.4 = (bf16[4,1024]{1,0:T(4,128)(2,1)S(1)}, bf16[4,1024]{1,0:T(4,128)(2,1)S(1)}, u32[]{:S(2)}, u32[]{:S(2)}) collective-permute-start(bf16[4,1024]{1,0:T(4,128)(2,1)S(1)} %get-tuple-element.46), channel_id=1, source_target_pairs={{0,6},{1,7},{2,4},{3,5},{4,2},{5,3},{6,0},{7,1},{8,14},{9,15},{10,... | collective-permute-start | bytes 24584 | tf_op jit(solution)/shard_map/ppermute | solution.py:29
  12.1 1.4 %collective-permute-done.4.refs_2_ = bf16[4,1024]{1,0:T(4,128)(2,1)S(1)} collective-permute-done((bf16[4,1024]{1,0:T(4,128)(2,1)S(1)}, bf16[4,1024]{1,0:T(4,128)(2,1)S(1)}, u32[]{:S(2)}, u32[]{:S(2)}) %collective-permute-start.4) | collective-permute-done | bytes 8224 | tf_op jit(solution)/shard_map/ppermute | solution.py:29
  13.4 3.6 %collective-permute-done.5.refs_3_ = bf16[4,1024]{1,0:T(4,128)(2,1)S(1)} collective-permute-done((bf16[4,1024]{1,0:T(4,128)(2,1)S(1)}, bf16[4,1024]{1,0:T(4,128)(2,1)S(1)}, u32[]{:S(2)}, u32[]{:S(2)}) %collective-permute-start.5) | collective-permute-done | bytes 8224 | tf_op jit(solution)/shard_map/ppermute | solution.py:29
  17.0 1.2 %shard_map.130 = (f32[4,4096]{1,0:T(4,128)S(1)}, bf16[4,4096]{1,0:T(4,128)(2,1)S(1)}, bf16[4,4096]{1,0:T(4,128)(2,1)S(1)}, bf16[4,4096]{1,0:T(4,128)(2,1)S(1)}) custom-call(bf16[4,1024]{1,0:T(4,128)(2,1)S(1)} %get-tuple-element.44.refs_0_, bf16[4,1024]{1,0:T(4,128)(2,1)S(1)} %collective-permute-done.3.refs_1_, ...), custom_call_target="tpu_custom_call" | custom-call | flops 134217728 | bytes 8388608 | tf_op jit(solution)/shard_map/pallas_call | solution.py:410
  18.7 3.4 %collective-permute-start.8 = (bf16[4,4096]{1,0:T(4,128)(2,1)S(1)}, bf16[4,4096]{1,0:T(4,128)(2,1)S(1)}, u32[]{:S(2)}, u32[]{:S(2)}) collective-permute-start(bf16[4,4096]{1,0:T(4,128)(2,1)S(1)} %get-tuple-element.51), channel_id=1, source_target_pairs={{0,7},{1,6},{2,5},{3,4},{4,3},{5,2},{6,1},{7,0},{8,15},{9,14},{10,... | collective-permute-start | bytes 98312 | tf_op jit(solution)/shard_map/ppermute | solution.py:29
  22.6 1.6 %collective-permute-done.8.refs_3_ = bf16[4,4096]{1,0:T(4,128)(2,1)S(1)} collective-permute-done((bf16[4,4096]{1,0:T(4,128)(2,1)S(1)}, bf16[4,4096]{1,0:T(4,128)(2,1)S(1)}, u32[]{:S(2)}, u32[]{:S(2)}) %collective-permute-start.8) | collective-permute-done | bytes 32800 | tf_op jit(solution)/shard_map/ppermute | solution.py:29
  24.4 3.1 %collective-permute-start.11 = (bf16[4,4224]{1,0:T(4,128)(2,1)S(1)}, bf16[4,4224]{1,0:T(4,128)(2,1)S(1)}, u32[]{:S(2)}, u32[]{:S(2)}) collective-permute-start(bf16[4,4224]{1,0:T(4,128)(2,1)S(1)} %get-tuple-element.54), channel_id=1, source_target_pairs={{0,7},{1,6},{2,5},{3,4},{4,3},{5,2},{6,1},{7,0},{8,15},{9,14},{10,... | collective-permute-start | bytes 101384 | tf_op jit(solution)/shard_map/ppermute | solution.py:29
  27.5 1.1 %collective-permute-start.9 = (bf16[4,4224]{1,0:T(4,128)(2,1)S(1)}, bf16[4,4224]{1,0:T(4,128)(2,1)S(1)}, u32[]{:S(2)}, u32[]{:S(2)}) collective-permute-start(bf16[4,4224]{1,0:T(4,128)(2,1)S(1)} %get-tuple-element.54), channel_id=1, source_target_pairs={{0,5},{1,4},{2,7},{3,6},{4,1},{5,0},{6,3},{7,2},{8,13},{9,12},{10,... | collective-permute-start | bytes 101384 | tf_op jit(solution)/shard_map/ppermute | solution.py:29
  29.6 1.1 %collective-permute-start.15 = (bf16[4,4224]{1,0:T(4,128)(2,1)S(1)}, bf16[4,4224]{1,0:T(4,128)(2,1)S(1)}, u32[]{:S(2)}, u32[]{:S(2)}) collective-permute-start(bf16[4,4224]{1,0:T(4,128)(2,1)S(1)} %shard_map.132), channel_id=1, source_target_pairs={{0,12},{4,8},{8,4},{12,0},{1,13},{5,9},{9,5},{13,1},{2,14},{6,10},... | collective-permute-start | bytes 101384 | tf_op jit(solution)/shard_map/ppermute | solution.py:372
  30.7 1.1 %collective-permute-done.10 = bf16[4,4224]{1,0:T(4,128)(2,1)S(1)} collective-permute-done((bf16[4,4224]{1,0:T(4,128)(2,1)S(1)}, bf16[4,4224]{1,0:T(4,128)(2,1)S(1)}, u32[]{:S(2)}, u32[]{:S(2)}) %collective-permute-start.10) | collective-permute-done | bytes 33824 | tf_op jit(solution)/shard_map/ppermute | solution.py:29
  33.1 2.7 %collective-permute-done.14 = bf16[2,4,4224]{2,1,0:T(4,128)(2,1)S(1)} collective-permute-done((bf16[2,4,4224]{2,1,0:T(4,128)(2,1)S(1)}, bf16[2,4,4224]{2,1,0:T(4,128)(2,1)S(1)}, u32[]{:S(2)}, u32[]{:S(2)}) %collective-permute-start.14) | collective-permute-done | bytes 67616 | tf_op jit(solution)/shard_map/ppermute | solution.py:372
  36.4 1.0 %collective-permute-done.16.refs_3_ = bf16[16,4224]{1,0:T(8,128)(2,1)S(1)} collective-permute-done((bf16[16,4224]{1,0:T(8,128)(2,1)S(1)}, bf16[16,4224]{1,0:T(8,128)(2,1)S(1)}, u32[]{:S(2)}, u32[]{:S(2)}) %collective-permute-start.16) | collective-permute-done | bytes 135200 | tf_op jit(solution)/shard_map/ppermute | solution.py:372
  37.4 1.9 %shard_map.133 = (bf16[3,4,4096]{2,1,0:T(4,128)(2,1)S(1)}, bf16[3,4,4096]{2,1,0:T(4,128)(2,1)S(1)}, bf16[3,4,4096]{2,1,0:T(4,128)(2,1)S(1)}, bf16[3,4,4096]{2,1,...) custom-call(s32[24,128]{1,0:T(8,128)S(1)} %get-tuple-element.39.refs, ...), custom_call_target="tpu_custom_call" | custom-call | flops 603979776 | bytes 9437184 | tf_op jit(solution)/shard_map/pallas_call | solution.py:447
  40.7 1.0 %collective-permute-start.20 = (bf16[2,4,4096]{2,1,0:T(4,128)(2,1)S(1)}, bf16[2,4,4096]{2,1,0:T(4,128)(2,1)S(1)}, u32[]{:S(2)}, u32[]{:S(2)}) collective-permute-start(bf16[2,4,4096]{2,1,0:T(4,128)(2,1)S(1)} %get-tuple-element.62), channel_id=1, source_target_pairs={{0,12},{4,8},{8,4},{12,0},{1,13},{5,9},{9,5},{13,1},{2,14},{6,10},... | collective-permute-start | bytes 196616 | tf_op jit(solution)/shard_map/ppermute | solution.py:372
  42.6 2.8 %collective-permute-done.24.block_ref = bf16[1,4,4096]{2,1,0:T(4,128)(2,1)S(1)} collective-permute-done((bf16[1,4,4096]{2,1,0:T(4,128)(2,1)S(1)}, bf16[1,4,4096]{2,1,0:T(4,128)(2,1)S(1)}, u32[]{:S(2)}, u32[]{:S(2)}) %collective-permute-start.24) | collective-permute-done | bytes 32800 | tf_op jit(solution)/shard_map/ppermute | solution.py:372
  45.5 2.4 %collective-permute-start.26 = (bf16[4,4096]{1,0:T(4,128)(2,1)S(1)}, bf16[4,4096]{1,0:T(4,128)(2,1)S(1)}, u32[]{:S(2)}, u32[]{:S(2)}) collective-permute-start(bf16[4,4096]{1,0:T(4,128)(2,1)S(1)} %shard_map.138), channel_id=1, source_target_pairs={{0,7},{1,6},{2,5},{3,4},{4,3},{5,2},{6,1},{7,0},{8,15},{9,14},{10,... | collective-permute-start | bytes 98312 | tf_op jit(solution)/shard_map/ppermute | solution.py:29
  47.9 1.0 %collective-permute-start.18 = (bf16[1,4,4096]{2,1,0:T(4,128)(2,1)S(1)}, bf16[1,4,4096]{2,1,0:T(4,128)(2,1)S(1)}, u32[]{:S(2)}, u32[]{:S(2)}) collective-permute-start(bf16[1,4,4096]{2,1,0:T(4,128)(2,1)S(1)} %get-tuple-element.59), channel_id=1, source_target_pairs={{0,12},{4,8},{8,4},{12,0},{1,13},{5,9},{9,5},{13,1},{2,14},{6,10},... | collective-permute-start | bytes 98312 | tf_op jit(solution)/shard_map/ppermute | solution.py:372
  49.0 1.6 %collective-permute-start.22 = (bf16[4,4096]{1,0:T(4,128)(2,1)S(1)}, bf16[4,4096]{1,0:T(4,128)(2,1)S(1)}, u32[]{:S(2)}, u32[]{:S(2)}) collective-permute-start(bf16[4,4096]{1,0:T(4,128)(2,1)S(1)} %shard_map.137), channel_id=1, source_target_pairs={{0,6},{1,7},{2,4},{3,5},{4,2},{5,3},{6,0},{7,1},{8,14},{9,15},{10,... | collective-permute-start | bytes 98312 | tf_op jit(solution)/shard_map/ppermute | solution.py:29
  51.2 1.1 %collective-permute-done.21 = bf16[4,4096]{1,0:T(4,128)(2,1)S(1)} collective-permute-done((bf16[4,4096]{1,0:T(4,128)(2,1)S(1)}, bf16[4,4096]{1,0:T(4,128)(2,1)S(1)}, u32[]{:S(2)}, u32[]{:S(2)}) %collective-permute-start.21) | collective-permute-done | bytes 32800 | tf_op jit(solution)/shard_map/ppermute | solution.py:29
  52.4 1.0 %collective-permute-done.22 = bf16[4,4096]{1,0:T(4,128)(2,1)S(1)} collective-permute-done((bf16[4,4096]{1,0:T(4,128)(2,1)S(1)}, bf16[4,4096]{1,0:T(4,128)(2,1)S(1)}, u32[]{:S(2)}, u32[]{:S(2)}) %collective-permute-start.22) | collective-permute-done | bytes 32800 | tf_op jit(solution)/shard_map/ppermute | solution.py:29
  (63 shorter events, 10.1 us)
Async XLA Ops:
  1.0 4.3 %collective-permute-start.2 = (bf16[1,8832]{1,0:T(2,128)(2,1)S(1)}, bf16[1,8832]{1,0:T(2,128)(2,1)S(1)}, u32[]{:S(2)}, u32[]{:S(2)}) collective-permute-start(bf16[1,8832]{1,0:T(2,128)(2,1)S(1)} %get-tuple-element.40.refs_1_), channel_id=1, source_target_pairs={{0,12},{4,8},{8,4},{12,0},{1,13},{5,9},{9,5},{13,1},{2,14},{6,10},... | collective-permute-start | bytes 53000 | tf_op jit(solution)/shard_map/ppermute | solution.py:372
  3.5 4.0 %collective-permute-start.1 = (bf16[1,8832]{1,0:T(2,128)(2,1)S(1)}, bf16[1,8832]{1,0:T(2,128)(2,1)S(1)}, u32[]{:S(2)}, u32[]{:S(2)}) collective-permute-start(bf16[1,8832]{1,0:T(2,128)(2,1)S(1)} %get-tuple-element.40.refs_1_), channel_id=1, source_target_pairs={{0,8},{4,12},{8,0},{12,4},{1,9},{5,13},{9,1},{13,5},{2,10},{6,14},... | collective-permute-start | bytes 53000 | tf_op jit(solution)/shard_map/ppermute | solution.py:372
  4.2 3.4 %collective-permute-start = (bf16[1,8832]{1,0:T(2,128)(2,1)S(1)}, bf16[1,8832]{1,0:T(2,128)(2,1)S(1)}, u32[]{:S(2)}, u32[]{:S(2)}) collective-permute-start(bf16[1,8832]{1,0:T(2,128)(2,1)S(1)} %get-tuple-element.40.refs_1_), channel_id=1, source_target_pairs={{0,4},{4,0},{8,12},{12,8},{1,5},{5,1},{9,13},{13,9},{2,6},{6,2},{1... | collective-permute-start | bytes 53000 | tf_op jit(solution)/shard_map/ppermute | solution.py:372
  8.1 4.0 %collective-permute-start.3 = (bf16[4,1024]{1,0:T(4,128)(2,1)S(1)}, bf16[4,1024]{1,0:T(4,128)(2,1)S(1)}, u32[]{:S(2)}, u32[]{:S(2)}) collective-permute-start(bf16[4,1024]{1,0:T(4,128)(2,1)S(1)} %get-tuple-element.45), channel_id=1, source_target_pairs={{0,5},{1,4},{2,7},{3,6},{4,1},{5,0},{6,3},{7,2},{8,13},{9,12},{10,... | collective-permute-start | bytes 24584 | tf_op jit(solution)/shard_map/ppermute | solution.py:29
  9.2 4.3 %collective-permute-start.4 = (bf16[4,1024]{1,0:T(4,128)(2,1)S(1)}, bf16[4,1024]{1,0:T(4,128)(2,1)S(1)}, u32[]{:S(2)}, u32[]{:S(2)}) collective-permute-start(bf16[4,1024]{1,0:T(4,128)(2,1)S(1)} %get-tuple-element.46), channel_id=1, source_target_pairs={{0,6},{1,7},{2,4},{3,5},{4,2},{5,3},{6,0},{7,1},{8,14},{9,15},{10,... | collective-permute-start | bytes 24584 | tf_op jit(solution)/shard_map/ppermute | solution.py:29
  12.1 5.0 %collective-permute-start.5 = (bf16[4,1024]{1,0:T(4,128)(2,1)S(1)}, bf16[4,1024]{1,0:T(4,128)(2,1)S(1)}, u32[]{:S(2)}, u32[]{:S(2)}) collective-permute-start(bf16[4,1024]{1,0:T(4,128)(2,1)S(1)} %get-tuple-element.47), channel_id=1, source_target_pairs={{0,7},{1,6},{2,5},{3,4},{4,3},{5,2},{6,1},{7,0},{8,15},{9,14},{10,... | collective-permute-start | bytes 24584 | tf_op jit(solution)/shard_map/ppermute | solution.py:29
  18.2 3.8 %collective-permute-start.6 = (bf16[4,4096]{1,0:T(4,128)(2,1)S(1)}, bf16[4,4096]{1,0:T(4,128)(2,1)S(1)}, u32[]{:S(2)}, u32[]{:S(2)}) collective-permute-start(bf16[4,4096]{1,0:T(4,128)(2,1)S(1)} %get-tuple-element.49), channel_id=1, source_target_pairs={{0,5},{1,4},{2,7},{3,6},{4,1},{5,0},{6,3},{7,2},{8,13},{9,12},{10,... | collective-permute-start | bytes 98312 | tf_op jit(solution)/shard_map/ppermute | solution.py:29
  18.2 4.4 %collective-permute-start.7 = (bf16[4,4096]{1,0:T(4,128)(2,1)S(1)}, bf16[4,4096]{1,0:T(4,128)(2,1)S(1)}, u32[]{:S(2)}, u32[]{:S(2)}) collective-permute-start(bf16[4,4096]{1,0:T(4,128)(2,1)S(1)} %get-tuple-element.50), channel_id=1, source_target_pairs={{0,6},{1,7},{2,4},{3,5},{4,2},{5,3},{6,0},{7,1},{8,14},{9,15},{10,... | collective-permute-start | bytes 98312 | tf_op jit(solution)/shard_map/ppermute | solution.py:29
  18.7 5.6 %collective-permute-start.8 = (bf16[4,4096]{1,0:T(4,128)(2,1)S(1)}, bf16[4,4096]{1,0:T(4,128)(2,1)S(1)}, u32[]{:S(2)}, u32[]{:S(2)}) collective-permute-start(bf16[4,4096]{1,0:T(4,128)(2,1)S(1)} %get-tuple-element.51), channel_id=1, source_target_pairs={{0,7},{1,6},{2,5},{3,4},{4,3},{5,2},{6,1},{7,0},{8,15},{9,14},{10,... | collective-permute-start | bytes 98312 | tf_op jit(solution)/shard_map/ppermute | solution.py:29
  24.4 5.2 %collective-permute-start.11 = (bf16[4,4224]{1,0:T(4,128)(2,1)S(1)}, bf16[4,4224]{1,0:T(4,128)(2,1)S(1)}, u32[]{:S(2)}, u32[]{:S(2)}) collective-permute-start(bf16[4,4224]{1,0:T(4,128)(2,1)S(1)} %get-tuple-element.54), channel_id=1, source_target_pairs={{0,7},{1,6},{2,5},{3,4},{4,3},{5,2},{6,1},{7,0},{8,15},{9,14},{10,... | collective-permute-start | bytes 101384 | tf_op jit(solution)/shard_map/ppermute | solution.py:29
  27.5 4.3 %collective-permute-start.10 = (bf16[4,4224]{1,0:T(4,128)(2,1)S(1)}, bf16[4,4224]{1,0:T(4,128)(2,1)S(1)}, u32[]{:S(2)}, u32[]{:S(2)}) collective-permute-start(bf16[4,4224]{1,0:T(4,128)(2,1)S(1)} %get-tuple-element.54), channel_id=1, source_target_pairs={{0,6},{1,7},{2,4},{3,5},{4,2},{5,3},{6,0},{7,1},{8,14},{9,15},{10,... | collective-permute-start | bytes 101384 | tf_op jit(solution)/shard_map/ppermute | solution.py:29
  27.5 4.3 %collective-permute-start.9 = (bf16[4,4224]{1,0:T(4,128)(2,1)S(1)}, bf16[4,4224]{1,0:T(4,128)(2,1)S(1)}, u32[]{:S(2)}, u32[]{:S(2)}) collective-permute-start(bf16[4,4224]{1,0:T(4,128)(2,1)S(1)} %get-tuple-element.54), channel_id=1, source_target_pairs={{0,5},{1,4},{2,7},{3,6},{4,1},{5,0},{6,3},{7,2},{8,13},{9,12},{10,... | collective-permute-start | bytes 101384 | tf_op jit(solution)/shard_map/ppermute | solution.py:29
  28.6 7.3 %collective-permute-start.13 = (bf16[4,4224]{1,0:T(4,128)(2,1)S(1)}, bf16[4,4224]{1,0:T(4,128)(2,1)S(1)}, u32[]{:S(2)}, u32[]{:S(2)}) collective-permute-start(bf16[4,4224]{1,0:T(4,128)(2,1)S(1)} %get-tuple-element.54), channel_id=1, source_target_pairs={{0,12},{4,8},{8,4},{12,0},{1,13},{5,9},{9,5},{13,1},{2,14},{6,10},... | collective-permute-start | bytes 101384 | tf_op jit(solution)/shard_map/ppermute | solution.py:372
  29.6 6.2 %collective-permute-start.15 = (bf16[4,4224]{1,0:T(4,128)(2,1)S(1)}, bf16[4,4224]{1,0:T(4,128)(2,1)S(1)}, u32[]{:S(2)}, u32[]{:S(2)}) collective-permute-start(bf16[4,4224]{1,0:T(4,128)(2,1)S(1)} %shard_map.132), channel_id=1, source_target_pairs={{0,12},{4,8},{8,4},{12,0},{1,13},{5,9},{9,5},{13,1},{2,14},{6,10},... | collective-permute-start | bytes 101384 | tf_op jit(solution)/shard_map/ppermute | solution.py:372
  31.9 4.0 %collective-permute-start.14 = (bf16[2,4,4224]{2,1,0:T(4,128)(2,1)S(1)}, bf16[2,4,4224]{2,1,0:T(4,128)(2,1)S(1)}, u32[]{:S(2)}, u32[]{:S(2)}) collective-permute-start(bf16[2,4,4224]{2,1,0:T(4,128)(2,1)S(1)} %pad_maximum_fusion.2), channel_id=1, source_target_pairs={{0,12},{4,8},{8,4},{12,0},{1,13},{5,9},{9,5},{13,1},{2,14},{6,10},... | collective-permute-start | bytes 202760 | tf_op jit(solution)/shard_map/ppermute | solution.py:372
  32.9 3.5 %collective-permute-start.12 = (bf16[16,4224]{1,0:T(8,128)(2,1)S(1)}, bf16[16,4224]{1,0:T(8,128)(2,1)S(1)}, u32[]{:S(2)}, u32[]{:S(2)}) collective-permute-start(bf16[16,4224]{1,0:T(8,128)(2,1)S(1)} %pad_maximum_fusion.refs_1_), channel_id=1, source_target_pairs={{0,4},{4,0},{8,12},{12,8},{1,5},{5,1},{9,13},{13,9},{2,6},{6,2},{1... | collective-permute-start | bytes 405512 | tf_op jit(solution)/shard_map/ppermute | solution.py:372
  39.8 2.8 %collective-permute-start.25 = (bf16[1,4,4096]{2,1,0:T(4,128)(2,1)S(1)}, bf16[1,4,4096]{2,1,0:T(4,128)(2,1)S(1)}, u32[]{:S(2)}, u32[]{:S(2)}) collective-permute-start(bf16[1,4,4096]{2,1,0:T(4,128)(2,1)S(1)} %get-tuple-element.66), channel_id=1, source_target_pairs={{0,4},{4,0},{8,12},{12,8},{1,5},{5,1},{9,13},{13,9},{2,6},{6,2},{1... | collective-permute-start | bytes 98312 | tf_op jit(solution)/shard_map/ppermute | solution.py:372
  40.2 8.7 %collective-permute-start.19 = (bf16[3,4,4096]{2,1,0:T(4,128)(2,1)S(1)}, bf16[3,4,4096]{2,1,0:T(4,128)(2,1)S(1)}, u32[]{:S(2)}, u32[]{:S(2)}) collective-permute-start(bf16[3,4,4096]{2,1,0:T(4,128)(2,1)S(1)} %get-tuple-element.61), channel_id=1, source_target_pairs={{0,4},{4,0},{8,12},{12,8},{1,5},{5,1},{9,13},{13,9},{2,6},{6,2},{1... | collective-permute-start | bytes 294920 | tf_op jit(solution)/shard_map/ppermute | solution.py:372
  40.7 8.2 %collective-permute-start.20 = (bf16[2,4,4096]{2,1,0:T(4,128)(2,1)S(1)}, bf16[2,4,4096]{2,1,0:T(4,128)(2,1)S(1)}, u32[]{:S(2)}, u32[]{:S(2)}) collective-permute-start(bf16[2,4,4096]{2,1,0:T(4,128)(2,1)S(1)} %get-tuple-element.62), channel_id=1, source_target_pairs={{0,12},{4,8},{8,4},{12,0},{1,13},{5,9},{9,5},{13,1},{2,14},{6,10},... | collective-permute-start | bytes 196616 | tf_op jit(solution)/shard_map/ppermute | solution.py:372
  41.7 3.8 %collective-permute-start.24 = (bf16[1,4,4096]{2,1,0:T(4,128)(2,1)S(1)}, bf16[1,4,4096]{2,1,0:T(4,128)(2,1)S(1)}, u32[]{:S(2)}, u32[]{:S(2)}) collective-permute-start(bf16[1,4,4096]{2,1,0:T(4,128)(2,1)S(1)} %add_convert_fusion.1), channel_id=1, source_target_pairs={{0,12},{4,8},{8,4},{12,0},{1,13},{5,9},{9,5},{13,1},{2,14},{6,10},... | collective-permute-start | bytes 98312 | tf_op jit(solution)/shard_map/ppermute | solution.py:372
  45.5 5.8 %collective-permute-start.26 = (bf16[4,4096]{1,0:T(4,128)(2,1)S(1)}, bf16[4,4096]{1,0:T(4,128)(2,1)S(1)}, u32[]{:S(2)}, u32[]{:S(2)}) collective-permute-start(bf16[4,4096]{1,0:T(4,128)(2,1)S(1)} %shard_map.138), channel_id=1, source_target_pairs={{0,7},{1,6},{2,5},{3,4},{4,3},{5,2},{6,1},{7,0},{8,15},{9,14},{10,... | collective-permute-start | bytes 98312 | tf_op jit(solution)/shard_map/ppermute | solution.py:29
  47.9 3.3 %collective-permute-start.18 = (bf16[1,4,4096]{2,1,0:T(4,128)(2,1)S(1)}, bf16[1,4,4096]{2,1,0:T(4,128)(2,1)S(1)}, u32[]{:S(2)}, u32[]{:S(2)}) collective-permute-start(bf16[1,4,4096]{2,1,0:T(4,128)(2,1)S(1)} %get-tuple-element.59), channel_id=1, source_target_pairs={{0,12},{4,8},{8,4},{12,0},{1,13},{5,9},{9,5},{13,1},{2,14},{6,10},... | collective-permute-start | bytes 98312 | tf_op jit(solution)/shard_map/ppermute | solution.py:372
  48.9 3.4 %collective-permute-start.21 = (bf16[4,4096]{1,0:T(4,128)(2,1)S(1)}, bf16[4,4096]{1,0:T(4,128)(2,1)S(1)}, u32[]{:S(2)}, u32[]{:S(2)}) collective-permute-start(bf16[4,4096]{1,0:T(4,128)(2,1)S(1)} %shard_map.136), channel_id=1, source_target_pairs={{0,5},{1,4},{2,7},{3,6},{4,1},{5,0},{6,3},{7,2},{8,13},{9,12},{10,... | collective-permute-start | bytes 98312 | tf_op jit(solution)/shard_map/ppermute | solution.py:29
  49.0 4.3 %collective-permute-start.22 = (bf16[4,4096]{1,0:T(4,128)(2,1)S(1)}, bf16[4,4096]{1,0:T(4,128)(2,1)S(1)}, u32[]{:S(2)}, u32[]{:S(2)}) collective-permute-start(bf16[4,4096]{1,0:T(4,128)(2,1)S(1)} %shard_map.137), channel_id=1, source_target_pairs={{0,6},{1,7},{2,4},{3,5},{4,2},{5,3},{6,0},{7,1},{8,14},{9,15},{10,... | collective-permute-start | bytes 98312 | tf_op jit(solution)/shard_map/ppermute | solution.py:29
  (10 other events, 74.5 us)

commit v9 on v7

--- a/solution.py
+++ b/solution.py
@@ -255,8 +255,8 @@
     pay_ref[:, model:] = ext.astype(BF16)
 
 
-def add_kernel(at, block_ref, *refs):
-    total = block_ref[...].astype(F32)
+def add_kernel(at, block, block_ref, *refs):
+    total = block_ref[block].astype(F32)
     for ref in refs[:-1]:
         total = total + ref[at].astype(F32)
     refs[-1][...] = total.astype(refs[-1].dtype)
@@ -271,7 +271,7 @@
     pieces = refs[1 : 1 + n_dp]
     gate_ref, up_ref, down_ref, gain_ref, hid_ref = refs[1 + n_dp : 6 + n_dp]
     outs = refs[6 + n_dp : 6 + 2 * n_dp]
-    real_ref, lhs, act_scr, new_scr = refs[6 + 2 * n_dp :]
+    real_ref, act_scr, new_scr = refs[6 + 2 * n_dp :]
     dp = lax.axis_index("dp")
     model = gain_ref.shape[1]
     rows = n_ex * tokens
@@ -279,7 +279,6 @@
     rel = to_ref[n_dp * n_ex : n_dp * n_ex + 1, 0:1]
     carried = jnp.zeros((1, pieces[0].shape[1]), F32)
     for r in range(n_dp):
-        lhs[r * rows : (r + 1) * rows, :] = pieces[r][:, :model]
         ext = pieces[r][:, model:].astype(F32)
         lane = lax.broadcasted_iota(jnp.int32, ext.shape, 1)
         mine = (lane == dp) | (lane == dp + n_dp) | (lane == dp + 2 * n_dp)
@@ -292,7 +291,7 @@
     )
     first = lax.broadcasted_iota(jnp.int32, (tokens, 1), 0) == 0
     real_ref[...] = jnp.where(first, carried[:, :model] * root / gain_ref[...], hid_ref[...])
-    x = lhs[...]
+    x = jnp.concatenate([piece[:, :model] for piece in pieces], axis=0)
     gate = jnp.dot(x, gate_ref[0], preferred_element_type=F32)
     up = jnp.dot(x, up_ref[0], preferred_element_type=F32)
     act = gate / (1.0 + jnp.exp(-gate)) * up
@@ -435,7 +434,6 @@
         [shape((n_ex, tokens, model), BF16)] * n_dp + [shape((tokens, model), F32)],
         [spec()] * (n_dp + 6),
         scratch=[
-            pltpu.VMEM((all_rows, model), BF16),
             pltpu.VMEM((all_rows, hidden_units), F32),
             pltpu.VMEM((all_rows, hidden_units), F32),
         ],
@@ -462,14 +460,17 @@
     def across(at):
         return over_dp(added([t[at] for t in terms[top]]).astype(BF16), top)
 
-    arrived = [across(s) for s in range(n_ex)]
+    arrived = {}
+    for blocks in ([last], range(1, last), [0]):
+        got = across(slice(blocks[0], blocks[-1] + 1))
+        arrived |= {s: (got, s - blocks[0]) for s in blocks}
     mixed = [
         call(
-            functools.partial(add_kernel, s),
+            functools.partial(add_kernel, s, arrived[s][1]),
             shape((tokens, model), BF16 if s else F32),
             [spec()] * (len(terms[0]) + 1),
             limit=1 << 20,
-        )(arrived[s], *terms[0])
+        )(arrived[s][0], *terms[0])
         for s in range(n_ex)
     ]
     back = crossed_exchange(mixed, n_dp, n_ex)

time: 53.9 us -> 53.7 us (level)
    ppermute x14 -> x13, waiting for transfers between devices: 7.13 us -> 9.06 us  [over_dp(): return lax.ppermute(array, 'dp', [(j, j ^ turn) for j in range(n_dp)])]
    ppermute x12, waiting for transfers between devices: 12.9 us -> 11.2 us  [crossed_exchange(): moved[step] = lax.ppermute(blocks[step], ('dp', 'expert'), pairs)]
    ppermute x14 -> x13, starting transfers between devices: 10.7 us -> 9.94 us  [over_dp(): return lax.ppermute(array, 'dp', [(j, j ^ turn) for j in range(n_dp)])]
  transfers between devices with their start and end apart: 26 -> 25, of which waited for: 13 -> 15; matrix products, arithmetic and copies ran while one was open for 1% -> 1% of each run, Pallas kernels for 2% -> 2%
where the time goes in v9:
time: 53.7 us; the launch traced here: 53.6 us
  starting transfers between devices  26.6 us (50%)
  waiting for transfers between devices  20.3 us (38%)
  Pallas kernels  5.61 us (10%)
  other arithmetic  0.95 us (2%)
    ppermute x12, starting transfers between devices, crossed_exchange(): moved[step] = lax.ppermute(blocks[step], ('dp', 'expert'), pairs)  16.6 us
    ppermute x12, waiting for transfers between devices, crossed_exchange(): moved[step] = lax.ppermute(blocks[step], ('dp', 'expert'), pairs)  11.2 us
    ppermute x13, starting transfers between devices, over_dp(): return lax.ppermute(array, 'dp', [(j, j ^ turn) for j in range(n_dp)])  9.94 us
    ppermute x13, waiting for transfers between devices, over_dp(): return lax.ppermute(array, 'dp', [(j, j ^ turn) for j in range(n_dp)])  9.06 us
    pallas_call x1, Pallas kernels, per_device(): call(functools.partial(expert_kernel, n_dp, n_ex, tokens), [shape((n_ex,...  1.86 us
    pallas_call x1, Pallas kernels, per_device(): call(functools.partial(project_kernel, n_ex), [shape((tokens, model), F32...  1.21 us
  transfers between devices with their start and end apart: 25, of which 15 were waited for; matrix products, arithmetic and copies ran while one was open for 1% of the time, Pallas kernels for 2%

profile of v9, /device:TPU:0, one launch (start us, length us, event | category | flops | bytes accessed | tf_op | source)
XLA Modules:
  0.0 53.6 jit_solution(550981155719368725)
XLA Ops:
  0.0 1.0 %shard_map.127 = (bf16[1,8832]{1,0:T(2,128)(2,1)S(1)}, bf16[4,4096]{1,0:T(4,128)(2,1)S(1)}, bf16[4,512]{1,0:T(4,128)(2,1)S(1)}, bf16[4,4096]{1,0:T(4,128)(2,1)S(...) custom-call(bf16[4,4096]{1,0:T(4,128)(2,1)} %q_hbm.1, bf16[4,512]{1,0:T(4,128)(2,1)} %fresh_hbm.1, ...), custom_call_target="tpu_custom_call" | custom-call | flops 10000000000 | bytes 65536 | tf_op jit(solution)/shard_map/pallas_call | solution.py:332
  1.0 2.5 %collective-permute-start.2 = (bf16[1,8832]{1,0:T(2,128)(2,1)S(1)}, bf16[1,8832]{1,0:T(2,128)(2,1)S(1)}, u32[]{:S(2)}, u32[]{:S(2)}) collective-permute-start(bf16[1,8832]{1,0:T(2,128)(2,1)S(1)} %get-tuple-element.34.refs_1_), channel_id=1, source_target_pairs={{0,12},{4,8},{8,4},{12,0},{1,13},{5,9},{9,5},{13,1},{2,14},{6,10},... | collective-permute-start | bytes 53000 | tf_op jit(solution)/shard_map/ppermute | solution.py:357
  5.4 2.2 %collective-permute-done.1.refs_3_ = bf16[1,8832]{1,0:T(2,128)(2,1)S(1)} collective-permute-done((bf16[1,8832]{1,0:T(2,128)(2,1)S(1)}, bf16[1,8832]{1,0:T(2,128)(2,1)S(1)}, u32[]{:S(2)}, u32[]{:S(2)}) %collective-permute-start.1) | collective-permute-done | bytes 17696 | tf_op jit(solution)/shard_map/ppermute | solution.py:357
  8.1 1.1 %collective-permute-start.3 = (bf16[4,1024]{1,0:T(4,128)(2,1)S(1)}, bf16[4,1024]{1,0:T(4,128)(2,1)S(1)}, u32[]{:S(2)}, u32[]{:S(2)}) collective-permute-start(bf16[4,1024]{1,0:T(4,128)(2,1)S(1)} %get-tuple-element.39), channel_id=1, source_target_pairs={{0,5},{1,4},{2,7},{3,6},{4,1},{5,0},{6,3},{7,2},{8,13},{9,12},{10,... | collective-permute-start | bytes 24584 | tf_op jit(solution)/shard_map/ppermute | solution.py:29
  9.2 2.9 %collective-permute-start.4 = (bf16[4,1024]{1,0:T(4,128)(2,1)S(1)}, bf16[4,1024]{1,0:T(4,128)(2,1)S(1)}, u32[]{:S(2)}, u32[]{:S(2)}) collective-permute-start(bf16[4,1024]{1,0:T(4,128)(2,1)S(1)} %get-tuple-element.40), channel_id=1, source_target_pairs={{0,6},{1,7},{2,4},{3,5},{4,2},{5,3},{6,0},{7,1},{8,14},{9,15},{10,... | collective-permute-start | bytes 24584 | tf_op jit(solution)/shard_map/ppermute | solution.py:29
  12.1 1.4 %collective-permute-done.4.refs_2_ = bf16[4,1024]{1,0:T(4,128)(2,1)S(1)} collective-permute-done((bf16[4,1024]{1,0:T(4,128)(2,1)S(1)}, bf16[4,1024]{1,0:T(4,128)(2,1)S(1)}, u32[]{:S(2)}, u32[]{:S(2)}) %collective-permute-start.4) | collective-permute-done | bytes 8224 | tf_op jit(solution)/shard_map/ppermute | solution.py:29
  13.4 3.6 %collective-permute-done.5.refs_3_ = bf16[4,1024]{1,0:T(4,128)(2,1)S(1)} collective-permute-done((bf16[4,1024]{1,0:T(4,128)(2,1)S(1)}, bf16[4,1024]{1,0:T(4,128)(2,1)S(1)}, u32[]{:S(2)}, u32[]{:S(2)}) %collective-permute-start.5) | collective-permute-done | bytes 8224 | tf_op jit(solution)/shard_map/ppermute | solution.py:29
  17.0 1.2 %shard_map.130 = (f32[4,4096]{1,0:T(4,128)S(1)}, bf16[4,4096]{1,0:T(4,128)(2,1)S(1)}, bf16[4,4096]{1,0:T(4,128)(2,1)S(1)}, bf16[4,4096]{1,0:T(4,128)(2,1)S(1)}) custom-call(bf16[4,1024]{1,0:T(4,128)(2,1)S(1)} %get-tuple-element.38.refs_0_, bf16[4,1024]{1,0:T(4,128)(2,1)S(1)} %collective-permute-done.3.refs_1_, ...), custom_call_target="tpu_custom_call" | custom-call | flops 134217728 | bytes 8388608 | tf_op jit(solution)/shard_map/pallas_call | solution.py:395
  18.7 3.4 %collective-permute-start.8 = (bf16[4,4096]{1,0:T(4,128)(2,1)S(1)}, bf16[4,4096]{1,0:T(4,128)(2,1)S(1)}, u32[]{:S(2)}, u32[]{:S(2)}) collective-permute-start(bf16[4,4096]{1,0:T(4,128)(2,1)S(1)} %get-tuple-element.45), channel_id=1, source_target_pairs={{0,7},{1,6},{2,5},{3,4},{4,3},{5,2},{6,1},{7,0},{8,15},{9,14},{10,... | collective-permute-start | bytes 98312 | tf_op jit(solution)/shard_map/ppermute | solution.py:29
  22.6 1.6 %collective-permute-done.8.refs_3_ = bf16[4,4096]{1,0:T(4,128)(2,1)S(1)} collective-permute-done((bf16[4,4096]{1,0:T(4,128)(2,1)S(1)}, bf16[4,4096]{1,0:T(4,128)(2,1)S(1)}, u32[]{:S(2)}, u32[]{:S(2)}) %collective-permute-start.8) | collective-permute-done | bytes 32800 | tf_op jit(solution)/shard_map/ppermute | solution.py:29
  24.4 3.1 %collective-permute-start.11 = (bf16[4,4224]{1,0:T(4,128)(2,1)S(1)}, bf16[4,4224]{1,0:T(4,128)(2,1)S(1)}, u32[]{:S(2)}, u32[]{:S(2)}) collective-permute-start(bf16[4,4224]{1,0:T(4,128)(2,1)S(1)} %get-tuple-element.48), channel_id=1, source_target_pairs={{0,7},{1,6},{2,5},{3,4},{4,3},{5,2},{6,1},{7,0},{8,15},{9,14},{10,... | collective-permute-start | bytes 101384 | tf_op jit(solution)/shard_map/ppermute | solution.py:29
  27.5 1.1 %collective-permute-start.9 = (bf16[4,4224]{1,0:T(4,128)(2,1)S(1)}, bf16[4,4224]{1,0:T(4,128)(2,1)S(1)}, u32[]{:S(2)}, u32[]{:S(2)}) collective-permute-start(bf16[4,4224]{1,0:T(4,128)(2,1)S(1)} %get-tuple-element.48), channel_id=1, source_target_pairs={{0,5},{1,4},{2,7},{3,6},{4,1},{5,0},{6,3},{7,2},{8,13},{9,12},{10,... | collective-permute-start | bytes 101384 | tf_op jit(solution)/shard_map/ppermute | solution.py:29
  29.6 1.1 %collective-permute-start.15 = (bf16[4,4224]{1,0:T(4,128)(2,1)S(1)}, bf16[4,4224]{1,0:T(4,128)(2,1)S(1)}, u32[]{:S(2)}, u32[]{:S(2)}) collective-permute-start(bf16[4,4224]{1,0:T(4,128)(2,1)S(1)} %shard_map.132), channel_id=1, source_target_pairs={{0,12},{4,8},{8,4},{12,0},{1,13},{5,9},{9,5},{13,1},{2,14},{6,10},... | collective-permute-start | bytes 101384 | tf_op jit(solution)/shard_map/ppermute | solution.py:357
  30.7 1.1 %collective-permute-done.10 = bf16[4,4224]{1,0:T(4,128)(2,1)S(1)} collective-permute-done((bf16[4,4224]{1,0:T(4,128)(2,1)S(1)}, bf16[4,4224]{1,0:T(4,128)(2,1)S(1)}, u32[]{:S(2)}, u32[]{:S(2)}) %collective-permute-start.10) | collective-permute-done | bytes 33824 | tf_op jit(solution)/shard_map/ppermute | solution.py:29
  31.9 1.0 %collective-permute-start.14 = (bf16[2,4,4224]{2,1,0:T(4,128)(2,1)S(1)}, bf16[2,4,4224]{2,1,0:T(4,128)(2,1)S(1)}, u32[]{:S(2)}, u32[]{:S(2)}) collective-permute-start(bf16[2,4,4224]{2,1,0:T(4,128)(2,1)S(1)} %pad_maximum_fusion.2), channel_id=1, source_target_pairs={{0,12},{4,8},{8,4},{12,0},{1,13},{5,9},{9,5},{13,1},{2,14},{6,10},... | collective-permute-start | bytes 202760 | tf_op jit(solution)/shard_map/ppermute | solution.py:357
  33.1 2.7 %collective-permute-done.14 = bf16[2,4,4224]{2,1,0:T(4,128)(2,1)S(1)} collective-permute-done((bf16[2,4,4224]{2,1,0:T(4,128)(2,1)S(1)}, bf16[2,4,4224]{2,1,0:T(4,128)(2,1)S(1)}, u32[]{:S(2)}, u32[]{:S(2)}) %collective-permute-start.14) | collective-permute-done | bytes 67616 | tf_op jit(solution)/shard_map/ppermute | solution.py:357
  36.4 1.0 %collective-permute-done.16.refs_3_ = bf16[16,4224]{1,0:T(8,128)(2,1)S(1)} collective-permute-done((bf16[16,4224]{1,0:T(8,128)(2,1)S(1)}, bf16[16,4224]{1,0:T(8,128)(2,1)S(1)}, u32[]{:S(2)}, u32[]{:S(2)}) %collective-permute-start.16) | collective-permute-done | bytes 135200 | tf_op jit(solution)/shard_map/ppermute | solution.py:357
  37.4 1.9 %shard_map.133 = (bf16[4,4,4096]{2,1,0:T(4,128)(2,1)S(1)}, bf16[4,4,4096]{2,1,0:T(4,128)(2,1)S(1)}, bf16[4,4,4096]{2,1,0:T(4,128)(2,1)S(1)}, bf16[4,4,4096]{2,1,0:T(4,128)(2,1)S(1)}, f32[4,4096]{1,0:T(4,128)S(1)}) custom-call(s32[24,128]{1,0:T(8,128)S(1)} %get-tuple-element.33.refs_0_, bf16[16,4224]{1,0:T(8,128)(2,1)S(1)} %pad_maximum_fusion.refs_1_, ...), custom_call_target="tpu_custom_call" | custom-call | flops 603979776 | bytes 9437184 | tf_op jit(solution)/shard_map/pallas_call | solution.py:432
  40.7 1.0 %collective-permute-start.20 = (bf16[2,4,4096]{2,1,0:T(4,128)(2,1)S(1)}, bf16[2,4,4096]{2,1,0:T(4,128)(2,1)S(1)}, u32[]{:S(2)}, u32[]{:S(2)}) collective-permute-start(bf16[2,4,4096]{2,1,0:T(4,128)(2,1)S(1)} %add_convert_fusion), channel_id=1, source_target_pairs={{0,12},{4,8},{8,4},{12,0},{1,13},{5,9},{9,5},{13,1},{2,14},{6,10},... | collective-permute-start | bytes 196616 | tf_op jit(solution)/shard_map/ppermute | solution.py:357
  42.6 0.9 %collective-permute-start.18 = (bf16[1,4,4096]{2,1,0:T(4,128)(2,1)S(1)}, bf16[1,4,4096]{2,1,0:T(4,128)(2,1)S(1)}, u32[]{:S(2)}, u32[]{:S(2)}) collective-permute-start(bf16[1,4,4096]{2,1,0:T(4,128)(2,1)S(1)} %get-tuple-element.55), channel_id=1, source_target_pairs={{0,12},{4,8},{8,4},{12,0},{1,13},{5,9},{9,5},{13,1},{2,14},{6,10},... | collective-permute-start | bytes 98312 | tf_op jit(solution)/shard_map/ppermute | solution.py:357
  43.5 1.9 %collective-permute-done.23.block_ref = bf16[1,4,4096]{2,1,0:T(4,128)(2,1)S(1)} collective-permute-done((bf16[1,4,4096]{2,1,0:T(4,128)(2,1)S(1)}, bf16[1,4,4096]{2,1,0:T(4,128)(2,1)S(1)}, u32[]{:S(2)}, u32[]{:S(2)}) %collective-permute-start.23) | collective-permute-done | bytes 32800 | tf_op jit(solution)/shard_map/ppermute | solution.py:357
  45.5 3.0 %collective-permute-start.24 = (bf16[4,4096]{1,0:T(4,128)(2,1)S(1)}, bf16[4,4096]{1,0:T(4,128)(2,1)S(1)}, u32[]{:S(2)}, u32[]{:S(2)}) collective-permute-start(bf16[4,4096]{1,0:T(4,128)(2,1)S(1)} %shard_map.137), channel_id=1, source_target_pairs={{0,7},{1,6},{2,5},{3,4},{4,3},{5,2},{6,1},{7,0},{8,15},{9,14},{10,... | collective-permute-start | bytes 98312 | tf_op jit(solution)/shard_map/ppermute | solution.py:29
  48.6 1.6 %collective-permute-start.22 = (bf16[4,4096]{1,0:T(4,128)(2,1)S(1)}, bf16[4,4096]{1,0:T(4,128)(2,1)S(1)}, u32[]{:S(2)}, u32[]{:S(2)}) collective-permute-start(bf16[4,4096]{1,0:T(4,128)(2,1)S(1)} %shard_map.136), channel_id=1, source_target_pairs={{0,6},{1,7},{2,4},{3,5},{4,2},{5,3},{6,0},{7,1},{8,14},{9,15},{10,... | collective-permute-start | bytes 98312 | tf_op jit(solution)/shard_map/ppermute | solution.py:29
  50.7 1.6 %collective-permute-done.21 = bf16[4,4096]{1,0:T(4,128)(2,1)S(1)} collective-permute-done((bf16[4,4096]{1,0:T(4,128)(2,1)S(1)}, bf16[4,4096]{1,0:T(4,128)(2,1)S(1)}, u32[]{:S(2)}, u32[]{:S(2)}) %collective-permute-start.21) | collective-permute-done | bytes 32800 | tf_op jit(solution)/shard_map/ppermute | solution.py:29
  (59 shorter events, 9.6 us)
Async XLA Ops:
  1.0 4.3 %collective-permute-start.2 = (bf16[1,8832]{1,0:T(2,128)(2,1)S(1)}, bf16[1,8832]{1,0:T(2,128)(2,1)S(1)}, u32[]{:S(2)}, u32[]{:S(2)}) collective-permute-start(bf16[1,8832]{1,0:T(2,128)(2,1)S(1)} %get-tuple-element.34.refs_1_), channel_id=1, source_target_pairs={{0,12},{4,8},{8,4},{12,0},{1,13},{5,9},{9,5},{13,1},{2,14},{6,10},... | collective-permute-start | bytes 53000 | tf_op jit(solution)/shard_map/ppermute | solution.py:357
  3.5 4.0 %collective-permute-start.1 = (bf16[1,8832]{1,0:T(2,128)(2,1)S(1)}, bf16[1,8832]{1,0:T(2,128)(2,1)S(1)}, u32[]{:S(2)}, u32[]{:S(2)}) collective-permute-start(bf16[1,8832]{1,0:T(2,128)(2,1)S(1)} %get-tuple-element.34.refs_1_), channel_id=1, source_target_pairs={{0,8},{4,12},{8,0},{12,4},{1,9},{5,13},{9,1},{13,5},{2,10},{6,14},... | collective-permute-start | bytes 53000 | tf_op jit(solution)/shard_map/ppermute | solution.py:357
  4.2 3.4 %collective-permute-start = (bf16[1,8832]{1,0:T(2,128)(2,1)S(1)}, bf16[1,8832]{1,0:T(2,128)(2,1)S(1)}, u32[]{:S(2)}, u32[]{:S(2)}) collective-permute-start(bf16[1,8832]{1,0:T(2,128)(2,1)S(1)} %get-tuple-element.34.refs_1_), channel_id=1, source_target_pairs={{0,4},{4,0},{8,12},{12,8},{1,5},{5,1},{9,13},{13,9},{2,6},{6,2},{1... | collective-permute-start | bytes 53000 | tf_op jit(solution)/shard_map/ppermute | solution.py:357
  8.1 4.0 %collective-permute-start.3 = (bf16[4,1024]{1,0:T(4,128)(2,1)S(1)}, bf16[4,1024]{1,0:T(4,128)(2,1)S(1)}, u32[]{:S(2)}, u32[]{:S(2)}) collective-permute-start(bf16[4,1024]{1,0:T(4,128)(2,1)S(1)} %get-tuple-element.39), channel_id=1, source_target_pairs={{0,5},{1,4},{2,7},{3,6},{4,1},{5,0},{6,3},{7,2},{8,13},{9,12},{10,... | collective-permute-start | bytes 24584 | tf_op jit(solution)/shard_map/ppermute | solution.py:29
  9.2 4.3 %collective-permute-start.4 = (bf16[4,1024]{1,0:T(4,128)(2,1)S(1)}, bf16[4,1024]{1,0:T(4,128)(2,1)S(1)}, u32[]{:S(2)}, u32[]{:S(2)}) collective-permute-start(bf16[4,1024]{1,0:T(4,128)(2,1)S(1)} %get-tuple-element.40), channel_id=1, source_target_pairs={{0,6},{1,7},{2,4},{3,5},{4,2},{5,3},{6,0},{7,1},{8,14},{9,15},{10,... | collective-permute-start | bytes 24584 | tf_op jit(solution)/shard_map/ppermute | solution.py:29
  12.1 5.0 %collective-permute-start.5 = (bf16[4,1024]{1,0:T(4,128)(2,1)S(1)}, bf16[4,1024]{1,0:T(4,128)(2,1)S(1)}, u32[]{:S(2)}, u32[]{:S(2)}) collective-permute-start(bf16[4,1024]{1,0:T(4,128)(2,1)S(1)} %get-tuple-element.41), channel_id=1, source_target_pairs={{0,7},{1,6},{2,5},{3,4},{4,3},{5,2},{6,1},{7,0},{8,15},{9,14},{10,... | collective-permute-start | bytes 24584 | tf_op jit(solution)/shard_map/ppermute | solution.py:29
  18.2 3.8 %collective-permute-start.6 = (bf16[4,4096]{1,0:T(4,128)(2,1)S(1)}, bf16[4,4096]{1,0:T(4,128)(2,1)S(1)}, u32[]{:S(2)}, u32[]{:S(2)}) collective-permute-start(bf16[4,4096]{1,0:T(4,128)(2,1)S(1)} %get-tuple-element.43), channel_id=1, source_target_pairs={{0,5},{1,4},{2,7},{3,6},{4,1},{5,0},{6,3},{7,2},{8,13},{9,12},{10,... | collective-permute-start | bytes 98312 | tf_op jit(solution)/shard_map/ppermute | solution.py:29
  18.2 4.4 %collective-permute-start.7 = (bf16[4,4096]{1,0:T(4,128)(2,1)S(1)}, bf16[4,4096]{1,0:T(4,128)(2,1)S(1)}, u32[]{:S(2)}, u32[]{:S(2)}) collective-permute-start(bf16[4,4096]{1,0:T(4,128)(2,1)S(1)} %get-tuple-element.44), channel_id=1, source_target_pairs={{0,6},{1,7},{2,4},{3,5},{4,2},{5,3},{6,0},{7,1},{8,14},{9,15},{10,... | collective-permute-start | bytes 98312 | tf_op jit(solution)/shard_map/ppermute | solution.py:29
  18.7 5.6 %collective-permute-start.8 = (bf16[4,4096]{1,0:T(4,128)(2,1)S(1)}, bf16[4,4096]{1,0:T(4,128)(2,1)S(1)}, u32[]{:S(2)}, u32[]{:S(2)}) collective-permute-start(bf16[4,4096]{1,0:T(4,128)(2,1)S(1)} %get-tuple-element.45), channel_id=1, source_target_pairs={{0,7},{1,6},{2,5},{3,4},{4,3},{5,2},{6,1},{7,0},{8,15},{9,14},{10,... | collective-permute-start | bytes 98312 | tf_op jit(solution)/shard_map/ppermute | solution.py:29
  24.4 5.2 %collective-permute-start.11 = (bf16[4,4224]{1,0:T(4,128)(2,1)S(1)}, bf16[4,4224]{1,0:T(4,128)(2,1)S(1)}, u32[]{:S(2)}, u32[]{:S(2)}) collective-permute-start(bf16[4,4224]{1,0:T(4,128)(2,1)S(1)} %get-tuple-element.48), channel_id=1, source_target_pairs={{0,7},{1,6},{2,5},{3,4},{4,3},{5,2},{6,1},{7,0},{8,15},{9,14},{10,... | collective-permute-start | bytes 101384 | tf_op jit(solution)/shard_map/ppermute | solution.py:29
  27.5 4.3 %collective-permute-start.10 = (bf16[4,4224]{1,0:T(4,128)(2,1)S(1)}, bf16[4,4224]{1,0:T(4,128)(2,1)S(1)}, u32[]{:S(2)}, u32[]{:S(2)}) collective-permute-start(bf16[4,4224]{1,0:T(4,128)(2,1)S(1)} %get-tuple-element.48), channel_id=1, source_target_pairs={{0,6},{1,7},{2,4},{3,5},{4,2},{5,3},{6,0},{7,1},{8,14},{9,15},{10,... | collective-permute-start | bytes 101384 | tf_op jit(solution)/shard_map/ppermute | solution.py:29
  27.5 4.3 %collective-permute-start.9 = (bf16[4,4224]{1,0:T(4,128)(2,1)S(1)}, bf16[4,4224]{1,0:T(4,128)(2,1)S(1)}, u32[]{:S(2)}, u32[]{:S(2)}) collective-permute-start(bf16[4,4224]{1,0:T(4,128)(2,1)S(1)} %get-tuple-element.48), channel_id=1, source_target_pairs={{0,5},{1,4},{2,7},{3,6},{4,1},{5,0},{6,3},{7,2},{8,13},{9,12},{10,... | collective-permute-start | bytes 101384 | tf_op jit(solution)/shard_map/ppermute | solution.py:29
  28.6 7.3 %collective-permute-start.13 = (bf16[4,4224]{1,0:T(4,128)(2,1)S(1)}, bf16[4,4224]{1,0:T(4,128)(2,1)S(1)}, u32[]{:S(2)}, u32[]{:S(2)}) collective-permute-start(bf16[4,4224]{1,0:T(4,128)(2,1)S(1)} %get-tuple-element.48), channel_id=1, source_target_pairs={{0,12},{4,8},{8,4},{12,0},{1,13},{5,9},{9,5},{13,1},{2,14},{6,10},... | collective-permute-start | bytes 101384 | tf_op jit(solution)/shard_map/ppermute | solution.py:357
  29.6 6.2 %collective-permute-start.15 = (bf16[4,4224]{1,0:T(4,128)(2,1)S(1)}, bf16[4,4224]{1,0:T(4,128)(2,1)S(1)}, u32[]{:S(2)}, u32[]{:S(2)}) collective-permute-start(bf16[4,4224]{1,0:T(4,128)(2,1)S(1)} %shard_map.132), channel_id=1, source_target_pairs={{0,12},{4,8},{8,4},{12,0},{1,13},{5,9},{9,5},{13,1},{2,14},{6,10},... | collective-permute-start | bytes 101384 | tf_op jit(solution)/shard_map/ppermute | solution.py:357
  31.9 4.0 %collective-permute-start.14 = (bf16[2,4,4224]{2,1,0:T(4,128)(2,1)S(1)}, bf16[2,4,4224]{2,1,0:T(4,128)(2,1)S(1)}, u32[]{:S(2)}, u32[]{:S(2)}) collective-permute-start(bf16[2,4,4224]{2,1,0:T(4,128)(2,1)S(1)} %pad_maximum_fusion.2), channel_id=1, source_target_pairs={{0,12},{4,8},{8,4},{12,0},{1,13},{5,9},{9,5},{13,1},{2,14},{6,10},... | collective-permute-start | bytes 202760 | tf_op jit(solution)/shard_map/ppermute | solution.py:357
  32.9 3.5 %collective-permute-start.12 = (bf16[16,4224]{1,0:T(8,128)(2,1)S(1)}, bf16[16,4224]{1,0:T(8,128)(2,1)S(1)}, u32[]{:S(2)}, u32[]{:S(2)}) collective-permute-start(bf16[16,4224]{1,0:T(8,128)(2,1)S(1)} %pad_maximum_fusion.refs_1_), channel_id=1, source_target_pairs={{0,4},{4,0},{8,12},{12,8},{1,5},{5,1},{9,13},{13,9},{2,6},{6,2},{1... | collective-permute-start | bytes 405512 | tf_op jit(solution)/shard_map/ppermute | solution.py:357
  36.0 1.4 %collective-permute-start.16 = (bf16[16,4224]{1,0:T(8,128)(2,1)S(1)}, bf16[16,4224]{1,0:T(8,128)(2,1)S(1)}, u32[]{:S(2)}, u32[]{:S(2)}) collective-permute-start(bf16[16,4224]{1,0:T(8,128)(2,1)S(1)} %pad_maximum_fusion.1.refs_4_), channel_id=1, source_target_pairs={{0,4},{4,0},{8,12},{12,8},{1,5},{5,1},{9,13},{13,9},{2,6},{6,2},{1... | collective-permute-start | bytes 405512 | tf_op jit(solution)/shard_map/ppermute | solution.py:357
  39.7 3.9 %collective-permute-start.19 = (bf16[4,4,4096]{2,1,0:T(4,128)(2,1)S(1)}, bf16[4,4,4096]{2,1,0:T(4,128)(2,1)S(1)}, u32[]{:S(2)}, u32[]{:S(2)}) collective-permute-start(bf16[4,4,4096]{2,1,0:T(4,128)(2,1)S(1)} %get-tuple-element.54), channel_id=1, source_target_pairs={{0,4},{4,0},{8,12},{12,8},{1,5},{5,1},{9,13},{13,9},{2,6},{6,2},{1... | collective-permute-start | bytes 393224 | tf_op jit(solution)/shard_map/ppermute | solution.py:357
  40.7 7.8 %collective-permute-start.20 = (bf16[2,4,4096]{2,1,0:T(4,128)(2,1)S(1)}, bf16[2,4,4096]{2,1,0:T(4,128)(2,1)S(1)}, u32[]{:S(2)}, u32[]{:S(2)}) collective-permute-start(bf16[2,4,4096]{2,1,0:T(4,128)(2,1)S(1)} %add_convert_fusion), channel_id=1, source_target_pairs={{0,12},{4,8},{8,4},{12,0},{1,13},{5,9},{9,5},{13,1},{2,14},{6,10},... | collective-permute-start | bytes 196616 | tf_op jit(solution)/shard_map/ppermute | solution.py:357
  41.7 3.8 %collective-permute-start.23 = (bf16[1,4,4096]{2,1,0:T(4,128)(2,1)S(1)}, bf16[1,4,4096]{2,1,0:T(4,128)(2,1)S(1)}, u32[]{:S(2)}, u32[]{:S(2)}) collective-permute-start(bf16[1,4,4096]{2,1,0:T(4,128)(2,1)S(1)} %get-tuple-element.56), channel_id=1, source_target_pairs={{0,12},{4,8},{8,4},{12,0},{1,13},{5,9},{9,5},{13,1},{2,14},{6,10},... | collective-permute-start | bytes 98312 | tf_op jit(solution)/shard_map/ppermute | solution.py:357
  42.6 7.6 %collective-permute-start.18 = (bf16[1,4,4096]{2,1,0:T(4,128)(2,1)S(1)}, bf16[1,4,4096]{2,1,0:T(4,128)(2,1)S(1)}, u32[]{:S(2)}, u32[]{:S(2)}) collective-permute-start(bf16[1,4,4096]{2,1,0:T(4,128)(2,1)S(1)} %get-tuple-element.55), channel_id=1, source_target_pairs={{0,12},{4,8},{8,4},{12,0},{1,13},{5,9},{9,5},{13,1},{2,14},{6,10},... | collective-permute-start | bytes 98312 | tf_op jit(solution)/shard_map/ppermute | solution.py:357
  45.5 5.2 %collective-permute-start.24 = (bf16[4,4096]{1,0:T(4,128)(2,1)S(1)}, bf16[4,4096]{1,0:T(4,128)(2,1)S(1)}, u32[]{:S(2)}, u32[]{:S(2)}) collective-permute-start(bf16[4,4096]{1,0:T(4,128)(2,1)S(1)} %shard_map.137), channel_id=1, source_target_pairs={{0,7},{1,6},{2,5},{3,4},{4,3},{5,2},{6,1},{7,0},{8,15},{9,14},{10,... | collective-permute-start | bytes 98312 | tf_op jit(solution)/shard_map/ppermute | solution.py:29
  48.5 3.9 %collective-permute-start.21 = (bf16[4,4096]{1,0:T(4,128)(2,1)S(1)}, bf16[4,4096]{1,0:T(4,128)(2,1)S(1)}, u32[]{:S(2)}, u32[]{:S(2)}) collective-permute-start(bf16[4,4096]{1,0:T(4,128)(2,1)S(1)} %shard_map.135), channel_id=1, source_target_pairs={{0,5},{1,4},{2,7},{3,6},{4,1},{5,0},{6,3},{7,2},{8,13},{9,12},{10,... | collective-permute-start | bytes 98312 | tf_op jit(solution)/shard_map/ppermute | solution.py:29
  48.6 4.3 %collective-permute-start.22 = (bf16[4,4096]{1,0:T(4,128)(2,1)S(1)}, bf16[4,4096]{1,0:T(4,128)(2,1)S(1)}, u32[]{:S(2)}, u32[]{:S(2)}) collective-permute-start(bf16[4,4096]{1,0:T(4,128)(2,1)S(1)} %shard_map.136), channel_id=1, source_target_pairs={{0,6},{1,7},{2,4},{3,5},{4,2},{5,3},{6,0},{7,1},{8,14},{9,15},{10,... | collective-permute-start | bytes 98312 | tf_op jit(solution)/shard_map/ppermute | solution.py:29
  (8 other events, 71.2 us)

commit v10 on v9

--- a/solution.py
+++ b/solution.py
@@ -271,7 +271,7 @@
     pieces = refs[1 : 1 + n_dp]
     gate_ref, up_ref, down_ref, gain_ref, hid_ref = refs[1 + n_dp : 6 + n_dp]
     outs = refs[6 + n_dp : 6 + 2 * n_dp]
-    real_ref, act_scr, new_scr = refs[6 + 2 * n_dp :]
+    real_ref, lhs, act_scr, new_scr = refs[6 + 2 * n_dp :]
     dp = lax.axis_index("dp")
     model = gain_ref.shape[1]
     rows = n_ex * tokens
@@ -279,6 +279,7 @@
     rel = to_ref[n_dp * n_ex : n_dp * n_ex + 1, 0:1]
     carried = jnp.zeros((1, pieces[0].shape[1]), F32)
     for r in range(n_dp):
+        lhs[r * rows : (r + 1) * rows, :] = pieces[r][:, :model]
         ext = pieces[r][:, model:].astype(F32)
         lane = lax.broadcasted_iota(jnp.int32, ext.shape, 1)
         mine = (lane == dp) | (lane == dp + n_dp) | (lane == dp + 2 * n_dp)
@@ -291,7 +292,7 @@
     )
     first = lax.broadcasted_iota(jnp.int32, (tokens, 1), 0) == 0
     real_ref[...] = jnp.where(first, carried[:, :model] * root / gain_ref[...], hid_ref[...])
-    x = jnp.concatenate([piece[:, :model] for piece in pieces], axis=0)
+    x = lhs[...]
     gate = jnp.dot(x, gate_ref[0], preferred_element_type=F32)
     up = jnp.dot(x, up_ref[0], preferred_element_type=F32)
     act = gate / (1.0 + jnp.exp(-gate)) * up
@@ -434,6 +435,7 @@
         [shape((n_ex, tokens, model), BF16)] * n_dp + [shape((tokens, model), F32)],
         [spec()] * (n_dp + 6),
         scratch=[
+            pltpu.VMEM((all_rows, model), BF16),
             pltpu.VMEM((all_rows, hidden_units), F32),
             pltpu.VMEM((all_rows, hidden_units), F32),
         ],
@@ -461,7 +463,7 @@
         return over_dp(added([t[at] for t in terms[top]]).astype(BF16), top)
 
     arrived = {}
-    for blocks in ([last], range(1, last), [0]):
+    for blocks in ([last], range(last)):
         got = across(slice(blocks[0], blocks[-1] + 1))
         arrived |= {s: (got, s - blocks[0]) for s in blocks}
     mixed = [

time: 53.7 us -> 53.9 us (level)
  waiting for transfers between devices: 20.3 us -> 21.7 us
  starting transfers between devices: 26.6 us -> 25.3 us
    ppermute x13 -> x12, waiting for transfers between devices: 9.06 us -> 10.5 us  [over_dp(): return lax.ppermute(array, 'dp', [(j, j ^ turn) for j in range(n_dp)])]
    ppermute x13 -> x12, starting transfers between devices: 9.94 us -> 9.03 us  [over_dp(): return lax.ppermute(array, 'dp', [(j, j ^ turn) for j in range(n_dp)])]
  transfers between devices with their start and end apart: 25 -> 24, of which waited for: 15 -> 15; matrix products, arithmetic and copies ran while one was open for 1% -> 1% of each run, Pallas kernels for 2% -> 2%
where the time goes in v10:
time: 53.9 us; the launch traced here: 53.7 us
  starting transfers between devices  25.3 us (47%)
  waiting for transfers between devices  21.7 us (40%)
  Pallas kernels  5.61 us (10%)
  other arithmetic  0.95 us (2%)
    ppermute x12, starting transfers between devices, crossed_exchange(): moved[step] = lax.ppermute(blocks[step], ('dp', 'expert'), pairs)  16.2 us
    ppermute x12, waiting for transfers between devices, crossed_exchange(): moved[step] = lax.ppermute(blocks[step], ('dp', 'expert'), pairs)  11.2 us
    ppermute x12, waiting for transfers between devices, over_dp(): return lax.ppermute(array, 'dp', [(j, j ^ turn) for j in range(n_dp)])  10.5 us
    ppermute x12, starting transfers between devices, over_dp(): return lax.ppermute(array, 'dp', [(j, j ^ turn) for j in range(n_dp)])  9.03 us
    pallas_call x1, Pallas kernels, per_device(): call(functools.partial(expert_kernel, n_dp, n_ex, tokens), [shape((n_ex,...  1.86 us
    pallas_call x1, Pallas kernels, per_device(): call(functools.partial(project_kernel, n_ex), [shape((tokens, model), F32...  1.21 us
  transfers between devices with their start and end apart: 24, of which 15 were waited for; matrix products, arithmetic and copies ran while one was open for 1% of the time, Pallas kernels for 2%

profile of v10, /device:TPU:0, one launch (start us, length us, event | category | flops | bytes accessed | tf_op | source)
XLA Modules:
  0.0 53.7 jit_solution(10085303830305466618)
XLA Ops:
  0.0 1.0 %shard_map.127 = (bf16[1,8832]{1,0:T(2,128)(2,1)S(1)}, bf16[4,4096]{1,0:T(4,128)(2,1)S(1)}, bf16[4,512]{1,0:T(4,128)(2,1)S(1)}, bf16[4,4096]{1,0:T(4,128)(2,1)S(...) custom-call(bf16[4,4096]{1,0:T(4,128)(2,1)} %q_hbm.1, bf16[4,512]{1,0:T(4,128)(2,1)} %fresh_hbm.1, ...), custom_call_target="tpu_custom_call" | custom-call | flops 10000000000 | bytes 65536 | tf_op jit(solution)/shard_map/pallas_call | solution.py:333
  1.0 2.5 %collective-permute-start.2 = (bf16[1,8832]{1,0:T(2,128)(2,1)S(1)}, bf16[1,8832]{1,0:T(2,128)(2,1)S(1)}, u32[]{:S(2)}, u32[]{:S(2)}) collective-permute-start(bf16[1,8832]{1,0:T(2,128)(2,1)S(1)} %get-tuple-element.34.refs_1_), channel_id=1, source_target_pairs={{0,12},{4,8},{8,4},{12,0},{1,13},{5,9},{9,5},{13,1},{2,14},{6,10},... | collective-permute-start | bytes 53000 | tf_op jit(solution)/shard_map/ppermute | solution.py:358
  5.4 2.2 %collective-permute-done.1.refs_3_ = bf16[1,8832]{1,0:T(2,128)(2,1)S(1)} collective-permute-done((bf16[1,8832]{1,0:T(2,128)(2,1)S(1)}, bf16[1,8832]{1,0:T(2,128)(2,1)S(1)}, u32[]{:S(2)}, u32[]{:S(2)}) %collective-permute-start.1) | collective-permute-done | bytes 17696 | tf_op jit(solution)/shard_map/ppermute | solution.py:358
  8.1 1.1 %collective-permute-start.3 = (bf16[4,1024]{1,0:T(4,128)(2,1)S(1)}, bf16[4,1024]{1,0:T(4,128)(2,1)S(1)}, u32[]{:S(2)}, u32[]{:S(2)}) collective-permute-start(bf16[4,1024]{1,0:T(4,128)(2,1)S(1)} %get-tuple-element.39), channel_id=1, source_target_pairs={{0,5},{1,4},{2,7},{3,6},{4,1},{5,0},{6,3},{7,2},{8,13},{9,12},{10,... | collective-permute-start | bytes 24584 | tf_op jit(solution)/shard_map/ppermute | solution.py:29
  9.2 2.9 %collective-permute-start.4 = (bf16[4,1024]{1,0:T(4,128)(2,1)S(1)}, bf16[4,1024]{1,0:T(4,128)(2,1)S(1)}, u32[]{:S(2)}, u32[]{:S(2)}) collective-permute-start(bf16[4,1024]{1,0:T(4,128)(2,1)S(1)} %get-tuple-element.40), channel_id=1, source_target_pairs={{0,6},{1,7},{2,4},{3,5},{4,2},{5,3},{6,0},{7,1},{8,14},{9,15},{10,... | collective-permute-start | bytes 24584 | tf_op jit(solution)/shard_map/ppermute | solution.py:29
  12.1 1.4 %collective-permute-done.4.refs_2_ = bf16[4,1024]{1,0:T(4,128)(2,1)S(1)} collective-permute-done((bf16[4,1024]{1,0:T(4,128)(2,1)S(1)}, bf16[4,1024]{1,0:T(4,128)(2,1)S(1)}, u32[]{:S(2)}, u32[]{:S(2)}) %collective-permute-start.4) | collective-permute-done | bytes 8224 | tf_op jit(solution)/shard_map/ppermute | solution.py:29
  13.4 3.6 %collective-permute-done.5.refs_3_ = bf16[4,1024]{1,0:T(4,128)(2,1)S(1)} collective-permute-done((bf16[4,1024]{1,0:T(4,128)(2,1)S(1)}, bf16[4,1024]{1,0:T(4,128)(2,1)S(1)}, u32[]{:S(2)}, u32[]{:S(2)}) %collective-permute-start.5) | collective-permute-done | bytes 8224 | tf_op jit(solution)/shard_map/ppermute | solution.py:29
  17.0 1.2 %shard_map.130 = (f32[4,4096]{1,0:T(4,128)S(1)}, bf16[4,4096]{1,0:T(4,128)(2,1)S(1)}, bf16[4,4096]{1,0:T(4,128)(2,1)S(1)}, bf16[4,4096]{1,0:T(4,128)(2,1)S(1)}) custom-call(bf16[4,1024]{1,0:T(4,128)(2,1)S(1)} %get-tuple-element.38.refs_0_, bf16[4,1024]{1,0:T(4,128)(2,1)S(1)} %collective-permute-done.3.refs_1_, ...), custom_call_target="tpu_custom_call" | custom-call | flops 134217728 | bytes 8388608 | tf_op jit(solution)/shard_map/pallas_call | solution.py:396
  18.7 3.4 %collective-permute-start.8 = (bf16[4,4096]{1,0:T(4,128)(2,1)S(1)}, bf16[4,4096]{1,0:T(4,128)(2,1)S(1)}, u32[]{:S(2)}, u32[]{:S(2)}) collective-permute-start(bf16[4,4096]{1,0:T(4,128)(2,1)S(1)} %get-tuple-element.45), channel_id=1, source_target_pairs={{0,7},{1,6},{2,5},{3,4},{4,3},{5,2},{6,1},{7,0},{8,15},{9,14},{10,... | collective-permute-start | bytes 98312 | tf_op jit(solution)/shard_map/ppermute | solution.py:29
  22.6 1.6 %collective-permute-done.8.refs_3_ = bf16[4,4096]{1,0:T(4,128)(2,1)S(1)} collective-permute-done((bf16[4,4096]{1,0:T(4,128)(2,1)S(1)}, bf16[4,4096]{1,0:T(4,128)(2,1)S(1)}, u32[]{:S(2)}, u32[]{:S(2)}) %collective-permute-start.8) | collective-permute-done | bytes 32800 | tf_op jit(solution)/shard_map/ppermute | solution.py:29
  24.4 3.1 %collective-permute-start.11 = (bf16[4,4224]{1,0:T(4,128)(2,1)S(1)}, bf16[4,4224]{1,0:T(4,128)(2,1)S(1)}, u32[]{:S(2)}, u32[]{:S(2)}) collective-permute-start(bf16[4,4224]{1,0:T(4,128)(2,1)S(1)} %get-tuple-element.48), channel_id=1, source_target_pairs={{0,7},{1,6},{2,5},{3,4},{4,3},{5,2},{6,1},{7,0},{8,15},{9,14},{10,... | collective-permute-start | bytes 101384 | tf_op jit(solution)/shard_map/ppermute | solution.py:29
  27.5 1.1 %collective-permute-start.9 = (bf16[4,4224]{1,0:T(4,128)(2,1)S(1)}, bf16[4,4224]{1,0:T(4,128)(2,1)S(1)}, u32[]{:S(2)}, u32[]{:S(2)}) collective-permute-start(bf16[4,4224]{1,0:T(4,128)(2,1)S(1)} %get-tuple-element.48), channel_id=1, source_target_pairs={{0,5},{1,4},{2,7},{3,6},{4,1},{5,0},{6,3},{7,2},{8,13},{9,12},{10,... | collective-permute-start | bytes 101384 | tf_op jit(solution)/shard_map/ppermute | solution.py:29
  29.6 1.1 %collective-permute-start.15 = (bf16[4,4224]{1,0:T(4,128)(2,1)S(1)}, bf16[4,4224]{1,0:T(4,128)(2,1)S(1)}, u32[]{:S(2)}, u32[]{:S(2)}) collective-permute-start(bf16[4,4224]{1,0:T(4,128)(2,1)S(1)} %shard_map.132), channel_id=1, source_target_pairs={{0,12},{4,8},{8,4},{12,0},{1,13},{5,9},{9,5},{13,1},{2,14},{6,10},... | collective-permute-start | bytes 101384 | tf_op jit(solution)/shard_map/ppermute | solution.py:358
  30.7 1.1 %collective-permute-done.10 = bf16[4,4224]{1,0:T(4,128)(2,1)S(1)} collective-permute-done((bf16[4,4224]{1,0:T(4,128)(2,1)S(1)}, bf16[4,4224]{1,0:T(4,128)(2,1)S(1)}, u32[]{:S(2)}, u32[]{:S(2)}) %collective-permute-start.10) | collective-permute-done | bytes 33824 | tf_op jit(solution)/shard_map/ppermute | solution.py:29
  31.9 1.0 %collective-permute-start.14 = (bf16[2,4,4224]{2,1,0:T(4,128)(2,1)S(1)}, bf16[2,4,4224]{2,1,0:T(4,128)(2,1)S(1)}, u32[]{:S(2)}, u32[]{:S(2)}) collective-permute-start(bf16[2,4,4224]{2,1,0:T(4,128)(2,1)S(1)} %pad_maximum_fusion.2), channel_id=1, source_target_pairs={{0,12},{4,8},{8,4},{12,0},{1,13},{5,9},{9,5},{13,1},{2,14},{6,10},... | collective-permute-start | bytes 202760 | tf_op jit(solution)/shard_map/ppermute | solution.py:358
  33.1 2.7 %collective-permute-done.14 = bf16[2,4,4224]{2,1,0:T(4,128)(2,1)S(1)} collective-permute-done((bf16[2,4,4224]{2,1,0:T(4,128)(2,1)S(1)}, bf16[2,4,4224]{2,1,0:T(4,128)(2,1)S(1)}, u32[]{:S(2)}, u32[]{:S(2)}) %collective-permute-start.14) | collective-permute-done | bytes 67616 | tf_op jit(solution)/shard_map/ppermute | solution.py:358
  36.4 1.0 %collective-permute-done.16.refs_3_ = bf16[16,4224]{1,0:T(8,128)(2,1)S(1)} collective-permute-done((bf16[16,4224]{1,0:T(8,128)(2,1)S(1)}, bf16[16,4224]{1,0:T(8,128)(2,1)S(1)}, u32[]{:S(2)}, u32[]{:S(2)}) %collective-permute-start.16) | collective-permute-done | bytes 135200 | tf_op jit(solution)/shard_map/ppermute | solution.py:358
  37.4 1.9 %shard_map.133 = (bf16[4,4,4096]{2,1,0:T(4,128)(2,1)S(1)}, bf16[4,4,4096]{2,1,0:T(4,128)(2,1)S(1)}, bf16[4,4,4096]{2,1,0:T(4,128)(2,1)S(1)}, bf16[4,4,4096]{2,1,0:T(4,128)(2,1)S(1)}, f32[4,4096]{1,0:T(4,128)S(1)}) custom-call(s32[24,128]{1,0:T(8,128)S(1)} %get-tuple-element.33.refs_0_, bf16[16,4224]{1,0:T(8,128)(2,1)S(1)} %pad_maximum_fusion.refs_1_, ...), custom_call_target="tpu_custom_call" | custom-call | flops 603979776 | bytes 9437184 | tf_op jit(solution)/shard_map/pallas_call | solution.py:433
  40.7 1.0 %collective-permute-start.18 = (bf16[3,4,4096]{2,1,0:T(4,128)(2,1)S(1)}, bf16[3,4,4096]{2,1,0:T(4,128)(2,1)S(1)}, u32[]{:S(2)}, u32[]{:S(2)}) collective-permute-start(bf16[3,4,4096]{2,1,0:T(4,128)(2,1)S(1)} %add_convert_fusion), channel_id=1, source_target_pairs={{0,12},{4,8},{8,4},{12,0},{1,13},{5,9},{9,5},{13,1},{2,14},{6,10},... | collective-permute-start | bytes 294920 | tf_op jit(solution)/shard_map/ppermute | solution.py:358
  41.7 0.9 %collective-permute-start.22 = (bf16[1,4,4096]{2,1,0:T(4,128)(2,1)S(1)}, bf16[1,4,4096]{2,1,0:T(4,128)(2,1)S(1)}, u32[]{:S(2)}, u32[]{:S(2)}) collective-permute-start(bf16[1,4,4096]{2,1,0:T(4,128)(2,1)S(1)} %add_convert_fusion.2), channel_id=1, source_target_pairs={{0,12},{4,8},{8,4},{12,0},{1,13},{5,9},{9,5},{13,1},{2,14},{6,10},... | collective-permute-start | bytes 98312 | tf_op jit(solution)/shard_map/ppermute | solution.py:358
  42.6 3.4 %collective-permute-done.22.block_ref = bf16[1,4,4096]{2,1,0:T(4,128)(2,1)S(1)} collective-permute-done((bf16[1,4,4096]{2,1,0:T(4,128)(2,1)S(1)}, bf16[1,4,4096]{2,1,0:T(4,128)(2,1)S(1)}, u32[]{:S(2)}, u32[]{:S(2)}) %collective-permute-start.22) | collective-permute-done | bytes 32800 | tf_op jit(solution)/shard_map/ppermute | solution.py:358
  46.1 2.6 %collective-permute-start.23 = (bf16[4,4096]{1,0:T(4,128)(2,1)S(1)}, bf16[4,4096]{1,0:T(4,128)(2,1)S(1)}, u32[]{:S(2)}, u32[]{:S(2)}) collective-permute-start(bf16[4,4096]{1,0:T(4,128)(2,1)S(1)} %shard_map.137), channel_id=1, source_target_pairs={{0,7},{1,6},{2,5},{3,4},{4,3},{5,2},{6,1},{7,0},{8,15},{9,14},{10,... | collective-permute-start | bytes 98312 | tf_op jit(solution)/shard_map/ppermute | solution.py:29
  48.8 1.6 %collective-permute-start.21 = (bf16[4,4096]{1,0:T(4,128)(2,1)S(1)}, bf16[4,4096]{1,0:T(4,128)(2,1)S(1)}, u32[]{:S(2)}, u32[]{:S(2)}) collective-permute-start(bf16[4,4096]{1,0:T(4,128)(2,1)S(1)} %shard_map.136), channel_id=1, source_target_pairs={{0,6},{1,7},{2,4},{3,5},{4,2},{5,3},{6,0},{7,1},{8,14},{9,15},{10,... | collective-permute-start | bytes 98312 | tf_op jit(solution)/shard_map/ppermute | solution.py:29
  51.3 1.1 %collective-permute-done.20 = bf16[4,4096]{1,0:T(4,128)(2,1)S(1)} collective-permute-done((bf16[4,4096]{1,0:T(4,128)(2,1)S(1)}, bf16[4,4096]{1,0:T(4,128)(2,1)S(1)}, u32[]{:S(2)}, u32[]{:S(2)}) %collective-permute-start.20) | collective-permute-done | bytes 32800 | tf_op jit(solution)/shard_map/ppermute | solution.py:29
  (57 shorter events, 9.3 us)
Async XLA Ops:
  1.0 4.3 %collective-permute-start.2 = (bf16[1,8832]{1,0:T(2,128)(2,1)S(1)}, bf16[1,8832]{1,0:T(2,128)(2,1)S(1)}, u32[]{:S(2)}, u32[]{:S(2)}) collective-permute-start(bf16[1,8832]{1,0:T(2,128)(2,1)S(1)} %get-tuple-element.34.refs_1_), channel_id=1, source_target_pairs={{0,12},{4,8},{8,4},{12,0},{1,13},{5,9},{9,5},{13,1},{2,14},{6,10},... | collective-permute-start | bytes 53000 | tf_op jit(solution)/shard_map/ppermute | solution.py:358
  3.5 4.0 %collective-permute-start.1 = (bf16[1,8832]{1,0:T(2,128)(2,1)S(1)}, bf16[1,8832]{1,0:T(2,128)(2,1)S(1)}, u32[]{:S(2)}, u32[]{:S(2)}) collective-permute-start(bf16[1,8832]{1,0:T(2,128)(2,1)S(1)} %get-tuple-element.34.refs_1_), channel_id=1, source_target_pairs={{0,8},{4,12},{8,0},{12,4},{1,9},{5,13},{9,1},{13,5},{2,10},{6,14},... | collective-permute-start | bytes 53000 | tf_op jit(solution)/shard_map/ppermute | solution.py:358
  4.2 3.4 %collective-permute-start = (bf16[1,8832]{1,0:T(2,128)(2,1)S(1)}, bf16[1,8832]{1,0:T(2,128)(2,1)S(1)}, u32[]{:S(2)}, u32[]{:S(2)}) collective-permute-start(bf16[1,8832]{1,0:T(2,128)(2,1)S(1)} %get-tuple-element.34.refs_1_), channel_id=1, source_target_pairs={{0,4},{4,0},{8,12},{12,8},{1,5},{5,1},{9,13},{13,9},{2,6},{6,2},{1... | collective-permute-start | bytes 53000 | tf_op jit(solution)/shard_map/ppermute | solution.py:358
  8.1 4.0 %collective-permute-start.3 = (bf16[4,1024]{1,0:T(4,128)(2,1)S(1)}, bf16[4,1024]{1,0:T(4,128)(2,1)S(1)}, u32[]{:S(2)}, u32[]{:S(2)}) collective-permute-start(bf16[4,1024]{1,0:T(4,128)(2,1)S(1)} %get-tuple-element.39), channel_id=1, source_target_pairs={{0,5},{1,4},{2,7},{3,6},{4,1},{5,0},{6,3},{7,2},{8,13},{9,12},{10,... | collective-permute-start | bytes 24584 | tf_op jit(solution)/shard_map/ppermute | solution.py:29
  9.2 4.3 %collective-permute-start.4 = (bf16[4,1024]{1,0:T(4,128)(2,1)S(1)}, bf16[4,1024]{1,0:T(4,128)(2,1)S(1)}, u32[]{:S(2)}, u32[]{:S(2)}) collective-permute-start(bf16[4,1024]{1,0:T(4,128)(2,1)S(1)} %get-tuple-element.40), channel_id=1, source_target_pairs={{0,6},{1,7},{2,4},{3,5},{4,2},{5,3},{6,0},{7,1},{8,14},{9,15},{10,... | collective-permute-start | bytes 24584 | tf_op jit(solution)/shard_map/ppermute | solution.py:29
  12.1 5.0 %collective-permute-start.5 = (bf16[4,1024]{1,0:T(4,128)(2,1)S(1)}, bf16[4,1024]{1,0:T(4,128)(2,1)S(1)}, u32[]{:S(2)}, u32[]{:S(2)}) collective-permute-start(bf16[4,1024]{1,0:T(4,128)(2,1)S(1)} %get-tuple-element.41), channel_id=1, source_target_pairs={{0,7},{1,6},{2,5},{3,4},{4,3},{5,2},{6,1},{7,0},{8,15},{9,14},{10,... | collective-permute-start | bytes 24584 | tf_op jit(solution)/shard_map/ppermute | solution.py:29
  18.2 3.8 %collective-permute-start.6 = (bf16[4,4096]{1,0:T(4,128)(2,1)S(1)}, bf16[4,4096]{1,0:T(4,128)(2,1)S(1)}, u32[]{:S(2)}, u32[]{:S(2)}) collective-permute-start(bf16[4,4096]{1,0:T(4,128)(2,1)S(1)} %get-tuple-element.43), channel_id=1, source_target_pairs={{0,5},{1,4},{2,7},{3,6},{4,1},{5,0},{6,3},{7,2},{8,13},{9,12},{10,... | collective-permute-start | bytes 98312 | tf_op jit(solution)/shard_map/ppermute | solution.py:29
  18.2 4.4 %collective-permute-start.7 = (bf16[4,4096]{1,0:T(4,128)(2,1)S(1)}, bf16[4,4096]{1,0:T(4,128)(2,1)S(1)}, u32[]{:S(2)}, u32[]{:S(2)}) collective-permute-start(bf16[4,4096]{1,0:T(4,128)(2,1)S(1)} %get-tuple-element.44), channel_id=1, source_target_pairs={{0,6},{1,7},{2,4},{3,5},{4,2},{5,3},{6,0},{7,1},{8,14},{9,15},{10,... | collective-permute-start | bytes 98312 | tf_op jit(solution)/shard_map/ppermute | solution.py:29
  18.7 5.6 %collective-permute-start.8 = (bf16[4,4096]{1,0:T(4,128)(2,1)S(1)}, bf16[4,4096]{1,0:T(4,128)(2,1)S(1)}, u32[]{:S(2)}, u32[]{:S(2)}) collective-permute-start(bf16[4,4096]{1,0:T(4,128)(2,1)S(1)} %get-tuple-element.45), channel_id=1, source_target_pairs={{0,7},{1,6},{2,5},{3,4},{4,3},{5,2},{6,1},{7,0},{8,15},{9,14},{10,... | collective-permute-start | bytes 98312 | tf_op jit(solution)/shard_map/ppermute | solution.py:29
  24.4 5.2 %collective-permute-start.11 = (bf16[4,4224]{1,0:T(4,128)(2,1)S(1)}, bf16[4,4224]{1,0:T(4,128)(2,1)S(1)}, u32[]{:S(2)}, u32[]{:S(2)}) collective-permute-start(bf16[4,4224]{1,0:T(4,128)(2,1)S(1)} %get-tuple-element.48), channel_id=1, source_target_pairs={{0,7},{1,6},{2,5},{3,4},{4,3},{5,2},{6,1},{7,0},{8,15},{9,14},{10,... | collective-permute-start | bytes 101384 | tf_op jit(solution)/shard_map/ppermute | solution.py:29
  27.5 4.3 %collective-permute-start.10 = (bf16[4,4224]{1,0:T(4,128)(2,1)S(1)}, bf16[4,4224]{1,0:T(4,128)(2,1)S(1)}, u32[]{:S(2)}, u32[]{:S(2)}) collective-permute-start(bf16[4,4224]{1,0:T(4,128)(2,1)S(1)} %get-tuple-element.48), channel_id=1, source_target_pairs={{0,6},{1,7},{2,4},{3,5},{4,2},{5,3},{6,0},{7,1},{8,14},{9,15},{10,... | collective-permute-start | bytes 101384 | tf_op jit(solution)/shard_map/ppermute | solution.py:29
  27.5 4.3 %collective-permute-start.9 = (bf16[4,4224]{1,0:T(4,128)(2,1)S(1)}, bf16[4,4224]{1,0:T(4,128)(2,1)S(1)}, u32[]{:S(2)}, u32[]{:S(2)}) collective-permute-start(bf16[4,4224]{1,0:T(4,128)(2,1)S(1)} %get-tuple-element.48), channel_id=1, source_target_pairs={{0,5},{1,4},{2,7},{3,6},{4,1},{5,0},{6,3},{7,2},{8,13},{9,12},{10,... | collective-permute-start | bytes 101384 | tf_op jit(solution)/shard_map/ppermute | solution.py:29
  28.6 7.3 %collective-permute-start.13 = (bf16[4,4224]{1,0:T(4,128)(2,1)S(1)}, bf16[4,4224]{1,0:T(4,128)(2,1)S(1)}, u32[]{:S(2)}, u32[]{:S(2)}) collective-permute-start(bf16[4,4224]{1,0:T(4,128)(2,1)S(1)} %get-tuple-element.48), channel_id=1, source_target_pairs={{0,12},{4,8},{8,4},{12,0},{1,13},{5,9},{9,5},{13,1},{2,14},{6,10},... | collective-permute-start | bytes 101384 | tf_op jit(solution)/shard_map/ppermute | solution.py:358
  29.6 6.2 %collective-permute-start.15 = (bf16[4,4224]{1,0:T(4,128)(2,1)S(1)}, bf16[4,4224]{1,0:T(4,128)(2,1)S(1)}, u32[]{:S(2)}, u32[]{:S(2)}) collective-permute-start(bf16[4,4224]{1,0:T(4,128)(2,1)S(1)} %shard_map.132), channel_id=1, source_target_pairs={{0,12},{4,8},{8,4},{12,0},{1,13},{5,9},{9,5},{13,1},{2,14},{6,10},... | collective-permute-start | bytes 101384 | tf_op jit(solution)/shard_map/ppermute | solution.py:358
  31.9 4.0 %collective-permute-start.14 = (bf16[2,4,4224]{2,1,0:T(4,128)(2,1)S(1)}, bf16[2,4,4224]{2,1,0:T(4,128)(2,1)S(1)}, u32[]{:S(2)}, u32[]{:S(2)}) collective-permute-start(bf16[2,4,4224]{2,1,0:T(4,128)(2,1)S(1)} %pad_maximum_fusion.2), channel_id=1, source_target_pairs={{0,12},{4,8},{8,4},{12,0},{1,13},{5,9},{9,5},{13,1},{2,14},{6,10},... | collective-permute-start | bytes 202760 | tf_op jit(solution)/shard_map/ppermute | solution.py:358
  32.9 3.5 %collective-permute-start.12 = (bf16[16,4224]{1,0:T(8,128)(2,1)S(1)}, bf16[16,4224]{1,0:T(8,128)(2,1)S(1)}, u32[]{:S(2)}, u32[]{:S(2)}) collective-permute-start(bf16[16,4224]{1,0:T(8,128)(2,1)S(1)} %pad_maximum_fusion.refs_1_), channel_id=1, source_target_pairs={{0,4},{4,0},{8,12},{12,8},{1,5},{5,1},{9,13},{13,9},{2,6},{6,2},{1... | collective-permute-start | bytes 405512 | tf_op jit(solution)/shard_map/ppermute | solution.py:358
  36.0 1.4 %collective-permute-start.16 = (bf16[16,4224]{1,0:T(8,128)(2,1)S(1)}, bf16[16,4224]{1,0:T(8,128)(2,1)S(1)}, u32[]{:S(2)}, u32[]{:S(2)}) collective-permute-start(bf16[16,4224]{1,0:T(8,128)(2,1)S(1)} %pad_maximum_fusion.1.refs_4_), channel_id=1, source_target_pairs={{0,4},{4,0},{8,12},{12,8},{1,5},{5,1},{9,13},{13,9},{2,6},{6,2},{1... | collective-permute-start | bytes 405512 | tf_op jit(solution)/shard_map/ppermute | solution.py:358
  39.3 1.4 %collective-permute-start.17 = (bf16[4,4,4096]{2,1,0:T(4,128)(2,1)S(1)}, bf16[4,4,4096]{2,1,0:T(4,128)(2,1)S(1)}, u32[]{:S(2)}, u32[]{:S(2)}) collective-permute-start(bf16[4,4,4096]{2,1,0:T(4,128)(2,1)S(1)} %get-tuple-element.52), channel_id=1, source_target_pairs={{0,4},{4,0},{8,12},{12,8},{1,5},{5,1},{9,13},{13,9},{2,6},{6,2},{1... | collective-permute-start | bytes 393224 | tf_op jit(solution)/shard_map/ppermute | solution.py:358
  39.7 2.9 %collective-permute-start.19 = (bf16[4,4,4096]{2,1,0:T(4,128)(2,1)S(1)}, bf16[4,4,4096]{2,1,0:T(4,128)(2,1)S(1)}, u32[]{:S(2)}, u32[]{:S(2)}) collective-permute-start(bf16[4,4,4096]{2,1,0:T(4,128)(2,1)S(1)} %get-tuple-element.54), channel_id=1, source_target_pairs={{0,4},{4,0},{8,12},{12,8},{1,5},{5,1},{9,13},{13,9},{2,6},{6,2},{1... | collective-permute-start | bytes 393224 | tf_op jit(solution)/shard_map/ppermute | solution.py:358
  40.7 7.9 %collective-permute-start.18 = (bf16[3,4,4096]{2,1,0:T(4,128)(2,1)S(1)}, bf16[3,4,4096]{2,1,0:T(4,128)(2,1)S(1)}, u32[]{:S(2)}, u32[]{:S(2)}) collective-permute-start(bf16[3,4,4096]{2,1,0:T(4,128)(2,1)S(1)} %add_convert_fusion), channel_id=1, source_target_pairs={{0,12},{4,8},{8,4},{12,0},{1,13},{5,9},{9,5},{13,1},{2,14},{6,10},... | collective-permute-start | bytes 294920 | tf_op jit(solution)/shard_map/ppermute | solution.py:358
  41.7 4.3 %collective-permute-start.22 = (bf16[1,4,4096]{2,1,0:T(4,128)(2,1)S(1)}, bf16[1,4,4096]{2,1,0:T(4,128)(2,1)S(1)}, u32[]{:S(2)}, u32[]{:S(2)}) collective-permute-start(bf16[1,4,4096]{2,1,0:T(4,128)(2,1)S(1)} %add_convert_fusion.2), channel_id=1, source_target_pairs={{0,12},{4,8},{8,4},{12,0},{1,13},{5,9},{9,5},{13,1},{2,14},{6,10},... | collective-permute-start | bytes 98312 | tf_op jit(solution)/shard_map/ppermute | solution.py:358
  46.1 5.2 %collective-permute-start.23 = (bf16[4,4096]{1,0:T(4,128)(2,1)S(1)}, bf16[4,4096]{1,0:T(4,128)(2,1)S(1)}, u32[]{:S(2)}, u32[]{:S(2)}) collective-permute-start(bf16[4,4096]{1,0:T(4,128)(2,1)S(1)} %shard_map.137), channel_id=1, source_target_pairs={{0,7},{1,6},{2,5},{3,4},{4,3},{5,2},{6,1},{7,0},{8,15},{9,14},{10,... | collective-permute-start | bytes 98312 | tf_op jit(solution)/shard_map/ppermute | solution.py:29
  48.7 3.7 %collective-permute-start.20 = (bf16[4,4096]{1,0:T(4,128)(2,1)S(1)}, bf16[4,4096]{1,0:T(4,128)(2,1)S(1)}, u32[]{:S(2)}, u32[]{:S(2)}) collective-permute-start(bf16[4,4096]{1,0:T(4,128)(2,1)S(1)} %shard_map.135), channel_id=1, source_target_pairs={{0,5},{1,4},{2,7},{3,6},{4,1},{5,0},{6,3},{7,2},{8,13},{9,12},{10,... | collective-permute-start | bytes 98312 | tf_op jit(solution)/shard_map/ppermute | solution.py:29
  48.8 4.3 %collective-permute-start.21 = (bf16[4,4096]{1,0:T(4,128)(2,1)S(1)}, bf16[4,4096]{1,0:T(4,128)(2,1)S(1)}, u32[]{:S(2)}, u32[]{:S(2)}) collective-permute-start(bf16[4,4096]{1,0:T(4,128)(2,1)S(1)} %shard_map.136), channel_id=1, source_target_pairs={{0,6},{1,7},{2,4},{3,5},{4,2},{5,3},{6,0},{7,1},{8,14},{9,15},{10,... | collective-permute-start | bytes 98312 | tf_op jit(solution)/shard_map/ppermute | solution.py:29
  (7 other events, 69.8 us)
